TPU v7x, 32 devices: a whole 2x2x4 slice. The times are simulated.
32 devices in a mesh: dp: 8 (over y, x, core), seq: 4 (over z).
Axes of the slice: x: 2, y: 2, z: 4, core: 2. Of those that a mesh axis runs over, the one named last changes fastest.
Arguments:
- hidden_in: bfloat16 [16, 1024, 768], P('dp', 'seq'), may hold values from -6 to 6
- segment_ids: int32 [16, 1024], P('dp'), may hold values from 0 to 7, never falling along the last dimension, each value on 1 to 512 neighbouring positions
- query_weight: bfloat16 [768, 768], P('dp'), may hold values from -0.21875 to 0.21875
- query_bias: bfloat16 [768], P('dp'), may hold values from -3 to 3
- key_weight: bfloat16 [768, 768], P('dp'), may hold values from -0.21875 to 0.21875
- value_weight: bfloat16 [768, 768], P('dp'), may hold values from -0.21875 to 0.21875
- value_bias: bfloat16 [768], P('dp'), may hold values from -3 to 3
- out_weight: bfloat16 [768, 768], P('dp'), may hold values from -0.875 to 0.875
- out_bias: bfloat16 [768], P('dp'), may hold values from -3 to 3
- first_gain: bfloat16 [768], P('dp'), may hold values from 0.5 to 1.5
- first_shift: bfloat16 [768], P('dp'), may hold values from -3 to 3
- up_weight: bfloat16 [768, 3072], P('dp'), may hold values from -0.21875 to 0.21875
- up_bias: bfloat16 [3072], P('dp'), may hold values from -3 to 3
- down_weight: bfloat16 [3072, 768], P('dp'), may hold values from -0.109375 to 0.109375
- down_bias: bfloat16 [768], P('dp'), may hold values from -3 to 3
- second_gain: bfloat16 [768], P('dp'), may hold values from 0.5 to 1.5
- second_shift: bfloat16 [768], P('dp'), may hold values from -3 to 3
- cotangent: bfloat16 [16, 1024, 768], P('dp', 'seq'), may hold values from -6 to 6
Outputs:
- layer_out: bfloat16 [16, 1024, 768], P('dp', 'seq')
- input_gradient: float32 [16, 1024, 768], P('dp', 'seq')
- query_weight_grad: float32 [768, 768], P(('dp', 'seq'))
- query_bias_grad: float32 [768], P(('dp', 'seq'))
- key_weight_grad: float32 [768, 768], P(('dp', 'seq'))
- value_weight_grad: float32 [768, 768], P(('dp', 'seq'))
- value_bias_grad: float32 [768], P(('dp', 'seq'))
- out_weight_grad: float32 [768, 768], P(('dp', 'seq'))
- out_bias_grad: float32 [768], P(('dp', 'seq'))
- first_gain_grad: float32 [768], P(('dp', 'seq'))
- first_shift_grad: float32 [768], P(('dp', 'seq'))
- up_weight_grad: float32 [768, 3072], P(('dp', 'seq'))
- up_bias_grad: float32 [3072], P(('dp', 'seq'))
- down_weight_grad: float32 [3072, 768], P(('dp', 'seq'))
- down_bias_grad: float32 [768], P(('dp', 'seq'))
- second_gain_grad: float32 [768], P(('dp', 'seq'))
- second_shift_grad: float32 [768], P(('dp', 'seq'))
All inputs are finite; a program needn't handle non-finite values.
Results may differ from a plain program's by a relative error of at most 0.013.
Values may be sent and summed in bfloat16 or wider, within the bound.
No kernel may reach another device: no remote copies, remote signals or barrier semaphores. Data moves between devices by JAX's collectives and lax.ppermute only.
A program may use at most 128 MiB of HBM per device.

v0:
```python
import functools
import math

import jax
import jax.numpy as jnp
from jax import lax
from jax.experimental import pallas as pl
from jax.experimental.pallas import tpu as pltpu
from jax.sharding import PartitionSpec as P

HEAD_DIM = 64
LANES = 128
NEGATIVE = -1e30


def nt(left, right):
    return lax.dot_general(left, right, (((1,), (1,)), ((), ())), preferred_element_type=jnp.float32)


def nn(left, right):
    return lax.dot_general(left, right, (((1,), (0,)), ((), ())), preferred_element_type=jnp.float32)


def head_parts(block):
    lane = lax.broadcasted_iota(jnp.int32, block.shape, 1)
    zero = jnp.zeros_like(block)
    return (jnp.where(lane < HEAD_DIM, block, zero), jnp.where(lane < HEAD_DIM, zero, block))


def same_document(column_tile, row):
    column = jnp.concatenate([column_tile] * (row.shape[1] // LANES), axis=1)
    return column == jnp.broadcast_to(row, column.shape)


def pair_lanes(pair):
    return slice(pair * LANES, (pair + 1) * LANES)


def chunk_of(bounds, block, step, chunks):
    own = bounds[4 * block + 1] - bounds[4 * block]
    return jnp.where(step < own, bounds[4 * block] + step, chunks + bounds[4 * block + 2] + step - own)


def live_chunks(bounds, block):
    return bounds[4 * block + 1] - bounds[4 * block] + bounds[4 * block + 3] - bounds[4 * block + 2]


def forward_body(qblock, chunk, bounds, q_ref, k_ref, v_ref, ko_ref, vo_ref, sq_ref, sk_ref, o_ref, lse_ref, kall, vt):
    half, lanes = k_ref.shape
    chunks, pairs = half // chunk, lanes // LANES
    for j in range(chunks):
        rows = slice(j * chunk, (j + 1) * chunk)
        kall[j] = k_ref[rows, :]
        kall[chunks + j] = ko_ref[rows, :]
        vt[j] = v_ref[rows, :].T
        vt[chunks + j] = vo_ref[rows, :].T
    for b in range(q_ref.shape[0] // qblock):
        span = slice(b * qblock, (b + 1) * qblock)
        parts = []
        for pair in range(pairs):
            parts += head_parts(q_ref[span, pair_lanes(pair)] * jnp.bfloat16(HEAD_DIM**-0.5))
        row = sq_ref[:, span]

        def one(step, carry):
            j = chunk_of(bounds, b, step, chunks)
            mask = same_document(sk_ref[j], row)
            scores = [jnp.where(mask, nt(kall[j, :, pair_lanes(h // 2)], part), NEGATIVE) for h, part in enumerate(parts)]
            out = []
            for h, score in enumerate(scores):
                top, total, acc = carry[h]
                new_top = jnp.maximum(top, jnp.max(score, axis=0, keepdims=True))
                expo = jnp.exp(score - new_top)
                scale = jnp.exp(top - new_top)
                total = total * scale + jnp.sum(expo, axis=0, keepdims=True)
                acc = acc * scale + nn(vt[j, h * HEAD_DIM : (h + 1) * HEAD_DIM, :], expo.astype(jnp.bfloat16))
                out.append((new_top, total, acc))
            return tuple(out)

        init = (
            jnp.full((1, qblock), NEGATIVE, jnp.float32),
            jnp.zeros((1, qblock), jnp.float32),
            jnp.zeros((HEAD_DIM, qblock), jnp.float32),
        )
        carry = lax.fori_loop(0, live_chunks(bounds, b), one, (init,) * len(parts))
        result = jnp.concatenate([acc / total for _, total, acc in carry], axis=0)
        o_ref[span, :] = result.T.astype(jnp.bfloat16)
        for h, (top, total, _) in enumerate(carry):
            lse_ref[0, h : h + 1, span] = top + jnp.log(total)


def backward_body(
    qblock, chunk, bounds, q_ref, k_ref, v_ref, ko_ref, vo_ref, o_ref, do_ref, lse_ref, sq_ref, sk_ref,
    dq_ref, dk_ref, dv_ref, far_ref, kall, vall, kt, dkall, dvall,
):
    half, lanes = k_ref.shape
    chunks, pairs = half // chunk, lanes // LANES
    for j in range(chunks):
        rows = slice(j * chunk, (j + 1) * chunk)
        kall[j] = k_ref[rows, :]
        kall[chunks + j] = ko_ref[rows, :]
        vall[j] = v_ref[rows, :]
        vall[chunks + j] = vo_ref[rows, :]
        kt[j] = k_ref[rows, :].T
        kt[chunks + j] = ko_ref[rows, :].T
    dkall[...] = jnp.zeros_like(dkall)
    dvall[...] = jnp.zeros_like(dvall)
    for b in range(q_ref.shape[0] // qblock):
        span = slice(b * qblock, (b + 1) * qblock)
        parts, dparts, delta = [], [], []
        for pair in range(pairs):
            parts.append(head_parts(q_ref[span, pair_lanes(pair)] * jnp.bfloat16(HEAD_DIM**-0.5)))
            dparts.append(head_parts(do_ref[span, pair_lanes(pair)]))
            product = do_ref[span, pair_lanes(pair)].astype(jnp.float32) * o_ref[span, pair_lanes(pair)].astype(jnp.float32)
            product = product.T
            delta += [jnp.sum(product[h * HEAD_DIM : (h + 1) * HEAD_DIM], axis=0, keepdims=True) for h in range(2)]
        both = [jnp.concatenate(p, axis=0) for p in parts]
        dboth = [jnp.concatenate(p, axis=0) for p in dparts]
        row = sq_ref[:, span]
        lse = [lse_ref[0, h : h + 1, span] for h in range(2 * pairs)]

        def one(step, carry):
            j = chunk_of(bounds, b, step, chunks)
            mask = same_document(sk_ref[j], row)
            out = []
            for pair in range(pairs):
                key, val = kall[j, :, pair_lanes(pair)], vall[j, :, pair_lanes(pair)]
                probs, grads = [], []
                for side in range(2):
                    h = 2 * pair + side
                    score = jnp.where(mask, nt(key, parts[pair][side]), NEGATIVE)
                    prob = jnp.exp(score - lse[h])
                    grad = (prob * (nt(val, dparts[pair][side]) - delta[h])).astype(jnp.bfloat16)
                    probs.append(prob.astype(jnp.bfloat16))
                    grads.append(grad)
                    out.append(carry[h] + nn(kt[j, h * HEAD_DIM : (h + 1) * HEAD_DIM, :], grad))
                dvall[j, :, pair_lanes(pair)] += nn(jnp.concatenate(probs, axis=1), dboth[pair])
                dkall[j, :, pair_lanes(pair)] += nn(jnp.concatenate(grads, axis=1), both[pair])
            return tuple(out)

        zero = jnp.zeros((HEAD_DIM, qblock), jnp.float32)
        carry = lax.fori_loop(0, live_chunks(bounds, b), one, (zero,) * (2 * pairs))
        dq_ref[span, :] = (jnp.concatenate(carry, axis=0).T * HEAD_DIM**-0.5).astype(jnp.bfloat16)
    for j in range(chunks):
        rows = slice(j * chunk, (j + 1) * chunk)
        dk_ref[rows, :] = dkall[j]
        dv_ref[rows, :] = dvall[j]
        far_ref[0, rows, :] = dkall[chunks + j].astype(jnp.bfloat16)
        far_ref[1, rows, :] = dvall[chunks + j].astype(jnp.bfloat16)


def chunk_bounds(own, other, qblock, chunk):
    rows = own.reshape(-1, qblock)
    low, high = rows[:, 0], rows[:, -1]
    found = []
    for part in (own, other):
        tiles = part.reshape(-1, chunk)
        live = (tiles[None, :, 0] <= high[:, None]) & (tiles[None, :, -1] >= low[:, None])
        first = jnp.argmax(live, axis=1).astype(jnp.int32)
        found += [first, first + jnp.sum(live, axis=1).astype(jnp.int32)]
    return jnp.stack(found, axis=1).reshape(-1)


def segment_tiles(own, other, chunk):
    both = jnp.concatenate([own, other])
    return jnp.broadcast_to(both[:, None], (both.shape[0], LANES)).reshape(-1, chunk, LANES)


def attend_forward(query, keys, values, keys_other, values_other, row, tiles, bounds, qblock, chunk, pairs):
    tokens, width = query.shape
    half = keys.shape[0]
    lanes = pairs * LANES
    steps = width // lanes
    q = pl.BlockSpec((tokens, lanes), lambda i, *_: (0, i))
    k = pl.BlockSpec((half, lanes), lambda i, *_: (0, i))
    lse = pl.BlockSpec((1, 8, tokens), lambda i, *_: (i, 0, 0))
    area = tokens * half * 2
    return pl.pallas_call(
        functools.partial(forward_body, qblock, chunk),
        grid_spec=pltpu.PrefetchScalarGridSpec(
            num_scalar_prefetch=1,
            grid=(steps,),
            in_specs=[q, k, k, k, k, pl.BlockSpec((1, tokens), lambda i, *_: (0, 0)), pl.BlockSpec(tiles.shape, lambda i, *_: (0, 0, 0))],
            out_specs=[q, lse],
            scratch_shapes=[
                pltpu.VMEM((2 * half // chunk, chunk, lanes), jnp.bfloat16),
                pltpu.VMEM((2 * half // chunk, lanes, chunk), jnp.bfloat16),
            ],
        ),
        out_shape=[
            jax.ShapeDtypeStruct((tokens, width), jnp.bfloat16),
            jax.ShapeDtypeStruct((steps, 8, tokens), jnp.float32),
        ],
        cost_estimate=pl.CostEstimate(flops=1, transcendentals=0, bytes_accessed=1),
        compiler_params=pltpu.CompilerParams(vmem_limit_bytes=32 << 20),
        name="attend_forward",
    )(bounds, query, keys, values, keys_other, values_other, row, tiles)


def attend_back(query, keys, values, keys_other, values_other, attended, grad, lse_rows, row, tiles, bounds, qblock, chunk, pairs, side):
    tokens, width = query.shape
    half = keys.shape[0]
    lanes = pairs * LANES
    q = pl.BlockSpec((tokens, lanes), lambda i, *_: (0, side))
    k = pl.BlockSpec((half, lanes), lambda i, *_: (0, side))
    lse = pl.BlockSpec((1, 8, tokens), lambda i, *_: (side, 0, 0))
    to_q = pl.BlockSpec((tokens, lanes), lambda i, *_: (0, 0))
    to_k = pl.BlockSpec((half, lanes), lambda i, *_: (0, 0))
    area = tokens * half * 2
    shape = lambda rows, dtype: jax.ShapeDtypeStruct((rows, lanes), dtype)
    n = 2 * half // chunk
    return pl.pallas_call(
        functools.partial(backward_body, qblock, chunk),
        grid_spec=pltpu.PrefetchScalarGridSpec(
            num_scalar_prefetch=1,
            grid=(1,),
            in_specs=[q, k, k, k, k, q, q, lse, pl.BlockSpec((1, tokens), lambda i, *_: (0, 0)), pl.BlockSpec(tiles.shape, lambda i, *_: (0, 0, 0))],
            out_specs=[to_q, to_k, to_k, pl.BlockSpec((2, half, lanes), lambda i, *_: (0, 0, 0))],
            scratch_shapes=[
                pltpu.VMEM((n, chunk, lanes), jnp.bfloat16),
                pltpu.VMEM((n, chunk, lanes), jnp.bfloat16),
                pltpu.VMEM((n, lanes, chunk), jnp.bfloat16),
                pltpu.VMEM((n, chunk, lanes), jnp.float32),
                pltpu.VMEM((n, chunk, lanes), jnp.float32),
            ],
        ),
        out_shape=[
            shape(tokens, jnp.bfloat16), shape(half, jnp.float32), shape(half, jnp.float32), jax.ShapeDtypeStruct((2, half, lanes), jnp.bfloat16),
        ],
        cost_estimate=pl.CostEstimate(flops=1, transcendentals=0, bytes_accessed=1),
        compiler_params=pltpu.CompilerParams(vmem_limit_bytes=48 << 20),
        name="attend_back",
    )(bounds, query, keys, values, keys_other, values_other, attended, grad, lse_rows, row, tiles)


AXES = ("dp", "seq")
PARTS = 8
SHARDS = 6
epsilon = 1e-12


def tn(left, right):
    return lax.dot_general(left, right, (((0,), (0,)), ((), ())), preferred_element_type=jnp.float32)


def norm_parts(value):
    center = value - jnp.mean(value, axis=-1, keepdims=True)
    spread = jnp.mean(center * center, axis=-1, keepdims=True)
    scale = lax.rsqrt(spread + epsilon)
    return (center * scale, scale)


def norm_back(upstream, normal, scale, gain):
    scaled = upstream * gain
    return scale * (
        scaled
        - jnp.mean(scaled, axis=-1, keepdims=True)
        - normal * jnp.mean(scaled * normal, axis=-1, keepdims=True)
    )


def row_sum(matrix):
    return jnp.sum(matrix.astype(jnp.float32), axis=0, keepdims=True)


def parts_of(refs):
    own, own_far, near_x, near_y, near_d, far = refs
    rows = own.shape[0]
    near = [(ref, 0, rows) for ref in (own, own_far, near_x, near_y, near_d)]
    other = [(far, i * rows, rows) for i in range(3)]
    return [near[0], near[1], near[2], other[0], near[3], other[1], near[4], other[2]]


def load_pieces(me, pieces, targets, sems):
    copies = [[] for _ in targets]
    for place, (ref, first, rows) in enumerate(pieces):
        where = pl.ds(pl.multiple_of((me ^ place) * rows, 32), rows)
        for i, (target, columns) in enumerate(targets):
            copy = pltpu.make_async_copy(ref.at[first : first + rows, columns], target.at[where, :], sems.at[i, place])
            copy.start()
            copies[i].append(copy)
    return copies


def wait_all(copies):
    for copy in copies:
        copy.wait()


def step_of(block, size):
    return pl.ds(pl.multiple_of(block * size, size), size)


BLOCK = 256
ROWS = 256


def widen_body(scalars, *refs):
    pieces = parts_of(refs[:SHARDS])
    (attended, tokens, vec, up_add, normal_ref, scale_ref, low_ref, active_ref, slope_ref, wo_out, wu_out, wo, wu, sems, out_sems) = refs[SHARDS:]
    width, wide = wu.shape
    loads = load_pieces(scalars[0], pieces, [(wo, slice(0, width)), (wu, slice(width, width + wide))], sems)
    wait_all(loads[0])

    @pl.loop(0, tokens.shape[0] // ROWS)
    def _(i):
        rows = step_of(i, ROWS)
        branch = nn(attended[rows, :], wo[...]) + vec[2:3, :]
        normal, scale = norm_parts(tokens[rows, :].astype(jnp.float32) + branch)
        first = normal * vec[3:4, :] + vec[4:5, :]
        normal_ref[rows, :] = normal
        scale_ref[rows, :] = jnp.broadcast_to(scale, (ROWS, LANES))
        low_ref[rows, :] = first.astype(jnp.bfloat16)

    wait_all(loads[1])
    saves = [pltpu.make_async_copy(wo, wo_out, out_sems.at[0]), pltpu.make_async_copy(wu, wu_out, out_sems.at[1])]
    for save in saves:
        save.start()

    @pl.loop(0, wide // BLOCK)
    def _(j):
        cols = step_of(j, BLOCK)
        inner = nn(low_ref[...], wu[:, cols]) + up_add[:, cols]
        cumulative = 0.5 * (1.0 + lax.erf(inner * math.sqrt(0.5)))
        density = jnp.exp(-0.5 * inner * inner) * (1.0 / math.sqrt(2.0 * math.pi))
        active_ref[:, cols] = (inner * cumulative).astype(jnp.bfloat16)
        slope_ref[:, cols] = (cumulative + inner * density).astype(jnp.bfloat16)

    wait_all(saves)


def narrow_body(scalars, *refs):
    pieces = parts_of(refs[:SHARDS])
    (active, normal_one, vec, upstream, out_ref, grad_ref, low_ref, sums_ref, send_ref, keep_ref, wd_out, wd, sums, sems, out_sem) = refs[SHARDS:]
    wide, width = wd.shape
    (loads,) = load_pieces(scalars[0], pieces, [(wd, slice(0, width))], sems)
    wait_all(loads)
    save = pltpu.make_async_copy(wd, wd_out, out_sem)
    save.start()
    sums[...] = jnp.zeros_like(sums)

    @pl.loop(0, normal_one.shape[0] // ROWS)
    def _(i):
        rows = step_of(i, ROWS)
        second = nn(active[rows, :], wd[...]) + vec[5:6, :]
        normal, scale = norm_parts(normal_one[rows, :] * vec[3:4, :] + vec[4:5, :] + second)
        out_ref[rows, :] = (normal * vec[6:7, :] + vec[7:8, :]).astype(jnp.bfloat16)
        up = upstream[rows, :].astype(jnp.float32)
        grad = norm_back(up, normal, scale, vec[6:7, :])
        low = grad.astype(jnp.bfloat16)
        grad_ref[rows, :] = grad
        low_ref[rows, :] = low
        sums[0:1, :] += row_sum(low)
        sums[1:2, :] += row_sum(up * normal)
        sums[2:3, :] += row_sum(up)

    sums_ref[...] = sums[...]
    size = wide // PARTS

    @pl.loop(0, PARTS // 2)
    def _(i):
        send_ref[i] = tn(active[:, step_of(2 * i + 1 - scalars[1], size)], low_ref[...]).astype(jnp.bfloat16)
        keep_ref[i] = tn(active[:, step_of(2 * i + scalars[1], size)], low_ref[...]).astype(jnp.bfloat16)

    save.wait()


def turn_parts(core, turned, ordered):
    for i in range(PARTS // 2):
        ordered[0, i] = turned[2 * i + 1 - core]
        ordered[1, i] = turned[2 * i + core]


def inner_back_body(scalars, low, wd, slope, first_low, grad_ref, sums_ref, send_ref, keep_ref, turned, ordered):
    size = first_low.shape[1] // PARTS
    flipped = first_low[...].T
    for i in range(PARTS):
        turned[i] = flipped[i * size : (i + 1) * size, :]
    turn_parts(scalars[1], turned, ordered)
    rows = (PARTS // 2) * size

    @pl.loop(0, slope.shape[1] // BLOCK)
    def _(j):
        cols = step_of(j, BLOCK)
        grad = (nt(low[...], wd[cols, :]) * slope[:, cols].astype(jnp.float32)).astype(jnp.bfloat16)
        grad_ref[:, cols] = grad
        sums_ref[:, cols] = row_sum(grad)
        for side, ref in enumerate((send_ref, keep_ref)):
            left = ordered[side].reshape(rows, low.shape[0])
            ref[:, :, cols] = nn(left, grad).astype(jnp.bfloat16).reshape(PARTS // 2, size, BLOCK)


def outer_back_body(scalars, grad, wu, up_grad, normal_ref, scale_ref, vec, wo, attended, sum_ref, result_ref, sums_ref, send_ref, keep_ref, low, sums, turned):
    width = wo.shape[0]
    sums[...] = jnp.zeros_like(sums)

    @pl.loop(0, grad.shape[0] // ROWS)
    def _(i):
        rows = step_of(i, ROWS)
        first = up_grad[rows, :] + nt(grad[rows, :], wu[...])
        normal = normal_ref[rows, :]
        total = norm_back(first, normal, scale_ref[rows, 0:1], vec[3:4, :])
        branch = total.astype(jnp.bfloat16)
        sum_ref[rows, :] = total
        low[rows, :] = branch
        result_ref[rows, :] = nt(branch, wo[...]).astype(jnp.bfloat16)
        sums[0:1, :] += row_sum(branch)
        sums[1:2, :] += row_sum(first * normal)
        sums[2:3, :] += row_sum(first)

    sums_ref[...] = sums[...]
    size = width // PARTS
    product = tn(attended[...], low[...]).astype(jnp.bfloat16)
    for i in range(PARTS):
        turned[i] = product[i * size : (i + 1) * size, :]
    for i in range(PARTS // 2):
        send_ref[i] = turned[2 * i + 1 - scalars[1]]
        keep_ref[i] = turned[2 * i + scalars[1]]


def whole_call(body, name, scalars, hbm, inputs, outputs, hbm_outputs, scratch, flops):
    shape_of = lambda x: jax.ShapeDtypeStruct(x.shape, x.dtype)
    full = lambda x: pl.BlockSpec(x.shape, lambda i, *_, n=len(x.shape): (0,) * n)
    stay = pl.BlockSpec(memory_space=pl.ANY)
    return pl.pallas_call(
        body,
        grid_spec=pltpu.PrefetchScalarGridSpec(
            num_scalar_prefetch=1,
            grid=(1,),
            in_specs=[stay] * len(hbm) + [full(x) for x in inputs],
            out_specs=[full(x) for x in outputs] + [stay] * len(hbm_outputs),
            scratch_shapes=scratch,
        ),
        out_shape=[shape_of(x) for x in list(outputs) + list(hbm_outputs)],
        cost_estimate=pl.CostEstimate(flops=flops, transcendentals=0, bytes_accessed=1),
        compiler_params=pltpu.CompilerParams(vmem_limit_bytes=56 << 20),
        name=name,
    )(scalars, *hbm, *inputs)


def array(dtype, *shape):
    return jax.ShapeDtypeStruct(shape, dtype)


def widen(scalars, pieces, attended, tokens, vec, up_add):
    count, width = tokens.shape
    wide = up_add.shape[1]
    f32, b16 = jnp.float32, jnp.bfloat16
    return whole_call(
        widen_body, "widen", scalars, pieces, [attended, tokens, vec, up_add],
        [array(f32, count, width), array(f32, count, LANES), array(b16, count, width),
         array(b16, count, wide), array(b16, count, wide)],
        [array(b16, width, width), array(b16, width, wide)],
        [pltpu.VMEM((width, width), b16), pltpu.VMEM((width, wide), b16), pltpu.SemaphoreType.DMA((2, PARTS)),
         pltpu.SemaphoreType.DMA((2,))], 1,
    )


def narrow(scalars, pieces, active, normal, vec, upstream):
    count, wide = active.shape
    width = normal.shape[1]
    f32, b16 = jnp.float32, jnp.bfloat16
    half = array(b16, PARTS // 2, wide // PARTS, width)
    return whole_call(
        narrow_body, "narrow", scalars, pieces, [active, normal, vec, upstream],
        [array(b16, count, width), array(f32, count, width), array(b16, count, width), array(f32, 8, width), half, half],
        [array(b16, wide, width)],
        [pltpu.VMEM((wide, width), b16), pltpu.VMEM((8, width), f32), pltpu.SemaphoreType.DMA((1, PARTS)), pltpu.SemaphoreType.DMA], 1,
    )


def inner_back(scalars, low, wd, slope, first_low):
    count, wide = slope.shape
    width = low.shape[1]
    size = width // PARTS
    f32, b16 = jnp.float32, jnp.bfloat16
    half = array(b16, PARTS // 2, size, wide)
    return whole_call(
        inner_back_body, "inner_back", scalars, [], [low, wd, slope, first_low],
        [array(b16, count, wide), array(f32, 1, wide), half, half], [],
        [pltpu.VMEM((PARTS, size, count), b16), pltpu.VMEM((2, PARTS // 2, size, count), b16)], 1,
    )


def outer_back(scalars, grad, wu, up_grad, normal, scale, vec, wo, attended):
    count, width = normal.shape
    f32, b16 = jnp.float32, jnp.bfloat16
    half = array(b16, PARTS // 2, width // PARTS, width)
    return whole_call(
        outer_back_body, "outer_back", scalars, [], [grad, wu, up_grad, normal, scale, vec, wo, attended],
        [array(f32, count, width), array(b16, count, width), array(f32, 8, width), half, half], [],
        [pltpu.VMEM((count, width), b16), pltpu.VMEM((8, width), f32), pltpu.VMEM((PARTS, width // PARTS, width), b16)], 1,
    )


def split_rows(core, parts, send, keep, cols):
    for i in range(PARTS // 2):
        send[i, :, cols] = parts[2 * i + 1 - core]
        keep[i, :, cols] = parts[2 * i + core]


def sums_to_slots(core, lines, parts, send, keep, first):
    turned = lines[...].T.astype(jnp.bfloat16)
    rows = turned.shape[0] // PARTS
    for i in range(PARTS):
        parts[i] = turned[i * rows : (i + 1) * rows, :]
    split_rows(core, parts, send, keep, slice(first, first + LANES))


def qkv_back_body(side, scalars, dq, dk, dv, far, ordered, weight, gradient, *refs):
    core = scalars[1]
    if side == 0:
        out_send, out_keep, sums_one, sums_two, wide_sums, send, keep, result, sums_ref, both, lines, parts = refs
    else:
        first_sums, send, keep, result, sums_ref, both, lines, parts = refs
    half = dq.shape[1]
    both[:, :half] = dq[...]
    both[:, half : 2 * half] = (dk[...] + far[0].astype(jnp.float32)).astype(jnp.bfloat16)
    both[:, 2 * half :] = (dv[...] + far[1].astype(jnp.float32)).astype(jnp.bfloat16)
    sums_ref[...] = jnp.zeros_like(sums_ref)
    sums_ref[0:1, :] = row_sum(dq[...])
    sums_ref[1:2, :] = row_sum(both[:, 2 * half :])
    rows = ordered.shape[1] * ordered.shape[2]
    for i, ref in enumerate((send, keep)):
        left = ordered[i].reshape(rows, ordered.shape[3])
        product = nn(left, both[...]).astype(jnp.bfloat16)
        ref[:, :, : 3 * half] = product.reshape(ordered.shape[1], ordered.shape[2], 3 * half)
    lines[...] = jnp.zeros_like(lines)
    if side == 0:
        width = out_send.shape[2]
        send[:, :, 3 * half : 3 * half + width] = out_send[...]
        keep[:, :, 3 * half : 3 * half + width] = out_keep[...]
        lines[0:8, :] = sums_one[...]
        lines[8:16, :] = sums_two[...]
        lines[16:24, :] = wide_sums[...]
        sums_to_slots(core, lines, parts, send, keep, 3 * half + width)
    else:
        lines[0:8, :half] = first_sums[...]
        lines[0:8, half:] = sums_ref[...]
        sums_to_slots(core, lines, parts, send, keep, 3 * half)
    result[...] = (gradient[...] + nt(both[...], weight[side])).astype(result.dtype)


def qkv_back(side, scalars, dq, dk, dv, far, ordered, weights, gradient, *more):
    count, half = dq.shape
    width = gradient.shape[1]
    f32, b16 = jnp.float32, jnp.bfloat16
    total = array(b16, PARTS // 2, width // PARTS, 3 * half + LANES + (width if side == 0 else 0))
    return whole_call(
        functools.partial(qkv_back_body, side), "qkv_back", scalars, [], [dq, dk, dv, far, ordered, weights, gradient, *more],
        [total, total, array(b16 if side else f32, count, width), array(f32, 8, half)], [],
        [pltpu.VMEM((count, 3 * half), b16), pltpu.VMEM((LANES, width), f32), pltpu.VMEM((PARTS, width // PARTS, LANES), b16)], 1,
    )


STRIPE = 32


def fold_body(plans, scalars, *refs):
    for item, (outer, inner, bit) in enumerate(plans):
        keep, got = refs[2 * item : 2 * item + 2]
        send, left = refs[2 * (len(plans) + item) : 2 * (len(plans) + item) + 2]
        mine = scalars[bit]
        rows = keep.shape[1]
        stripe = STRIPE if rows % STRIPE == 0 else rows

        @pl.loop(0, rows // stripe)
        def _(k):
            span = step_of(k, stripe) if stripe != rows else slice(None)
            for i in range(outer):
                for j in range(inner):
                    for target, side in ((send, 1 - mine), (left, mine)):
                        place = (2 * i + side) * inner + j
                        value = keep[place, span, :].astype(jnp.float32) + got[place, span, :].astype(jnp.float32)
                        target[i * inner + j, span, :] = value.astype(target.dtype)


def fold(scalars, items):
    outs, plans = [], []
    for keep, got, (outer, inner, bit) in items:
        shape = (keep.shape[0] // 2,) + keep.shape[1:]
        outs += [array(jnp.bfloat16, *shape), array(keep.dtype, *shape)]
        plans.append((outer, inner, bit))
    got = whole_call(
        functools.partial(fold_body, plans), "fold", scalars, [], [x for keep, got, _ in items for x in (keep, got)], outs, [], [], 1
    )
    return [(got[2 * i], got[2 * i + 1]) for i in range(len(items))]


def merge_body(shapes, scalars, *refs):
    send, left = refs[-2:]
    mine = scalars[4]
    low = send.shape[1]
    first = 0
    for item, (rows, wide) in enumerate(shapes):
        keep, got = refs[2 * item : 2 * item + 2]
        for part in range(rows // low):
            span = slice(part * low, (part + 1) * low)
            for high in range(2):
                for target, side in ((send, 1 - mine), (left, mine)):
                    value = keep[2 * high + side, span, :].astype(jnp.float32) + got[2 * high + side, span, :].astype(jnp.float32)
                    target[high, :, first : first + wide] = value.astype(target.dtype)
            first += wide


def merge(scalars, items, low):
    items = [(k.reshape(4, k.shape[-2] // 4, k.shape[-1]), g.reshape(4, g.shape[-2] // 4, g.shape[-1])) for k, g in items]
    shapes = [k.shape[1:] for k, _ in items]
    wide = sum(rows // low * n for rows, n in shapes)
    return whole_call(
        functools.partial(merge_body, shapes), "merge", scalars, [], [x for pair in items for x in pair],
        [array(jnp.bfloat16, 2, low, wide), array(jnp.float32, 2, low, wide)], [], [], 1,
    )


def last_ff_body(scalars, keep, got, down_ref, up_ref):
    low = keep.shape[1]
    width = down_ref.shape[1]
    for part in range(down_ref.shape[0] // low):
        cols = slice(part * width, (part + 1) * width)
        down_ref[part * low : (part + 1) * low, :] = keep[0, :, cols] + got[0, :, cols].astype(jnp.float32)
    cols = slice(4 * width, 4 * width + up_ref.shape[1])
    up_ref[...] = keep[0, :, cols] + got[0, :, cols].astype(jnp.float32)


def last_ff(scalars, keep, got, width):
    low = keep.shape[1]
    return whole_call(
        last_ff_body, "last_ff", scalars, [], [keep, got], [array(jnp.float32, 4 * low, width), array(jnp.float32, low, 4 * width)], [], [], 1
    )


def last_qkv_body(scalars, keep, got, query_ref, key_ref, value_ref, out_ref, small_ref, late_ref, turned):
    low = keep.shape[1]
    width = query_ref.shape[1]
    half = width // 2
    second = 3 * half + width + LANES

    def total(first, size):
        return keep[0, :, first : first + size] + got[0, :, first : first + size].astype(jnp.float32)

    for i, ref in enumerate((query_ref, key_ref, value_ref)):
        ref[:, :half] = total(i * half, half)
        ref[:, half:] = total(second + i * half, half)
    out_ref[...] = total(3 * half, width)
    for ref, first in ((small_ref, 3 * half + width), (late_ref, second + 3 * half)):
        turned[...] = jnp.zeros_like(turned)
        turned[:low, :] = total(first, LANES)
        ref[...] = turned[...].T[: ref.shape[0], :]


def last_qkv(scalars, keep, got, width):
    low = keep.shape[1]
    f32 = jnp.float32
    return whole_call(
        last_qkv_body, "last_qkv", scalars, [], [keep, got],
        [array(f32, low, width)] * 4 + [array(f32, 24, LANES), array(f32, 8, LANES)], [], [pltpu.VMEM((LANES, LANES), f32)], 1,
    )


def after(value, *others):
    return lax.optimization_barrier((value,) + others)[0]


def bit_count(size):
    return size.bit_length() - 1


def swap_dp(value, mask):
    return lax.ppermute(value, "dp", [(i, i ^ mask) for i in range(lax.axis_size("dp"))])


def swap_seq(value, mask):
    return lax.ppermute(value, "seq", [(i, i ^ mask) for i in range(lax.axis_size("seq"))])


def column_sum(matrix):
    return jnp.sum(matrix.astype(jnp.float32), axis=0)


def spread_pairs(first):
    dps, seqs = lax.axis_size("dp"), lax.axis_size("seq")
    pairs = []
    for dp in range(dps):
        for seq in range(seqs):
            piece = first ^ (seq & 1)
            to_dp = (dp & ~1) | (seq >> 1)
            to_seq = 2 * (dp & 1) + piece
            pairs.append((dp * seqs + seq, to_dp * seqs + to_seq))
    return pairs


def to_sequences(local, order):
    odd = (lax.axis_index("seq") & 1) == 1
    got = []
    pieces = [jnp.where(odd, local[1 - first], local[first]) for first in range(2)]
    order.mark(*pieces)
    for first, piece in enumerate(pieces):
        got.append(lax.ppermute(piece, AXES, spread_pairs(first)))
    return got, odd


def in_order(got, odd, rows):
    return jnp.where(odd, jnp.concatenate([g[:rows] for g in got[::-1]]), jnp.concatenate([g[:rows] for g in got]))


def from_sequences(tokens, order):
    odd = (lax.axis_index("seq") & 1) == 1
    half = tokens.shape[0] // 2
    got = []
    for first in range(2):
        near, far = tokens[first * half : (first + 1) * half], tokens[(1 - first) * half : (2 - first) * half]
        piece = order.mark(jnp.where(order.gate(odd), far, near))
        got.append(lax.ppermute(piece, AXES, [(b, a) for a, b in spread_pairs(first)]))
    return got


def both_sequences(order, got):
    odd = order.gate((lax.axis_index("seq") & 1) == 1)
    return jnp.where(odd, jnp.stack(got[::-1]), jnp.stack(got))


def weight_lines(weights, lines):
    width = weights[0].shape[-1]
    lines = [jnp.pad(v[..., None, :], [(0, 0)] * v.ndim + [(0, width - v.shape[-1])]) for v in lines]
    lines.append(jnp.zeros(lines[0].shape[:-2] + (16 - len(lines), width), jnp.bfloat16))
    return jnp.concatenate(weights + lines, axis=-2)


def shards_of(part, ready=None):
    if lax.axis_size("dp") != PARTS:
        p = part if part.ndim == 3 else jnp.stack(jnp.split(lax.all_gather(part, "dp", axis=0, tiled=True), PARTS))
        return [p[0], p[1], p[2], p[4], p[6], jnp.concatenate([p[3], p[5], p[7]])]
    shards = [part, swap_dp(part, 1), swap_dp(part, 2), swap_dp(part, 4), swap_dp(part, 6)]
    return shards if ready is False else last_shards(shards)


def last_shards(shards, *ready):
    if len(shards) == SHARDS:
        return shards
    near = lax.optimization_barrier((*shards[2:], *ready))[:3]
    return shards[:2] + list(near) + [swap_dp(jnp.concatenate(near), 1)]


def projection_shards(weights, vectors):
    if lax.axis_size("dp") == PARTS:
        return shards_of(weight_lines(weights, vectors))
    gather = lambda v: lax.all_gather(v, "dp", axis=0, tiled=True)
    split = lambda v: gather(v).reshape((PARTS, -1) + v.shape[1:])
    return shards_of(weight_lines([split(w) for w in weights], [split(v) for v in vectors]))


def project_body(counts, me, *refs):
    devices, rows, wide, vectors = counts
    pieces = parts_of(refs[:SHARDS])
    tokens, far, q_ref, k_ref, v_ref, ko_ref, vo_ref, vec_ref, up_ref, ordered, out, held, small, turned, sems, small_sems, out_sem = refs[SHARDS:]
    width = tokens.shape[1]
    half = width // 2
    copies = []

    def start(source, target, sem):
        copy = pltpu.make_async_copy(source, target, sem)
        copy.start()
        copies.append(copy)

    for place in range(devices):
        ref, first, size = pieces[place]
        where = me[0] ^ place
        start(ref.at[first + 3 * rows : first + size, :], small.at[where], small_sems.at[place])
        target = pl.ds(where * rows, rows)
        for weight in range(3):
            for side in range(2):
                start(
                    ref.at[first + weight * rows : first + (weight + 1) * rows, side * half : (side + 1) * half],
                    held.at[side, target, weight * half : (weight + 1) * half],
                    sems.at[len(copies) - place - 1],
                )
    for copy in copies:
        copy.wait()
    save = pltpu.make_async_copy(held, out, out_sem)
    save.start()
    vec_ref[...] = jnp.concatenate([small[i, :, :rows] for i in range(devices)], axis=1).astype(jnp.float32)
    up_ref[...] = jnp.concatenate([small[i, vectors : vectors + 1, :wide] for i in range(devices)], axis=1).astype(jnp.float32)
    for weight, add, goal, source in ((1, None, k_ref, tokens), (1, None, ko_ref, far), (2, 1, v_ref, tokens), (2, 1, vo_ref, far), (0, 0, q_ref, tokens)):
        for side in range(2):
            cols = slice(side * half, (side + 1) * half)
            product = nn(source[...], held[side, :, weight * half : (weight + 1) * half])
            if add is not None:
                product = product + vec_ref[add : add + 1, cols]
            goal[:, cols] = product.astype(jnp.bfloat16)
    flipped = tokens[...].T
    for i in range(PARTS):
        turned[i] = flipped[i * rows : (i + 1) * rows, :]
    turn_parts(me[1], turned, ordered)
    save.wait()


def project(me, pieces, tokens, far, rows, wide, vectors):
    count, width = tokens.shape
    devices = width // rows
    lines = pieces[0].shape[-2] - 3 * rows
    whole = lambda shape: pl.BlockSpec(shape, lambda i, *_: (0,) * len(shape))
    result = jax.ShapeDtypeStruct(tokens.shape, jnp.bfloat16)
    any_space = pl.BlockSpec(memory_space=pl.ANY)
    return pl.pallas_call(
        functools.partial(project_body, (devices, rows, wide, vectors)),
        grid_spec=pltpu.PrefetchScalarGridSpec(
            num_scalar_prefetch=1,
            grid=(1,),
            in_specs=[any_space] * len(pieces) + [whole(tokens.shape)] * 2,
            out_specs=[whole(tokens.shape)] * 5
            + [whole((lines, width)), whole((1, wide * devices)), whole((2, PARTS // 2, rows, count)), any_space],
            scratch_shapes=[
                pltpu.VMEM((2, width, 3 * width // 2), jnp.bfloat16),
                pltpu.VMEM((devices, lines, width), jnp.bfloat16),
                pltpu.VMEM((PARTS, rows, count), jnp.bfloat16),
                pltpu.SemaphoreType.DMA((6 * devices,)),
                pltpu.SemaphoreType.DMA((devices,)),
                pltpu.SemaphoreType.DMA,
            ],
        ),
        out_shape=[result] * 5
        + [
            jax.ShapeDtypeStruct((lines, width), jnp.float32),
            jax.ShapeDtypeStruct((1, wide * devices), jnp.float32),
            jax.ShapeDtypeStruct((2, PARTS // 2, rows, count), jnp.bfloat16),
            jax.ShapeDtypeStruct((2, width, 3 * width // 2), jnp.bfloat16),
        ],
        cost_estimate=pl.CostEstimate(flops=1, transcendentals=0, bytes_accessed=1),
        compiler_params=pltpu.CompilerParams(vmem_limit_bytes=32 << 20),
        name="project",
    )(me, *pieces, tokens, far)


class Order:
    def __init__(self):
        self.last = ()

    def gate(self, value):
        return lax.optimization_barrier((value, *self.last))[0] if self.last else value

    def mark(self, *values):
        self.last = values
        return values[0] if len(values) == 1 else values


def all_rows(send, keep):
    return jnp.stack([keep, send], axis=1).reshape(-1, keep.shape[-1]).astype(jnp.float32)


def scatter_all(send, keep):
    return lax.psum_scatter(all_rows(send, keep), AXES, scatter_dimension=0, tiled=True)


def per_device(
    hidden_in, segment_ids, query_weight, query_bias, key_weight, value_weight, value_bias, out_weight, out_bias,
    first_gain, first_shift, up_weight, up_bias, down_weight, down_bias, second_gain, second_shift, cotangent,
):
    dps, seqs = lax.axis_size("dp"), lax.axis_size("seq")
    inner_width, width = up_weight.shape[1], query_weight.shape[1]
    block = hidden_in.shape[1]
    length = segment_ids.shape[1]
    share = width // (dps * seqs)
    qblock = chunk = 256

    vectors = [query_bias, value_bias, out_bias, first_gain, first_shift, down_bias, second_gain, second_shift]
    direct = dps == PARTS and seqs == 4
    scalars = jnp.zeros((6,), jnp.int32)
    if direct:
        dp, seq = lax.axis_index("dp"), lax.axis_index("seq")
        scalars = jnp.stack([dp, dp & 1, (dp >> 1) & 1, dp >> 2, seq & 1, seq >> 1]).astype(jnp.int32)
    shards = projection_shards([query_weight, key_weight, value_weight], vectors + [up_bias])
    ids = segment_ids.astype(jnp.bfloat16).reshape(segment_ids.shape[0], 2, length // 2)
    ids = jnp.pad(ids, ((0, 0), (0, 14), (0, width - length // 2)))
    order = Order()
    got, odd = to_sequences(jnp.concatenate([hidden_in, ids], axis=1), order)

    tokens = in_order(got, odd, block)
    tokens_other = swap_dp(tokens, 1)
    segment = got[0][block : block + 2, : length // 2].astype(jnp.int32)
    core = lax.axis_index("dp") & 1
    half = length // 2
    own = lax.dynamic_index_in_dim(segment, core, 0, keepdims=False)
    other = lax.dynamic_index_in_dim(segment, 1 - core, 0, keepdims=False)
    bounds = chunk_bounds(own, other, qblock, chunk)
    row, tiles = own[None, :], segment_tiles(own, other, chunk)

    out_up, down_part = lax.optimization_barrier(
        (jnp.concatenate([out_weight, up_weight], axis=1), down_weight, *shards[2:5])
    )[:2]
    out_up_shards = shards_of(out_up, False)
    query, keys, values, keys_other, values_other, vec, up_add, ordered, w_qkv = project(
        scalars, shards, tokens, tokens_other, width // PARTS, inner_width // PARTS, len(vectors)
    )
    got_up, _ = to_sequences(after(cotangent, query), order)
    attended, lse = attend_forward(query, keys, values, keys_other, values_other, row, tiles, bounds, qblock, chunk, 3)

    upstream = in_order(lax.optimization_barrier((*got_up, attended))[:2], odd, block)
    out_up_shards = last_shards(out_up_shards, attended, upstream)
    down_shards = shards_of(after(down_part, attended, *out_up_shards[2:5]), False)
    normal_one, scale_one, first_low, active, slope, wo, wu = widen(scalars, out_up_shards, attended, tokens, vec, up_add)
    layer_low, sum_two_grad, second_grad, sums_two, *halves, wd = narrow(
        scalars, last_shards(down_shards, active), active, normal_one, vec, upstream
    )
    swap = (lambda value: swap_dp(value, 1)) if direct else (lambda value: value)
    order = Order()
    order.mark(second_grad)
    down_send, down_keep = halves
    down_got = swap(down_send)
    out_pieces = from_sequences(layer_low, order)
    inner_grad, up_sum, *halves = inner_back(scalars, order.gate(second_grad), wd, slope, first_low)
    up_send, up_keep = halves
    up_got = swap(up_send)
    order.mark(inner_grad)
    if direct:
        (send, down_keep), (other, up_keep) = fold(
            order.gate(scalars), [(down_keep, down_got, (2, 1, 2)), (up_keep, up_got, (1, 2, 3))]
        )
        order.mark(send, other)
        down_got, up_got = swap_dp(send, 2), swap_dp(other, 4)
    sum_one_grad, attended_grad, sums_one, *halves = outer_back(
        order.gate(scalars), inner_grad, wu, sum_two_grad, normal_one, scale_one, vec, wo, attended
    )
    order.mark(attended_grad)
    layer_out = order.mark(both_sequences(order, out_pieces))
    devices = dps * seqs
    wide_sums = order.gate(up_sum).reshape(devices, 4, share).transpose(1, 0, 2).reshape(4, width)
    wide_sums = order.mark(jnp.pad(wide_sums, ((0, 4), (0, 0))))

    def attend(side):
        given = (query, keys, values, keys_other, values_other, attended, order.gate(attended_grad), lse, row, tiles, bounds)
        return order.mark(*attend_back(*given, qblock, chunk, 3, side))

    dq, dk, dv, far = attend(0)
    if direct:
        (send, down_keep), (other, up_keep) = fold(
            order.gate(scalars), [(down_keep, down_got, (1, 1, 3)), (up_keep, up_got, (1, 1, 2))]
        )
        order.mark(send, other)
        down_got, up_got = swap_dp(send, 4), swap_dp(other, 2)
    one_send, one_keep, gradient, sums_first = qkv_back(
        0, order.gate(scalars), dq, dk, dv, swap_dp(far, 1), ordered, w_qkv, sum_one_grad, *halves, sums_one, sums_two, wide_sums
    )
    order.mark(gradient)
    one_got = swap(one_send)
    dq, dk, dv, far = attend(1)
    if direct:
        ((send, one_keep),) = fold(order.gate(scalars), [(one_keep, one_got, (1, 2, 3))])
        one_got = swap_dp(order.mark(send), 4)
    two_send, two_keep, gradient, _ = qkv_back(
        1, order.gate(scalars), dq, dk, dv, swap_dp(far, 1), ordered, w_qkv, gradient, sums_first
    )
    order.mark(gradient)
    two_got = swap(two_send)
    if direct:
        send, ff_keep = merge(order.gate(scalars), [(down_keep, down_got), (up_keep, up_got)], share)
        ff_got = swap_seq(order.mark(send), 1)
    in_pieces = from_sequences(gradient, order)
    if not direct:
        down_grad, up_grad = scatter_all(down_send, down_keep), scatter_all(up_send, up_keep)
        one, two = scatter_all(one_send, one_keep), scatter_all(two_send, two_keep)
        cut = width // 2
        query_grad, key_grad, value_grad = [
            jnp.concatenate([side[:, i * cut : (i + 1) * cut] for side in (one, two)], axis=1) for i in range(3)
        ]
        out_grad = one[:, 3 * cut : 3 * cut + width]
        small, late = one[:, 3 * cut + width :].T, two[:, 3 * cut :].T
    else:
        (send, two_keep), (other, ff_keep) = fold(
            order.gate(scalars), [(two_keep, two_got, (2, 1, 2)), (ff_keep, ff_got, (1, 1, 5))]
        )
        order.mark(send, other)
        two_got, ff_got = swap_dp(send, 2), swap_seq(other, 2)
        (send, one_keep), (other, two_keep) = fold(
            order.gate(scalars), [(one_keep, one_got, (1, 1, 2)), (two_keep, two_got, (1, 1, 3))]
        )
        order.mark(send, other)
        one_got, two_got = swap_dp(send, 2), swap_dp(other, 4)
        down_grad, up_grad = order.mark(*last_ff(order.gate(scalars), ff_keep, ff_got, width))
        send, keep = merge(order.gate(scalars), [(one_keep, one_got), (two_keep, two_got)], share)
        got = swap_seq(order.mark(send), 1)
    input_grad = order.mark(both_sequences(order, in_pieces).astype(jnp.float32))
    if direct:
        ((send, keep),) = fold(order.gate(scalars), [(keep, got, (1, 1, 5))])
        got = swap_seq(order.mark(send), 2)
        query_grad, key_grad, value_grad, out_grad, small, late = last_qkv(order.gate(scalars), keep, got, width)
    ob, g1, s1 = [small[i, :share] for i in (0, 1, 2)]
    db, g2, s2 = [small[i, :share] for i in (8, 9, 10)]
    ub = small[16:20, :share].reshape(-1)
    qb, vb = [late[i, :share] for i in (0, 1)]
    return (
        layer_out, input_grad, query_grad, qb, key_grad, value_grad, vb, out_grad, ob, g1, s1, up_grad, ub, down_grad, db, g2, s2,
    )


def solution(mesh):
    wide, flat = P("dp", None), P("dp")
    in_specs = (
        P("dp", "seq", None), wide, wide, flat, wide, wide, flat, wide, flat, flat, flat, wide, flat, wide, flat,
        flat, flat, P("dp", "seq", None),
    )
    rows, cells = P(AXES, None), P(AXES)
    out_specs = (
        P("dp", "seq", None), P("dp", "seq", None), rows, cells, rows, rows, cells, rows, cells, cells, cells, rows,
        cells, rows, cells, cells, cells,
    )
    return jax.shard_map(per_device, mesh=mesh, in_specs=in_specs, out_specs=out_specs, check_vma=False)
```

profile of v0, /device:TPU:0, one launch (start us, length us, event | category | flops | bytes accessed | tf_op | source)
XLA Modules:
  0.0 375.5 jit_solution(6552444625420625077)
XLA Ops:
  6.6 2.9 concatenate.35.refs_0_
  9.5 3.0 collective-permute-start
  17.0 5.0 %collective-permute-start.3 = (bf16[272,768]{1,0:T(8,128)(2,1)}, bf16[272,768]{1,0:T(8,128)(2,1)}, u32[]{:S(2)}, u32[]{:S(2)}) collective-permute-start(bf16[272,768]{1,0:T(8,128)(2,1)} %get-tuple-element.268), channel_id=1, source_target_pairs={{0,0},{1,1},{2,4},{3,5},{4,2},{5,3},{6,6},{7,7},{8,8},{9,9},{10,12... | collective-permute-start | bytes 1253384 | tf_op jit(solution)/shard_map/ppermute | solution.py:698
  26.2 8.5 %collective-permute-done.1.refs_3_ = bf16[304,768]{1,0:T(8,128)(2,1)S(1)} collective-permute-done((bf16[304,768]{1,0:T(8,128)(2,1)S(1)}, bf16[304,768]{1,0:T(8,128)(2,1)S(1)}, u32[]{:S(2)}, u32[]{:S(2)}) %collective-permute-start.1) | collective-permute-done | bytes 466976 | tf_op jit(solution)/shard_map/ppermute | solution.py:669
  51.8 8.1 %project.1 = (bf16[512,768]{1,0:T(8,128)(2,1)S(1)}, bf16[512,768]{1,0:T(8,128)(2,1)S(1)}, bf16[512,768]{1,0:T(8,128)(2,1)S(1)}, bf16[512,768]{1,0:T(8,128)(2,1)S...) custom-call(s32[6]{0:T(128)S(1)} %stack.70.me.scalars, ...), custom_call_target="tpu_custom_call" | custom-call | flops 1 | bytes 1 | tf_op jit(solution)/shard_map/project/pallas_call | solution.py:804
  73.2 13.2 %attend_forward.1 = (bf16[512,768]{1,0:T(8,128)(2,1)S(1)}, f32[2,8,512]{2,1,0:T(8,128)S(1)}) custom-call(s32[8]{0:T(128)S(1)} %reshape.108.bounds, bf16[512,768]{1,0:T(8,128)(2,1)S(1)} %get-tuple-element.144.q_ref, bf16[512,768]{1,0:T(8,128)(2,1)S(1)} %get-tuple-element.145.k_ref, bf16[512,768]{1,0:T(8,128)(2,1)S(1)} %copy-done.4, ...), custom_call_target="tpu_custom_call" | custom-call | flops 1 | bytes 1 | tf_op jit(solution)/shard_map/attend_forward/pallas_call | solution.py:177
  100.7 15.7 %widen.1 = (f32[512,768]{1,0:T(8,128)}, f32[512,128]{1,0:T(8,128)}, bf16[512,768]{1,0:T(8,128)(2,1)}, bf16[512,3072]{1,0:T(8,128)(2,1)}, bf16[512,3072]{1,0:T(8,...) custom-call(s32[6]{0:T(128)} %copy-done.23, bf16[96,3840]{1,0:T(8,128)(2,1)} %pad_maximum_fusion.3.refs_0_, ...), custom_call_target="tpu_custom_call" | custom-call | flops 1 | bytes 1 | tf_op jit(solution)/shard_map/widen/pallas_call | solution.py:424
  116.3 6.7 %collective-permute-done.15.refs_3_ = bf16[384,768]{1,0:T(8,128)(2,1)S(1)} collective-permute-done((bf16[384,768]{1,0:T(8,128)(2,1)S(1)}, bf16[384,768]{1,0:T(8,128)(2,1)S(1)}, u32[]{:S(2)}, u32[]{:S(2)}) %collective-permute-start.15) | collective-permute-done | bytes 589856 | tf_op jit(solution)/shard_map/ppermute | solution.py:669
  124.6 4.0 %collective-permute-done.13.refs_1_ = bf16[384,768]{1,0:T(8,128)(2,1)S(1)} collective-permute-done((bf16[384,768]{1,0:T(8,128)(2,1)S(1)}, bf16[384,768]{1,0:T(8,128)(2,1)S(1)}, u32[]{:S(2)}, u32[]{:S(2)}) %collective-permute-start.13) | collective-permute-done | bytes 589856 | tf_op jit(solution)/shard_map/ppermute | solution.py:669
  130.1 16.2 %narrow.1 = (bf16[512,768]{1,0:T(8,128)(2,1)}, f32[512,768]{1,0:T(8,128)}, bf16[512,768]{1,0:T(8,128)(2,1)}, f32[8,768]{1,0:T(8,128)}, bf16[4,384,768]{2,1,0:T(8...) custom-call(s32[6]{0:T(128)} %copy-done.23, bf16[384,768]{1,0:T(8,128)(2,1)} %refs_0_, ...), custom_call_target="tpu_custom_call" | custom-call | flops 1 | bytes 1 | tf_op jit(solution)/shard_map/narrow/pallas_call | solution.py:424
  148.5 20.0 %inner_back.1 = (bf16[512,3072]{1,0:T(8,128)(2,1)}, f32[1,3072]{1,0:T(1,128)}, bf16[4,96,3072]{2,1,0:T(8,128)(2,1)}, bf16[4,96,3072]{2,1,0:T(8,128)(2,1)}) custom-call(s32[6]{0:T(128)} %copy-done.23, bf16[512,768]{1,0:T(8,128)(2,1)} %get-tuple-element.169.low, bf16[3072,768]{1,0:T(8,128)(2,1)} %get-tuple-element.170.wd, ...), custom_call_target="tpu_custom_call" | custom-call | flops 1 | bytes 1 | tf_op jit(solution)/shard_map/inner_back/pallas_call | solution.py:424
  173.3 3.4 collective-permute-done.20.refs_1_
  178.1 7.8 %fold.6 = (bf16[2,384,768]{2,1,0:T(8,128)(2,1)}, bf16[2,384,768]{2,1,0:T(8,128)(2,1)}, bf16[2,96,3072]{2,1,0:T(8,128)(2,1)}, bf16[2,96,3072]{2,1,0:T(8,128)(2,1)}) custom-call(s32[6]{0:T(128)} %copy-done.23, bf16[4,384,768]{2,1,0:T(8,128)(2,1)} %get-tuple-element.175.refs_0_, bf16[4,384,768]{2,1,0:T(8,128)(2,1)} %copy-done.32, ...), custom_call_target="tpu_custom_call" | custom-call | flops 1 | bytes 1 | tf_op jit(solution)/shard_map/fold/pallas_call | solution.py:424
  187.9 12.7 %outer_back.1 = (f32[512,768]{1,0:T(8,128)}, bf16[512,768]{1,0:T(8,128)(2,1)}, f32[8,768]{1,0:T(8,128)}, bf16[4,96,768]{2,1,0:T(8,128)(2,1)}, bf16[4,96,768]{2,1,0:T(8,128)(2,1)}) custom-call(s32[6]{0:T(128)} %copy-done.23, bf16[512,3072]{1,0:T(8,128)(2,1)} %get-tuple-element.173.grad, bf16[768,3072]{1,0:T(8,128)(2,1)} %get-tuple-element.182.wu, ...), custom_call_target="tpu_custom_call" | custom-call | flops 1 | bytes 1 | tf_op jit(solution)/shard_map/outer_back/pallas_call | solution.py:424
  205.2 14.8 %attend_back.2 = (bf16[512,384]{1,0:T(8,128)(2,1)S(1)}, f32[512,384]{1,0:T(8,128)S(1)}, f32[512,384]{1,0:T(8,128)S(1)}, bf16[2,512,384]{2,1,0:T(8,128)(2,1)S(1)}) custom-call(s32[8]{0:T(128)S(1)} %reshape.108.bounds, bf16[512,768]{1,0:T(8,128)(2,1)S(1)} %get-tuple-element.144.q_ref, bf16[512,768]{1,0:T(8,128)(2,1)S(1)} %get-tuple-element.145.k_ref, ...), custom_call_target="tpu_custom_call" | custom-call | flops 1 | bytes 1 | tf_op jit(solution)/shard_map/attend_back/pallas_call | solution.py:211
  222.6 5.0 %fold.7 = (bf16[1,384,768]{2,1,0:T(8,128)(2,1)}, bf16[1,384,768]{2,1,0:T(8,128)(2,1)}, bf16[1,96,3072]{2,1,0:T(8,128)(2,1)}, bf16[1,96,3072]{2,1,0:T(8,128)(2,1)}) custom-call(s32[6]{0:T(128)} %copy-done.23, bf16[2,384,768]{2,1,0:T(8,128)(2,1)} %get-tuple-element.197.refs_0_, bf16[2,384,768]{2,1,0:T(8,128)(2,1)} %collective-permute-done.24.refs_1_, ...), custom_call_target="tpu_custom_call" | custom-call | flops 1 | bytes 1 | tf_op jit(solution)/shard_map/fold/pallas_call | solution.py:424
  228.6 9.0 %qkv_back.2 = (bf16[4,96,2048]{2,1,0:T(8,128)(2,1)}, bf16[4,96,2048]{2,1,0:T(8,128)(2,1)}, f32[512,768]{1,0:T(8,128)}, f32[8,384]{1,0:T(8,128)}) custom-call(s32[6]{0:T(128)} %copy-done.23, bf16[512,384]{1,0:T(8,128)(2,1)} %copy-done.22, f32[512,384]{1,0:T(8,128)} %copy-done.18, f32[512,384]{1,0:T(8,128)} %copy-done.19, bf16[2,512,384]{2,1,0:T(8,128)(2,1)} %copy-done.37, ...), custom_call_target="tpu_custom_call" | custom-call | flops 1 | bytes 1 | tf_op jit(solution)/shard_map/qkv_back/pallas_call | solution.py:424
  238.0 15.1 %attend_back.3 = (bf16[512,384]{1,0:T(8,128)(2,1)S(1)}, f32[512,384]{1,0:T(8,128)S(1)}, f32[512,384]{1,0:T(8,128)S(1)}, bf16[2,512,384]{2,1,0:T(8,128)(2,1)S(1)}) custom-call(s32[8]{0:T(128)S(1)} %reshape.108.bounds, bf16[512,768]{1,0:T(8,128)(2,1)S(1)} %get-tuple-element.144.q_ref, bf16[512,768]{1,0:T(8,128)(2,1)S(1)} %get-tuple-element.145.k_ref, ...), custom_call_target="tpu_custom_call" | custom-call | flops 1 | bytes 1 | tf_op jit(solution)/shard_map/attend_back/pallas_call | solution.py:211
  258.9 4.1 %fold.8 = (bf16[2,96,2048]{2,1,0:T(8,128)(2,1)}, bf16[2,96,2048]{2,1,0:T(8,128)(2,1)}) custom-call(s32[6]{0:T(128)} %copy-done.23, bf16[4,96,2048]{2,1,0:T(8,128)(2,1)} %get-tuple-element.216.refs_0_, bf16[4,96,2048]{2,1,0:T(8,128)(2,1)} %copy-done.35), custom_call_target="tpu_custom_call" | custom-call | flops 1 | bytes 1 | tf_op jit(solution)/shard_map/fold/pallas_call | solution.py:424
  263.9 7.9 %qkv_back.3 = (bf16[4,96,1280]{2,1,0:T(8,128)(2,1)}, bf16[4,96,1280]{2,1,0:T(8,128)(2,1)}, bf16[512,768]{1,0:T(8,128)(2,1)}, f32[8,384]{1,0:T(8,128)}) custom-call(s32[6]{0:T(128)} %copy-done.23, bf16[512,384]{1,0:T(8,128)(2,1)} %copy-done.21, f32[512,384]{1,0:T(8,128)} %copy-done.16, f32[512,384]{1,0:T(8,128)} %copy-done.17, ...), custom_call_target="tpu_custom_call" | custom-call | flops 1 | bytes 1 | tf_op jit(solution)/shard_map/qkv_back/pallas_call | solution.py:424
  273.0 3.7 merge.2
  280.3 12.3 %collective-permute-done.32.refs_3_ = bf16[2,24,6144]{2,1,0:T(8,128)(2,1)S(1)} collective-permute-done((bf16[2,24,6144]{2,1,0:T(8,128)(2,1)}, bf16[2,24,6144]{2,1,0:T(8,128)(2,1)S(1)}, u32[]{:S(2)}, u32[]{:S(2)}) %collective-permute-start.32) | collective-permute-done | bytes 589856 | tf_op jit(solution)/shard_map/ppermute | solution.py:673
  293.8 4.2 %fold.9 = (bf16[2,96,1280]{2,1,0:T(8,128)(2,1)}, bf16[2,96,1280]{2,1,0:T(8,128)(2,1)}, bf16[1,24,6144]{2,1,0:T(8,128)(2,1)}, f32[1,24,6144]{2,1,0:T(8,128)}) custom-call(s32[6]{0:T(128)} %copy-done.23, bf16[4,96,1280]{2,1,0:T(8,128)(2,1)} %get-tuple-element.229.refs_0_, bf16[4,96,1280]{2,1,0:T(8,128)(2,1)} %copy-done.36, ...), custom_call_target="tpu_custom_call" | custom-call | flops 1 | bytes 1 | tf_op jit(solution)/shard_map/fold/pallas_call | solution.py:424
  298.9 12.1 %collective-permute-done.34.refs_3_ = bf16[2,96,1280]{2,1,0:T(8,128)(2,1)S(1)} collective-permute-done((bf16[2,96,1280]{2,1,0:T(8,128)(2,1)}, bf16[2,96,1280]{2,1,0:T(8,128)(2,1)S(1)}, u32[]{:S(2)}, u32[]{:S(2)}) %collective-permute-start.34) | collective-permute-done | bytes 491552 | tf_op jit(solution)/shard_map/ppermute | solution.py:669
  311.8 3.7 fold.10
  316.0 3.3 collective-permute-start.35
  321.9 17.7 %collective-permute-done.35.got = bf16[1,24,6144]{2,1,0:T(8,128)(2,1)S(1)} collective-permute-done((bf16[1,24,6144]{2,1,0:T(8,128)(2,1)S(1)}, bf16[1,24,6144]{2,1,0:T(8,128)(2,1)S(1)}, u32[]{:S(2)}, u32[]{:S(2)}) %collective-permute-start.35) | collective-permute-done | bytes 294944 | tf_op jit(solution)/shard_map/ppermute | solution.py:673
  340.3 2.6 last_ff.1
  343.8 3.0 merge.3
  348.9 7.5 %collective-permute-done.40.refs_1_ = bf16[2,24,3328]{2,1,0:T(8,128)(2,1)S(1)} collective-permute-done((bf16[2,24,3328]{2,1,0:T(8,128)(2,1)}, bf16[2,24,3328]{2,1,0:T(8,128)(2,1)S(1)}, u32[]{:S(2)}, u32[]{:S(2)}) %collective-permute-start.40) | collective-permute-done | bytes 319520 | tf_op jit(solution)/shard_map/ppermute | solution.py:673
  357.1 2.7 fold.11
  360.3 8.3 %collective-permute-done.41.got = bf16[1,24,3328]{2,1,0:T(8,128)(2,1)S(1)} collective-permute-done((bf16[1,24,3328]{2,1,0:T(8,128)(2,1)}, bf16[1,24,3328]{2,1,0:T(8,128)(2,1)S(1)}, u32[]{:S(2)}, u32[]{:S(2)}) %collective-permute-start.41) | collective-permute-done | bytes 159776 | tf_op jit(solution)/shard_map/ppermute | solution.py:673
  (248 shorter events, 110.3 us)
Async XLA Ops:
  9.5 14.5 %collective-permute-start = (bf16[304,768]{1,0:T(8,128)(2,1)S(1)}, bf16[304,768]{1,0:T(8,128)(2,1)S(1)}, u32[]{:S(2)}, u32[]{:S(2)}) collective-permute-start(bf16[304,768]{1,0:T(8,128)(2,1)S(1)} %concatenate.35.refs_0_), channel_id=1, source_target_pairs={{0,8},{4,12},{8,0},{12,4},{16,24},{20,28},{24,16},{28,20},{1,9},{5... | collective-permute-start | bytes 1400840 | tf_op jit(solution)/shard_map/ppermute | solution.py:669
  12.5 22.2 %collective-permute-start.1 = (bf16[304,768]{1,0:T(8,128)(2,1)S(1)}, bf16[304,768]{1,0:T(8,128)(2,1)S(1)}, u32[]{:S(2)}, u32[]{:S(2)}) collective-permute-start(bf16[304,768]{1,0:T(8,128)(2,1)S(1)} %concatenate.35.refs_0_), channel_id=1, source_target_pairs={{0,16},{4,20},{8,24},{12,28},{16,0},{20,4},{24,8},{28,12},{1,17},{... | collective-permute-start | bytes 1400840 | tf_op jit(solution)/shard_map/ppermute | solution.py:669
  14.0 20.6 %collective-permute-start.2 = (bf16[304,768]{1,0:T(8,128)(2,1)S(1)}, bf16[304,768]{1,0:T(8,128)(2,1)S(1)}, u32[]{:S(2)}, u32[]{:S(2)}) collective-permute-start(bf16[304,768]{1,0:T(8,128)(2,1)S(1)} %concatenate.35.refs_0_), channel_id=1, source_target_pairs={{0,24},{4,28},{8,16},{12,20},{16,8},{20,12},{24,0},{28,4},{1,25},{... | collective-permute-start | bytes 1400840 | tf_op jit(solution)/shard_map/ppermute | solution.py:669
  14.1 32.9 %collective-permute-start.4 = (bf16[304,768]{1,0:T(8,128)(2,1)S(1)}, bf16[304,768]{1,0:T(8,128)(2,1)}, u32[]{:S(2)}, u32[]{:S(2)}) collective-permute-start(bf16[304,768]{1,0:T(8,128)(2,1)S(1)} %concatenate.35.refs_0_), channel_id=1, source_target_pairs={{0,4},{4,0},{8,12},{12,8},{16,20},{20,16},{24,28},{28,24},{1,5},{5... | collective-permute-start | bytes 1400840 | tf_op jit(solution)/shard_map/ppermute | solution.py:669
  17.0 20.0 %collective-permute-start.3 = (bf16[272,768]{1,0:T(8,128)(2,1)}, bf16[272,768]{1,0:T(8,128)(2,1)}, u32[]{:S(2)}, u32[]{:S(2)}) collective-permute-start(bf16[272,768]{1,0:T(8,128)(2,1)} %get-tuple-element.268), channel_id=1, source_target_pairs={{0,0},{1,1},{2,4},{3,5},{4,2},{5,3},{6,6},{7,7},{8,8},{9,9},{10,12... | collective-permute-start | bytes 1253384 | tf_op jit(solution)/shard_map/ppermute | solution.py:698
  24.0 15.9 %collective-permute-start.6 = (bf16[272,768]{1,0:T(8,128)(2,1)}, bf16[272,768]{1,0:T(8,128)(2,1)}, u32[]{:S(2)}, u32[]{:S(2)}) collective-permute-start(bf16[272,768]{1,0:T(8,128)(2,1)} %get-tuple-element.267), channel_id=1, source_target_pairs={{0,1},{1,0},{2,5},{3,4},{4,3},{5,2},{6,7},{7,6},{8,9},{9,8},{10,13... | collective-permute-start | bytes 1253384 | tf_op jit(solution)/shard_map/ppermute | solution.py:698
  35.9 11.4 %collective-permute-start.5 = (bf16[912,768]{1,0:T(8,128)(2,1)}, bf16[912,768]{1,0:T(8,128)(2,1)S(1)}, u32[]{:S(2)}, u32[]{:S(2)}) collective-permute-start(bf16[912,768]{1,0:T(8,128)(2,1)} %pad_maximum_fusion.2), channel_id=1, source_target_pairs={{0,4},{4,0},{8,12},{12,8},{16,20},{20,16},{24,28},{28,24},{1,5},{5... | collective-permute-start | bytes 4202504 | tf_op jit(solution)/shard_map/ppermute | solution.py:669
  43.8 45.2 %collective-permute-start.10 = (bf16[96,3840]{1,0:T(8,128)(2,1)}, bf16[96,3840]{1,0:T(8,128)(2,1)}, u32[]{:S(2)}, u32[]{:S(2)}) collective-permute-start(bf16[96,3840]{1,0:T(8,128)(2,1)} %pad_maximum_fusion.3.refs_0_), channel_id=1, source_target_pairs={{0,24},{4,28},{8,16},{12,20},{16,8},{20,12},{24,0},{28,4},{1,25},{... | collective-permute-start | bytes 2211848 | tf_op jit(solution)/shard_map/ppermute | solution.py:669
  46.4 42.6 %collective-permute-start.8 = (bf16[96,3840]{1,0:T(8,128)(2,1)}, bf16[96,3840]{1,0:T(8,128)(2,1)}, u32[]{:S(2)}, u32[]{:S(2)}) collective-permute-start(bf16[96,3840]{1,0:T(8,128)(2,1)} %pad_maximum_fusion.3.refs_0_), channel_id=1, source_target_pairs={{0,8},{4,12},{8,0},{12,4},{16,24},{20,28},{24,16},{28,20},{1,9},{5... | collective-permute-start | bytes 2211848 | tf_op jit(solution)/shard_map/ppermute | solution.py:669
  47.0 42.1 %collective-permute-start.9 = (bf16[96,3840]{1,0:T(8,128)(2,1)}, bf16[96,3840]{1,0:T(8,128)(2,1)}, u32[]{:S(2)}, u32[]{:S(2)}) collective-permute-start(bf16[96,3840]{1,0:T(8,128)(2,1)} %pad_maximum_fusion.3.refs_0_), channel_id=1, source_target_pairs={{0,16},{4,20},{8,24},{12,28},{16,0},{20,4},{24,8},{28,12},{1,17},{... | collective-permute-start | bytes 2211848 | tf_op jit(solution)/shard_map/ppermute | solution.py:669
  67.0 19.5 %collective-permute-start.11 = (bf16[256,768]{1,0:T(8,128)(2,1)}, bf16[256,768]{1,0:T(8,128)(2,1)S(1)}, u32[]{:S(2)}, u32[]{:S(2)}) collective-permute-start(bf16[256,768]{1,0:T(8,128)(2,1)} %get-tuple-element.270), channel_id=1, source_target_pairs={{0,0},{1,1},{2,4},{3,5},{4,2},{5,3},{6,6},{7,7},{8,8},{9,9},{10,12... | collective-permute-start | bytes 1179656 | tf_op jit(solution)/shard_map/ppermute | solution.py:698
  68.6 17.9 %collective-permute-start.12 = (bf16[256,768]{1,0:T(8,128)(2,1)}, bf16[256,768]{1,0:T(8,128)(2,1)}, u32[]{:S(2)}, u32[]{:S(2)}) collective-permute-start(bf16[256,768]{1,0:T(8,128)(2,1)} %get-tuple-element.269), channel_id=1, source_target_pairs={{0,1},{1,0},{2,5},{3,4},{4,3},{5,2},{6,7},{7,6},{8,9},{9,8},{10,13... | collective-permute-start | bytes 1179656 | tf_op jit(solution)/shard_map/ppermute | solution.py:698
  93.5 22.8 %collective-permute-start.14 = (bf16[384,768]{1,0:T(8,128)(2,1)S(1)}, bf16[384,768]{1,0:T(8,128)(2,1)S(1)}, u32[]{:S(2)}, u32[]{:S(2)}) collective-permute-start(bf16[384,768]{1,0:T(8,128)(2,1)S(1)} %copy-done.42), channel_id=1, source_target_pairs={{0,8},{4,12},{8,0},{12,4},{16,24},{20,28},{24,16},{28,20},{1,9},{5... | collective-permute-start | bytes 1769480 | tf_op jit(solution)/shard_map/ppermute | solution.py:669
  95.0 28.0 %collective-permute-start.15 = (bf16[384,768]{1,0:T(8,128)(2,1)S(1)}, bf16[384,768]{1,0:T(8,128)(2,1)S(1)}, u32[]{:S(2)}, u32[]{:S(2)}) collective-permute-start(bf16[384,768]{1,0:T(8,128)(2,1)S(1)} %copy-done.42), channel_id=1, source_target_pairs={{0,16},{4,20},{8,24},{12,28},{16,0},{20,4},{24,8},{28,12},{1,17},{... | collective-permute-start | bytes 1769480 | tf_op jit(solution)/shard_map/ppermute | solution.py:669
  96.5 26.5 %collective-permute-start.16 = (bf16[384,768]{1,0:T(8,128)(2,1)S(1)}, bf16[384,768]{1,0:T(8,128)(2,1)S(1)}, u32[]{:S(2)}, u32[]{:S(2)}) collective-permute-start(bf16[384,768]{1,0:T(8,128)(2,1)S(1)} %copy-done.42), channel_id=1, source_target_pairs={{0,24},{4,28},{8,16},{12,20},{16,8},{20,12},{24,0},{28,4},{1,25},{... | collective-permute-start | bytes 1769480 | tf_op jit(solution)/shard_map/ppermute | solution.py:669
  169.0 31.6 %collective-permute-start.22 = (bf16[256,768]{1,0:T(8,128)(2,1)}, bf16[256,768]{1,0:T(8,128)(2,1)}, u32[]{:S(2)}, u32[]{:S(2)}) collective-permute-start(bf16[256,768]{1,0:T(8,128)(2,1)} %broadcast_select_fusion.2), channel_id=1, source_target_pairs={{1,0},{0,1},{5,2},{4,3},{3,4},{2,5},{7,6},{6,7},{9,8},{8,9},{13,10... | collective-permute-start | bytes 1179656 | tf_op jit(solution)/shard_map/ppermute | solution.py:713
  170.9 29.7 %collective-permute-start.23 = (bf16[256,768]{1,0:T(8,128)(2,1)S(1)}, bf16[256,768]{1,0:T(8,128)(2,1)}, u32[]{:S(2)}, u32[]{:S(2)}) collective-permute-start(bf16[256,768]{1,0:T(8,128)(2,1)S(1)} %broadcast_select_fusion.3), channel_id=1, source_target_pairs={{0,0},{1,1},{4,2},{5,3},{2,4},{3,5},{6,6},{7,7},{8,8},{9,9},{12,10... | collective-permute-start | bytes 1179656 | tf_op jit(solution)/shard_map/ppermute | solution.py:713
  185.9 36.7 %collective-permute-start.24 = (bf16[2,384,768]{2,1,0:T(8,128)(2,1)}, bf16[2,384,768]{2,1,0:T(8,128)(2,1)}, u32[]{:S(2)}, u32[]{:S(2)}) collective-permute-start(bf16[2,384,768]{2,1,0:T(8,128)(2,1)} %get-tuple-element.179), channel_id=1, source_target_pairs={{0,8},{4,12},{8,0},{12,4},{16,24},{20,28},{24,16},{28,20},{1,9},{5... | collective-permute-start | bytes 3538952 | tf_op jit(solution)/shard_map/ppermute | solution.py:669
  186.9 35.7 %collective-permute-start.25 = (bf16[2,96,3072]{2,1,0:T(8,128)(2,1)}, bf16[2,96,3072]{2,1,0:T(8,128)(2,1)}, u32[]{:S(2)}, u32[]{:S(2)}) collective-permute-start(bf16[2,96,3072]{2,1,0:T(8,128)(2,1)} %get-tuple-element.180), channel_id=1, source_target_pairs={{0,16},{4,20},{8,24},{12,28},{16,0},{20,4},{24,8},{28,12},{1,17},{... | collective-permute-start | bytes 3538952 | tf_op jit(solution)/shard_map/ppermute | solution.py:669
  237.5 20.3 %collective-permute-start.27 = (bf16[4,96,2048]{2,1,0:T(8,128)(2,1)}, bf16[4,96,2048]{2,1,0:T(8,128)(2,1)S(1)}, u32[]{:S(2)}, u32[]{:S(2)}) collective-permute-start(bf16[4,96,2048]{2,1,0:T(8,128)(2,1)} %get-tuple-element.217), channel_id=1, source_target_pairs={{0,4},{4,0},{8,12},{12,8},{16,20},{20,16},{24,28},{28,24},{1,5},{5... | collective-permute-start | bytes 4718600 | tf_op jit(solution)/shard_map/ppermute | solution.py:669
  255.8 16.1 %collective-permute-start.29 = (bf16[1,384,768]{2,1,0:T(8,128)(2,1)}, bf16[1,384,768]{2,1,0:T(8,128)(2,1)S(1)}, u32[]{:S(2)}, u32[]{:S(2)}) collective-permute-start(bf16[1,384,768]{2,1,0:T(8,128)(2,1)} %get-tuple-element.199), channel_id=1, source_target_pairs={{0,16},{4,20},{8,24},{12,28},{16,0},{20,4},{24,8},{28,12},{1,17},{... | collective-permute-start | bytes 1769480 | tf_op jit(solution)/shard_map/ppermute | solution.py:669
  256.8 15.4 %collective-permute-start.30 = (bf16[1,96,3072]{2,1,0:T(8,128)(2,1)S(1)}, bf16[1,96,3072]{2,1,0:T(8,128)(2,1)S(1)}, u32[]{:S(2)}, u32[]{:S(2)}) collective-permute-start(bf16[1,96,3072]{2,1,0:T(8,128)(2,1)S(1)} %copy-done.57), channel_id=1, source_target_pairs={{0,8},{4,12},{8,0},{12,4},{16,24},{20,28},{24,16},{28,20},{1,9},{5... | collective-permute-start | bytes 1769480 | tf_op jit(solution)/shard_map/ppermute | solution.py:669
  271.8 20.8 %collective-permute-start.31 = (bf16[4,96,1280]{2,1,0:T(8,128)(2,1)}, bf16[4,96,1280]{2,1,0:T(8,128)(2,1)S(1)}, u32[]{:S(2)}, u32[]{:S(2)}) collective-permute-start(bf16[4,96,1280]{2,1,0:T(8,128)(2,1)} %get-tuple-element.230), channel_id=1, source_target_pairs={{0,4},{4,0},{8,12},{12,8},{16,20},{20,16},{24,28},{28,24},{1,5},{5... | collective-permute-start | bytes 2949128 | tf_op jit(solution)/shard_map/ppermute | solution.py:669
  276.7 15.9 %collective-permute-start.32 = (bf16[2,24,6144]{2,1,0:T(8,128)(2,1)}, bf16[2,24,6144]{2,1,0:T(8,128)(2,1)S(1)}, u32[]{:S(2)}, u32[]{:S(2)}) collective-permute-start(bf16[2,24,6144]{2,1,0:T(8,128)(2,1)} %get-tuple-element.225), channel_id=1, source_target_pairs={{0,1},{1,0},{2,3},{3,2},{4,5},{5,4},{6,7},{7,6},{8,9},{9,8},{10,11... | collective-permute-start | bytes 1769480 | tf_op jit(solution)/shard_map/ppermute | solution.py:673
  278.8 20.1 %collective-permute-start.33 = (bf16[2,96,2048]{2,1,0:T(8,128)(2,1)S(1)}, bf16[2,96,2048]{2,1,0:T(8,128)(2,1)S(1)}, u32[]{:S(2)}, u32[]{:S(2)}) collective-permute-start(bf16[2,96,2048]{2,1,0:T(8,128)(2,1)S(1)} %copy-done.56), channel_id=1, source_target_pairs={{0,16},{4,20},{8,24},{12,28},{16,0},{20,4},{24,8},{28,12},{1,17},{... | collective-permute-start | bytes 2359304 | tf_op jit(solution)/shard_map/ppermute | solution.py:669
  298.0 13.0 %collective-permute-start.34 = (bf16[2,96,1280]{2,1,0:T(8,128)(2,1)}, bf16[2,96,1280]{2,1,0:T(8,128)(2,1)S(1)}, u32[]{:S(2)}, u32[]{:S(2)}) collective-permute-start(bf16[2,96,1280]{2,1,0:T(8,128)(2,1)} %get-tuple-element.232), channel_id=1, source_target_pairs={{0,8},{4,12},{8,0},{12,4},{16,24},{20,28},{24,16},{28,20},{1,9},{5... | collective-permute-start | bytes 1474568 | tf_op jit(solution)/shard_map/ppermute | solution.py:669
  315.5 27.5 %collective-permute-start.36 = (bf16[1,96,2048]{2,1,0:T(8,128)(2,1)}, bf16[1,96,2048]{2,1,0:T(8,128)(2,1)S(1)}, u32[]{:S(2)}, u32[]{:S(2)}) collective-permute-start(bf16[1,96,2048]{2,1,0:T(8,128)(2,1)} %get-tuple-element.237), channel_id=1, source_target_pairs={{0,8},{4,12},{8,0},{12,4},{16,24},{20,28},{24,16},{28,20},{1,9},{5... | collective-permute-start | bytes 1179656 | tf_op jit(solution)/shard_map/ppermute | solution.py:669
  316.0 23.6 %collective-permute-start.35 = (bf16[1,24,6144]{2,1,0:T(8,128)(2,1)S(1)}, bf16[1,24,6144]{2,1,0:T(8,128)(2,1)S(1)}, u32[]{:S(2)}, u32[]{:S(2)}) collective-permute-start(bf16[1,24,6144]{2,1,0:T(8,128)(2,1)S(1)} %copy-done.58), channel_id=1, source_target_pairs={{0,2},{1,3},{2,0},{3,1},{4,6},{5,7},{6,4},{7,5},{8,10},{9,11},{10,... | collective-permute-start | bytes 884744 | tf_op jit(solution)/shard_map/ppermute | solution.py:673
  319.2 23.7 %collective-permute-start.37 = (bf16[1,96,1280]{2,1,0:T(8,128)(2,1)}, bf16[1,96,1280]{2,1,0:T(8,128)(2,1)S(1)}, u32[]{:S(2)}, u32[]{:S(2)}) collective-permute-start(bf16[1,96,1280]{2,1,0:T(8,128)(2,1)} %get-tuple-element.238), channel_id=1, source_target_pairs={{0,16},{4,20},{8,24},{12,28},{16,0},{20,4},{24,8},{28,12},{1,17},{... | collective-permute-start | bytes 737288 | tf_op jit(solution)/shard_map/ppermute | solution.py:669
  320.9 26.7 %collective-permute-start.38 = (bf16[256,768]{1,0:T(8,128)(2,1)S(1)}, bf16[256,768]{1,0:T(8,128)(2,1)S(1)}, u32[]{:S(2)}, u32[]{:S(2)}) collective-permute-start(bf16[256,768]{1,0:T(8,128)(2,1)S(1)} %broadcast_select_fusion), channel_id=1, source_target_pairs={{1,0},{0,1},{5,2},{4,3},{3,4},{2,5},{7,6},{6,7},{9,8},{8,9},{13,10... | collective-permute-start | bytes 1179656 | tf_op jit(solution)/shard_map/ppermute | solution.py:713
  321.2 26.4 %collective-permute-start.39 = (bf16[256,768]{1,0:T(8,128)(2,1)S(1)}, bf16[256,768]{1,0:T(8,128)(2,1)S(1)}, u32[]{:S(2)}, u32[]{:S(2)}) collective-permute-start(bf16[256,768]{1,0:T(8,128)(2,1)S(1)} %broadcast_select_fusion.1), channel_id=1, source_target_pairs={{0,0},{1,1},{4,2},{5,3},{2,4},{3,5},{6,6},{7,7},{8,8},{9,9},{12,10... | collective-permute-start | bytes 1179656 | tf_op jit(solution)/shard_map/ppermute | solution.py:713
  346.8 9.6 %collective-permute-start.40 = (bf16[2,24,3328]{2,1,0:T(8,128)(2,1)}, bf16[2,24,3328]{2,1,0:T(8,128)(2,1)S(1)}, u32[]{:S(2)}, u32[]{:S(2)}) collective-permute-start(bf16[2,24,3328]{2,1,0:T(8,128)(2,1)} %get-tuple-element.246), channel_id=1, source_target_pairs={{0,1},{1,0},{2,3},{3,2},{4,5},{5,4},{6,7},{7,6},{8,9},{9,8},{10,11... | collective-permute-start | bytes 958472 | tf_op jit(solution)/shard_map/ppermute | solution.py:673
  (69 other events, 310.9 us)
where the time goes:
time: 377 us; the launch traced here: 376 us
  Pallas kernels  172 us (46%)
  waiting for transfers between devices  85.2 us (23%)
  local copies, waits for them, and re-layouts  51 us (14%)
  starting transfers between devices  46.6 us (12%)
  other arithmetic  19.7 us (5%)
    pallas_call x16, Pallas kernels, whole_call(): pl.pallas_call(body, grid_spec=pltpu.PrefetchScalarGridSpec(num_scalar_pr...  121 us
    ppermute x4, waiting for transfers between devices, swap_seq(): lax.ppermute(value, 'seq', [(i, i ^ mask) for i in range(lax.axis_size('s...  45.8 us
    ppermute x30, waiting for transfers between devices, swap_dp(): lax.ppermute(value, 'dp', [(i, i ^ mask) for i in range(lax.axis_size('dp...  39.4 us
    unnamed x118, local copies, waits for them, and re-layouts  32.9 us
    pallas_call x2, Pallas kernels, attend_back(): pl.pallas_call(functools.partial(backward_body, qblock, chunk), grid_spec...  29.9 us
    ppermute x30, starting transfers between devices, swap_dp(): lax.ppermute(value, 'dp', [(i, i ^ mask) for i in range(lax.axis_size('dp...  24.8 us
    pallas_call x1, Pallas kernels, attend_forward(): pl.pallas_call(functools.partial(forward_body, qblock, chunk), grid_spec=...  13.2 us
    ppermute x4, starting transfers between devices, to_sequences(): got.append(lax.ppermute(piece, AXES, spread_pairs(first)))  10.8 us
  transfers between devices with their start and end apart: 42, of which 13 were waited for; matrix products, arithmetic and copies ran while one was open for 6% of the time, Pallas kernels for 31%

commit v1 on v0

v1 whole, which is shorter than its diff:
```python
import functools
import math

import jax
import jax.numpy as jnp
from jax import lax
from jax.experimental import pallas as pl
from jax.experimental.pallas import tpu as pltpu
from jax.sharding import PartitionSpec as P

HEAD_DIM = 64
LANES = 128
NEGATIVE = -1e30


def nt(left, right):
    return lax.dot_general(left, right, (((1,), (1,)), ((), ())), preferred_element_type=jnp.float32)


def nn(left, right):
    return lax.dot_general(left, right, (((1,), (0,)), ((), ())), preferred_element_type=jnp.float32)


def head_parts(block):
    lane = lax.broadcasted_iota(jnp.int32, block.shape, 1)
    zero = jnp.zeros_like(block)
    return (jnp.where(lane < HEAD_DIM, block, zero), jnp.where(lane < HEAD_DIM, zero, block))


def same_document(column_tile, row):
    column = jnp.concatenate([column_tile] * (row.shape[1] // LANES), axis=1)
    return column == jnp.broadcast_to(row, column.shape)


def pair_lanes(pair):
    return slice(pair * LANES, (pair + 1) * LANES)


def segment_tables(segments, tiles, half, qblock, chunk):
    ids = segments[...]
    for j in range(tiles.shape[0]):
        for i in range(chunk // LANES):
            start = j * chunk + i * LANES
            tiles[j, i * LANES : (i + 1) * LANES, :] = jnp.broadcast_to(ids[:, start : start + LANES], (LANES, LANES)).T
    chunks = half // chunk
    low = [jnp.min(ids[:, j * chunk : (j + 1) * chunk]) for j in range(2 * chunks)]
    high = [jnp.max(ids[:, j * chunk : (j + 1) * chunk]) for j in range(2 * chunks)]
    found = []
    for b in range(half // qblock):
        mine = slice(b * qblock, (b + 1) * qblock)
        first, last = jnp.min(ids[:, mine]), jnp.max(ids[:, mine])
        bounds = []
        for side in range(2):
            before = sum((high[side * chunks + j] < first).astype(jnp.int32) for j in range(chunks))
            behind = sum((low[side * chunks + j] > last).astype(jnp.int32) for j in range(chunks))
            bounds += [before, chunks - behind]
        found.append((bounds[0], bounds[1] - bounds[0], bounds[2], bounds[1] - bounds[0] + bounds[3] - bounds[2]))
    return found


def chunk_of(bounds, step, chunks):
    first, own, other, _ = bounds
    return jnp.where(step < own, first + step, chunks + other + step - own)


def forward_body(qblock, chunk, lanes, q_all, k_all, v_all, ko_all, vo_all, segments, o_all, lse_all, kall, vt, sk_ref):
    half = k_all.shape[0]
    tables = segment_tables(segments, sk_ref, half, qblock, chunk)
    chunks, pairs = half // chunk, lanes // LANES

    @pl.loop(0, q_all.shape[1] // lanes)
    def _(group):
        cols = step_of(group, lanes)
        q_ref, k_ref, v_ref, ko_ref, vo_ref, o_ref = (r.at[:, cols] for r in (q_all, k_all, v_all, ko_all, vo_all, o_all))
        lse_ref = lse_all.at[pl.ds(group, 1)]
        for j in range(chunks):
            rows = slice(j * chunk, (j + 1) * chunk)
            kall[j] = k_ref[rows, :]
            kall[chunks + j] = ko_ref[rows, :]
            vt[j] = v_ref[rows, :].T
            vt[chunks + j] = vo_ref[rows, :].T
        for b in range(q_ref.shape[0] // qblock):
            span = slice(b * qblock, (b + 1) * qblock)
            parts = []
            for pair in range(pairs):
                parts += head_parts(q_ref[span, pair_lanes(pair)] * jnp.bfloat16(HEAD_DIM**-0.5))
            row = segments[:, span]

            def one(step, carry):
                j = chunk_of(tables[b], step, chunks)
                mask = same_document(sk_ref[j], row)
                scores = [jnp.where(mask, nt(kall[j, :, pair_lanes(h // 2)], part), NEGATIVE) for h, part in enumerate(parts)]
                out = []
                for h, score in enumerate(scores):
                    top, total, acc = carry[h]
                    new_top = jnp.maximum(top, jnp.max(score, axis=0, keepdims=True))
                    expo = jnp.exp(score - new_top)
                    scale = jnp.exp(top - new_top)
                    total = total * scale + jnp.sum(expo, axis=0, keepdims=True)
                    acc = acc * scale + nn(vt[j, h * HEAD_DIM : (h + 1) * HEAD_DIM, :], expo.astype(jnp.bfloat16))
                    out.append((new_top, total, acc))
                return tuple(out)

            init = (
                jnp.full((1, qblock), NEGATIVE, jnp.float32),
                jnp.zeros((1, qblock), jnp.float32),
                jnp.zeros((HEAD_DIM, qblock), jnp.float32),
            )
            carry = lax.fori_loop(0, tables[b][3], one, (init,) * len(parts))
            result = jnp.concatenate([acc / total for _, total, acc in carry], axis=0)
            o_ref[span, :] = result.T.astype(jnp.bfloat16)
            for h, (top, total, _) in enumerate(carry):
                lse_ref[0, h : h + 1, span] = top + jnp.log(total)


def backward_body(
    qblock, chunk, lanes, side, scalars, q_ref, k_ref, v_ref, ko_ref, vo_ref, o_ref, do_ref, lse_all, segments,
    dq_ref, dk_ref, dv_ref, far_ref, kall, vall, kt, dkall, dvall, sk_ref,
):
    half = k_ref.shape[0]
    tables = segment_tables(segments, sk_ref, half, qblock, chunk)
    lse_ref = lse_all.at[side : side + 1]
    chunks, pairs = half // chunk, lanes // LANES
    for j in range(chunks):
        rows = slice(j * chunk, (j + 1) * chunk)
        kall[j] = k_ref[rows, :]
        kall[chunks + j] = ko_ref[rows, :]
        vall[j] = v_ref[rows, :]
        vall[chunks + j] = vo_ref[rows, :]
        kt[j] = k_ref[rows, :].T
        kt[chunks + j] = ko_ref[rows, :].T
    dkall[...] = jnp.zeros_like(dkall)
    dvall[...] = jnp.zeros_like(dvall)
    for b in range(q_ref.shape[0] // qblock):
        span = slice(b * qblock, (b + 1) * qblock)
        parts, dparts, delta = [], [], []
        for pair in range(pairs):
            parts.append(head_parts(q_ref[span, pair_lanes(pair)] * jnp.bfloat16(HEAD_DIM**-0.5)))
            dparts.append(head_parts(do_ref[span, pair_lanes(pair)]))
            product = do_ref[span, pair_lanes(pair)].astype(jnp.float32) * o_ref[span, pair_lanes(pair)].astype(jnp.float32)
            product = product.T
            delta += [jnp.sum(product[h * HEAD_DIM : (h + 1) * HEAD_DIM], axis=0, keepdims=True) for h in range(2)]
        both = [jnp.concatenate(p, axis=0) for p in parts]
        dboth = [jnp.concatenate(p, axis=0) for p in dparts]
        row = segments[:, span]
        lse = [lse_ref[0, h : h + 1, span] for h in range(2 * pairs)]

        def one(step, carry):
            j = chunk_of(tables[b], step, chunks)
            mask = same_document(sk_ref[j], row)
            out = []
            for pair in range(pairs):
                key, val = kall[j, :, pair_lanes(pair)], vall[j, :, pair_lanes(pair)]
                probs, grads = [], []
                for side in range(2):
                    h = 2 * pair + side
                    score = jnp.where(mask, nt(key, parts[pair][side]), NEGATIVE)
                    prob = jnp.exp(score - lse[h])
                    grad = (prob * (nt(val, dparts[pair][side]) - delta[h])).astype(jnp.bfloat16)
                    probs.append(prob.astype(jnp.bfloat16))
                    grads.append(grad)
                    out.append(carry[h] + nn(kt[j, h * HEAD_DIM : (h + 1) * HEAD_DIM, :], grad))
                dvall[j, :, pair_lanes(pair)] += nn(jnp.concatenate(probs, axis=1), dboth[pair])
                dkall[j, :, pair_lanes(pair)] += nn(jnp.concatenate(grads, axis=1), both[pair])
            return tuple(out)

        zero = jnp.zeros((HEAD_DIM, qblock), jnp.float32)
        carry = lax.fori_loop(0, tables[b][3], one, (zero,) * (2 * pairs))
        dq_ref[span, :] = (jnp.concatenate(carry, axis=0).T * HEAD_DIM**-0.5).astype(jnp.bfloat16)
    for j in range(chunks):
        rows = slice(j * chunk, (j + 1) * chunk)
        dk_ref[rows, :] = dkall[j]
        dv_ref[rows, :] = dvall[j]
        far_ref[0, rows, :] = dkall[chunks + j].astype(jnp.bfloat16)
        far_ref[1, rows, :] = dvall[chunks + j].astype(jnp.bfloat16)


def attend_back(scalars, query, keys, values, keys_other, values_other, attended, grad, lse_rows, segments, qblock, chunk, pairs, side):
    tokens, width = query.shape
    half = keys.shape[0]
    lanes = pairs * LANES
    n = 2 * half // chunk
    f32, b16 = jnp.float32, jnp.bfloat16
    cols = slice(side * lanes, (side + 1) * lanes)
    far = [Far(x, cols) for x in (query, keys, values, keys_other, values_other, attended, grad)]
    return whole_call(
        functools.partial(backward_body, qblock, chunk, lanes, side), "attend_back", scalars, [], far + [lse_rows, segments],
        [array(b16, tokens, lanes), array(f32, half, lanes), array(f32, half, lanes), array(b16, 2, half, lanes)], [],
        [pltpu.VMEM((n, chunk, lanes), b16), pltpu.VMEM((n, chunk, lanes), b16), pltpu.VMEM((n, lanes, chunk), b16),
         pltpu.VMEM((n, chunk, lanes), f32), pltpu.VMEM((n, chunk, lanes), f32), pltpu.VMEM((n, chunk, LANES), f32)], 24,
    )


AXES = ("dp", "seq")
PARTS = 8
SHARDS = 8
epsilon = 1e-12


def tn(left, right):
    return lax.dot_general(left, right, (((0,), (0,)), ((), ())), preferred_element_type=jnp.float32)


def norm_parts(value):
    center = value - jnp.mean(value, axis=-1, keepdims=True)
    spread = jnp.mean(center * center, axis=-1, keepdims=True)
    scale = lax.rsqrt(spread + epsilon)
    return (center * scale, scale)


def norm_back(upstream, normal, scale, gain):
    scaled = upstream * gain
    return scale * (
        scaled
        - jnp.mean(scaled, axis=-1, keepdims=True)
        - normal * jnp.mean(scaled * normal, axis=-1, keepdims=True)
    )


def row_sum(matrix):
    return jnp.sum(matrix.astype(jnp.float32), axis=0, keepdims=True)


def parts_of(refs):
    return [(ref, 0, ref.shape[0]) for ref in refs]


def load_pieces(me, pieces, targets, sems):
    copies = [[] for _ in targets]
    for place, (ref, first, rows) in enumerate(pieces):
        where = pl.ds(pl.multiple_of((me ^ place) * rows, 32), rows)
        for i, (target, columns) in enumerate(targets):
            copy = pltpu.make_async_copy(ref.at[first : first + rows, columns], target.at[where, :], sems.at[i, place])
            copy.start()
            copies[i].append(copy)
    return copies


def wait_all(copies):
    for copy in copies:
        copy.wait()


def step_of(block, size):
    return pl.ds(pl.multiple_of(block * size, size), size)


BLOCK = 256
ROWS = 256


def widen_body(scalars, *refs):
    pieces = parts_of(refs[:SHARDS])
    (attended, tokens, vec, up_add, normal_ref, scale_ref, low_ref, active_ref, slope_ref, wo, wu, sems) = refs[SHARDS:]
    width, wide = wu.shape
    loads = load_pieces(scalars[0], pieces, [(wo, slice(0, width)), (wu, slice(width, width + wide))], sems)
    wait_all(loads[0])

    @pl.loop(0, tokens.shape[0] // ROWS)
    def _(i):
        rows = step_of(i, ROWS)
        branch = nn(attended[rows, :], wo[...]) + vec[2:3, :]
        normal, scale = norm_parts(tokens[rows, :].astype(jnp.float32) + branch)
        first = normal * vec[3:4, :] + vec[4:5, :]
        normal_ref[rows, :] = normal
        scale_ref[rows, :] = jnp.broadcast_to(scale, (ROWS, LANES))
        low_ref[rows, :] = first.astype(jnp.bfloat16)

    wait_all(loads[1])

    @pl.loop(0, wide // BLOCK)
    def _(j):
        cols = step_of(j, BLOCK)
        inner = nn(low_ref[...], wu[:, cols]) + up_add[:, cols]
        cumulative = 0.5 * (1.0 + lax.erf(inner * math.sqrt(0.5)))
        density = jnp.exp(-0.5 * inner * inner) * (1.0 / math.sqrt(2.0 * math.pi))
        active_ref[:, cols] = (inner * cumulative).astype(jnp.bfloat16)
        slope_ref[:, cols] = (cumulative + inner * density).astype(jnp.bfloat16)


def narrow_body(scalars, *refs):
    pieces = parts_of(refs[:SHARDS])
    (active, normal_one, vec, upstream, out_ref, grad_ref, low_ref, sums_ref, send_ref, keep_ref, wd, sums, sems) = refs[SHARDS:]
    wide, width = wd.shape
    (loads,) = load_pieces(scalars[0], pieces, [(wd, slice(0, width))], sems)
    wait_all(loads)
    sums[...] = jnp.zeros_like(sums)

    @pl.loop(0, normal_one.shape[0] // ROWS)
    def _(i):
        rows = step_of(i, ROWS)
        second = nn(active[rows, :], wd[...]) + vec[5:6, :]
        normal, scale = norm_parts(normal_one[rows, :] * vec[3:4, :] + vec[4:5, :] + second)
        out_ref[rows, :] = (normal * vec[6:7, :] + vec[7:8, :]).astype(jnp.bfloat16)
        up = upstream[rows, :].astype(jnp.float32)
        grad = norm_back(up, normal, scale, vec[6:7, :])
        low = grad.astype(jnp.bfloat16)
        grad_ref[rows, :] = grad
        low_ref[rows, :] = low
        sums[0:1, :] += row_sum(low)
        sums[1:2, :] += row_sum(up * normal)
        sums[2:3, :] += row_sum(up)

    sums_ref[...] = sums[...]
    size = wide // PARTS

    @pl.loop(0, PARTS // 2)
    def _(i):
        send_ref[i] = tn(active[:, step_of(2 * i + 1 - scalars[1], size)], low_ref[...]).astype(jnp.bfloat16)
        keep_ref[i] = tn(active[:, step_of(2 * i + scalars[1], size)], low_ref[...]).astype(jnp.bfloat16)


def turn_parts(core, turned, ordered):
    for i in range(PARTS // 2):
        ordered[0, i] = turned[2 * i + 1 - core]
        ordered[1, i] = turned[2 * i + core]


def inner_back_body(scalars, low, wd, slope, first_low, grad_ref, sums_ref, send_ref, keep_ref, turned, ordered):
    size = first_low.shape[1] // PARTS
    flipped = first_low[...].T
    for i in range(PARTS):
        turned[i] = flipped[i * size : (i + 1) * size, :]
    turn_parts(scalars[1], turned, ordered)
    rows = (PARTS // 2) * size

    @pl.loop(0, slope.shape[1] // BLOCK)
    def _(j):
        cols = step_of(j, BLOCK)
        grad = (nt(low[...], wd[cols, :]) * slope[:, cols].astype(jnp.float32)).astype(jnp.bfloat16)
        grad_ref[:, cols] = grad
        sums_ref[:, cols] = row_sum(grad)
        for side, ref in enumerate((send_ref, keep_ref)):
            left = ordered[side].reshape(rows, low.shape[0])
            ref[:, :, cols] = nn(left, grad).astype(jnp.bfloat16).reshape(PARTS // 2, size, BLOCK)


def outer_back_body(scalars, grad, wu, up_grad, normal_ref, scale_ref, vec, wo, attended, sum_ref, result_ref, sums_ref, send_ref, keep_ref, low, sums, turned):
    width = wo.shape[0]
    sums[...] = jnp.zeros_like(sums)

    @pl.loop(0, grad.shape[0] // ROWS)
    def _(i):
        rows = step_of(i, ROWS)
        first = up_grad[rows, :] + nt(grad[rows, :], wu[...])
        normal = normal_ref[rows, :]
        total = norm_back(first, normal, scale_ref[rows, 0:1], vec[3:4, :])
        branch = total.astype(jnp.bfloat16)
        sum_ref[rows, :] = total
        low[rows, :] = branch
        result_ref[rows, :] = nt(branch, wo[...]).astype(jnp.bfloat16)
        sums[0:1, :] += row_sum(branch)
        sums[1:2, :] += row_sum(first * normal)
        sums[2:3, :] += row_sum(first)

    sums_ref[...] = sums[...]
    size = width // PARTS
    product = tn(attended[...], low[...]).astype(jnp.bfloat16)
    for i in range(PARTS):
        turned[i] = product[i * size : (i + 1) * size, :]
    for i in range(PARTS // 2):
        send_ref[i] = turned[2 * i + 1 - scalars[1]]
        keep_ref[i] = turned[2 * i + scalars[1]]


class Far:
    def __init__(self, value, columns=None):
        self.value, self.columns = value, columns
        width = value.shape[-1] if columns is None else columns.stop - columns.start
        self.shape, self.dtype = value.shape[:-1] + (width,), value.dtype


def far_body(body, far, counts, scalars, *refs):
    hbm, inputs, outputs, held = counts
    given = list(refs[hbm : hbm + inputs])
    held_refs, sems = refs[len(refs) - held - 1 : -1], refs[-1]
    copies = []
    for i, (place, columns) in enumerate(far):
        source = given[place] if columns is None else given[place].at[:, columns]
        copies.append(pltpu.make_async_copy(source, held_refs[i], sems.at[i]))
        copies[-1].start()
        given[place] = held_refs[i]
    for copy in copies:
        copy.wait()
    body(scalars, *refs[:hbm], *given, *refs[hbm + inputs : len(refs) - held - 1])


def whole_call(body, name, scalars, hbm, inputs, outputs, hbm_outputs, scratch, room=8):
    shape_of = lambda x: jax.ShapeDtypeStruct(x.shape, x.dtype)
    near, stay = pl.BlockSpec(memory_space=pltpu.VMEM), pl.BlockSpec(memory_space=pltpu.HBM)
    far = [(i, x.columns) for i, x in enumerate(inputs) if isinstance(x, Far)]
    scratch = list(scratch)
    if far:
        held = [pltpu.VMEM(inputs[i].shape, inputs[i].dtype) for i, _ in far]
        counts = (len(hbm), len(inputs), len(outputs) + len(hbm_outputs), len(far))
        body = functools.partial(far_body, body, far, counts)
        scratch += held + [pltpu.SemaphoreType.DMA((len(far),))]
        room += sum(math.prod(inputs[i].shape) * inputs[i].dtype.itemsize for i, _ in far) // (1 << 20) + 1
    return pl.pallas_call(
        body,
        in_specs=[pl.BlockSpec(memory_space=pltpu.SMEM)]
        + [stay] * len(hbm)
        + [stay if isinstance(x, Far) else near for x in inputs],
        out_specs=[near] * len(outputs) + [stay] * len(hbm_outputs),
        scratch_shapes=scratch,
        out_shape=[shape_of(x) for x in list(outputs) + list(hbm_outputs)],
        cost_estimate=pl.CostEstimate(flops=1, transcendentals=0, bytes_accessed=1),
        compiler_params=pltpu.CompilerParams(vmem_limit_bytes=room << 20),
        name=name,
    )(scalars, *hbm, *[x.value if isinstance(x, Far) else x for x in inputs])


def array(dtype, *shape):
    return jax.ShapeDtypeStruct(shape, dtype)


def widen(scalars, pieces, attended, tokens, vec, up_add):
    count, width = tokens.shape
    wide = up_add.shape[1]
    f32, b16 = jnp.float32, jnp.bfloat16
    return whole_call(
        widen_body, "widen", scalars, pieces, [attended, tokens, vec, up_add],
        [array(f32, count, width), array(f32, count, LANES), array(b16, count, width),
         array(b16, count, wide), array(b16, count, wide), array(b16, width, width), array(b16, width, wide)],
        [], [pltpu.SemaphoreType.DMA((2, PARTS))],
    )


def narrow(scalars, pieces, active, normal, vec, upstream):
    count, wide = active.shape
    width = normal.shape[1]
    f32, b16 = jnp.float32, jnp.bfloat16
    half = array(b16, PARTS // 2, wide // PARTS, width)
    return whole_call(
        narrow_body, "narrow", scalars, pieces, [active, normal, vec, upstream],
        [array(b16, count, width), array(f32, count, width), array(b16, count, width), array(f32, 8, width), half, half, array(b16, wide, width)],
        [], [pltpu.VMEM((8, width), f32), pltpu.SemaphoreType.DMA((1, PARTS))],
    )


def inner_back(scalars, low, wd, slope, first_low):
    count, wide = slope.shape
    width = low.shape[1]
    size = width // PARTS
    f32, b16 = jnp.float32, jnp.bfloat16
    half = array(b16, PARTS // 2, size, wide)
    return whole_call(
        inner_back_body, "inner_back", scalars, [], [low, wd, slope, first_low],
        [array(b16, count, wide), array(f32, 1, wide), half, half], [],
        [pltpu.VMEM((PARTS, size, count), b16), pltpu.VMEM((2, PARTS // 2, size, count), b16)],
    )


def outer_back(scalars, grad, wu, up_grad, normal, scale, vec, wo, attended):
    count, width = normal.shape
    f32, b16 = jnp.float32, jnp.bfloat16
    half = array(b16, PARTS // 2, width // PARTS, width)
    return whole_call(
        outer_back_body, "outer_back", scalars, [], [grad, wu, up_grad, normal, scale, vec, wo, attended],
        [array(f32, count, width), array(b16, count, width), array(f32, 8, width), half, half], [],
        [pltpu.VMEM((count, width), b16), pltpu.VMEM((8, width), f32), pltpu.VMEM((PARTS, width // PARTS, width), b16)],
    )


def sums_to_slots(core, lines, parts, send, keep, first, wide=None):
    turned = lines[...].T
    rows = turned.shape[0] // PARTS
    for i in range(PARTS):
        parts[i] = turned[i * rows : (i + 1) * rows, :]
    if wide is not None:
        size = wide.shape[1] // (4 * PARTS)
        for i in range(4 * PARTS):
            place = (i % 4) * (rows // 4)
            parts[i // 4, place : place + 1, LANES - size :] = wide[:, i * size : (i + 1) * size]
    for i in range(PARTS // 2):
        send[i, :, first : first + LANES] = parts[2 * i + 1 - core].astype(jnp.bfloat16)
        keep[i, :, first : first + LANES] = parts[2 * i + core].astype(jnp.bfloat16)


def qkv_back_body(side, scalars, dq, dk, dv, far, ordered, weight, gradient, *refs):
    core = scalars[1]
    if side == 0:
        out_send, out_keep, sums_one, sums_two, wide_sums, send, keep, result, sums_ref, both, lines, parts = refs
    else:
        first_sums, send, keep, result, sums_ref, both, lines, parts = refs
    half = dq.shape[1]
    both[:, :half] = dq[...]
    both[:, half : 2 * half] = (dk[...] + far[0].astype(jnp.float32)).astype(jnp.bfloat16)
    both[:, 2 * half :] = (dv[...] + far[1].astype(jnp.float32)).astype(jnp.bfloat16)
    sums_ref[...] = jnp.zeros_like(sums_ref)
    sums_ref[0:1, :] = row_sum(dq[...])
    sums_ref[1:2, :] = row_sum(both[:, 2 * half :])
    rows = ordered.shape[1] * ordered.shape[2]
    for i, ref in enumerate((send, keep)):
        left = ordered[i].reshape(rows, ordered.shape[3])
        product = nn(left, both[...]).astype(jnp.bfloat16)
        ref[:, :, : 3 * half] = product.reshape(ordered.shape[1], ordered.shape[2], 3 * half)
    lines[...] = jnp.zeros_like(lines)
    if side == 0:
        width = out_send.shape[2]
        send[:, :, 3 * half : 3 * half + width] = out_send[...]
        keep[:, :, 3 * half : 3 * half + width] = out_keep[...]
        lines[0:8, :] = sums_one[...]
        lines[8:16, :] = sums_two[...]
        sums_to_slots(core, lines, parts, send, keep, 3 * half + width, wide_sums)
    else:
        lines[0:8, :half] = first_sums[...]
        lines[0:8, half:] = sums_ref[...]
        sums_to_slots(core, lines, parts, send, keep, 3 * half)
    result[...] = (gradient[...] + nt(both[...], weight[side])).astype(result.dtype)


def qkv_back(side, scalars, dq, dk, dv, far, ordered, weights, gradient, *more):
    count, half = dq.shape
    width = gradient.shape[1]
    f32, b16 = jnp.float32, jnp.bfloat16
    total = array(b16, PARTS // 2, width // PARTS, 3 * half + LANES + (width if side == 0 else 0))
    return whole_call(
        functools.partial(qkv_back_body, side), "qkv_back", scalars, [], [dq, dk, dv, far, Far(ordered), Far(weights), gradient, *more],
        [total, total, array(b16 if side else f32, count, width), array(f32, 8, half)], [],
        [pltpu.VMEM((count, 3 * half), b16), pltpu.VMEM((LANES, width), f32), pltpu.VMEM((PARTS, width // PARTS, LANES), f32)],
    )


STRIPE = 32


def fold_body(plans, scalars, *refs):
    for item, (outer, inner, bit) in enumerate(plans):
        keep, got = refs[2 * item : 2 * item + 2]
        send, left = refs[2 * (len(plans) + item) : 2 * (len(plans) + item) + 2]
        mine = scalars[bit]
        rows = keep.shape[1]
        stripe = STRIPE if rows % STRIPE == 0 else rows

        @pl.loop(0, rows // stripe)
        def _(k):
            span = step_of(k, stripe) if stripe != rows else slice(None)
            for i in range(outer):
                for j in range(inner):
                    for target, side in ((send, 1 - mine), (left, mine)):
                        place = (2 * i + side) * inner + j
                        value = keep[place, span, :].astype(jnp.float32) + got[place, span, :].astype(jnp.float32)
                        target[i * inner + j, span, :] = value.astype(target.dtype)


def fold(scalars, items):
    outs, plans = [], []
    for keep, got, (outer, inner, bit) in items:
        shape = (keep.shape[0] // 2,) + keep.shape[1:]
        outs += [array(jnp.bfloat16, *shape), array(keep.dtype, *shape)]
        plans.append((outer, inner, bit))
    got = whole_call(
        functools.partial(fold_body, plans), "fold", scalars, [], [x for keep, got, _ in items for x in (keep, got)], outs, [], []
    )
    return [(got[2 * i], got[2 * i + 1]) for i in range(len(items))]


def merge_body(shapes, scalars, *refs):
    send, left = refs[-2:]
    mine = scalars[4]
    low = send.shape[1]
    first = 0
    for item, (rows, wide) in enumerate(shapes):
        keep, got = refs[2 * item : 2 * item + 2]
        for part in range(rows // low):
            span = slice(part * low, (part + 1) * low)
            for high in range(2):
                for target, side in ((send, 1 - mine), (left, mine)):
                    value = keep[2 * high + side, span, :].astype(jnp.float32) + got[2 * high + side, span, :].astype(jnp.float32)
                    target[high, :, first : first + wide] = value.astype(target.dtype)
            first += wide


def merge(scalars, items, low):
    items = [(k.reshape(4, k.shape[-2] // 4, k.shape[-1]), g.reshape(4, g.shape[-2] // 4, g.shape[-1])) for k, g in items]
    shapes = [k.shape[1:] for k, _ in items]
    wide = sum(rows // low * n for rows, n in shapes)
    return whole_call(
        functools.partial(merge_body, shapes), "merge", scalars, [], [x for pair in items for x in pair],
        [array(jnp.bfloat16, 2, low, wide), array(jnp.float32, 2, low, wide)], [], [],
    )


def last_ff_body(scalars, keep, got, down_ref, up_ref):
    low = keep.shape[1]
    width = down_ref.shape[1]
    for part in range(down_ref.shape[0] // low):
        cols = slice(part * width, (part + 1) * width)
        down_ref[part * low : (part + 1) * low, :] = keep[0, :, cols] + got[0, :, cols].astype(jnp.float32)
    cols = slice(4 * width, 4 * width + up_ref.shape[1])
    up_ref[...] = keep[0, :, cols] + got[0, :, cols].astype(jnp.float32)


def last_ff(scalars, keep, got, width):
    low = keep.shape[1]
    return whole_call(
        last_ff_body, "last_ff", scalars, [], [keep, got], [array(jnp.float32, 4 * low, width), array(jnp.float32, low, 4 * width)], [], []
    )


def last_qkv_body(scalars, keep, got, query_ref, key_ref, value_ref, out_ref, small_ref, late_ref, wide_ref, turned):
    low = keep.shape[1]
    width = query_ref.shape[1]
    half = width // 2
    second = 3 * half + width + LANES

    def total(first, size):
        return keep[0, :, first : first + size] + got[0, :, first : first + size].astype(jnp.float32)

    for i, ref in enumerate((query_ref, key_ref, value_ref)):
        ref[:, :half] = total(i * half, half)
        ref[:, half:] = total(second + i * half, half)
    out_ref[...] = total(3 * half, width)
    wide_ref[...] = total(3 * half + width, LANES)[0:1, :]
    for ref, first in ((small_ref, 3 * half + width), (late_ref, second + 3 * half)):
        turned[...] = jnp.zeros_like(turned)
        turned[:low, :] = total(first, LANES)
        ref[...] = turned[...].T[: ref.shape[0], :]


def last_qkv(scalars, keep, got, width):
    low = keep.shape[1]
    f32 = jnp.float32
    return whole_call(
        last_qkv_body, "last_qkv", scalars, [], [keep, got],
        [array(f32, low, width)] * 4 + [array(f32, 24, LANES), array(f32, 8, LANES), array(f32, 1, LANES)], [], [pltpu.VMEM((LANES, LANES), f32)],
    )


def after(value, *others):
    return lax.optimization_barrier((value,) + others)[0]


def bit_count(size):
    return size.bit_length() - 1


def swap_dp(value, mask):
    return lax.ppermute(value, "dp", [(i, i ^ mask) for i in range(lax.axis_size("dp"))])


def swap_seq(value, mask):
    return lax.ppermute(value, "seq", [(i, i ^ mask) for i in range(lax.axis_size("seq"))])


def column_sum(matrix):
    return jnp.sum(matrix.astype(jnp.float32), axis=0)


def spread_pairs(first):
    dps, seqs = lax.axis_size("dp"), lax.axis_size("seq")
    pairs = []
    for dp in range(dps):
        for seq in range(seqs):
            piece = first ^ (seq & 1)
            to_dp = (dp & ~1) | (seq >> 1)
            to_seq = 2 * (dp & 1) + piece
            pairs.append((dp * seqs + seq, to_dp * seqs + to_seq))
    return pairs


def to_sequences(local, order):
    odd = (lax.axis_index("seq") & 1) == 1
    got = []
    pieces = [jnp.where(odd, local[1 - first], local[first]) for first in range(2)]
    order.mark(*pieces)
    for first, piece in enumerate(pieces):
        got.append(lax.ppermute(piece, AXES, spread_pairs(first)))
    return got, odd


def in_order(got, odd, rows):
    return jnp.where(odd, jnp.concatenate([g[:rows] for g in got[::-1]]), jnp.concatenate([g[:rows] for g in got]))


def from_sequences(tokens, order):
    odd = (lax.axis_index("seq") & 1) == 1
    half = tokens.shape[0] // 2
    got = []
    for first in range(2):
        near, far = tokens[first * half : (first + 1) * half], tokens[(1 - first) * half : (2 - first) * half]
        piece = order.mark(jnp.where(order.gate(odd), far, near))
        got.append(lax.ppermute(piece, AXES, [(b, a) for a, b in spread_pairs(first)]))
    return got


def both_sequences(order, got):
    odd = order.gate((lax.axis_index("seq") & 1) == 1)
    return jnp.where(odd, jnp.stack(got[::-1]), jnp.stack(got))


def weight_lines(weights, lines):
    width = weights[0].shape[-1]
    lines = [jnp.pad(v[..., None, :], [(0, 0)] * v.ndim + [(0, width - v.shape[-1])]) for v in lines]
    lines.append(jnp.zeros(lines[0].shape[:-2] + (16 - len(lines), width), jnp.bfloat16))
    return jnp.concatenate(weights + lines, axis=-2)


def near_shards(part):
    if lax.axis_size("dp") != PARTS:
        p = part if part.ndim == 3 else jnp.stack(jnp.split(lax.all_gather(part, "dp", axis=0, tiled=True), PARTS))
        return [p[i] for i in range(PARTS)]
    return [part, swap_dp(part, 2), swap_dp(part, 4), swap_dp(part, 6)]


def all_shards(near, *ready):
    if len(near) == PARTS:
        return near
    near = [near[0]] + list(lax.optimization_barrier((*near[1:], *ready))[:3])
    shards = []
    for part in near:
        shards += [part, swap_dp(part, 1)]
    return shards


def pack_body(scalars, query, key, value, *refs):
    vectors, (part, lines) = refs[:-2], refs[-2:]
    rows = query.shape[0]
    for i, ref in enumerate((query, key, value)):
        part[i * rows : (i + 1) * rows, :] = ref[...]
    lines[...] = jnp.zeros_like(lines)
    for i, ref in enumerate(vectors):
        lines[i : i + 1, : ref.shape[1]] = ref[...].astype(jnp.float32)
    part[3 * rows :, :] = lines[...].astype(jnp.bfloat16)


def projection_part(scalars, weights, vectors):
    if lax.axis_size("dp") == PARTS:
        rows, width = weights[0].shape
        return whole_call(
            pack_body, "pack", scalars, [], weights + [v[None, :] for v in vectors],
            [array(jnp.bfloat16, 3 * rows + 16, width)], [], [pltpu.VMEM((16, width), jnp.float32)],
        )[0]
    gather = lambda v: lax.all_gather(v, "dp", axis=0, tiled=True)
    split = lambda v: gather(v).reshape((PARTS, -1) + v.shape[1:])
    return weight_lines([split(w) for w in weights], [split(v) for v in vectors])


def spread_body(scalars, hidden, ids, *pieces):
    odd = scalars[7]
    block, half = hidden.shape[1], ids.shape[1] // 2
    for first, piece in enumerate(pieces):
        piece[:block, :] = hidden[first ^ odd]
        line = jnp.where(first ^ odd == 0, ids[0:1, :], ids[1:2, :]).astype(jnp.bfloat16)
        piece[block:, :] = jnp.zeros_like(piece[block:, :])
        piece[block : block + 1, :half] = line[:, :half]
        piece[block + 1 : block + 2, :half] = line[:, half:]


def spread_hidden(scalars, hidden, ids):
    piece = array(jnp.bfloat16, hidden.shape[1] + 16, hidden.shape[2])
    pieces = whole_call(spread_body, "spread", scalars, [], [hidden, ids], [piece, piece], [], [])
    return [lax.ppermute(piece, AXES, spread_pairs(first)) for first, piece in enumerate(pieces)]


def project_body(sizes, scalars, *refs):
    rows, wide, vectors, qblock, chunk, lanes = sizes
    pieces, hidden = parts_of(refs[:SHARDS]), refs[SHARDS : SHARDS + 4]
    (
        attended, lse, tokens, vec_ref, up_ref, segments, ordered, query_out, keys_out, values_out, keys_far_out, values_far_out, weights_out,
        query, keys, values, keys_far, values_far, far, held, small, turned, ids, sems, small_sems, hidden_sems, out_sems, kall, vt, tiles,
    ) = refs[SHARDS + 4 :]
    count, width = tokens.shape
    block = count // 2
    half = width // 2
    core, odd = scalars[6], scalars[7]
    copies, brought = [], []

    def start(copies, source, target, sem):
        copies.append(pltpu.make_async_copy(source, target, sem))
        copies[-1].start()

    for i, (ref, place) in enumerate(zip(hidden, (0, 1, 0, 1))):
        goal = tokens if i < 2 else far
        start(brought, ref.at[:block, :], goal.at[pl.ds(pl.multiple_of((place ^ odd) * block, block), block), :], hidden_sems.at[i])
    start(brought, hidden[0].at[block:, :], ids, hidden_sems.at[4])
    for place, (ref, _, size) in enumerate(pieces):
        where = scalars[0] ^ place
        start(copies, ref.at[3 * rows : size, :], small.at[where], small_sems.at[place])
        target = pl.ds(where * rows, rows)
        for weight in range(3):
            for side in range(2):
                start(
                    copies,
                    ref.at[weight * rows : (weight + 1) * rows, side * half : (side + 1) * half],
                    held.at[side, target, weight * half : (weight + 1) * half],
                    sems.at[len(copies) - place - 1],
                )
    wait_all(brought)
    line = ids[...].astype(jnp.float32)
    for i in range(2):
        segments[:, i * count : (i + 1) * count] = jnp.where(core == i, line[0:1, :count], line[1:2, :count])
    flipped = tokens[...].T
    for i in range(PARTS):
        turned[i] = flipped[i * rows : (i + 1) * rows, :]
    turn_parts(scalars[1], turned, ordered)
    wait_all(copies)
    saves = []
    start(saves, held, weights_out, out_sems.at[0])
    vec_ref[...] = jnp.concatenate([small[i, :, :rows] for i in range(PARTS)], axis=1).astype(jnp.float32)
    up_ref[...] = jnp.concatenate([small[i, vectors : vectors + 1, :wide] for i in range(PARTS)], axis=1).astype(jnp.float32)
    for i, (weight, add, goal, source, out) in enumerate((
        (1, None, keys, tokens, keys_out), (1, None, keys_far, far, keys_far_out), (2, 1, values, tokens, values_out),
        (2, 1, values_far, far, values_far_out), (0, 0, query, tokens, query_out),
    )):
        for side in range(2):
            cols = slice(side * half, (side + 1) * half)
            product = nn(source[...], held[side, :, weight * half : (weight + 1) * half])
            if add is not None:
                product = product + vec_ref[add : add + 1, cols]
            goal[:, cols] = product.astype(jnp.bfloat16)
        start(saves, goal, out, out_sems.at[i + 1])
    forward_body(qblock, chunk, lanes, query, keys, values, keys_far, values_far, segments, attended, lse, kall, vt, tiles)
    wait_all(saves)


def project(scalars, pieces, hidden, rows, wide, vectors, qblock, chunk, lanes):
    block, width = hidden[0].shape[0] - 16, hidden[0].shape[1]
    count = 2 * block
    lines = pieces[0].shape[-2] - 3 * rows
    n = 2 * count // chunk
    f32, b16 = jnp.float32, jnp.bfloat16
    whole = array(b16, count, width)
    vmem = lambda x: pltpu.VMEM(x.shape, x.dtype)
    return whole_call(
        functools.partial(project_body, (rows, wide, vectors, qblock, chunk, lanes)), "project", scalars, list(pieces) + list(hidden), [],
        [whole, array(f32, width // lanes, 8, count), whole, array(f32, lines, width), array(f32, 1, wide * PARTS), array(f32, 1, 2 * count),
         array(b16, 2, PARTS // 2, rows, count)],
        [whole] * 5 + [array(b16, 2, width, 3 * width // 2)],
        [vmem(whole)] * 6
        + [pltpu.VMEM((2, width, 3 * width // 2), b16), pltpu.VMEM((PARTS, lines, width), b16), pltpu.VMEM((PARTS, rows, count), b16),
           pltpu.VMEM((16, width), b16), pltpu.SemaphoreType.DMA((6 * PARTS,)), pltpu.SemaphoreType.DMA((PARTS,)),
           pltpu.SemaphoreType.DMA((5,)), pltpu.SemaphoreType.DMA((6,)), pltpu.VMEM((n, chunk, lanes), b16),
           pltpu.VMEM((n, lanes, chunk), b16), pltpu.VMEM((n, chunk, LANES), f32)],
        28,
    )


class Order:
    def __init__(self):
        self.last = ()

    def gate(self, value):
        return lax.optimization_barrier((value, *self.last))[0] if self.last else value

    def mark(self, *values):
        self.last = values
        return values[0] if len(values) == 1 else values


def all_rows(send, keep):
    return jnp.stack([keep, send], axis=1).reshape(-1, keep.shape[-1]).astype(jnp.float32)


def scatter_all(send, keep):
    return lax.psum_scatter(all_rows(send, keep), AXES, scatter_dimension=0, tiled=True)


def per_device(
    hidden_in, segment_ids, query_weight, query_bias, key_weight, value_weight, value_bias, out_weight, out_bias,
    first_gain, first_shift, up_weight, up_bias, down_weight, down_bias, second_gain, second_shift, cotangent,
):
    dps, seqs = lax.axis_size("dp"), lax.axis_size("seq")
    inner_width, width = up_weight.shape[1], query_weight.shape[1]
    devices = dps * seqs
    share = width // devices
    qblock = chunk = 256
    pairs = 3
    direct = dps == PARTS and seqs == 4
    dp, seq = lax.axis_index("dp"), lax.axis_index("seq")
    if direct:
        scalars = [dp, dp & 1, (dp >> 1) & 1, dp >> 2, seq & 1, seq >> 1, dp & 1, seq & 1]
    else:
        scalars = [0, 0, 0, 0, 0, 0, dp & 1, seq & 1]
    scalars = jnp.stack([jnp.asarray(v, jnp.int32) for v in scalars])

    vectors = [query_bias, value_bias, out_bias, first_gain, first_shift, down_bias, second_gain, second_shift]
    part = projection_part(scalars, [query_weight, key_weight, value_weight], vectors + [up_bias])
    near = near_shards(part)
    hidden = spread_hidden(after(scalars, part), hidden_in, segment_ids)
    out_up, down_part = lax.optimization_barrier((jnp.concatenate([out_weight, up_weight], axis=1), down_weight, *near[1:4]))[:2]
    shards = all_shards(near)
    hidden += [swap_dp(piece, 1) for piece in hidden]
    out_up_near = near_shards(out_up)
    attended, lse, tokens, vec, up_add, segments, ordered, query, keys, values, keys_other, values_other, w_qkv = project(
        scalars, shards, hidden, width // PARTS, inner_width // PARTS, len(vectors), qblock, chunk, pairs * LANES
    )
    order = Order()
    got_up, odd = to_sequences(after(cotangent, *near[1:4], *hidden[:2]), order)
    upstream = in_order(lax.optimization_barrier((*got_up, attended))[:2], odd, hidden_in.shape[1])
    out_up_shards = all_shards(out_up_near, attended, upstream)
    down_near = near_shards(after(down_part, attended, *out_up_near[1:4]))
    normal_one, scale_one, first_low, active, slope, wo, wu = widen(scalars, out_up_shards, attended, tokens, vec, up_add)
    layer_low, sum_two_grad, second_grad, sums_two, down_send, down_keep, wd = narrow(
        scalars, all_shards(down_near, active), active, normal_one, vec, upstream
    )
    swap = (lambda value: swap_dp(value, 1)) if direct else (lambda value: value)
    order = Order()
    order.mark(second_grad)
    down_got = swap(down_send)
    out_pieces = from_sequences(layer_low, order)
    inner_grad, up_sum, up_send, up_keep = inner_back(scalars, order.gate(second_grad), wd, slope, first_low)
    up_got = swap(up_send)
    order.mark(inner_grad)
    if direct:
        ((send, down_keep),) = fold(order.gate(scalars), [(down_keep, down_got, (2, 1, 2))])
        down_got = swap_dp(order.mark(send), 2)
        ((send, up_keep),) = fold(order.gate(scalars), [(up_keep, up_got, (1, 2, 3))])
        up_got = swap_dp(order.mark(send), 4)
    sum_one_grad, attended_grad, sums_one, out_send, out_keep = outer_back(
        order.gate(scalars), inner_grad, wu, sum_two_grad, normal_one, scale_one, vec, wo, attended
    )
    order.mark(attended_grad)
    layer_out = order.mark(both_sequences(order, out_pieces))

    def attend(side):
        given = (query, keys, values, keys_other, values_other, attended, attended_grad, lse, segments)
        return order.mark(*attend_back(order.gate(scalars), *given, qblock, chunk, pairs, side))

    dq, dk, dv, far = attend(0)
    if direct:
        (send, down_keep), (other, up_keep) = fold(
            order.gate(scalars), [(down_keep, down_got, (1, 1, 3)), (up_keep, up_got, (1, 1, 2))]
        )
        order.mark(send, other)
        down_got, up_got = swap_dp(send, 4), swap_dp(other, 2)
    one_send, one_keep, gradient, sums_first = qkv_back(
        0, order.gate(scalars), dq, dk, dv, swap_dp(order.gate(far), 1), ordered, w_qkv, sum_one_grad, out_send, out_keep,
        sums_one, sums_two, up_sum
    )
    order.mark(gradient)
    one_got = swap(one_send)
    dq, dk, dv, far = attend(1)
    if direct:
        send, ff_keep = merge(order.gate(scalars), [(down_keep, down_got), (up_keep, up_got)], share)
        ff_got = swap_seq(order.mark(send), 1)
        ((send, one_keep),) = fold(order.gate(scalars), [(one_keep, one_got, (1, 2, 3))])
        one_got = swap_dp(order.mark(send), 4)
    two_send, two_keep, gradient, _ = qkv_back(
        1, order.gate(scalars), dq, dk, dv, swap_dp(order.gate(far), 1), ordered, w_qkv, gradient, sums_first
    )
    order.mark(gradient)
    two_got = swap(two_send)
    in_pieces = from_sequences(gradient, order)
    if not direct:
        down_grad, up_grad = scatter_all(down_send, down_keep), scatter_all(up_send, up_keep)
        one, two = scatter_all(one_send, one_keep), scatter_all(two_send, two_keep)
        cut = width // 2
        query_grad, key_grad, value_grad = [
            jnp.concatenate([side[:, i * cut : (i + 1) * cut] for side in (one, two)], axis=1) for i in range(3)
        ]
        out_grad = one[:, 3 * cut : 3 * cut + width]
        small, late = one[:, 3 * cut + width :].T, two[:, 3 * cut :].T
        up_bias_grad = lax.psum_scatter(up_sum[0], AXES, scatter_dimension=0, tiled=True)
    else:
        ((send, two_keep),) = fold(order.gate(scalars), [(two_keep, two_got, (2, 1, 2))])
        two_got = swap_dp(order.mark(send), 2)
        ((send, one_keep),) = fold(order.gate(scalars), [(one_keep, one_got, (1, 1, 2))])
        one_got = swap_dp(order.mark(send), 2)
        ((send, ff_keep),) = fold(order.gate(scalars), [(ff_keep, ff_got, (1, 1, 5))])
        ff_got = swap_seq(order.mark(send), 2)
        ((send, two_keep),) = fold(order.gate(scalars), [(two_keep, two_got, (1, 1, 3))])
        two_got = swap_dp(order.mark(send), 4)
        send, keep = merge(order.gate(scalars), [(one_keep, one_got), (two_keep, two_got)], share)
        got = swap_seq(order.mark(send), 1)
        down_grad, up_grad = order.mark(*last_ff(order.gate(scalars), ff_keep, ff_got, width))
        ((send, keep),) = fold(order.gate(scalars), [(keep, got, (1, 1, 5))])
        got = swap_seq(order.mark(send), 2)
    input_grad = order.mark(both_sequences(order, in_pieces).astype(jnp.float32))
    if direct:
        query_grad, key_grad, value_grad, out_grad, small, late, line = last_qkv(order.gate(scalars), keep, got, width)
        up_bias_grad = line[0, LANES - inner_width // devices :]
    ob, g1, s1 = [small[i, :share] for i in (0, 1, 2)]
    db, g2, s2 = [small[i, :share] for i in (8, 9, 10)]
    qb, vb = [late[i, :share] for i in (0, 1)]
    return (
        layer_out, input_grad, query_grad, qb, key_grad, value_grad, vb, out_grad, ob, g1, s1, up_grad, up_bias_grad, down_grad, db, g2, s2,
    )


def solution(mesh):
    wide, flat = P("dp", None), P("dp")
    in_specs = (
        P("dp", "seq", None), wide, wide, flat, wide, wide, flat, wide, flat, flat, flat, wide, flat, wide, flat,
        flat, flat, P("dp", "seq", None),
    )
    rows, cells = P(AXES, None), P(AXES)
    out_specs = (
        P("dp", "seq", None), P("dp", "seq", None), rows, cells, rows, rows, cells, rows, cells, cells, cells, rows,
        cells, rows, cells, cells, cells,
    )
    return jax.shard_map(per_device, mesh=mesh, in_specs=in_specs, out_specs=out_specs, check_vma=False)
```

time: 377 us -> 277 us (0.73)
  Pallas kernels: 172 us -> 108 us
  local copies, waits for them, and re-layouts: 51 us -> 11.7 us
  other arithmetic: 19.7 us -> 3.99 us
  starting transfers between devices: 46.6 us -> 57.8 us
  waiting for transfers between devices: 85.2 us -> 93.6 us
    pallas_call x20 -> x24, Pallas kernels: 172 us -> 108 us  [whole_call(): pl.pallas_call(body, in_specs=[pl.BlockSpec(memory_space=pltpu.SMEM)] + [...]
    unnamed x118 -> x32, local copies, waits for them, and re-layouts: 32.9 us -> 9.81 us
    ppermute x4, waiting for transfers between devices: 45.8 us -> 27.4 us  [swap_seq(): lax.ppermute(value, 'seq', [(i, i ^ mask) for i in range(lax.axis_size('s...]
    ppermute x30 -> x37, starting transfers between devices: 24.8 us -> 43 us  [swap_dp(): lax.ppermute(value, 'dp', [(i, i ^ mask) for i in range(lax.axis_size('dp...]
    ppermute x30 -> x37, waiting for transfers between devices: 39.4 us -> 53.7 us  [swap_dp(): lax.ppermute(value, 'dp', [(i, i ^ mask) for i in range(lax.axis_size('dp...]
    ppermute x0 -> x2, waiting for transfers between devices: none -> 9.88 us  [spread_hidden(): lax.ppermute(piece, AXES, spread_pairs(first))]
    ppermute x4 -> x2, starting transfers between devices: 10.8 us -> 3.86 us  [to_sequences(): got.append(lax.ppermute(piece, AXES, spread_pairs(first)))]
    pad x10 -> x0, local copies, waits for them, and re-layouts: 5.91 us -> none  [the longest x9 5.3 us: weight_lines(): jnp.pad(v[..., None, :], [(0, 0)] * v.ndim + [(0, width - v.shape[-1])])]
  transfers between devices with their start and end apart: 42 -> 49, of which waited for: 13 -> 20; matrix products, arithmetic and copies ran while one was open for 6% -> 1% of each run, Pallas kernels for 31% -> 31%
where the time goes in v1:
time: 277 us; the launch traced here: 276 us
  Pallas kernels  108 us (39%)
  waiting for transfers between devices  93.6 us (34%)
  starting transfers between devices  57.8 us (21%)
  local copies, waits for them, and re-layouts  11.7 us (4%)
  other arithmetic  3.99 us (1%)
    pallas_call x24, Pallas kernels, whole_call(): pl.pallas_call(body, in_specs=[pl.BlockSpec(memory_space=pltpu.SMEM)] + [...  108 us
    ppermute x37, waiting for transfers between devices, swap_dp(): lax.ppermute(value, 'dp', [(i, i ^ mask) for i in range(lax.axis_size('dp...  53.7 us
    ppermute x37, starting transfers between devices, swap_dp(): lax.ppermute(value, 'dp', [(i, i ^ mask) for i in range(lax.axis_size('dp...  43 us
    ppermute x4, waiting for transfers between devices, swap_seq(): lax.ppermute(value, 'seq', [(i, i ^ mask) for i in range(lax.axis_size('s...  27.4 us
    ppermute x2, waiting for transfers between devices, spread_hidden(): lax.ppermute(piece, AXES, spread_pairs(first))  9.88 us
    unnamed x32, local copies, waits for them, and re-layouts  9.81 us
    ppermute x4, starting transfers between devices, from_sequences(): lax.ppermute(piece, AXES, [(b, a) for a, b in spread_pairs(first)])  5.85 us
  transfers between devices with their start and end apart: 49, of which 20 were waited for; matrix products, arithmetic and copies ran while one was open for 1% of the time, Pallas kernels for 31%

profile of v1, /device:TPU:0, one launch (start us, length us, event | category | flops | bytes accessed | tf_op | source)
XLA Modules:
  0.0 276.0 jit_solution(7168854529937615229)
XLA Ops:
  13.9 3.9 %collective-permute-start.2 = (bf16[304,768]{1,0:T(8,128)(2,1)S(1)}, bf16[304,768]{1,0:T(8,128)(2,1)S(1)}, u32[]{:S(2)}, u32[]{:S(2)}) collective-permute-start(bf16[304,768]{1,0:T(8,128)(2,1)S(1)} %pack.1.refs_0_), channel_id=1, source_target_pairs={{0,24},{4,28},{8,16},{12,20},{16,8},{20,12},{24,0},{28,4},{1,25},{... | collective-permute-start | bytes 1400840 | tf_op jit(solution)/shard_map/ppermute | solution.py:640
  18.3 2.9 %collective-permute-start.3 = (bf16[304,768]{1,0:T(8,128)(2,1)S(1)}, bf16[304,768]{1,0:T(8,128)(2,1)S(1)}, u32[]{:S(2)}, u32[]{:S(2)}) collective-permute-start(bf16[304,768]{1,0:T(8,128)(2,1)S(1)} %pack.1.refs_0_), channel_id=1, source_target_pairs={{0,4},{4,0},{8,12},{12,8},{16,20},{20,16},{24,28},{28,24},{1,5},{5... | collective-permute-start | bytes 1400840 | tf_op jit(solution)/shard_map/ppermute | solution.py:640
  21.2 1.6 collective-permute-start.8
  22.8 9.9 %collective-permute-done.8.refs_9_ = bf16[272,768]{1,0:T(8,128)(2,1)} collective-permute-done((bf16[272,768]{1,0:T(8,128)(2,1)S(1)}, bf16[272,768]{1,0:T(8,128)(2,1)}, u32[]{:S(2)}, u32[]{:S(2)}) %collective-permute-start.8) | collective-permute-done | bytes 417824 | tf_op jit(solution)/shard_map/ppermute | solution.py:754
  32.7 5.7 %collective-permute-start.9 = (bf16[272,768]{1,0:T(8,128)(2,1)}, bf16[272,768]{1,0:T(8,128)(2,1)}, u32[]{:S(2)}, u32[]{:S(2)}) collective-permute-start(bf16[272,768]{1,0:T(8,128)(2,1)} %collective-permute-done.7.refs_8_), channel_id=1, source_target_pairs={{0,4},{4,0},{8,12},{12,8},{16,20},{20,16},{24,28},{28,24},{1,5},{5... | collective-permute-start | bytes 1253384 | tf_op jit(solution)/shard_map/ppermute | solution.py:640
  40.3 2.3 collective-permute-start.13
  45.5 3.2 %collective-permute-start.20 = (bf16[256,768]{1,0:T(8,128)(2,1)S(1)}, bf16[256,768]{1,0:T(8,128)(2,1)S(1)}, u32[]{:S(2)}, u32[]{:S(2)}) collective-permute-start(bf16[256,768]{1,0:T(8,128)(2,1)S(1)} %get-tuple-element.275), channel_id=1, source_target_pairs={{0,1},{1,0},{2,5},{3,4},{4,3},{5,2},{6,7},{7,6},{8,9},{9,8},{10,13... | collective-permute-start | bytes 1179656 | tf_op jit(solution)/shard_map/ppermute | solution.py:669
  49.4 21.1 %project.1 = (bf16[512,768]{1,0:T(8,128)(2,1)S(1)}, f32[2,8,512]{2,1,0:T(8,128)S(1)}, bf16[512,768]{1,0:T(8,128)(2,1)S(1)}, f32[16,768]{1,0:T(8,128)S(1)}, f32[1...) custom-call(s32[8]{0:T(128)S(1)} %stack.57.scalars, ...), custom_call_target="tpu_custom_call" | custom-call | flops 1 | bytes 1 | tf_op jit(solution)/shard_map/project/pallas_call | solution.py:399
  70.5 2.3 collective-permute-start.18
  73.1 2.5 collective-permute-done.12.refs_4_
  76.6 2.0 collective-permute-start.17
  80.4 8.7 %widen.1 = (f32[512,768]{1,0:T(8,128)S(1)}, f32[512,128]{1,0:T(8,128)S(1)}, bf16[512,768]{1,0:T(8,128)(2,1)S(1)}, bf16[512,3072]{1,0:T(8,128)(2,1)S(1)}, bf16[51...) custom-call(s32[8]{0:T(128)S(1)} %stack.57.scalars, ...), custom_call_target="tpu_custom_call" | custom-call | flops 1 | bytes 1 | tf_op jit(solution)/shard_map/widen/pallas_call | solution.py:399
  89.1 4.5 %collective-permute-done.17.refs_6_ = bf16[384,768]{1,0:T(8,128)(2,1)S(1)} collective-permute-done((bf16[384,768]{1,0:T(8,128)(2,1)S(1)}, bf16[384,768]{1,0:T(8,128)(2,1)S(1)}, u32[]{:S(2)}, u32[]{:S(2)}) %collective-permute-start.17) | collective-permute-done | bytes 589856 | tf_op jit(solution)/shard_map/ppermute | solution.py:640
  93.6 12.2 %collective-permute-done.16.refs_4_ = bf16[384,768]{1,0:T(8,128)(2,1)S(1)} collective-permute-done((bf16[384,768]{1,0:T(8,128)(2,1)S(1)}, bf16[384,768]{1,0:T(8,128)(2,1)S(1)}, u32[]{:S(2)}, u32[]{:S(2)}) %collective-permute-start.16) | collective-permute-done | bytes 589856 | tf_op jit(solution)/shard_map/ppermute | solution.py:640
  109.5 9.1 %narrow.1 = (bf16[512,768]{1,0:T(8,128)(2,1)S(1)}, f32[512,768]{1,0:T(8,128)S(1)}, bf16[512,768]{1,0:T(8,128)(2,1)S(1)}, f32[8,768]{1,0:T(8,128)S(1)}, bf16[4,38...) custom-call(s32[8]{0:T(128)S(1)} %stack.57.scalars, ...), custom_call_target="tpu_custom_call" | custom-call | flops 1 | bytes 1 | tf_op jit(solution)/shard_map/narrow/pallas_call | solution.py:399
  119.0 13.6 %inner_back.1 = (bf16[512,3072]{1,0:T(8,128)(2,1)S(1)}, f32[1,3072]{1,0:T(1,128)S(1)}, bf16[4,96,3072]{2,1,0:T(8,128)(2,1)S(1)}, bf16[4,96,3072]{2,1,0:T(8,128)(2,1)S(1)}) custom-call(s32[8]{0:T(128)S(1)} %stack.57.scalars, bf16[512,768]{1,0:T(8,128)(2,1)S(1)} %get-tuple-element.174.low, bf16[3072,768]{1,0:T(8,128)(2,1)S(1)} %get-tuple-element.175.wd, ...), custom_call_target="tpu_custom_call" | custom-call | flops 1 | bytes 1 | tf_op jit(solution)/shard_map/inner_back/pallas_call | solution.py:399
  134.2 3.0 %collective-permute-done.28.refs_1_ = bf16[4,96,3072]{2,1,0:T(8,128)(2,1)S(1)} collective-permute-done((bf16[4,96,3072]{2,1,0:T(8,128)(2,1)S(1)}, bf16[4,96,3072]{2,1,0:T(8,128)(2,1)S(1)}, u32[]{:S(2)}, u32[]{:S(2)}) %collective-permute-start.28) | collective-permute-done | bytes 2359328 | tf_op jit(solution)/shard_map/ppermute | solution.py:640
  140.7 2.8 %collective-permute-start.29 = (bf16[256,768]{1,0:T(8,128)(2,1)S(1)}, bf16[256,768]{1,0:T(8,128)(2,1)S(1)}, u32[]{:S(2)}, u32[]{:S(2)}) collective-permute-start(bf16[256,768]{1,0:T(8,128)(2,1)S(1)} %broadcast_select_fusion.2), channel_id=1, source_target_pairs={{1,0},{0,1},{5,2},{4,3},{3,4},{2,5},{7,6},{6,7},{9,8},{8,9},{13,10... | collective-permute-start | bytes 1179656 | tf_op jit(solution)/shard_map/ppermute | solution.py:684
  144.1 6.7 %outer_back.1 = (f32[512,768]{1,0:T(8,128)S(1)}, bf16[512,768]{1,0:T(8,128)(2,1)S(1)}, f32[8,768]{1,0:T(8,128)S(1)}, bf16[4,96,768]{2,1,0:T(8,128)(2,1)S(1)}, bf16[4,96,768]{2,1,0:T(8,128)(2,1)S(1)}) custom-call(s32[8]{0:T(128)S(1)} %stack.57.scalars, bf16[512,3072]{1,0:T(8,128)(2,1)S(1)} %get-tuple-element.178.grad, ...), custom_call_target="tpu_custom_call" | custom-call | flops 1 | bytes 1 | tf_op jit(solution)/shard_map/outer_back/pallas_call | solution.py:399
  150.9 2.6 collective-permute-done.29
  154.4 14.1 %attend_back.2 = (bf16[512,384]{1,0:T(8,128)(2,1)S(1)}, f32[512,384]{1,0:T(8,128)S(1)}, f32[512,384]{1,0:T(8,128)S(1)}, bf16[2,512,384]{2,1,0:T(8,128)(2,1)S(1)}) custom-call(s32[8]{0:T(128)S(1)} %stack.57.scalars, bf16[512,768]{1,0:T(8,128)(2,1)S(1)} %get-tuple-element.195.refs_0_, bf16[512,768]{1,0:T(8,128)(2,1)S(1)} %get-tuple-element.196.refs_1_, ...), custom_call_target="tpu_custom_call" | custom-call | flops 1 | bytes 1 | tf_op jit(solution)/shard_map/attend_back/pallas_call | solution.py:399
  169.9 9.0 %collective-permute-start.33 = (bf16[2,512,384]{2,1,0:T(8,128)(2,1)S(1)}, bf16[2,512,384]{2,1,0:T(8,128)(2,1)S(1)}, u32[]{:S(2)}, u32[]{:S(2)}) collective-permute-start(bf16[2,512,384]{2,1,0:T(8,128)(2,1)S(1)} %get-tuple-element.212), channel_id=1, source_target_pairs={{0,4},{4,0},{8,12},{12,8},{16,20},{20,16},{24,28},{28,24},{1,5},{5... | collective-permute-start | bytes 2359304 | tf_op jit(solution)/shard_map/ppermute | solution.py:640
  178.9 1.9 collective-permute-done.33.refs_3_
  180.8 3.5 %qkv_back.2 = (bf16[4,96,2048]{2,1,0:T(8,128)(2,1)S(1)}, bf16[4,96,2048]{2,1,0:T(8,128)(2,1)S(1)}, f32[512,768]{1,0:T(8,128)S(1)}, f32[8,384]{1,0:T(8,128)S(1)}) custom-call(s32[8]{0:T(128)S(1)} %stack.57.scalars, bf16[512,384]{1,0:T(8,128)(2,1)S(1)} %get-tuple-element.202.refs_0_, f32[512,384]{1,0:T(8,128)S(1)} %get-tuple-element.203.refs_1_, ...), custom_call_target="tpu_custom_call" | custom-call | flops 1 | bytes 1 | tf_op jit(solution)/shard_map/qkv_back/pallas_call | solution.py:399
  186.5 14.1 %attend_back.3 = (bf16[512,384]{1,0:T(8,128)(2,1)S(1)}, f32[512,384]{1,0:T(8,128)S(1)}, f32[512,384]{1,0:T(8,128)S(1)}, bf16[2,512,384]{2,1,0:T(8,128)(2,1)S(1)}) custom-call(s32[8]{0:T(128)S(1)} %stack.57.scalars, bf16[512,768]{1,0:T(8,128)(2,1)S(1)} %get-tuple-element.195.refs_0_, bf16[512,768]{1,0:T(8,128)(2,1)S(1)} %get-tuple-element.196.refs_1_, ...), custom_call_target="tpu_custom_call" | custom-call | flops 1 | bytes 1 | tf_op jit(solution)/shard_map/attend_back/pallas_call | solution.py:399
  202.8 2.3 collective-permute-done.37.refs_3_
  205.1 3.7 %qkv_back.3 = (bf16[4,96,1280]{2,1,0:T(8,128)(2,1)S(1)}, bf16[4,96,1280]{2,1,0:T(8,128)(2,1)S(1)}, bf16[512,768]{1,0:T(8,128)(2,1)S(1)}, f32[8,384]{1,0:T(8,128)}) custom-call(s32[8]{0:T(128)S(1)} %stack.57.scalars, bf16[512,384]{1,0:T(8,128)(2,1)S(1)} %get-tuple-element.223.refs_0_, f32[512,384]{1,0:T(8,128)S(1)} %get-tuple-element.224.refs_1_, ...), custom_call_target="tpu_custom_call" | custom-call | flops 1 | bytes 1 | tf_op jit(solution)/shard_map/qkv_back/pallas_call | solution.py:399
  212.8 15.9 %collective-permute-done.39.refs_1_ = bf16[2,96,2048]{2,1,0:T(8,128)(2,1)S(1)} collective-permute-done((bf16[2,96,2048]{2,1,0:T(8,128)(2,1)S(1)}, bf16[2,96,2048]{2,1,0:T(8,128)(2,1)S(1)}, u32[]{:S(2)}, u32[]{:S(2)}) %collective-permute-start.39) | collective-permute-done | bytes 786464 | tf_op jit(solution)/shard_map/ppermute | solution.py:640
  232.9 1.7 collective-permute-start.46
  235.3 4.8 %collective-permute-done.42 = bf16[1,96,2048]{2,1,0:T(8,128)(2,1)S(1)} collective-permute-done((bf16[1,96,2048]{2,1,0:T(8,128)(2,1)S(1)}, bf16[1,96,2048]{2,1,0:T(8,128)(2,1)S(1)}, u32[]{:S(2)}, u32[]{:S(2)}) %collective-permute-start.42) | collective-permute-done | bytes 393248 | tf_op jit(solution)/shard_map/ppermute | solution.py:640
  242.8 22.6 %collective-permute-done.44.got = bf16[1,24,6144]{2,1,0:T(8,128)(2,1)S(1)} collective-permute-done((bf16[1,24,6144]{2,1,0:T(8,128)(2,1)S(1)}, bf16[1,24,6144]{2,1,0:T(8,128)(2,1)S(1)}, u32[]{:S(2)}, u32[]{:S(2)}) %collective-permute-start.44) | collective-permute-done | bytes 294944 | tf_op jit(solution)/shard_map/ppermute | solution.py:644
  268.8 4.9 %collective-permute-done.48.got = bf16[1,24,3328]{2,1,0:T(8,128)(2,1)S(1)} collective-permute-done((bf16[1,24,3328]{2,1,0:T(8,128)(2,1)S(1)}, bf16[1,24,3328]{2,1,0:T(8,128)(2,1)S(1)}, u32[]{:S(2)}, u32[]{:S(2)}) %collective-permute-start.48) | collective-permute-done | bytes 159776 | tf_op jit(solution)/shard_map/ppermute | solution.py:644
  (135 shorter events, 56.2 us)
Async XLA Ops:
  13.9 24.5 %collective-permute-start.2 = (bf16[304,768]{1,0:T(8,128)(2,1)S(1)}, bf16[304,768]{1,0:T(8,128)(2,1)S(1)}, u32[]{:S(2)}, u32[]{:S(2)}) collective-permute-start(bf16[304,768]{1,0:T(8,128)(2,1)S(1)} %pack.1.refs_0_), channel_id=1, source_target_pairs={{0,24},{4,28},{8,16},{12,20},{16,8},{20,12},{24,0},{28,4},{1,25},{... | collective-permute-start | bytes 1400840 | tf_op jit(solution)/shard_map/ppermute | solution.py:640
  17.8 21.5 %collective-permute-start.1 = (bf16[304,768]{1,0:T(8,128)(2,1)S(1)}, bf16[304,768]{1,0:T(8,128)(2,1)S(1)}, u32[]{:S(2)}, u32[]{:S(2)}) collective-permute-start(bf16[304,768]{1,0:T(8,128)(2,1)S(1)} %pack.1.refs_0_), channel_id=1, source_target_pairs={{0,16},{4,20},{8,24},{12,28},{16,0},{20,4},{24,8},{28,12},{1,17},{... | collective-permute-start | bytes 1400840 | tf_op jit(solution)/shard_map/ppermute | solution.py:640
  18.3 21.0 %collective-permute-start = (bf16[304,768]{1,0:T(8,128)(2,1)S(1)}, bf16[304,768]{1,0:T(8,128)(2,1)S(1)}, u32[]{:S(2)}, u32[]{:S(2)}) collective-permute-start(bf16[304,768]{1,0:T(8,128)(2,1)S(1)} %pack.1.refs_0_), channel_id=1, source_target_pairs={{0,8},{4,12},{8,0},{12,4},{16,24},{20,28},{24,16},{28,20},{1,9},{5... | collective-permute-start | bytes 1400840 | tf_op jit(solution)/shard_map/ppermute | solution.py:640
  18.3 21.4 %collective-permute-start.3 = (bf16[304,768]{1,0:T(8,128)(2,1)S(1)}, bf16[304,768]{1,0:T(8,128)(2,1)S(1)}, u32[]{:S(2)}, u32[]{:S(2)}) collective-permute-start(bf16[304,768]{1,0:T(8,128)(2,1)S(1)} %pack.1.refs_0_), channel_id=1, source_target_pairs={{0,4},{4,0},{8,12},{12,8},{16,20},{20,16},{24,28},{28,24},{1,5},{5... | collective-permute-start | bytes 1400840 | tf_op jit(solution)/shard_map/ppermute | solution.py:640
  21.2 11.5 %collective-permute-start.8 = (bf16[272,768]{1,0:T(8,128)(2,1)S(1)}, bf16[272,768]{1,0:T(8,128)(2,1)}, u32[]{:S(2)}, u32[]{:S(2)}) collective-permute-start(bf16[272,768]{1,0:T(8,128)(2,1)S(1)} %get-tuple-element.152), channel_id=1, source_target_pairs={{0,1},{1,0},{2,5},{3,4},{4,3},{5,2},{6,7},{7,6},{8,9},{9,8},{10,13... | collective-permute-start | bytes 1253384 | tf_op jit(solution)/shard_map/ppermute | solution.py:754
  39.7 9.0 %collective-permute-start.6 = (bf16[304,768]{1,0:T(8,128)(2,1)S(1)}, bf16[304,768]{1,0:T(8,128)(2,1)}, u32[]{:S(2)}, u32[]{:S(2)}) collective-permute-start(bf16[304,768]{1,0:T(8,128)(2,1)S(1)} %collective-permute-done.2.refs_6_), channel_id=1, source_target_pairs={{0,4},{4,0},{8,12},{12,8},{16,20},{20,16},{24,28},{28,24},{1,5},{5... | collective-permute-start | bytes 1400840 | tf_op jit(solution)/shard_map/ppermute | solution.py:640
  40.3 32.8 %collective-permute-start.13 = (bf16[96,3840]{1,0:T(8,128)(2,1)S(1)}, bf16[96,3840]{1,0:T(8,128)(2,1)S(1)}, u32[]{:S(2)}, u32[]{:S(2)}) collective-permute-start(bf16[96,3840]{1,0:T(8,128)(2,1)S(1)} %pad_maximum_fusion.refs_0_), channel_id=1, source_target_pairs={{0,24},{4,28},{8,16},{12,20},{16,8},{20,12},{24,0},{28,4},{1,25},{... | collective-permute-start | bytes 2211848 | tf_op jit(solution)/shard_map/ppermute | solution.py:640
  42.6 33.0 %collective-permute-start.12 = (bf16[96,3840]{1,0:T(8,128)(2,1)S(1)}, bf16[96,3840]{1,0:T(8,128)(2,1)S(1)}, u32[]{:S(2)}, u32[]{:S(2)}) collective-permute-start(bf16[96,3840]{1,0:T(8,128)(2,1)S(1)} %pad_maximum_fusion.refs_0_), channel_id=1, source_target_pairs={{0,16},{4,20},{8,24},{12,28},{16,0},{20,4},{24,8},{28,12},{1,17},{... | collective-permute-start | bytes 2211848 | tf_op jit(solution)/shard_map/ppermute | solution.py:640
  43.4 32.6 %collective-permute-start.11 = (bf16[96,3840]{1,0:T(8,128)(2,1)S(1)}, bf16[96,3840]{1,0:T(8,128)(2,1)S(1)}, u32[]{:S(2)}, u32[]{:S(2)}) collective-permute-start(bf16[96,3840]{1,0:T(8,128)(2,1)S(1)} %pad_maximum_fusion.refs_0_), channel_id=1, source_target_pairs={{0,8},{4,12},{8,0},{12,4},{16,24},{20,28},{24,16},{28,20},{1,9},{5... | collective-permute-start | bytes 2211848 | tf_op jit(solution)/shard_map/ppermute | solution.py:640
  45.5 25.0 %collective-permute-start.20 = (bf16[256,768]{1,0:T(8,128)(2,1)S(1)}, bf16[256,768]{1,0:T(8,128)(2,1)S(1)}, u32[]{:S(2)}, u32[]{:S(2)}) collective-permute-start(bf16[256,768]{1,0:T(8,128)(2,1)S(1)} %get-tuple-element.275), channel_id=1, source_target_pairs={{0,1},{1,0},{2,5},{3,4},{4,3},{5,2},{6,7},{7,6},{8,9},{9,8},{10,13... | collective-permute-start | bytes 1179656 | tf_op jit(solution)/shard_map/ppermute | solution.py:669
  48.7 24.1 %collective-permute-start.19 = (bf16[256,768]{1,0:T(8,128)(2,1)S(1)}, bf16[256,768]{1,0:T(8,128)(2,1)S(1)}, u32[]{:S(2)}, u32[]{:S(2)}) collective-permute-start(bf16[256,768]{1,0:T(8,128)(2,1)S(1)} %get-tuple-element.276), channel_id=1, source_target_pairs={{0,0},{1,1},{2,4},{3,5},{4,2},{5,3},{6,6},{7,7},{8,8},{9,9},{10,12... | collective-permute-start | bytes 1179656 | tf_op jit(solution)/shard_map/ppermute | solution.py:669
  76.6 17.1 %collective-permute-start.17 = (bf16[384,768]{1,0:T(8,128)(2,1)S(1)}, bf16[384,768]{1,0:T(8,128)(2,1)S(1)}, u32[]{:S(2)}, u32[]{:S(2)}) collective-permute-start(bf16[384,768]{1,0:T(8,128)(2,1)S(1)} %copy-done.1), channel_id=1, source_target_pairs={{0,24},{4,28},{8,16},{12,20},{16,8},{20,12},{24,0},{28,4},{1,25},{... | collective-permute-start | bytes 1769480 | tf_op jit(solution)/shard_map/ppermute | solution.py:640
  78.6 27.2 %collective-permute-start.16 = (bf16[384,768]{1,0:T(8,128)(2,1)S(1)}, bf16[384,768]{1,0:T(8,128)(2,1)S(1)}, u32[]{:S(2)}, u32[]{:S(2)}) collective-permute-start(bf16[384,768]{1,0:T(8,128)(2,1)S(1)} %copy-done.1), channel_id=1, source_target_pairs={{0,16},{4,20},{8,24},{12,28},{16,0},{20,4},{24,8},{28,12},{1,17},{... | collective-permute-start | bytes 1769480 | tf_op jit(solution)/shard_map/ppermute | solution.py:640
  79.4 26.4 %collective-permute-start.15 = (bf16[384,768]{1,0:T(8,128)(2,1)S(1)}, bf16[384,768]{1,0:T(8,128)(2,1)S(1)}, u32[]{:S(2)}, u32[]{:S(2)}) collective-permute-start(bf16[384,768]{1,0:T(8,128)(2,1)S(1)} %copy-done.1), channel_id=1, source_target_pairs={{0,8},{4,12},{8,0},{12,4},{16,24},{20,28},{24,16},{28,20},{1,9},{5... | collective-permute-start | bytes 1769480 | tf_op jit(solution)/shard_map/ppermute | solution.py:640
  80.1 26.3 %collective-permute-start.14 = (bf16[384,768]{1,0:T(8,128)(2,1)S(1)}, bf16[384,768]{1,0:T(8,128)(2,1)S(1)}, u32[]{:S(2)}, u32[]{:S(2)}) collective-permute-start(bf16[384,768]{1,0:T(8,128)(2,1)S(1)} %copy-done.1), channel_id=1, source_target_pairs={{0,4},{4,0},{8,12},{12,8},{16,20},{20,16},{24,28},{28,24},{1,5},{5... | collective-permute-start | bytes 1769480 | tf_op jit(solution)/shard_map/ppermute | solution.py:640
  118.8 14.3 %collective-permute-start.27 = (bf16[4,384,768]{2,1,0:T(8,128)(2,1)S(1)}, bf16[4,384,768]{2,1,0:T(8,128)(2,1)S(1)}, u32[]{:S(2)}, u32[]{:S(2)}) collective-permute-start(bf16[4,384,768]{2,1,0:T(8,128)(2,1)S(1)} %get-tuple-element.181), channel_id=1, source_target_pairs={{0,4},{4,0},{8,12},{12,8},{16,20},{20,16},{24,28},{28,24},{1,5},{5... | collective-permute-start | bytes 7077896 | tf_op jit(solution)/shard_map/ppermute | solution.py:640
  138.3 30.2 %collective-permute-start.32 = (bf16[2,96,3072]{2,1,0:T(8,128)(2,1)S(1)}, bf16[2,96,3072]{2,1,0:T(8,128)(2,1)S(1)}, u32[]{:S(2)}, u32[]{:S(2)}) collective-permute-start(bf16[2,96,3072]{2,1,0:T(8,128)(2,1)S(1)} %get-tuple-element.186), channel_id=1, source_target_pairs={{0,16},{4,20},{8,24},{12,28},{16,0},{20,4},{24,8},{28,12},{1,17},{... | collective-permute-start | bytes 3538952 | tf_op jit(solution)/shard_map/ppermute | solution.py:640
  139.8 28.7 %collective-permute-start.31 = (bf16[2,384,768]{2,1,0:T(8,128)(2,1)S(1)}, bf16[2,384,768]{2,1,0:T(8,128)(2,1)S(1)}, u32[]{:S(2)}, u32[]{:S(2)}) collective-permute-start(bf16[2,384,768]{2,1,0:T(8,128)(2,1)S(1)} %get-tuple-element.182), channel_id=1, source_target_pairs={{0,8},{4,12},{8,0},{12,4},{16,24},{20,28},{24,16},{28,20},{1,9},{5... | collective-permute-start | bytes 3538952 | tf_op jit(solution)/shard_map/ppermute | solution.py:640
  140.7 12.7 %collective-permute-start.29 = (bf16[256,768]{1,0:T(8,128)(2,1)S(1)}, bf16[256,768]{1,0:T(8,128)(2,1)S(1)}, u32[]{:S(2)}, u32[]{:S(2)}) collective-permute-start(bf16[256,768]{1,0:T(8,128)(2,1)S(1)} %broadcast_select_fusion.2), channel_id=1, source_target_pairs={{1,0},{0,1},{5,2},{4,3},{3,4},{2,5},{7,6},{6,7},{9,8},{8,9},{13,10... | collective-permute-start | bytes 1179656 | tf_op jit(solution)/shard_map/ppermute | solution.py:684
  143.5 10.0 %collective-permute-start.30 = (bf16[256,768]{1,0:T(8,128)(2,1)S(1)}, bf16[256,768]{1,0:T(8,128)(2,1)S(1)}, u32[]{:S(2)}, u32[]{:S(2)}) collective-permute-start(bf16[256,768]{1,0:T(8,128)(2,1)S(1)} %broadcast_select_fusion.3), channel_id=1, source_target_pairs={{0,0},{1,1},{4,2},{5,3},{2,4},{3,5},{6,6},{7,7},{8,8},{9,9},{12,10... | collective-permute-start | bytes 1179656 | tf_op jit(solution)/shard_map/ppermute | solution.py:684
  169.9 10.9 %collective-permute-start.33 = (bf16[2,512,384]{2,1,0:T(8,128)(2,1)S(1)}, bf16[2,512,384]{2,1,0:T(8,128)(2,1)S(1)}, u32[]{:S(2)}, u32[]{:S(2)}) collective-permute-start(bf16[2,512,384]{2,1,0:T(8,128)(2,1)S(1)} %get-tuple-element.212), channel_id=1, source_target_pairs={{0,4},{4,0},{8,12},{12,8},{16,20},{20,16},{24,28},{28,24},{1,5},{5... | collective-permute-start | bytes 2359304 | tf_op jit(solution)/shard_map/ppermute | solution.py:640
  184.3 17.5 %collective-permute-start.36 = (bf16[4,96,2048]{2,1,0:T(8,128)(2,1)S(1)}, bf16[4,96,2048]{2,1,0:T(8,128)(2,1)S(1)}, u32[]{:S(2)}, u32[]{:S(2)}) collective-permute-start(bf16[4,96,2048]{2,1,0:T(8,128)(2,1)S(1)} %get-tuple-element.233), channel_id=1, source_target_pairs={{0,4},{4,0},{8,12},{12,8},{16,20},{20,16},{24,28},{28,24},{1,5},{5... | collective-permute-start | bytes 4718600 | tf_op jit(solution)/shard_map/ppermute | solution.py:640
  184.7 15.8 %collective-permute-start.34 = (bf16[1,384,768]{2,1,0:T(8,128)(2,1)S(1)}, bf16[1,384,768]{2,1,0:T(8,128)(2,1)S(1)}, u32[]{:S(2)}, u32[]{:S(2)}) collective-permute-start(bf16[1,384,768]{2,1,0:T(8,128)(2,1)S(1)} %get-tuple-element.209), channel_id=1, source_target_pairs={{0,16},{4,20},{8,24},{12,28},{16,0},{20,4},{24,8},{28,12},{1,17},{... | collective-permute-start | bytes 1769480 | tf_op jit(solution)/shard_map/ppermute | solution.py:640
  185.9 15.1 %collective-permute-start.35 = (bf16[1,96,3072]{2,1,0:T(8,128)(2,1)S(1)}, bf16[1,96,3072]{2,1,0:T(8,128)(2,1)S(1)}, u32[]{:S(2)}, u32[]{:S(2)}) collective-permute-start(bf16[1,96,3072]{2,1,0:T(8,128)(2,1)S(1)} %get-tuple-element.210), channel_id=1, source_target_pairs={{0,8},{4,12},{8,0},{12,4},{16,24},{20,28},{24,16},{28,20},{1,9},{5... | collective-permute-start | bytes 1769480 | tf_op jit(solution)/shard_map/ppermute | solution.py:640
  208.9 21.2 %collective-permute-start.40 = (bf16[2,24,6144]{2,1,0:T(8,128)(2,1)S(1)}, bf16[2,24,6144]{2,1,0:T(8,128)(2,1)S(1)}, u32[]{:S(2)}, u32[]{:S(2)}) collective-permute-start(bf16[2,24,6144]{2,1,0:T(8,128)(2,1)S(1)} %get-tuple-element.230), channel_id=1, source_target_pairs={{0,1},{1,0},{2,3},{3,2},{4,5},{5,4},{6,7},{7,6},{8,9},{9,8},{10,11... | collective-permute-start | bytes 1769480 | tf_op jit(solution)/shard_map/ppermute | solution.py:644
  208.9 19.8 %collective-permute-start.39 = (bf16[2,96,2048]{2,1,0:T(8,128)(2,1)S(1)}, bf16[2,96,2048]{2,1,0:T(8,128)(2,1)S(1)}, u32[]{:S(2)}, u32[]{:S(2)}) collective-permute-start(bf16[2,96,2048]{2,1,0:T(8,128)(2,1)S(1)} %get-tuple-element.234), channel_id=1, source_target_pairs={{0,16},{4,20},{8,24},{12,28},{16,0},{20,4},{24,8},{28,12},{1,17},{... | collective-permute-start | bytes 2359304 | tf_op jit(solution)/shard_map/ppermute | solution.py:640
  212.2 18.7 %collective-permute-start.41 = (bf16[2,96,1280]{2,1,0:T(8,128)(2,1)S(1)}, bf16[2,96,1280]{2,1,0:T(8,128)(2,1)S(1)}, u32[]{:S(2)}, u32[]{:S(2)}) collective-permute-start(bf16[2,96,1280]{2,1,0:T(8,128)(2,1)S(1)} %get-tuple-element.244), channel_id=1, source_target_pairs={{0,8},{4,12},{8,0},{12,4},{16,24},{20,28},{24,16},{28,20},{1,9},{5... | collective-permute-start | bytes 1474568 | tf_op jit(solution)/shard_map/ppermute | solution.py:640
  229.5 10.6 %collective-permute-start.42 = (bf16[1,96,2048]{2,1,0:T(8,128)(2,1)S(1)}, bf16[1,96,2048]{2,1,0:T(8,128)(2,1)S(1)}, u32[]{:S(2)}, u32[]{:S(2)}) collective-permute-start(bf16[1,96,2048]{2,1,0:T(8,128)(2,1)S(1)} %get-tuple-element.247), channel_id=1, source_target_pairs={{0,8},{4,12},{8,0},{12,4},{16,24},{20,28},{24,16},{28,20},{1,9},{5... | collective-permute-start | bytes 1179656 | tf_op jit(solution)/shard_map/ppermute | solution.py:640
  232.9 34.6 %collective-permute-start.46 = (bf16[256,768]{1,0:T(8,128)(2,1)S(1)}, bf16[256,768]{1,0:T(8,128)(2,1)S(1)}, u32[]{:S(2)}, u32[]{:S(2)}) collective-permute-start(bf16[256,768]{1,0:T(8,128)(2,1)S(1)} %broadcast_select_fusion), channel_id=1, source_target_pairs={{1,0},{0,1},{5,2},{4,3},{3,4},{2,5},{7,6},{6,7},{9,8},{8,9},{13,10... | collective-permute-start | bytes 1179656 | tf_op jit(solution)/shard_map/ppermute | solution.py:684
  234.6 32.9 %collective-permute-start.47 = (bf16[256,768]{1,0:T(8,128)(2,1)S(1)}, bf16[256,768]{1,0:T(8,128)(2,1)S(1)}, u32[]{:S(2)}, u32[]{:S(2)}) collective-permute-start(bf16[256,768]{1,0:T(8,128)(2,1)S(1)} %broadcast_select_fusion.1), channel_id=1, source_target_pairs={{0,0},{1,1},{4,2},{5,3},{2,4},{3,5},{6,6},{7,7},{8,8},{9,9},{12,10... | collective-permute-start | bytes 1179656 | tf_op jit(solution)/shard_map/ppermute | solution.py:684
  240.8 26.0 %collective-permute-start.45 = (bf16[2,24,3328]{2,1,0:T(8,128)(2,1)S(1)}, bf16[2,24,3328]{2,1,0:T(8,128)(2,1)S(1)}, u32[]{:S(2)}, u32[]{:S(2)}) collective-permute-start(bf16[2,24,3328]{2,1,0:T(8,128)(2,1)S(1)} %get-tuple-element.257), channel_id=1, source_target_pairs={{0,1},{1,0},{2,3},{3,2},{4,5},{5,4},{6,7},{7,6},{8,9},{9,8},{10,11... | collective-permute-start | bytes 958472 | tf_op jit(solution)/shard_map/ppermute | solution.py:644
  242.3 23.1 %collective-permute-start.44 = (bf16[1,24,6144]{2,1,0:T(8,128)(2,1)S(1)}, bf16[1,24,6144]{2,1,0:T(8,128)(2,1)S(1)}, u32[]{:S(2)}, u32[]{:S(2)}) collective-permute-start(bf16[1,24,6144]{2,1,0:T(8,128)(2,1)S(1)} %get-tuple-element.250), channel_id=1, source_target_pairs={{0,2},{1,3},{2,0},{3,1},{4,6},{5,7},{6,4},{7,5},{8,10},{9,11},{10,... | collective-permute-start | bytes 884744 | tf_op jit(solution)/shard_map/ppermute | solution.py:644
  (33 other events, 159.8 us)

commit v2 on v1

--- a/solution.py
+++ b/solution.py
@@ -193,7 +193,6 @@
 
 AXES = ("dp", "seq")
 PARTS = 8
-SHARDS = 8
 epsilon = 1e-12
 
 
@@ -222,15 +221,22 @@
 
 
 def parts_of(refs):
-    return [(ref, 0, ref.shape[0]) for ref in refs]
-
-
-def load_pieces(me, pieces, targets, sems):
+    if len(refs) == PARTS:
+        return [(i, 0, ref) for i, ref in enumerate(refs)]
+    pieces = [(i, 0, ref) for i, ref in enumerate(refs[:6])]
+    for i in range(2):
+        top, bottom = refs[6 + i], refs[8 + i]
+        pieces += [(6 + i, 0, top), (6 + i, top.shape[0], bottom)]
+    return pieces
+
+
+def load_pieces(me, pieces, rows, targets, sems):
     copies = [[] for _ in targets]
-    for place, (ref, first, rows) in enumerate(pieces):
-        where = pl.ds(pl.multiple_of((me ^ place) * rows, 32), rows)
+    for place, (part, first, ref) in enumerate(pieces):
+        size = ref.shape[0]
+        where = pl.ds(pl.multiple_of((me ^ part) * rows + first, 32), size)
         for i, (target, columns) in enumerate(targets):
-            copy = pltpu.make_async_copy(ref.at[first : first + rows, columns], target.at[where, :], sems.at[i, place])
+            copy = pltpu.make_async_copy(ref.at[:, columns], target.at[where, :], sems.at[i, place])
             copy.start()
             copies[i].append(copy)
     return copies
@@ -245,15 +251,17 @@
     return pl.ds(pl.multiple_of(block * size, size), size)
 
 
-BLOCK = 256
+BLOCK = 1024
+GELU_BLOCK = 256
 ROWS = 256
 
 
 def widen_body(scalars, *refs):
-    pieces = parts_of(refs[:SHARDS])
-    (attended, tokens, vec, up_add, normal_ref, scale_ref, low_ref, active_ref, slope_ref, wo, wu, sems) = refs[SHARDS:]
+    shards = len(refs) - 12
+    pieces = parts_of(refs[:shards])
+    (attended, tokens, vec, up_add, normal_ref, scale_ref, low_ref, active_ref, slope_ref, wo, wu, sems) = refs[shards:]
     width, wide = wu.shape
-    loads = load_pieces(scalars[0], pieces, [(wo, slice(0, width)), (wu, slice(width, width + wide))], sems)
+    loads = load_pieces(scalars[0], pieces, width // PARTS, [(wo, slice(0, width)), (wu, slice(width, width + wide))], sems)
     wait_all(loads[0])
 
     @pl.loop(0, tokens.shape[0] // ROWS)
@@ -268,9 +276,9 @@
 
     wait_all(loads[1])
 
-    @pl.loop(0, wide // BLOCK)
+    @pl.loop(0, wide // GELU_BLOCK)
     def _(j):
-        cols = step_of(j, BLOCK)
+        cols = step_of(j, GELU_BLOCK)
         inner = nn(low_ref[...], wu[:, cols]) + up_add[:, cols]
         cumulative = 0.5 * (1.0 + lax.erf(inner * math.sqrt(0.5)))
         density = jnp.exp(-0.5 * inner * inner) * (1.0 / math.sqrt(2.0 * math.pi))
@@ -279,10 +287,11 @@
 
 
 def narrow_body(scalars, *refs):
-    pieces = parts_of(refs[:SHARDS])
-    (active, normal_one, vec, upstream, out_ref, grad_ref, low_ref, sums_ref, send_ref, keep_ref, wd, sums, sems) = refs[SHARDS:]
+    shards = len(refs) - 13
+    pieces = parts_of(refs[:shards])
+    (active, normal_one, vec, upstream, out_ref, grad_ref, low_ref, sums_ref, send_ref, keep_ref, wd, sums, sems) = refs[shards:]
     wide, width = wd.shape
-    (loads,) = load_pieces(scalars[0], pieces, [(wd, slice(0, width))], sems)
+    (loads,) = load_pieces(scalars[0], pieces, wide // PARTS, [(wd, slice(0, width))], sems)
     wait_all(loads)
     sums[...] = jnp.zeros_like(sums)
 
@@ -383,6 +392,10 @@
     for copy in copies:
         copy.wait()
     body(scalars, *refs[:hbm], *given, *refs[hbm + inputs : len(refs) - held - 1])
+
+
+def in_hbm(value):
+    return pltpu.with_memory_space_constraint(value, pltpu.HBM)
 
 
 def whole_call(body, name, scalars, hbm, inputs, outputs, hbm_outputs, scratch, room=8):
@@ -403,11 +416,11 @@
         + [stay if isinstance(x, Far) else near for x in inputs],
         out_specs=[near] * len(outputs) + [stay] * len(hbm_outputs),
         scratch_shapes=scratch,
-        out_shape=[shape_of(x) for x in list(outputs) + list(hbm_outputs)],
+        out_shape=[shape_of(x) for x in outputs] + [pltpu.HBM(x.shape, x.dtype) for x in hbm_outputs],
         cost_estimate=pl.CostEstimate(flops=1, transcendentals=0, bytes_accessed=1),
         compiler_params=pltpu.CompilerParams(vmem_limit_bytes=room << 20),
         name=name,
-    )(scalars, *hbm, *[x.value if isinstance(x, Far) else x for x in inputs])
+    )(scalars, *[in_hbm(x) for x in hbm], *[in_hbm(x.value) if isinstance(x, Far) else x for x in inputs])
 
 
 def array(dtype, *shape):
@@ -422,7 +435,7 @@
         widen_body, "widen", scalars, pieces, [attended, tokens, vec, up_add],
         [array(f32, count, width), array(f32, count, LANES), array(b16, count, width),
          array(b16, count, wide), array(b16, count, wide), array(b16, width, width), array(b16, width, wide)],
-        [], [pltpu.SemaphoreType.DMA((2, PARTS))],
+        [], [pltpu.SemaphoreType.DMA((2, len(pieces)))],
     )
 
 
@@ -434,7 +447,7 @@
     return whole_call(
         narrow_body, "narrow", scalars, pieces, [active, normal, vec, upstream],
         [array(b16, count, width), array(f32, count, width), array(b16, count, width), array(f32, 8, width), half, half, array(b16, wide, width)],
-        [], [pltpu.VMEM((8, width), f32), pltpu.SemaphoreType.DMA((1, PARTS))],
+        [], [pltpu.VMEM((8, width), f32), pltpu.SemaphoreType.DMA((1, len(pieces)))],
     )
 
 
@@ -697,47 +710,46 @@
     return jnp.concatenate(weights + lines, axis=-2)
 
 
-def near_shards(part):
+def near_shards(part, across=True):
     if lax.axis_size("dp") != PARTS:
         p = part if part.ndim == 3 else jnp.stack(jnp.split(lax.all_gather(part, "dp", axis=0, tiled=True), PARTS))
         return [p[i] for i in range(PARTS)]
-    return [part, swap_dp(part, 2), swap_dp(part, 4), swap_dp(part, 6)]
+    return [part, swap_dp(part, 2), swap_dp(part, 4)] + ([swap_dp(part, 6)] if across else [])
+
+
+def both_cores(parts):
+    return [shard for part in parts for shard in (part, swap_dp(part, 1))]
 
 
 def all_shards(near, *ready):
     if len(near) == PARTS:
         return near
-    near = [near[0]] + list(lax.optimization_barrier((*near[1:], *ready))[:3])
-    shards = []
-    for part in near:
-        shards += [part, swap_dp(part, 1)]
-    return shards
-
-
-def pack_body(scalars, query, key, value, *refs):
-    vectors, (part, lines) = refs[:-2], refs[-2:]
-    rows = query.shape[0]
-    for i, ref in enumerate((query, key, value)):
-        part[i * rows : (i + 1) * rows, :] = ref[...]
-    lines[...] = jnp.zeros_like(lines)
-    for i, ref in enumerate(vectors):
-        lines[i : i + 1, : ref.shape[1]] = ref[...].astype(jnp.float32)
-    part[3 * rows :, :] = lines[...].astype(jnp.bfloat16)
-
-
-def projection_part(scalars, weights, vectors):
-    if lax.axis_size("dp") == PARTS:
-        rows, width = weights[0].shape
-        return whole_call(
-            pack_body, "pack", scalars, [], weights + [v[None, :] for v in vectors],
-            [array(jnp.bfloat16, 3 * rows + 16, width)], [], [pltpu.VMEM((16, width), jnp.float32)],
-        )[0]
-    gather = lambda v: lax.all_gather(v, "dp", axis=0, tiled=True)
-    split = lambda v: gather(v).reshape((PARTS, -1) + v.shape[1:])
-    return weight_lines([split(w) for w in weights], [split(v) for v in vectors])
-
-
-def spread_body(scalars, hidden, ids, *pieces):
+    return both_cores([near[0]] + list(lax.optimization_barrier((*near[1:], *ready))[:3]))
+
+
+def relayed_shards(near, cut, *ready):
+    if len(near) == PARTS:
+        return near
+    own, along_x, along_y = near
+    along_x, along_y = lax.optimization_barrier((along_x, along_y, *ready))[:2]
+    sent = along_x[:cut], along_y[cut:]
+    top, bottom = swap_dp(sent[0], 4), swap_dp(sent[1], 2)
+    own, along_x, along_y = lax.optimization_barrier((own, along_x, along_y, *sent))[:3]
+    return both_cores([own, along_x, along_y, top, bottom])
+
+
+def pack_body(count, scalars, *refs):
+    weights, vectors, hidden, ids = refs[: min(3, count)], refs[3:count], refs[count], refs[count + 1]
+    pieces = refs[count + 2 : count + 4]
+    if vectors:
+        part, lines = refs[count + 4 :]
+        rows = weights[0].shape[0]
+        for i, ref in enumerate(weights):
+            part[i * rows : (i + 1) * rows, :] = ref[...]
+        lines[...] = jnp.zeros_like(lines)
+        for i, ref in enumerate(vectors):
+            lines[i : i + 1, : ref.shape[1]] = ref[...].astype(jnp.float32)
+        part[3 * rows :, :] = lines[...].astype(jnp.bfloat16)
     odd = scalars[7]
     block, half = hidden.shape[1], ids.shape[1] // 2
     for first, piece in enumerate(pieces):
@@ -748,19 +760,28 @@
         piece[block + 1 : block + 2, :half] = line[:, half:]
 
 
-def spread_hidden(scalars, hidden, ids):
+def pack(scalars, weights, vectors, hidden, ids):
     piece = array(jnp.bfloat16, hidden.shape[1] + 16, hidden.shape[2])
-    pieces = whole_call(spread_body, "spread", scalars, [], [hidden, ids], [piece, piece], [], [])
-    return [lax.ppermute(piece, AXES, spread_pairs(first)) for first, piece in enumerate(pieces)]
+    if lax.axis_size("dp") == PARTS:
+        rows, width = weights[0].shape
+        given = weights + [v[None, :] for v in vectors]
+        return whole_call(
+            functools.partial(pack_body, len(given)), "pack", scalars, [], [Far(x) for x in given + [hidden, ids]],
+            [piece, piece, array(jnp.bfloat16, 3 * rows + 16, width)], [], [pltpu.VMEM((16, width), jnp.float32)],
+        )
+    gather = lambda v: lax.all_gather(v, "dp", axis=0, tiled=True)
+    split = lambda v: gather(v).reshape((PARTS, -1) + v.shape[1:])
+    pieces = whole_call(functools.partial(pack_body, 0), "pack", scalars, [], [Far(hidden), Far(ids)], [piece, piece], [], [])
+    return *pieces, weight_lines([split(w) for w in weights], [split(v) for v in vectors])
 
 
 def project_body(sizes, scalars, *refs):
-    rows, wide, vectors, qblock, chunk, lanes = sizes
-    pieces, hidden = parts_of(refs[:SHARDS]), refs[SHARDS : SHARDS + 4]
+    rows, wide, vectors, qblock, chunk, lanes, shards = sizes
+    pieces, hidden = parts_of(refs[:shards]), refs[shards : shards + 4]
     (
         attended, lse, tokens, vec_ref, up_ref, segments, ordered, query_out, keys_out, values_out, keys_far_out, values_far_out, weights_out,
-        query, keys, values, keys_far, values_far, far, held, small, turned, ids, sems, small_sems, hidden_sems, out_sems, kall, vt, tiles,
-    ) = refs[SHARDS + 4 :]
+        query, keys, values, keys_far, values_far, far, held, small, turned, ids, sems, hidden_sems, out_sems, kall, vt, tiles,
+    ) = refs[shards + 4 :]
     count, width = tokens.shape
     block = count // 2
     half = width // 2
@@ -775,18 +796,19 @@
         goal = tokens if i < 2 else far
         start(brought, ref.at[:block, :], goal.at[pl.ds(pl.multiple_of((place ^ odd) * block, block), block), :], hidden_sems.at[i])
     start(brought, hidden[0].at[block:, :], ids, hidden_sems.at[4])
-    for place, (ref, _, size) in enumerate(pieces):
-        where = scalars[0] ^ place
-        start(copies, ref.at[3 * rows : size, :], small.at[where], small_sems.at[place])
+    for part, first, ref in pieces:
+        where = scalars[0] ^ part
         target = pl.ds(where * rows, rows)
-        for weight in range(3):
+        for weight in range(first // rows, (first + ref.shape[0]) // rows):
             for side in range(2):
                 start(
                     copies,
-                    ref.at[weight * rows : (weight + 1) * rows, side * half : (side + 1) * half],
+                    ref.at[weight * rows - first : (weight + 1) * rows - first, side * half : (side + 1) * half],
                     held.at[side, target, weight * half : (weight + 1) * half],
-                    sems.at[len(copies) - place - 1],
+                    sems.at[len(copies)],
                 )
+        if first + ref.shape[0] > 3 * rows:
+            start(copies, ref.at[3 * rows - first :, :], small.at[where], sems.at[len(copies)])
     wait_all(brought)
     line = ids[...].astype(jnp.float32)
     for i in range(2):
@@ -818,19 +840,19 @@
 def project(scalars, pieces, hidden, rows, wide, vectors, qblock, chunk, lanes):
     block, width = hidden[0].shape[0] - 16, hidden[0].shape[1]
     count = 2 * block
-    lines = pieces[0].shape[-2] - 3 * rows
+    lines = 16
     n = 2 * count // chunk
     f32, b16 = jnp.float32, jnp.bfloat16
     whole = array(b16, count, width)
     vmem = lambda x: pltpu.VMEM(x.shape, x.dtype)
     return whole_call(
-        functools.partial(project_body, (rows, wide, vectors, qblock, chunk, lanes)), "project", scalars, list(pieces) + list(hidden), [],
+        functools.partial(project_body, (rows, wide, vectors, qblock, chunk, lanes, len(pieces))), "project", scalars, list(pieces) + list(hidden), [],
         [whole, array(f32, width // lanes, 8, count), whole, array(f32, lines, width), array(f32, 1, wide * PARTS), array(f32, 1, 2 * count),
          array(b16, 2, PARTS // 2, rows, count)],
         [whole] * 5 + [array(b16, 2, width, 3 * width // 2)],
         [vmem(whole)] * 6
         + [pltpu.VMEM((2, width, 3 * width // 2), b16), pltpu.VMEM((PARTS, lines, width), b16), pltpu.VMEM((PARTS, rows, count), b16),
-           pltpu.VMEM((16, width), b16), pltpu.SemaphoreType.DMA((6 * PARTS,)), pltpu.SemaphoreType.DMA((PARTS,)),
+           pltpu.VMEM((16, width), b16), pltpu.SemaphoreType.DMA((7 * PARTS,)),
            pltpu.SemaphoreType.DMA((5,)), pltpu.SemaphoreType.DMA((6,)), pltpu.VMEM((n, chunk, lanes), b16),
            pltpu.VMEM((n, lanes, chunk), b16), pltpu.VMEM((n, chunk, LANES), f32)],
         28,
@@ -876,24 +898,30 @@
     scalars = jnp.stack([jnp.asarray(v, jnp.int32) for v in scalars])
 
     vectors = [query_bias, value_bias, out_bias, first_gain, first_shift, down_bias, second_gain, second_shift]
-    part = projection_part(scalars, [query_weight, key_weight, value_weight], vectors + [up_bias])
-    near = near_shards(part)
-    hidden = spread_hidden(after(scalars, part), hidden_in, segment_ids)
-    out_up, down_part = lax.optimization_barrier((jnp.concatenate([out_weight, up_weight], axis=1), down_weight, *near[1:4]))[:2]
-    shards = all_shards(near)
+    *hidden, part = pack(
+        scalars, [query_weight, key_weight, value_weight], vectors + [up_bias], hidden_in, segment_ids
+    )
+    near = near_shards(part, False)
+    hidden = [lax.ppermute(piece, AXES, spread_pairs(first)) for first, piece in enumerate(hidden)]
+    shards = relayed_shards(near, 2 * width // PARTS)
+    out_up, down_part = lax.optimization_barrier(
+        (jnp.concatenate([out_weight, up_weight], axis=1), down_weight, *near[1:3])
+    )[:2]
+    if direct:
+        hidden = list(lax.optimization_barrier((*hidden, near[1], near[2]))[:2])
     hidden += [swap_dp(piece, 1) for piece in hidden]
     out_up_near = near_shards(out_up)
     attended, lse, tokens, vec, up_add, segments, ordered, query, keys, values, keys_other, values_other, w_qkv = project(
         scalars, shards, hidden, width // PARTS, inner_width // PARTS, len(vectors), qblock, chunk, pairs * LANES
     )
     order = Order()
-    got_up, odd = to_sequences(after(cotangent, *near[1:4], *hidden[:2]), order)
-    upstream = in_order(lax.optimization_barrier((*got_up, attended))[:2], odd, hidden_in.shape[1])
-    out_up_shards = all_shards(out_up_near, attended, upstream)
-    down_near = near_shards(after(down_part, attended, *out_up_near[1:4]))
+    down_near = near_shards(after(down_part, attended, *out_up_near[1:4]), False)
+    got_up, odd = to_sequences(after(cotangent, attended), order)
+    out_up_shards = all_shards(out_up_near, attended)
     normal_one, scale_one, first_low, active, slope, wo, wu = widen(scalars, out_up_shards, attended, tokens, vec, up_add)
+    upstream = in_order(lax.optimization_barrier((*got_up, active))[:2], odd, hidden_in.shape[1])
     layer_low, sum_two_grad, second_grad, sums_two, down_send, down_keep, wd = narrow(
-        scalars, all_shards(down_near, active), active, normal_one, vec, upstream
+        scalars, relayed_shards(down_near, inner_width // PARTS // 2, active), active, normal_one, vec, upstream
     )
     swap = (lambda value: swap_dp(value, 1)) if direct else (lambda value: value)
     order = Order()
@@ -912,7 +940,6 @@
         order.gate(scalars), inner_grad, wu, sum_two_grad, normal_one, scale_one, vec, wo, attended
     )
     order.mark(attended_grad)
-    layer_out = order.mark(both_sequences(order, out_pieces))
 
     def attend(side):
         given = (query, keys, values, keys_other, values_other, attended, attended_grad, lse, segments)
@@ -925,6 +952,7 @@
         )
         order.mark(send, other)
         down_got, up_got = swap_dp(send, 4), swap_dp(other, 2)
+    layer_out = order.mark(both_sequences(order, out_pieces))
     one_send, one_keep, gradient, sums_first = qkv_back(
         0, order.gate(scalars), dq, dk, dv, swap_dp(order.gate(far), 1), ordered, w_qkv, sum_one_grad, out_send, out_keep,
         sums_one, sums_two, up_sum
@@ -962,12 +990,13 @@
         ff_got = swap_seq(order.mark(send), 2)
         ((send, two_keep),) = fold(order.gate(scalars), [(two_keep, two_got, (1, 1, 3))])
         two_got = swap_dp(order.mark(send), 4)
+    input_grad = order.mark(both_sequences(order, in_pieces).astype(jnp.float32))
+    if direct:
         send, keep = merge(order.gate(scalars), [(one_keep, one_got), (two_keep, two_got)], share)
         got = swap_seq(order.mark(send), 1)
-        down_grad, up_grad = order.mark(*last_ff(order.gate(scalars), ff_keep, ff_got, width))
         ((send, keep),) = fold(order.gate(scalars), [(keep, got, (1, 1, 5))])
         got = swap_seq(order.mark(send), 2)
-    input_grad = order.mark(both_sequences(order, in_pieces).astype(jnp.float32))
+        down_grad, up_grad = order.mark(*last_ff(order.gate(scalars), ff_keep, ff_got, width))
     if direct:
         query_grad, key_grad, value_grad, out_grad, small, late, line = last_qkv(order.gate(scalars), keep, got, width)
         up_bias_grad = line[0, LANES - inner_width // devices :]

time: 277 us -> 249 us (0.90)
  waiting for transfers between devices: 93.6 us -> 62.7 us
  starting transfers between devices: 57.8 us -> 63.8 us
  local copies, waits for them, and re-layouts: 11.7 us -> 6.69 us
  Pallas kernels: 108 us -> 111 us
    ppermute x4, waiting for transfers between devices: 27.4 us -> 15.7 us  [swap_seq(): lax.ppermute(value, 'seq', [(i, i ^ mask) for i in range(lax.axis_size('s...]
    ppermute x2, waiting for transfers between devices: 9.88 us -> 0.01 us  [per_device(): lax.ppermute(piece, AXES, spread_pairs(first))]
    ppermute x37 -> x41, waiting for transfers between devices: 53.7 us -> 44.4 us  [swap_dp(): lax.ppermute(value, 'dp', [(i, i ^ mask) for i in range(lax.axis_size('dp...]
    unnamed x32 -> x62, local copies, waits for them, and re-layouts: 9.81 us -> 4.1 us
    ppermute x4, starting transfers between devices: 2.07 us -> 6.11 us  [swap_seq(): lax.ppermute(value, 'seq', [(i, i ^ mask) for i in range(lax.axis_size('s...]
    pallas_call x24 -> x23, Pallas kernels: 108 us -> 111 us  [whole_call(): pl.pallas_call(body, in_specs=[pl.BlockSpec(memory_space=pltpu.SMEM)] + [...]
    ppermute x37 -> x41, starting transfers between devices: 43 us -> 44 us  [swap_dp(): lax.ppermute(value, 'dp', [(i, i ^ mask) for i in range(lax.axis_size('dp...]
  transfers between devices with their start and end apart: 49 -> 53, of which waited for: 20 -> 18; matrix products, arithmetic and copies ran while one was open for 1% -> 1% of each run, Pallas kernels for 31% -> 34%
where the time goes in v2:
time: 249 us
  Pallas kernels  111 us (45%)
  starting transfers between devices  63.8 us (26%)
  waiting for transfers between devices  62.7 us (25%)
  local copies, waits for them, and re-layouts  6.69 us (3%)
  other arithmetic  2.88 us (1%)
    pallas_call x23, Pallas kernels, whole_call(): pl.pallas_call(body, in_specs=[pl.BlockSpec(memory_space=pltpu.SMEM)] + [...  111 us
    ppermute x41, waiting for transfers between devices, swap_dp(): lax.ppermute(value, 'dp', [(i, i ^ mask) for i in range(lax.axis_size('dp...  44.4 us
    ppermute x41, starting transfers between devices, swap_dp(): lax.ppermute(value, 'dp', [(i, i ^ mask) for i in range(lax.axis_size('dp...  44 us
    ppermute x4, waiting for transfers between devices, swap_seq(): lax.ppermute(value, 'seq', [(i, i ^ mask) for i in range(lax.axis_size('s...  15.7 us
    ppermute x4, starting transfers between devices, swap_seq(): lax.ppermute(value, 'seq', [(i, i ^ mask) for i in range(lax.axis_size('s...  6.11 us
    ppermute x2, starting transfers between devices, to_sequences(): got.append(lax.ppermute(piece, AXES, spread_pairs(first)))  6.03 us
    ppermute x4, starting transfers between devices, from_sequences(): lax.ppermute(piece, AXES, [(b, a) for a, b in spread_pairs(first)])  5.34 us
  transfers between devices with their start and end apart: 53, of which 18 were waited for; matrix products, arithmetic and copies ran while one was open for 1% of the time, Pallas kernels for 34%

profile of v2, /device:TPU:0, one launch (start us, length us, event | category | flops | bytes accessed | tf_op | source)
XLA Modules:
  0.0 248.6 jit_solution(13648771327039231394)
XLA Ops:
  2.1 2.2 pack.1
  4.3 3.0 %collective-permute-start.1 = (bf16[304,768]{1,0:T(8,128)(2,1)S(1)}, bf16[304,768]{1,0:T(8,128)(2,1)S(1)}, u32[]{:S(2)}, u32[]{:S(2)}) collective-permute-start(bf16[304,768]{1,0:T(8,128)(2,1)S(1)} %get-tuple-element.156.refs_0_), channel_id=1, source_target_pairs={{0,16},{4,20},{8,24},{12,28},{16,0},{20,4},{24,8},{28,12},{1,17},{... | collective-permute-start | bytes 1400840 | tf_op jit(solution)/shard_map/ppermute | solution.py:653
  9.5 1.6 collective-permute-start.10
  11.2 6.9 %collective-permute-done.1.refs_4_ = bf16[304,768]{1,0:T(8,128)(2,1)S(1)} collective-permute-done((bf16[304,768]{1,0:T(8,128)(2,1)S(1)}, bf16[304,768]{1,0:T(8,128)(2,1)S(1)}, u32[]{:S(2)}, u32[]{:S(2)}) %collective-permute-start.1) | collective-permute-done | bytes 466976 | tf_op jit(solution)/shard_map/ppermute | solution.py:653
  20.0 1.7 collective-permute-start.7
  21.7 6.5 %collective-permute-start.11 = (bf16[272,768]{1,0:T(8,128)(2,1)S(1)}, bf16[272,768]{1,0:T(8,128)(2,1)S(1)}, u32[]{:S(2)}, u32[]{:S(2)}) collective-permute-start(bf16[272,768]{1,0:T(8,128)(2,1)S(1)} %collective-permute-done.9.refs_10_), channel_id=1, source_target_pairs={{0,4},{4,0},{8,12},{12,8},{16,20},{20,16},{24,28},{28,24},{1,5},{5... | collective-permute-start | bytes 1253384 | tf_op jit(solution)/shard_map/ppermute | solution.py:653
  29.4 2.4 collective-permute-done.8.refs_9_
  38.6 20.7 %project.1 = (bf16[512,768]{1,0:T(8,128)(2,1)S(1)}, f32[2,8,512]{2,1,0:T(8,128)S(1)}, bf16[512,768]{1,0:T(8,128)(2,1)S(1)}, f32[16,768]{1,0:T(8,128)S(1)}, f32[1...) custom-call(s32[8]{0:T(128)S(1)} %stack.57.scalars, ...), custom_call_target="tpu_custom_call" | custom-call | flops 1 | bytes 1 | tf_op jit(solution)/shard_map/project/pallas_call | solution.py:412
  60.3 6.4 %collective-permute-done.14.refs_4_ = bf16[96,3840]{1,0:T(8,128)(2,1)} collective-permute-done((bf16[96,3840]{1,0:T(8,128)(2,1)S(1)}, bf16[96,3840]{1,0:T(8,128)(2,1)}, u32[]{:S(2)}, u32[]{:S(2)}) %collective-permute-start.14) | collective-permute-done | bytes 737312 | tf_op jit(solution)/shard_map/ppermute | solution.py:653
  69.2 5.2 %collective-permute-start.30 = (bf16[256,768]{1,0:T(8,128)(2,1)S(1)}, bf16[256,768]{1,0:T(8,128)(2,1)S(1)}, u32[]{:S(2)}, u32[]{:S(2)}) collective-permute-start(bf16[256,768]{1,0:T(8,128)(2,1)S(1)} %get-tuple-element.287), channel_id=1, source_target_pairs={{0,1},{1,0},{2,5},{3,4},{4,3},{5,2},{6,7},{7,6},{8,9},{9,8},{10,13... | collective-permute-start | bytes 1179656 | tf_op jit(solution)/shard_map/ppermute | solution.py:682
  75.3 10.7 %widen.1 = (f32[512,768]{1,0:T(8,128)S(1)}, f32[512,128]{1,0:T(8,128)S(1)}, bf16[512,768]{1,0:T(8,128)(2,1)S(1)}, bf16[512,3072]{1,0:T(8,128)(2,1)S(1)}, bf16[51...) custom-call(s32[8]{0:T(128)S(1)} %stack.57.scalars, ...), custom_call_target="tpu_custom_call" | custom-call | flops 1 | bytes 1 | tf_op jit(solution)/shard_map/widen/pallas_call | solution.py:412
  88.3 3.4 %collective-permute-start.22 = (bf16[384,768]{1,0:T(8,128)(2,1)S(1)}, bf16[384,768]{1,0:T(8,128)(2,1)S(1)}, u32[]{:S(2)}, u32[]{:S(2)}) collective-permute-start(bf16[384,768]{1,0:T(8,128)(2,1)S(1)} %copy-done.10), channel_id=1, source_target_pairs={{0,4},{4,0},{8,12},{12,8},{16,20},{20,16},{24,28},{28,24},{1,5},{5... | collective-permute-start | bytes 1769480 | tf_op jit(solution)/shard_map/ppermute | solution.py:653
  92.9 3.2 %collective-permute-start.28 = (bf16[192,768]{1,0:T(8,128)(2,1)S(1)}, bf16[192,768]{1,0:T(8,128)(2,1)S(1)}, u32[]{:S(2)}, u32[]{:S(2)}) collective-permute-start(bf16[192,768]{1,0:T(8,128)(2,1)S(1)} %collective-permute-done.27.refs_8_), channel_id=1, source_target_pairs={{0,4},{4,0},{8,12},{12,8},{16,20},{20,16},{24,28},{28,24},{1,5},{5... | collective-permute-start | bytes 884744 | tf_op jit(solution)/shard_map/ppermute | solution.py:653
  99.8 10.4 %narrow.1 = (bf16[512,768]{1,0:T(8,128)(2,1)S(1)}, f32[512,768]{1,0:T(8,128)S(1)}, bf16[512,768]{1,0:T(8,128)(2,1)S(1)}, f32[8,768]{1,0:T(8,128)S(1)}, bf16[4,38...) custom-call(s32[8]{0:T(128)S(1)} %stack.57.scalars, ...), custom_call_target="tpu_custom_call" | custom-call | flops 1 | bytes 1 | tf_op jit(solution)/shard_map/narrow/pallas_call | solution.py:412
  110.7 6.5 %inner_back.1 = (bf16[512,3072]{1,0:T(8,128)(2,1)S(1)}, f32[1,3072]{1,0:T(1,128)S(1)}, bf16[4,96,3072]{2,1,0:T(8,128)(2,1)S(1)}, bf16[4,96,3072]{2,1,0:T(8,128)(2,1)S(1)}) custom-call(s32[8]{0:T(128)S(1)} %stack.57.scalars, bf16[512,768]{1,0:T(8,128)(2,1)S(1)} %get-tuple-element.186.low, bf16[3072,768]{1,0:T(8,128)(2,1)S(1)} %get-tuple-element.187.wd, ...), custom_call_target="tpu_custom_call" | custom-call | flops 1 | bytes 1 | tf_op jit(solution)/shard_map/inner_back/pallas_call | solution.py:412
  118.6 3.2 %collective-permute-done.32.refs_1_ = bf16[4,96,3072]{2,1,0:T(8,128)(2,1)S(1)} collective-permute-done((bf16[4,96,3072]{2,1,0:T(8,128)(2,1)S(1)}, bf16[4,96,3072]{2,1,0:T(8,128)(2,1)S(1)}, u32[]{:S(2)}, u32[]{:S(2)}) %collective-permute-start.32) | collective-permute-done | bytes 2359328 | tf_op jit(solution)/shard_map/ppermute | solution.py:653
  125.0 2.9 %collective-permute-start.35 = (bf16[256,768]{1,0:T(8,128)(2,1)S(1)}, bf16[256,768]{1,0:T(8,128)(2,1)S(1)}, u32[]{:S(2)}, u32[]{:S(2)}) collective-permute-start(bf16[256,768]{1,0:T(8,128)(2,1)S(1)} %broadcast_select_fusion.2), channel_id=1, source_target_pairs={{1,0},{0,1},{5,2},{4,3},{3,4},{2,5},{7,6},{6,7},{9,8},{8,9},{13,10... | collective-permute-start | bytes 1179656 | tf_op jit(solution)/shard_map/ppermute | solution.py:697
  128.6 6.6 %outer_back.1 = (f32[512,768]{1,0:T(8,128)S(1)}, bf16[512,768]{1,0:T(8,128)(2,1)S(1)}, f32[8,768]{1,0:T(8,128)S(1)}, bf16[4,96,768]{2,1,0:T(8,128)(2,1)S(1)}, bf16[4,96,768]{2,1,0:T(8,128)(2,1)S(1)}) custom-call(s32[8]{0:T(128)S(1)} %stack.57.scalars, bf16[512,3072]{1,0:T(8,128)(2,1)S(1)} %get-tuple-element.190.grad, ...), custom_call_target="tpu_custom_call" | custom-call | flops 1 | bytes 1 | tf_op jit(solution)/shard_map/outer_back/pallas_call | solution.py:412
  136.2 15.7 %attend_back.2 = (bf16[512,384]{1,0:T(8,128)(2,1)S(1)}, f32[512,384]{1,0:T(8,128)S(1)}, f32[512,384]{1,0:T(8,128)S(1)}, bf16[2,512,384]{2,1,0:T(8,128)(2,1)S(1)}) custom-call(s32[8]{0:T(128)S(1)} %stack.57.scalars, bf16[512,768]{1,0:T(8,128)(2,1)} %get-tuple-element.206.refs_0_, bf16[512,768]{1,0:T(8,128)(2,1)} %get-tuple-element.207.refs_1_, ...), custom_call_target="tpu_custom_call" | custom-call | flops 1 | bytes 1 | tf_op jit(solution)/shard_map/attend_back/pallas_call | solution.py:412
  154.1 2.2 collective-permute-start.37
  156.3 1.9 collective-permute-done.37.refs_3_
  158.2 5.2 %qkv_back.2 = (bf16[4,96,2048]{2,1,0:T(8,128)(2,1)S(1)}, bf16[4,96,2048]{2,1,0:T(8,128)(2,1)S(1)}, f32[512,768]{1,0:T(8,128)S(1)}, f32[8,384]{1,0:T(8,128)S(1)}) custom-call(s32[8]{0:T(128)S(1)} %stack.57.scalars, bf16[512,384]{1,0:T(8,128)(2,1)S(1)} %get-tuple-element.213.refs_0_, f32[512,384]{1,0:T(8,128)S(1)} %get-tuple-element.214.refs_1_, ...), custom_call_target="tpu_custom_call" | custom-call | flops 1 | bytes 1 | tf_op jit(solution)/shard_map/qkv_back/pallas_call | solution.py:412
  165.6 15.7 %attend_back.3 = (bf16[512,384]{1,0:T(8,128)(2,1)S(1)}, f32[512,384]{1,0:T(8,128)S(1)}, f32[512,384]{1,0:T(8,128)S(1)}, bf16[2,512,384]{2,1,0:T(8,128)(2,1)S(1)}) custom-call(s32[8]{0:T(128)S(1)} %stack.57.scalars, bf16[512,768]{1,0:T(8,128)(2,1)} %get-tuple-element.206.refs_0_, bf16[512,768]{1,0:T(8,128)(2,1)} %get-tuple-element.207.refs_1_, ...), custom_call_target="tpu_custom_call" | custom-call | flops 1 | bytes 1 | tf_op jit(solution)/shard_map/attend_back/pallas_call | solution.py:412
  183.1 2.3 collective-permute-done.41.refs_3_
  185.4 5.4 %qkv_back.3 = (bf16[4,96,1280]{2,1,0:T(8,128)(2,1)S(1)}, bf16[4,96,1280]{2,1,0:T(8,128)(2,1)S(1)}, bf16[512,768]{1,0:T(8,128)(2,1)S(1)}, f32[8,384]{1,0:T(8,128)}) custom-call(s32[8]{0:T(128)S(1)} %stack.57.scalars, bf16[512,384]{1,0:T(8,128)(2,1)S(1)} %get-tuple-element.235.refs_0_, f32[512,384]{1,0:T(8,128)S(1)} %get-tuple-element.236.refs_1_, ...), custom_call_target="tpu_custom_call" | custom-call | flops 1 | bytes 1 | tf_op jit(solution)/shard_map/qkv_back/pallas_call | solution.py:412
  197.1 14.4 %collective-permute-done.43.refs_1_ = bf16[2,96,2048]{2,1,0:T(8,128)(2,1)S(1)} collective-permute-done((bf16[2,96,2048]{2,1,0:T(8,128)(2,1)S(1)}, bf16[2,96,2048]{2,1,0:T(8,128)(2,1)S(1)}, u32[]{:S(2)}, u32[]{:S(2)}) %collective-permute-start.43) | collective-permute-done | bytes 786464 | tf_op jit(solution)/shard_map/ppermute | solution.py:653
  214.8 2.0 collective-permute-start.49
  216.7 2.6 %collective-permute-done.46 = bf16[256,768]{1,0:T(8,128)(2,1)S(1)} collective-permute-done((bf16[256,768]{1,0:T(8,128)(2,1)S(1)}, bf16[256,768]{1,0:T(8,128)(2,1)S(1)}, u32[]{:S(2)}, u32[]{:S(2)}) %collective-permute-start.46) | collective-permute-done | bytes 393248 | tf_op jit(solution)/shard_map/ppermute | solution.py:697
  220.6 2.1 collective-permute-done.48
  224.5 2.6 %collective-permute-start.51 = (bf16[1,24,6144]{2,1,0:T(8,128)(2,1)S(1)}, bf16[1,24,6144]{2,1,0:T(8,128)(2,1)S(1)}, u32[]{:S(2)}, u32[]{:S(2)}) collective-permute-start(bf16[1,24,6144]{2,1,0:T(8,128)(2,1)S(1)} %get-tuple-element.262), channel_id=1, source_target_pairs={{0,2},{1,3},{2,0},{3,1},{4,6},{5,7},{6,4},{7,5},{8,10},{9,11},{10,... | collective-permute-start | bytes 884744 | tf_op jit(solution)/shard_map/ppermute | solution.py:657
  227.1 9.9 %collective-permute-done.50.refs_1_ = bf16[2,24,3328]{2,1,0:T(8,128)(2,1)S(1)} collective-permute-done((bf16[2,24,3328]{2,1,0:T(8,128)(2,1)S(1)}, bf16[2,24,3328]{2,1,0:T(8,128)(2,1)S(1)}, u32[]{:S(2)}, u32[]{:S(2)}) %collective-permute-start.50) | collective-permute-done | bytes 319520 | tf_op jit(solution)/shard_map/ppermute | solution.py:657
  241.2 5.0 %collective-permute-done.52.got = bf16[1,24,3328]{2,1,0:T(8,128)(2,1)S(1)} collective-permute-done((bf16[1,24,3328]{2,1,0:T(8,128)(2,1)S(1)}, bf16[1,24,3328]{2,1,0:T(8,128)(2,1)S(1)}, u32[]{:S(2)}, u32[]{:S(2)}) %collective-permute-start.52) | collective-permute-done | bytes 159776 | tf_op jit(solution)/shard_map/ppermute | solution.py:657
  (176 shorter events, 56.6 us)
Async XLA Ops:
  4.3 13.7 %collective-permute-start.1 = (bf16[304,768]{1,0:T(8,128)(2,1)S(1)}, bf16[304,768]{1,0:T(8,128)(2,1)S(1)}, u32[]{:S(2)}, u32[]{:S(2)}) collective-permute-start(bf16[304,768]{1,0:T(8,128)(2,1)S(1)} %get-tuple-element.156.refs_0_), channel_id=1, source_target_pairs={{0,16},{4,20},{8,24},{12,28},{16,0},{20,4},{24,8},{28,12},{1,17},{... | collective-permute-start | bytes 1400840 | tf_op jit(solution)/shard_map/ppermute | solution.py:653
  7.4 12.2 %collective-permute-start = (bf16[304,768]{1,0:T(8,128)(2,1)S(1)}, bf16[304,768]{1,0:T(8,128)(2,1)S(1)}, u32[]{:S(2)}, u32[]{:S(2)}) collective-permute-start(bf16[304,768]{1,0:T(8,128)(2,1)S(1)} %get-tuple-element.156.refs_0_), channel_id=1, source_target_pairs={{0,8},{4,12},{8,0},{12,4},{16,24},{20,28},{24,16},{28,20},{1,9},{5... | collective-permute-start | bytes 1400840 | tf_op jit(solution)/shard_map/ppermute | solution.py:653
  8.9 12.8 %collective-permute-start.9 = (bf16[272,768]{1,0:T(8,128)(2,1)S(1)}, bf16[272,768]{1,0:T(8,128)(2,1)S(1)}, u32[]{:S(2)}, u32[]{:S(2)}) collective-permute-start(bf16[272,768]{1,0:T(8,128)(2,1)S(1)} %get-tuple-element.159), channel_id=1, source_target_pairs={{0,0},{1,1},{2,4},{3,5},{4,2},{5,3},{6,6},{7,7},{8,8},{9,9},{10,12... | collective-permute-start | bytes 1253384 | tf_op jit(solution)/shard_map/ppermute | solution.py:905
  9.5 12.2 %collective-permute-start.10 = (bf16[272,768]{1,0:T(8,128)(2,1)S(1)}, bf16[272,768]{1,0:T(8,128)(2,1)S(1)}, u32[]{:S(2)}, u32[]{:S(2)}) collective-permute-start(bf16[272,768]{1,0:T(8,128)(2,1)S(1)} %get-tuple-element.160), channel_id=1, source_target_pairs={{0,1},{1,0},{2,5},{3,4},{4,3},{5,2},{6,7},{7,6},{8,9},{9,8},{10,13... | collective-permute-start | bytes 1253384 | tf_op jit(solution)/shard_map/ppermute | solution.py:905
  19.5 9.3 %collective-permute-start.5 = (bf16[192,768]{1,0:T(8,128)(2,1)S(1)}, bf16[192,768]{1,0:T(8,128)(2,1)S(1)}, u32[]{:S(2)}, u32[]{:S(2)}) collective-permute-start(bf16[192,768]{1,0:T(8,128)(2,1)S(1)} %slice.63), channel_id=1, source_target_pairs={{0,16},{4,20},{8,24},{12,28},{16,0},{20,4},{24,8},{28,12},{1,17},{... | collective-permute-start | bytes 884744 | tf_op jit(solution)/shard_map/ppermute | solution.py:653
  20.0 8.8 %collective-permute-start.7 = (bf16[112,768]{1,0:T(8,128)(2,1)S(1)}, bf16[112,768]{1,0:T(8,128)(2,1)S(1)}, u32[]{:S(2)}, u32[]{:S(2)}) collective-permute-start(bf16[112,768]{1,0:T(8,128)(2,1)S(1)} %slice.64), channel_id=1, source_target_pairs={{0,8},{4,12},{8,0},{12,4},{16,24},{20,28},{24,16},{28,20},{1,9},{5... | collective-permute-start | bytes 516104 | tf_op jit(solution)/shard_map/ppermute | solution.py:653
  21.7 10.6 %collective-permute-start.11 = (bf16[272,768]{1,0:T(8,128)(2,1)S(1)}, bf16[272,768]{1,0:T(8,128)(2,1)S(1)}, u32[]{:S(2)}, u32[]{:S(2)}) collective-permute-start(bf16[272,768]{1,0:T(8,128)(2,1)S(1)} %collective-permute-done.9.refs_10_), channel_id=1, source_target_pairs={{0,4},{4,0},{8,12},{12,8},{16,20},{20,16},{24,28},{28,24},{1,5},{5... | collective-permute-start | bytes 1253384 | tf_op jit(solution)/shard_map/ppermute | solution.py:653
  31.8 28.5 %collective-permute-start.15 = (bf16[96,3840]{1,0:T(8,128)(2,1)S(1)}, bf16[96,3840]{1,0:T(8,128)(2,1)}, u32[]{:S(2)}, u32[]{:S(2)}) collective-permute-start(bf16[96,3840]{1,0:T(8,128)(2,1)S(1)} %pad_maximum_fusion.refs_0_), channel_id=1, source_target_pairs={{0,24},{4,28},{8,16},{12,20},{16,8},{20,12},{24,0},{28,4},{1,25},{... | collective-permute-start | bytes 2211848 | tf_op jit(solution)/shard_map/ppermute | solution.py:653
  32.3 34.4 %collective-permute-start.14 = (bf16[96,3840]{1,0:T(8,128)(2,1)S(1)}, bf16[96,3840]{1,0:T(8,128)(2,1)}, u32[]{:S(2)}, u32[]{:S(2)}) collective-permute-start(bf16[96,3840]{1,0:T(8,128)(2,1)S(1)} %pad_maximum_fusion.refs_0_), channel_id=1, source_target_pairs={{0,16},{4,20},{8,24},{12,28},{16,0},{20,4},{24,8},{28,12},{1,17},{... | collective-permute-start | bytes 2211848 | tf_op jit(solution)/shard_map/ppermute | solution.py:653
  33.8 32.9 %collective-permute-start.13 = (bf16[96,3840]{1,0:T(8,128)(2,1)S(1)}, bf16[96,3840]{1,0:T(8,128)(2,1)}, u32[]{:S(2)}, u32[]{:S(2)}) collective-permute-start(bf16[96,3840]{1,0:T(8,128)(2,1)S(1)} %pad_maximum_fusion.refs_0_), channel_id=1, source_target_pairs={{0,8},{4,12},{8,0},{12,4},{16,24},{20,28},{24,16},{28,20},{1,9},{5... | collective-permute-start | bytes 2211848 | tf_op jit(solution)/shard_map/ppermute | solution.py:653
  37.2 31.3 %collective-permute-start.18 = (bf16[96,3840]{1,0:T(8,128)(2,1)S(1)}, bf16[96,3840]{1,0:T(8,128)(2,1)}, u32[]{:S(2)}, u32[]{:S(2)}) collective-permute-start(bf16[96,3840]{1,0:T(8,128)(2,1)S(1)} %pad_maximum_fusion.refs_0_), channel_id=1, source_target_pairs={{0,4},{4,0},{8,12},{12,8},{16,20},{20,16},{24,28},{28,24},{1,5},{5... | collective-permute-start | bytes 2211848 | tf_op jit(solution)/shard_map/ppermute | solution.py:653
  67.2 18.8 %collective-permute-start.17 = (bf16[384,768]{1,0:T(8,128)(2,1)}, bf16[384,768]{1,0:T(8,128)(2,1)S(1)}, u32[]{:S(2)}, u32[]{:S(2)}) collective-permute-start(bf16[384,768]{1,0:T(8,128)(2,1)} %refs_0_.2), channel_id=1, source_target_pairs={{0,16},{4,20},{8,24},{12,28},{16,0},{20,4},{24,8},{28,12},{1,17},{... | collective-permute-start | bytes 1769480 | tf_op jit(solution)/shard_map/ppermute | solution.py:653
  68.5 17.5 %collective-permute-start.16 = (bf16[384,768]{1,0:T(8,128)(2,1)}, bf16[384,768]{1,0:T(8,128)(2,1)S(1)}, u32[]{:S(2)}, u32[]{:S(2)}) collective-permute-start(bf16[384,768]{1,0:T(8,128)(2,1)} %refs_0_.2), channel_id=1, source_target_pairs={{0,8},{4,12},{8,0},{12,4},{16,24},{20,28},{24,16},{28,20},{1,9},{5... | collective-permute-start | bytes 1769480 | tf_op jit(solution)/shard_map/ppermute | solution.py:653
  69.2 22.5 %collective-permute-start.30 = (bf16[256,768]{1,0:T(8,128)(2,1)S(1)}, bf16[256,768]{1,0:T(8,128)(2,1)S(1)}, u32[]{:S(2)}, u32[]{:S(2)}) collective-permute-start(bf16[256,768]{1,0:T(8,128)(2,1)S(1)} %get-tuple-element.287), channel_id=1, source_target_pairs={{0,1},{1,0},{2,5},{3,4},{4,3},{5,2},{6,7},{7,6},{8,9},{9,8},{10,13... | collective-permute-start | bytes 1179656 | tf_op jit(solution)/shard_map/ppermute | solution.py:682
  74.4 17.4 %collective-permute-start.29 = (bf16[256,768]{1,0:T(8,128)(2,1)S(1)}, bf16[256,768]{1,0:T(8,128)(2,1)S(1)}, u32[]{:S(2)}, u32[]{:S(2)}) collective-permute-start(bf16[256,768]{1,0:T(8,128)(2,1)S(1)} %get-tuple-element.288), channel_id=1, source_target_pairs={{0,0},{1,1},{2,4},{3,5},{4,2},{5,3},{6,6},{7,7},{8,8},{9,9},{10,12... | collective-permute-start | bytes 1179656 | tf_op jit(solution)/shard_map/ppermute | solution.py:682
  88.3 10.2 %collective-permute-start.22 = (bf16[384,768]{1,0:T(8,128)(2,1)S(1)}, bf16[384,768]{1,0:T(8,128)(2,1)S(1)}, u32[]{:S(2)}, u32[]{:S(2)}) collective-permute-start(bf16[384,768]{1,0:T(8,128)(2,1)S(1)} %copy-done.10), channel_id=1, source_target_pairs={{0,4},{4,0},{8,12},{12,8},{16,20},{20,16},{24,28},{28,24},{1,5},{5... | collective-permute-start | bytes 1769480 | tf_op jit(solution)/shard_map/ppermute | solution.py:653
  123.0 28.9 %collective-permute-start.34 = (bf16[2,96,3072]{2,1,0:T(8,128)(2,1)S(1)}, bf16[2,96,3072]{2,1,0:T(8,128)(2,1)S(1)}, u32[]{:S(2)}, u32[]{:S(2)}) collective-permute-start(bf16[2,96,3072]{2,1,0:T(8,128)(2,1)S(1)} %get-tuple-element.198), channel_id=1, source_target_pairs={{0,16},{4,20},{8,24},{12,28},{16,0},{20,4},{24,8},{28,12},{1,17},{... | collective-permute-start | bytes 3538952 | tf_op jit(solution)/shard_map/ppermute | solution.py:653
  123.8 28.1 %collective-permute-start.33 = (bf16[2,384,768]{2,1,0:T(8,128)(2,1)S(1)}, bf16[2,384,768]{2,1,0:T(8,128)(2,1)S(1)}, u32[]{:S(2)}, u32[]{:S(2)}) collective-permute-start(bf16[2,384,768]{2,1,0:T(8,128)(2,1)S(1)} %get-tuple-element.194), channel_id=1, source_target_pairs={{0,8},{4,12},{8,0},{12,4},{16,24},{20,28},{24,16},{28,20},{1,9},{5... | collective-permute-start | bytes 3538952 | tf_op jit(solution)/shard_map/ppermute | solution.py:653
  125.0 28.1 %collective-permute-start.35 = (bf16[256,768]{1,0:T(8,128)(2,1)S(1)}, bf16[256,768]{1,0:T(8,128)(2,1)S(1)}, u32[]{:S(2)}, u32[]{:S(2)}) collective-permute-start(bf16[256,768]{1,0:T(8,128)(2,1)S(1)} %broadcast_select_fusion.2), channel_id=1, source_target_pairs={{1,0},{0,1},{5,2},{4,3},{3,4},{2,5},{7,6},{6,7},{9,8},{8,9},{13,10... | collective-permute-start | bytes 1179656 | tf_op jit(solution)/shard_map/ppermute | solution.py:697
  127.9 25.2 %collective-permute-start.36 = (bf16[256,768]{1,0:T(8,128)(2,1)S(1)}, bf16[256,768]{1,0:T(8,128)(2,1)S(1)}, u32[]{:S(2)}, u32[]{:S(2)}) collective-permute-start(bf16[256,768]{1,0:T(8,128)(2,1)S(1)} %broadcast_select_fusion.3), channel_id=1, source_target_pairs={{0,0},{1,1},{4,2},{5,3},{2,4},{3,5},{6,6},{7,7},{8,8},{9,9},{12,10... | collective-permute-start | bytes 1179656 | tf_op jit(solution)/shard_map/ppermute | solution.py:697
  163.5 18.7 %collective-permute-start.40 = (bf16[4,96,2048]{2,1,0:T(8,128)(2,1)S(1)}, bf16[4,96,2048]{2,1,0:T(8,128)(2,1)S(1)}, u32[]{:S(2)}, u32[]{:S(2)}) collective-permute-start(bf16[4,96,2048]{2,1,0:T(8,128)(2,1)S(1)} %get-tuple-element.245), channel_id=1, source_target_pairs={{0,4},{4,0},{8,12},{12,8},{16,20},{20,16},{24,28},{28,24},{1,5},{5... | collective-permute-start | bytes 4718600 | tf_op jit(solution)/shard_map/ppermute | solution.py:653
  163.9 17.4 %collective-permute-start.38 = (bf16[1,384,768]{2,1,0:T(8,128)(2,1)S(1)}, bf16[1,384,768]{2,1,0:T(8,128)(2,1)S(1)}, u32[]{:S(2)}, u32[]{:S(2)}) collective-permute-start(bf16[1,384,768]{2,1,0:T(8,128)(2,1)S(1)} %get-tuple-element.220), channel_id=1, source_target_pairs={{0,16},{4,20},{8,24},{12,28},{16,0},{20,4},{24,8},{28,12},{1,17},{... | collective-permute-start | bytes 1769480 | tf_op jit(solution)/shard_map/ppermute | solution.py:653
  164.6 16.7 %collective-permute-start.39 = (bf16[1,96,3072]{2,1,0:T(8,128)(2,1)S(1)}, bf16[1,96,3072]{2,1,0:T(8,128)(2,1)S(1)}, u32[]{:S(2)}, u32[]{:S(2)}) collective-permute-start(bf16[1,96,3072]{2,1,0:T(8,128)(2,1)S(1)} %get-tuple-element.221), channel_id=1, source_target_pairs={{0,8},{4,12},{8,0},{12,4},{16,24},{20,28},{24,16},{28,20},{1,9},{5... | collective-permute-start | bytes 1769480 | tf_op jit(solution)/shard_map/ppermute | solution.py:653
  191.1 22.3 %collective-permute-start.44 = (bf16[2,24,6144]{2,1,0:T(8,128)(2,1)S(1)}, bf16[2,24,6144]{2,1,0:T(8,128)(2,1)S(1)}, u32[]{:S(2)}, u32[]{:S(2)}) collective-permute-start(bf16[2,24,6144]{2,1,0:T(8,128)(2,1)S(1)} %get-tuple-element.242), channel_id=1, source_target_pairs={{0,1},{1,0},{2,3},{3,2},{4,5},{5,4},{6,7},{7,6},{8,9},{9,8},{10,11... | collective-permute-start | bytes 1769480 | tf_op jit(solution)/shard_map/ppermute | solution.py:657
  192.0 19.5 %collective-permute-start.43 = (bf16[2,96,2048]{2,1,0:T(8,128)(2,1)S(1)}, bf16[2,96,2048]{2,1,0:T(8,128)(2,1)S(1)}, u32[]{:S(2)}, u32[]{:S(2)}) collective-permute-start(bf16[2,96,2048]{2,1,0:T(8,128)(2,1)S(1)} %get-tuple-element.246), channel_id=1, source_target_pairs={{0,16},{4,20},{8,24},{12,28},{16,0},{20,4},{24,8},{28,12},{1,17},{... | collective-permute-start | bytes 2359304 | tf_op jit(solution)/shard_map/ppermute | solution.py:653
  194.3 19.8 %collective-permute-start.45 = (bf16[2,96,1280]{2,1,0:T(8,128)(2,1)S(1)}, bf16[2,96,1280]{2,1,0:T(8,128)(2,1)S(1)}, u32[]{:S(2)}, u32[]{:S(2)}) collective-permute-start(bf16[2,96,1280]{2,1,0:T(8,128)(2,1)S(1)} %get-tuple-element.256), channel_id=1, source_target_pairs={{0,8},{4,12},{8,0},{12,4},{16,24},{20,28},{24,16},{28,20},{1,9},{5... | collective-permute-start | bytes 1474568 | tf_op jit(solution)/shard_map/ppermute | solution.py:653
  195.4 23.9 %collective-permute-start.46 = (bf16[256,768]{1,0:T(8,128)(2,1)S(1)}, bf16[256,768]{1,0:T(8,128)(2,1)S(1)}, u32[]{:S(2)}, u32[]{:S(2)}) collective-permute-start(bf16[256,768]{1,0:T(8,128)(2,1)S(1)} %broadcast_select_fusion), channel_id=1, source_target_pairs={{1,0},{0,1},{5,2},{4,3},{3,4},{2,5},{7,6},{6,7},{9,8},{8,9},{13,10... | collective-permute-start | bytes 1179656 | tf_op jit(solution)/shard_map/ppermute | solution.py:697
  196.5 22.9 %collective-permute-start.47 = (bf16[256,768]{1,0:T(8,128)(2,1)S(1)}, bf16[256,768]{1,0:T(8,128)(2,1)S(1)}, u32[]{:S(2)}, u32[]{:S(2)}) collective-permute-start(bf16[256,768]{1,0:T(8,128)(2,1)S(1)} %broadcast_select_fusion.1), channel_id=1, source_target_pairs={{0,0},{1,1},{4,2},{5,3},{2,4},{3,5},{6,6},{7,7},{8,8},{9,9},{12,10... | collective-permute-start | bytes 1179656 | tf_op jit(solution)/shard_map/ppermute | solution.py:697
  212.3 10.3 %collective-permute-start.48 = (bf16[1,96,2048]{2,1,0:T(8,128)(2,1)S(1)}, bf16[1,96,2048]{2,1,0:T(8,128)(2,1)S(1)}, u32[]{:S(2)}, u32[]{:S(2)}) collective-permute-start(bf16[1,96,2048]{2,1,0:T(8,128)(2,1)S(1)} %get-tuple-element.259), channel_id=1, source_target_pairs={{0,8},{4,12},{8,0},{12,4},{16,24},{20,28},{24,16},{28,20},{1,9},{5... | collective-permute-start | bytes 1179656 | tf_op jit(solution)/shard_map/ppermute | solution.py:653
  223.3 13.7 %collective-permute-start.50 = (bf16[2,24,3328]{2,1,0:T(8,128)(2,1)S(1)}, bf16[2,24,3328]{2,1,0:T(8,128)(2,1)S(1)}, u32[]{:S(2)}, u32[]{:S(2)}) collective-permute-start(bf16[2,24,3328]{2,1,0:T(8,128)(2,1)S(1)} %get-tuple-element.270), channel_id=1, source_target_pairs={{0,1},{1,0},{2,3},{3,2},{4,5},{5,4},{6,7},{7,6},{8,9},{9,8},{10,11... | collective-permute-start | bytes 958472 | tf_op jit(solution)/shard_map/ppermute | solution.py:657
  224.5 15.3 %collective-permute-start.51 = (bf16[1,24,6144]{2,1,0:T(8,128)(2,1)S(1)}, bf16[1,24,6144]{2,1,0:T(8,128)(2,1)S(1)}, u32[]{:S(2)}, u32[]{:S(2)}) collective-permute-start(bf16[1,24,6144]{2,1,0:T(8,128)(2,1)S(1)} %get-tuple-element.262), channel_id=1, source_target_pairs={{0,2},{1,3},{2,0},{3,1},{4,6},{5,7},{6,4},{7,5},{8,10},{9,11},{10,... | collective-permute-start | bytes 884744 | tf_op jit(solution)/shard_map/ppermute | solution.py:657
  237.7 8.6 %collective-permute-start.52 = (bf16[1,24,3328]{2,1,0:T(8,128)(2,1)S(1)}, bf16[1,24,3328]{2,1,0:T(8,128)(2,1)S(1)}, u32[]{:S(2)}, u32[]{:S(2)}) collective-permute-start(bf16[1,24,3328]{2,1,0:T(8,128)(2,1)S(1)} %get-tuple-element.273), channel_id=1, source_target_pairs={{0,2},{1,3},{2,0},{3,1},{4,6},{5,7},{6,4},{7,5},{8,10},{9,11},{10,... | collective-permute-start | bytes 479240 | tf_op jit(solution)/shard_map/ppermute | solution.py:657
  (52 other events, 499.0 us)

commit v3 on v2

--- a/solution.py
+++ b/solution.py
@@ -114,23 +114,23 @@
 
 
 def backward_body(
-    qblock, chunk, lanes, side, scalars, q_ref, k_ref, v_ref, ko_ref, vo_ref, o_ref, do_ref, lse_all, segments,
-    dq_ref, dk_ref, dv_ref, far_ref, kall, vall, kt, dkall, dvall, sk_ref,
+    qblock, chunk, lanes, side, copies, scalars, q_ref, k_ref, v_ref, ko_ref, vo_ref, o_ref, do_ref, lse_all, segments,
+    dq_ref, dk_ref, dv_ref, far_keys, far_values, kall, vall, kt, dkall, dvall, sk_ref,
 ):
     half = k_ref.shape[0]
     tables = segment_tables(segments, sk_ref, half, qblock, chunk)
     lse_ref = lse_all.at[side : side + 1]
     chunks, pairs = half // chunk, lanes // LANES
-    for j in range(chunks):
-        rows = slice(j * chunk, (j + 1) * chunk)
-        kall[j] = k_ref[rows, :]
-        kall[chunks + j] = ko_ref[rows, :]
-        vall[j] = v_ref[rows, :]
-        vall[chunks + j] = vo_ref[rows, :]
-        kt[j] = k_ref[rows, :].T
-        kt[chunks + j] = ko_ref[rows, :].T
     dkall[...] = jnp.zeros_like(dkall)
     dvall[...] = jnp.zeros_like(dvall)
+    for first, keys, values in ((0, k_ref, v_ref), (chunks, ko_ref, vo_ref)):
+        wait_all(copies[1:3] if first == 0 else copies[3:5])
+        for j in range(chunks):
+            rows = slice(j * chunk, (j + 1) * chunk)
+            kall[first + j] = keys[rows, :]
+            vall[first + j] = values[rows, :]
+            kt[first + j] = keys[rows, :].T
+    wait_all(copies[:1] + copies[5:])
     for b in range(q_ref.shape[0] // qblock):
         span = slice(b * qblock, (b + 1) * qblock)
         parts, dparts, delta = [], [], []
@@ -149,19 +149,21 @@
             j = chunk_of(tables[b], step, chunks)
             mask = same_document(sk_ref[j], row)
             out = []
+            both_mask = jnp.concatenate([mask, mask], axis=1)
+            scores = [nt(kall[j, :, pair_lanes(pair)], both[pair]) for pair in range(pairs)]
+            products = [nt(vall[j, :, pair_lanes(pair)], dboth[pair]) for pair in range(pairs)]
+            adds = []
             for pair in range(pairs):
-                key, val = kall[j, :, pair_lanes(pair)], vall[j, :, pair_lanes(pair)]
-                probs, grads = [], []
+                score = jnp.where(both_mask, scores[pair], NEGATIVE)
+                prob = jnp.exp(score - jnp.concatenate(lse[2 * pair : 2 * pair + 2], axis=1))
+                grad = (prob * (products[pair] - jnp.concatenate(delta[2 * pair : 2 * pair + 2], axis=1))).astype(jnp.bfloat16)
                 for side in range(2):
                     h = 2 * pair + side
-                    score = jnp.where(mask, nt(key, parts[pair][side]), NEGATIVE)
-                    prob = jnp.exp(score - lse[h])
-                    grad = (prob * (nt(val, dparts[pair][side]) - delta[h])).astype(jnp.bfloat16)
-                    probs.append(prob.astype(jnp.bfloat16))
-                    grads.append(grad)
-                    out.append(carry[h] + nn(kt[j, h * HEAD_DIM : (h + 1) * HEAD_DIM, :], grad))
-                dvall[j, :, pair_lanes(pair)] += nn(jnp.concatenate(probs, axis=1), dboth[pair])
-                dkall[j, :, pair_lanes(pair)] += nn(jnp.concatenate(grads, axis=1), both[pair])
+                    out.append(carry[h] + nn(kt[j, h * HEAD_DIM : (h + 1) * HEAD_DIM, :], grad[:, side * qblock : (side + 1) * qblock]))
+                adds.append((nn(prob.astype(jnp.bfloat16), dboth[pair]), nn(grad, both[pair])))
+            for pair in range(pairs):
+                dvall[j, :, pair_lanes(pair)] += adds[pair][0]
+                dkall[j, :, pair_lanes(pair)] += adds[pair][1]
             return tuple(out)
 
         zero = jnp.zeros((HEAD_DIM, qblock), jnp.float32)
@@ -171,8 +173,8 @@
         rows = slice(j * chunk, (j + 1) * chunk)
         dk_ref[rows, :] = dkall[j]
         dv_ref[rows, :] = dvall[j]
-        far_ref[0, rows, :] = dkall[chunks + j].astype(jnp.bfloat16)
-        far_ref[1, rows, :] = dvall[chunks + j].astype(jnp.bfloat16)
+        far_keys[rows, :] = dkall[chunks + j].astype(jnp.bfloat16)
+        far_values[rows, :] = dvall[chunks + j].astype(jnp.bfloat16)
 
 
 def attend_back(scalars, query, keys, values, keys_other, values_other, attended, grad, lse_rows, segments, qblock, chunk, pairs, side):
@@ -185,9 +187,9 @@
     far = [Far(x, cols) for x in (query, keys, values, keys_other, values_other, attended, grad)]
     return whole_call(
         functools.partial(backward_body, qblock, chunk, lanes, side), "attend_back", scalars, [], far + [lse_rows, segments],
-        [array(b16, tokens, lanes), array(f32, half, lanes), array(f32, half, lanes), array(b16, 2, half, lanes)], [],
+        [array(b16, tokens, lanes), array(f32, half, lanes), array(f32, half, lanes), array(b16, half, lanes), array(b16, half, lanes)], [],
         [pltpu.VMEM((n, chunk, lanes), b16), pltpu.VMEM((n, chunk, lanes), b16), pltpu.VMEM((n, lanes, chunk), b16),
-         pltpu.VMEM((n, chunk, lanes), f32), pltpu.VMEM((n, chunk, lanes), f32), pltpu.VMEM((n, chunk, LANES), f32)], 24,
+         pltpu.VMEM((n, chunk, lanes), f32), pltpu.VMEM((n, chunk, lanes), f32), pltpu.VMEM((n, chunk, LANES), f32)], 24, True,
     )
 
 
@@ -373,42 +375,50 @@
 
 
 class Far:
-    def __init__(self, value, columns=None):
-        self.value, self.columns = value, columns
-        width = value.shape[-1] if columns is None else columns.stop - columns.start
-        self.shape, self.dtype = value.shape[:-1] + (width,), value.dtype
+    def __init__(self, value, columns=None, index=None):
+        self.value, self.columns, self.index = value, columns, index
+        shape = value.shape if index is None else value.shape[1:]
+        width = shape[-1] if columns is None else columns.stop - columns.start
+        self.shape, self.dtype = shape[:-1] + (width,), value.dtype
 
 
 def far_body(body, far, counts, scalars, *refs):
-    hbm, inputs, outputs, held = counts
+    hbm, inputs, outputs, held, lazy = counts
     given = list(refs[hbm : hbm + inputs])
     held_refs, sems = refs[len(refs) - held - 1 : -1], refs[-1]
     copies = []
-    for i, (place, columns) in enumerate(far):
-        source = given[place] if columns is None else given[place].at[:, columns]
+    for i, (place, columns, index) in enumerate(far):
+        source = given[place]
+        if index is not None:
+            source = source.at[index]
+        if columns is not None:
+            source = source.at[:, columns]
         copies.append(pltpu.make_async_copy(source, held_refs[i], sems.at[i]))
         copies[-1].start()
         given[place] = held_refs[i]
-    for copy in copies:
-        copy.wait()
-    body(scalars, *refs[:hbm], *given, *refs[hbm + inputs : len(refs) - held - 1])
+    rest = (*refs[:hbm], *given, *refs[hbm + inputs : len(refs) - held - 1])
+    if lazy:
+        body(copies, scalars, *rest)
+    else:
+        wait_all(copies)
+        body(scalars, *rest)
 
 
 def in_hbm(value):
     return pltpu.with_memory_space_constraint(value, pltpu.HBM)
 
 
-def whole_call(body, name, scalars, hbm, inputs, outputs, hbm_outputs, scratch, room=8):
+def whole_call(body, name, scalars, hbm, inputs, outputs, hbm_outputs, scratch, room=8, lazy=False):
     shape_of = lambda x: jax.ShapeDtypeStruct(x.shape, x.dtype)
     near, stay = pl.BlockSpec(memory_space=pltpu.VMEM), pl.BlockSpec(memory_space=pltpu.HBM)
-    far = [(i, x.columns) for i, x in enumerate(inputs) if isinstance(x, Far)]
+    far = [(i, x.columns, x.index) for i, x in enumerate(inputs) if isinstance(x, Far)]
     scratch = list(scratch)
     if far:
-        held = [pltpu.VMEM(inputs[i].shape, inputs[i].dtype) for i, _ in far]
-        counts = (len(hbm), len(inputs), len(outputs) + len(hbm_outputs), len(far))
+        held = [pltpu.VMEM(inputs[i].shape, inputs[i].dtype) for i, *_ in far]
+        counts = (len(hbm), len(inputs), len(outputs) + len(hbm_outputs), len(far), lazy)
         body = functools.partial(far_body, body, far, counts)
         scratch += held + [pltpu.SemaphoreType.DMA((len(far),))]
-        room += sum(math.prod(inputs[i].shape) * inputs[i].dtype.itemsize for i, _ in far) // (1 << 20) + 1
+        room += sum(math.prod(inputs[i].shape) * inputs[i].dtype.itemsize for i, *_ in far) // (1 << 20) + 1
     return pl.pallas_call(
         body,
         in_specs=[pl.BlockSpec(memory_space=pltpu.SMEM)]
@@ -490,48 +500,52 @@
         keep[i, :, first : first + LANES] = parts[2 * i + core].astype(jnp.bfloat16)
 
 
-def qkv_back_body(side, scalars, dq, dk, dv, far, ordered, weight, gradient, *refs):
+def qkv_back_body(side, copies, scalars, dq, dk, dv, far_keys, far_values, ordered, weight, gradient, *refs):
     core = scalars[1]
     if side == 0:
-        out_send, out_keep, sums_one, sums_two, wide_sums, send, keep, result, sums_ref, both, lines, parts = refs
+        sums_one, sums_two, wide_sums, send_low, send_high, keep, result, sums_ref, both, lines, parts, send = refs
     else:
-        first_sums, send, keep, result, sums_ref, both, lines, parts = refs
+        first_sums, send_low, send_high, keep, result, sums_ref, both, lines, parts, send = refs
     half = dq.shape[1]
     both[:, :half] = dq[...]
-    both[:, half : 2 * half] = (dk[...] + far[0].astype(jnp.float32)).astype(jnp.bfloat16)
-    both[:, 2 * half :] = (dv[...] + far[1].astype(jnp.float32)).astype(jnp.bfloat16)
+    both[:, half : 2 * half] = (dk[...] + far_keys[...].astype(jnp.float32)).astype(jnp.bfloat16)
+    both[:, 2 * half :] = (dv[...] + far_values[...].astype(jnp.float32)).astype(jnp.bfloat16)
     sums_ref[...] = jnp.zeros_like(sums_ref)
     sums_ref[0:1, :] = row_sum(dq[...])
     sums_ref[1:2, :] = row_sum(both[:, 2 * half :])
     rows = ordered.shape[1] * ordered.shape[2]
+    copies[0].wait()
     for i, ref in enumerate((send, keep)):
         left = ordered[i].reshape(rows, ordered.shape[3])
         product = nn(left, both[...]).astype(jnp.bfloat16)
         ref[:, :, : 3 * half] = product.reshape(ordered.shape[1], ordered.shape[2], 3 * half)
     lines[...] = jnp.zeros_like(lines)
     if side == 0:
-        width = out_send.shape[2]
-        send[:, :, 3 * half : 3 * half + width] = out_send[...]
-        keep[:, :, 3 * half : 3 * half + width] = out_keep[...]
         lines[0:8, :] = sums_one[...]
         lines[8:16, :] = sums_two[...]
-        sums_to_slots(core, lines, parts, send, keep, 3 * half + width, wide_sums)
+        sums_to_slots(core, lines, parts, send, keep, 3 * half, wide_sums)
     else:
         lines[0:8, :half] = first_sums[...]
         lines[0:8, half:] = sums_ref[...]
         sums_to_slots(core, lines, parts, send, keep, 3 * half)
-    result[...] = (gradient[...] + nt(both[...], weight[side])).astype(result.dtype)
-
-
-def qkv_back(side, scalars, dq, dk, dv, far, ordered, weights, gradient, *more):
+    send_low[...] = send[:2]
+    send_high[...] = send[2:]
+    copies[1].wait()
+    result[...] = (gradient[...] + nt(both[...], weight[...])).astype(result.dtype)
+
+
+def qkv_back(side, scalars, dq, dk, dv, far_keys, far_values, ordered, weights, gradient, *more):
     count, half = dq.shape
     width = gradient.shape[1]
     f32, b16 = jnp.float32, jnp.bfloat16
-    total = array(b16, PARTS // 2, width // PARTS, 3 * half + LANES + (width if side == 0 else 0))
+    total = array(b16, PARTS // 2, width // PARTS, 3 * half + LANES)
+    part = array(b16, PARTS // 4, width // PARTS, 3 * half + LANES)
     return whole_call(
-        functools.partial(qkv_back_body, side), "qkv_back", scalars, [], [dq, dk, dv, far, Far(ordered), Far(weights), gradient, *more],
-        [total, total, array(b16 if side else f32, count, width), array(f32, 8, half)], [],
-        [pltpu.VMEM((count, 3 * half), b16), pltpu.VMEM((LANES, width), f32), pltpu.VMEM((PARTS, width // PARTS, LANES), f32)],
+        functools.partial(qkv_back_body, side), "qkv_back", scalars, [], [dq, dk, dv, far_keys, far_values, Far(ordered), Far(weights, None, side), gradient, *more],
+        [part, part, total, array(b16 if side else f32, count, width), array(f32, 8, half)], [],
+        [pltpu.VMEM((count, 3 * half), b16), pltpu.VMEM((LANES, width), f32), pltpu.VMEM((PARTS, width // PARTS, LANES), f32),
+         pltpu.VMEM(total.shape, b16)],
+        8, True,
     )
 
 
@@ -539,9 +553,12 @@
 
 
 def fold_body(plans, scalars, *refs):
-    for item, (outer, inner, bit) in enumerate(plans):
-        keep, got = refs[2 * item : 2 * item + 2]
-        send, left = refs[2 * (len(plans) + item) : 2 * (len(plans) + item) + 2]
+    places = [0]
+    for *_, count in plans:
+        places.append(places[-1] + 1 + count)
+    for item, (outer, inner, bit, count) in enumerate(plans):
+        keep, *gots = refs[places[item] : places[item + 1]]
+        send, left = refs[places[-1] + 2 * item : places[-1] + 2 * item + 2]
         mine = scalars[bit]
         rows = keep.shape[1]
         stripe = STRIPE if rows % STRIPE == 0 else rows
@@ -553,19 +570,20 @@
                 for j in range(inner):
                     for target, side in ((send, 1 - mine), (left, mine)):
                         place = (2 * i + side) * inner + j
-                        value = keep[place, span, :].astype(jnp.float32) + got[place, span, :].astype(jnp.float32)
+                        got = gots[0][place, span, :] if count == 1 else gots[i][side * inner + j, span, :]
+                        value = keep[place, span, :].astype(jnp.float32) + got.astype(jnp.float32)
                         target[i * inner + j, span, :] = value.astype(target.dtype)
 
 
 def fold(scalars, items):
-    outs, plans = [], []
+    outs, plans, given = [], [], []
     for keep, got, (outer, inner, bit) in items:
+        gots = got if isinstance(got, tuple) else (got,)
         shape = (keep.shape[0] // 2,) + keep.shape[1:]
         outs += [array(jnp.bfloat16, *shape), array(keep.dtype, *shape)]
-        plans.append((outer, inner, bit))
-    got = whole_call(
-        functools.partial(fold_body, plans), "fold", scalars, [], [x for keep, got, _ in items for x in (keep, got)], outs, [], []
-    )
+        plans.append((outer, inner, bit, len(gots)))
+        given += [keep, *gots]
+    got = whole_call(functools.partial(fold_body, plans), "fold", scalars, [], given, outs, [], [])
     return [(got[2 * i], got[2 * i + 1]) for i in range(len(items))]
 
 
@@ -616,7 +634,8 @@
     low = keep.shape[1]
     width = query_ref.shape[1]
     half = width // 2
-    second = 3 * half + width + LANES
+    second = 3 * half + LANES
+    third = 2 * second
 
     def total(first, size):
         return keep[0, :, first : first + size] + got[0, :, first : first + size].astype(jnp.float32)
@@ -624,9 +643,9 @@
     for i, ref in enumerate((query_ref, key_ref, value_ref)):
         ref[:, :half] = total(i * half, half)
         ref[:, half:] = total(second + i * half, half)
-    out_ref[...] = total(3 * half, width)
-    wide_ref[...] = total(3 * half + width, LANES)[0:1, :]
-    for ref, first in ((small_ref, 3 * half + width), (late_ref, second + 3 * half)):
+    out_ref[...] = total(third, width)
+    wide_ref[...] = total(3 * half, LANES)[0:1, :]
+    for ref, first in ((small_ref, 3 * half), (late_ref, second + 3 * half)):
         turned[...] = jnp.zeros_like(turned)
         turned[:low, :] = total(first, LANES)
         ref[...] = turned[...].T[: ref.shape[0], :]
@@ -901,15 +920,15 @@
     *hidden, part = pack(
         scalars, [query_weight, key_weight, value_weight], vectors + [up_bias], hidden_in, segment_ids
     )
-    near = near_shards(part, False)
+    near = near_shards(part)
     hidden = [lax.ppermute(piece, AXES, spread_pairs(first)) for first, piece in enumerate(hidden)]
-    shards = relayed_shards(near, 2 * width // PARTS)
     out_up, down_part = lax.optimization_barrier(
-        (jnp.concatenate([out_weight, up_weight], axis=1), down_weight, *near[1:3])
+        (jnp.concatenate([out_weight, up_weight], axis=1), down_weight, *near[1:4])
     )[:2]
+    hidden += [swap_dp(piece, 1) for piece in hidden]
     if direct:
-        hidden = list(lax.optimization_barrier((*hidden, near[1], near[2]))[:2])
-    hidden += [swap_dp(piece, 1) for piece in hidden]
+        near = list(lax.optimization_barrier((*near, *hidden))[:4])
+    shards = both_cores(near) if direct else near
     out_up_near = near_shards(out_up)
     attended, lse, tokens, vec, up_add, segments, ordered, query, keys, values, keys_other, values_other, w_qkv = project(
         scalars, shards, hidden, width // PARTS, inner_width // PARTS, len(vectors), qblock, chunk, pairs * LANES
@@ -940,59 +959,64 @@
         order.gate(scalars), inner_grad, wu, sum_two_grad, normal_one, scale_one, vec, wo, attended
     )
     order.mark(attended_grad)
+    out_got = swap(out_send)
 
     def attend(side):
         given = (query, keys, values, keys_other, values_other, attended, attended_grad, lse, segments)
         return order.mark(*attend_back(order.gate(scalars), *given, qblock, chunk, pairs, side))
 
-    dq, dk, dv, far = attend(0)
+    dq, dk, dv, *far = attend(0)
     if direct:
-        (send, down_keep), (other, up_keep) = fold(
-            order.gate(scalars), [(down_keep, down_got, (1, 1, 3)), (up_keep, up_got, (1, 1, 2))]
+        (send, down_keep), (other, up_keep), (third, out_keep) = fold(
+            order.gate(scalars),
+            [(down_keep, down_got, (1, 1, 3)), (up_keep, up_got, (1, 1, 2)), (out_keep, out_got, (1, 2, 3))],
         )
-        order.mark(send, other)
-        down_got, up_got = swap_dp(send, 4), swap_dp(other, 2)
+        order.mark(send, other, third)
+        down_got, up_got, out_got = swap_dp(send, 4), swap_dp(other, 2), swap_dp(third, 4)
     layer_out = order.mark(both_sequences(order, out_pieces))
-    one_send, one_keep, gradient, sums_first = qkv_back(
-        0, order.gate(scalars), dq, dk, dv, swap_dp(order.gate(far), 1), ordered, w_qkv, sum_one_grad, out_send, out_keep,
+    one_low, one_high, one_keep, gradient, sums_first = qkv_back(
+        0, order.gate(scalars), dq, dk, dv, *[swap_dp(x, 1) for x in order.gate(far)], ordered, w_qkv, sum_one_grad,
         sums_one, sums_two, up_sum
     )
     order.mark(gradient)
-    one_got = swap(one_send)
-    dq, dk, dv, far = attend(1)
+    one_got = (swap(one_low), swap(one_high))
+    dq, dk, dv, *far = attend(1)
     if direct:
         send, ff_keep = merge(order.gate(scalars), [(down_keep, down_got), (up_keep, up_got)], share)
         ff_got = swap_seq(order.mark(send), 1)
-        ((send, one_keep),) = fold(order.gate(scalars), [(one_keep, one_got, (1, 2, 3))])
-        one_got = swap_dp(order.mark(send), 4)
-    two_send, two_keep, gradient, _ = qkv_back(
-        1, order.gate(scalars), dq, dk, dv, swap_dp(order.gate(far), 1), ordered, w_qkv, gradient, sums_first
+        (send, one_keep), (other, out_keep) = fold(
+            order.gate(scalars), [(one_keep, one_got, (2, 1, 2)), (out_keep, out_got, (1, 1, 2))]
+        )
+        order.mark(send, other)
+        one_got, out_got = swap_dp(send, 2), swap_dp(other, 2)
+    two_low, two_high, two_keep, gradient, _ = qkv_back(
+        1, order.gate(scalars), dq, dk, dv, *[swap_dp(x, 1) for x in order.gate(far)], ordered, w_qkv, gradient, sums_first
     )
     order.mark(gradient)
-    two_got = swap(two_send)
+    two_got = (swap(two_low), swap(two_high))
     in_pieces = from_sequences(gradient, order)
     if not direct:
         down_grad, up_grad = scatter_all(down_send, down_keep), scatter_all(up_send, up_keep)
-        one, two = scatter_all(one_send, one_keep), scatter_all(two_send, two_keep)
+        one, two = scatter_all(jnp.concatenate([one_low, one_high]), one_keep), scatter_all(jnp.concatenate([two_low, two_high]), two_keep)
         cut = width // 2
         query_grad, key_grad, value_grad = [
             jnp.concatenate([side[:, i * cut : (i + 1) * cut] for side in (one, two)], axis=1) for i in range(3)
         ]
-        out_grad = one[:, 3 * cut : 3 * cut + width]
-        small, late = one[:, 3 * cut + width :].T, two[:, 3 * cut :].T
+        out_grad = scatter_all(out_send, out_keep)
+        small, late = one[:, 3 * cut :].T, two[:, 3 * cut :].T
         up_bias_grad = lax.psum_scatter(up_sum[0], AXES, scatter_dimension=0, tiled=True)
     else:
+        ((send, one_keep),) = fold(order.gate(scalars), [(one_keep, one_got, (1, 1, 3))])
+        one_got = swap_dp(order.mark(send), 4)
+        ((send, ff_keep),) = fold(order.gate(scalars), [(ff_keep, ff_got, (1, 1, 5))])
+        ff_got = swap_seq(order.mark(send), 2)
         ((send, two_keep),) = fold(order.gate(scalars), [(two_keep, two_got, (2, 1, 2))])
         two_got = swap_dp(order.mark(send), 2)
-        ((send, one_keep),) = fold(order.gate(scalars), [(one_keep, one_got, (1, 1, 2))])
-        one_got = swap_dp(order.mark(send), 2)
-        ((send, ff_keep),) = fold(order.gate(scalars), [(ff_keep, ff_got, (1, 1, 5))])
-        ff_got = swap_seq(order.mark(send), 2)
         ((send, two_keep),) = fold(order.gate(scalars), [(two_keep, two_got, (1, 1, 3))])
         two_got = swap_dp(order.mark(send), 4)
     input_grad = order.mark(both_sequences(order, in_pieces).astype(jnp.float32))
     if direct:
-        send, keep = merge(order.gate(scalars), [(one_keep, one_got), (two_keep, two_got)], share)
+        send, keep = merge(order.gate(scalars), [(one_keep, one_got), (two_keep, two_got), (out_keep, out_got)], share)
         got = swap_seq(order.mark(send), 1)
         ((send, keep),) = fold(order.gate(scalars), [(keep, got, (1, 1, 5))])
         got = swap_seq(order.mark(send), 2)

time: 249 us -> 243 us (0.976)
  waiting for transfers between devices: 62.7 us -> 75.6 us
  Pallas kernels: 111 us -> 99.4 us
  starting transfers between devices: 63.8 us -> 56 us
    ppermute x41 -> x46, waiting for transfers between devices: 44.4 us -> 57.4 us  [swap_dp(): lax.ppermute(value, 'dp', [(i, i ^ mask) for i in range(lax.axis_size('dp...]
    pallas_call x23, Pallas kernels: 111 us -> 99.4 us  [whole_call(): pl.pallas_call(body, in_specs=[pl.BlockSpec(memory_space=pltpu.SMEM)] + [...]
    ppermute x2, starting transfers between devices: 6.03 us -> 1.15 us  [to_sequences(): got.append(lax.ppermute(piece, AXES, spread_pairs(first)))]
    ppermute x4, starting transfers between devices: 5.34 us -> 1.91 us  [from_sequences(): lax.ppermute(piece, AXES, [(b, a) for a, b in spread_pairs(first)])]
    ppermute x4, waiting for transfers between devices: 2.58 us -> 0.01 us  [from_sequences(): lax.ppermute(piece, AXES, [(b, a) for a, b in spread_pairs(first)])]
    ppermute x41 -> x46, starting transfers between devices: 44 us -> 42.7 us  [swap_dp(): lax.ppermute(value, 'dp', [(i, i ^ mask) for i in range(lax.axis_size('dp...]
  transfers between devices with their start and end apart: 53 -> 58, of which waited for: 18 -> 25; matrix products, arithmetic and copies ran while one was open for 1% -> 1% of each run, Pallas kernels for 34% -> 34%
where the time goes in v3:
time: 243 us
  Pallas kernels  99.4 us (41%)
  waiting for transfers between devices  75.6 us (31%)
  starting transfers between devices  56 us (23%)
  local copies, waits for them, and re-layouts  6.47 us (3%)
  other arithmetic  3.78 us (2%)
    pallas_call x23, Pallas kernels, whole_call(): pl.pallas_call(body, in_specs=[pl.BlockSpec(memory_space=pltpu.SMEM)] + [...  99.4 us
    ppermute x46, waiting for transfers between devices, swap_dp(): lax.ppermute(value, 'dp', [(i, i ^ mask) for i in range(lax.axis_size('dp...  57.4 us
    ppermute x46, starting transfers between devices, swap_dp(): lax.ppermute(value, 'dp', [(i, i ^ mask) for i in range(lax.axis_size('dp...  42.7 us
    ppermute x4, waiting for transfers between devices, swap_seq(): lax.ppermute(value, 'seq', [(i, i ^ mask) for i in range(lax.axis_size('s...  18.2 us
    ppermute x4, starting transfers between devices, swap_seq(): lax.ppermute(value, 'seq', [(i, i ^ mask) for i in range(lax.axis_size('s...  6.45 us
  transfers between devices with their start and end apart: 58, of which 25 were waited for; matrix products, arithmetic and copies ran while one was open for 1% of the time, Pallas kernels for 34%

profile of v3, /device:TPU:0, one launch (start us, length us, event | category | flops | bytes accessed | tf_op | source)
XLA Modules:
  0.0 242.6 jit_solution(4687565152111076799)
XLA Ops:
  2.1 2.2 pack.1
  5.0 3.1 %collective-permute-start.4 = (bf16[272,768]{1,0:T(8,128)(2,1)S(1)}, bf16[272,768]{1,0:T(8,128)(2,1)S(1)}, u32[]{:S(2)}, u32[]{:S(2)}) collective-permute-start(bf16[272,768]{1,0:T(8,128)(2,1)S(1)} %get-tuple-element.162), channel_id=1, source_target_pairs={{0,1},{1,0},{2,5},{3,4},{4,3},{5,2},{6,7},{7,6},{8,9},{9,8},{10,13... | collective-permute-start | bytes 1253384 | tf_op jit(solution)/shard_map/ppermute | solution.py:924
  8.1 2.4 %collective-permute-start.2 = (bf16[304,768]{1,0:T(8,128)(2,1)S(1)}, bf16[304,768]{1,0:T(8,128)(2,1)S(1)}, u32[]{:S(2)}, u32[]{:S(2)}) collective-permute-start(bf16[304,768]{1,0:T(8,128)(2,1)S(1)} %get-tuple-element.163.refs_0_), channel_id=1, source_target_pairs={{0,24},{4,28},{8,16},{12,20},{16,8},{20,12},{24,0},{28,4},{1,25},{... | collective-permute-start | bytes 1400840 | tf_op jit(solution)/shard_map/ppermute | solution.py:672
  11.6 13.5 %collective-permute-start.5 = (bf16[272,768]{1,0:T(8,128)(2,1)S(1)}, bf16[272,768]{1,0:T(8,128)(2,1)S(1)}, u32[]{:S(2)}, u32[]{:S(2)}) collective-permute-start(bf16[272,768]{1,0:T(8,128)(2,1)S(1)} %collective-permute-done.3.refs_8_), channel_id=1, source_target_pairs={{0,4},{4,0},{8,12},{12,8},{16,20},{20,16},{24,28},{28,24},{1,5},{5... | collective-permute-start | bytes 1253384 | tf_op jit(solution)/shard_map/ppermute | solution.py:672
  25.2 7.3 %collective-permute-done.1.refs_4_ = bf16[304,768]{1,0:T(8,128)(2,1)S(1)} collective-permute-done((bf16[304,768]{1,0:T(8,128)(2,1)S(1)}, bf16[304,768]{1,0:T(8,128)(2,1)S(1)}, u32[]{:S(2)}, u32[]{:S(2)}) %collective-permute-start.1) | collective-permute-done | bytes 466976 | tf_op jit(solution)/shard_map/ppermute | solution.py:672
  34.1 1.6 collective-permute-start.13
  35.7 1.4 collective-permute-start.12
  41.0 20.6 %project.1 = (bf16[512,768]{1,0:T(8,128)(2,1)S(1)}, f32[2,8,512]{2,1,0:T(8,128)S(1)}, bf16[512,768]{1,0:T(8,128)(2,1)S(1)}, f32[16,768]{1,0:T(8,128)S(1)}, f32[1...) custom-call(s32[8]{0:T(128)S(1)} %stack.57.scalars, ...), custom_call_target="tpu_custom_call" | custom-call | flops 1 | bytes 1 | tf_op jit(solution)/shard_map/project/pallas_call | solution.py:422
  62.6 6.8 %collective-permute-done.12.refs_4_ = bf16[96,3840]{1,0:T(8,128)(2,1)} collective-permute-done((bf16[96,3840]{1,0:T(8,128)(2,1)S(1)}, bf16[96,3840]{1,0:T(8,128)(2,1)}, u32[]{:S(2)}, u32[]{:S(2)}) %collective-permute-start.12) | collective-permute-done | bytes 737312 | tf_op jit(solution)/shard_map/ppermute | solution.py:672
  70.1 1.4 collective-permute-start.15
  74.2 10.7 %widen.1 = (f32[512,768]{1,0:T(8,128)S(1)}, f32[512,128]{1,0:T(8,128)S(1)}, bf16[512,768]{1,0:T(8,128)(2,1)S(1)}, bf16[512,3072]{1,0:T(8,128)(2,1)S(1)}, bf16[51...) custom-call(s32[8]{0:T(128)S(1)} %stack.57.scalars, ...), custom_call_target="tpu_custom_call" | custom-call | flops 1 | bytes 1 | tf_op jit(solution)/shard_map/widen/pallas_call | solution.py:422
  89.8 2.2 collective-permute-start.22
  92.0 4.5 %collective-permute-done.25.refs_8_ = bf16[192,768]{1,0:T(8,128)(2,1)S(1)} collective-permute-done((bf16[192,768]{1,0:T(8,128)(2,1)S(1)}, bf16[192,768]{1,0:T(8,128)(2,1)S(1)}, u32[]{:S(2)}, u32[]{:S(2)}) %collective-permute-start.25) | collective-permute-done | bytes 294944 | tf_op jit(solution)/shard_map/ppermute | solution.py:672
  100.6 10.3 %narrow.1 = (bf16[512,768]{1,0:T(8,128)(2,1)S(1)}, f32[512,768]{1,0:T(8,128)S(1)}, bf16[512,768]{1,0:T(8,128)(2,1)S(1)}, f32[8,768]{1,0:T(8,128)S(1)}, bf16[4,38...) custom-call(s32[8]{0:T(128)S(1)} %stack.57.scalars, ...), custom_call_target="tpu_custom_call" | custom-call | flops 1 | bytes 1 | tf_op jit(solution)/shard_map/narrow/pallas_call | solution.py:422
  111.3 6.5 %inner_back.1 = (bf16[512,3072]{1,0:T(8,128)(2,1)S(1)}, f32[1,3072]{1,0:T(1,128)S(1)}, bf16[4,96,3072]{2,1,0:T(8,128)(2,1)S(1)}, bf16[4,96,3072]{2,1,0:T(8,128)(2,1)S(1)}) custom-call(s32[8]{0:T(128)S(1)} %stack.57.scalars, bf16[512,768]{1,0:T(8,128)(2,1)S(1)} %get-tuple-element.190.low, bf16[3072,768]{1,0:T(8,128)(2,1)S(1)} %get-tuple-element.191.wd, ...), custom_call_target="tpu_custom_call" | custom-call | flops 1 | bytes 1 | tf_op jit(solution)/shard_map/inner_back/pallas_call | solution.py:422
  119.4 3.0 %collective-permute-done.30.refs_1_ = bf16[4,96,3072]{2,1,0:T(8,128)(2,1)S(1)} collective-permute-done((bf16[4,96,3072]{2,1,0:T(8,128)(2,1)S(1)}, bf16[4,96,3072]{2,1,0:T(8,128)(2,1)S(1)}, u32[]{:S(2)}, u32[]{:S(2)}) %collective-permute-start.30) | collective-permute-done | bytes 2359328 | tf_op jit(solution)/shard_map/ppermute | solution.py:672
  125.5 6.8 %outer_back.1 = (f32[512,768]{1,0:T(8,128)S(1)}, bf16[512,768]{1,0:T(8,128)(2,1)S(1)}, f32[8,768]{1,0:T(8,128)S(1)}, bf16[4,96,768]{2,1,0:T(8,128)(2,1)S(1)}, bf16[4,96,768]{2,1,0:T(8,128)(2,1)S(1)}) custom-call(s32[8]{0:T(128)S(1)} %stack.57.scalars, bf16[512,3072]{1,0:T(8,128)(2,1)S(1)} %get-tuple-element.194.grad, ...), custom_call_target="tpu_custom_call" | custom-call | flops 1 | bytes 1 | tf_op jit(solution)/shard_map/outer_back/pallas_call | solution.py:422
  134.1 10.8 %attend_back.2 = (bf16[512,384]{1,0:T(8,128)(2,1)S(1)}, f32[512,384]{1,0:T(8,128)S(1)}, f32[512,384]{1,0:T(8,128)S(1)}, bf16[512,384]{1,0:T(8,128)(2,1)S(1)}, bf16[512,384]{1,0:T(8,128)(2,1)S(1)}) custom-call(s32[8]{0:T(128)S(1)} %stack.57.scalars, bf16[512,768]{1,0:T(8,128)(2,1)} %get-tuple-element.210.refs_0_, ...), custom_call_target="tpu_custom_call" | custom-call | flops 1 | bytes 1 | tf_op jit(solution)/shard_map/attend_back/pallas_call | solution.py:422
  144.9 6.9 %collective-permute-done.32.refs_3_ = bf16[2,96,3072]{2,1,0:T(8,128)(2,1)S(1)} collective-permute-done((bf16[2,96,3072]{2,1,0:T(8,128)(2,1)S(1)}, bf16[2,96,3072]{2,1,0:T(8,128)(2,1)S(1)}, u32[]{:S(2)}, u32[]{:S(2)}) %collective-permute-start.32) | collective-permute-done | bytes 1179680 | tf_op jit(solution)/shard_map/ppermute | solution.py:672
  157.0 4.3 %qkv_back.2 = (bf16[2,96,1280]{2,1,0:T(8,128)(2,1)S(1)}, bf16[2,96,1280]{2,1,0:T(8,128)(2,1)S(1)}, bf16[4,96,1280]{2,1,0:T(8,128)(2,1)S(1)}, f32[512,768]{1,0:T(8,128)S(1)}, f32[8,384]{1,0:T(8,128)S(1)}) custom-call(s32[8]{0:T(128)S(1)} %stack.57.scalars, bf16[512,384]{1,0:T(8,128)(2,1)S(1)} %get-tuple-element.217.refs_0_, ...), custom_call_target="tpu_custom_call" | custom-call | flops 1 | bytes 1 | tf_op jit(solution)/shard_map/qkv_back/pallas_call | solution.py:422
  163.3 10.8 %attend_back.3 = (bf16[512,384]{1,0:T(8,128)(2,1)S(1)}, f32[512,384]{1,0:T(8,128)S(1)}, f32[512,384]{1,0:T(8,128)S(1)}, bf16[512,384]{1,0:T(8,128)(2,1)S(1)}, bf16[512,384]{1,0:T(8,128)(2,1)S(1)}) custom-call(s32[8]{0:T(128)S(1)} %stack.57.scalars, bf16[512,768]{1,0:T(8,128)(2,1)} %get-tuple-element.210.refs_0_, ...), custom_call_target="tpu_custom_call" | custom-call | flops 1 | bytes 1 | tf_op jit(solution)/shard_map/attend_back/pallas_call | solution.py:422
  174.9 1.7 collective-permute-done.42.refs_4_
  179.9 4.3 %qkv_back.3 = (bf16[2,96,1280]{2,1,0:T(8,128)(2,1)S(1)}, bf16[2,96,1280]{2,1,0:T(8,128)(2,1)S(1)}, bf16[4,96,1280]{2,1,0:T(8,128)(2,1)S(1)}, bf16[512,768]{1,0:T(8,128)(2,1)S(1)}, f32[8,384]{1,0:T(8,128)}) custom-call(s32[8]{0:T(128)S(1)} %stack.57.scalars, bf16[512,384]{1,0:T(8,128)(2,1)S(1)} %get-tuple-element.242.refs_0_, ...), custom_call_target="tpu_custom_call" | custom-call | flops 1 | bytes 1 | tf_op jit(solution)/shard_map/qkv_back/pallas_call | solution.py:422
  184.9 6.8 %collective-permute-done.45.refs_1_ = bf16[2,96,1280]{2,1,0:T(8,128)(2,1)S(1)} collective-permute-done((bf16[2,96,1280]{2,1,0:T(8,128)(2,1)S(1)}, bf16[2,96,1280]{2,1,0:T(8,128)(2,1)S(1)}, u32[]{:S(2)}, u32[]{:S(2)}) %collective-permute-start.45) | collective-permute-done | bytes 491552 | tf_op jit(solution)/shard_map/ppermute | solution.py:672
  198.5 8.8 %collective-permute-done.49.refs_1_ = bf16[2,96,1280]{2,1,0:T(8,128)(2,1)S(1)} collective-permute-done((bf16[2,96,1280]{2,1,0:T(8,128)(2,1)S(1)}, bf16[2,96,1280]{2,1,0:T(8,128)(2,1)S(1)}, u32[]{:S(2)}, u32[]{:S(2)}) %collective-permute-start.49) | collective-permute-done | bytes 491552 | tf_op jit(solution)/shard_map/ppermute | solution.py:672
  211.3 3.2 %collective-permute-done.54 = bf16[1,96,768]{2,1,0:T(8,128)(2,1)S(1)} collective-permute-done((bf16[1,96,768]{2,1,0:T(8,128)(2,1)S(1)}, bf16[1,96,768]{2,1,0:T(8,128)(2,1)S(1)}, u32[]{:S(2)}, u32[]{:S(2)}) %collective-permute-start.54) | collective-permute-done | bytes 147488 | tf_op jit(solution)/shard_map/ppermute | solution.py:672
  215.9 3.5 %collective-permute-start.56 = (bf16[1,24,6144]{2,1,0:T(8,128)(2,1)S(1)}, bf16[1,24,6144]{2,1,0:T(8,128)(2,1)S(1)}, u32[]{:S(2)}, u32[]{:S(2)}) collective-permute-start(bf16[1,24,6144]{2,1,0:T(8,128)(2,1)S(1)} %get-tuple-element.270), channel_id=1, source_target_pairs={{0,2},{1,3},{2,0},{3,1},{4,6},{5,7},{6,4},{7,5},{8,10},{9,11},{10,... | collective-permute-start | bytes 884744 | tf_op jit(solution)/shard_map/ppermute | solution.py:676
  219.4 8.7 %collective-permute-done.55.refs_1_ = bf16[2,24,3328]{2,1,0:T(8,128)(2,1)S(1)} collective-permute-done((bf16[2,24,3328]{2,1,0:T(8,128)(2,1)S(1)}, bf16[2,24,3328]{2,1,0:T(8,128)(2,1)S(1)}, u32[]{:S(2)}, u32[]{:S(2)}) %collective-permute-start.55) | collective-permute-done | bytes 319520 | tf_op jit(solution)/shard_map/ppermute | solution.py:676
  228.7 1.6 collective-permute-start.57
  230.3 6.7 %collective-permute-done.56.got = bf16[1,24,6144]{2,1,0:T(8,128)(2,1)S(1)} collective-permute-done((bf16[1,24,6144]{2,1,0:T(8,128)(2,1)S(1)}, bf16[1,24,6144]{2,1,0:T(8,128)(2,1)S(1)}, u32[]{:S(2)}, u32[]{:S(2)}) %collective-permute-start.56) | collective-permute-done | bytes 294944 | tf_op jit(solution)/shard_map/ppermute | solution.py:676
  237.1 1.4 last_ff.1
  238.5 1.7 collective-permute-done.57.got
  (178 shorter events, 55.5 us)
Async XLA Ops:
  5.0 20.1 %collective-permute-start.4 = (bf16[272,768]{1,0:T(8,128)(2,1)S(1)}, bf16[272,768]{1,0:T(8,128)(2,1)S(1)}, u32[]{:S(2)}, u32[]{:S(2)}) collective-permute-start(bf16[272,768]{1,0:T(8,128)(2,1)S(1)} %get-tuple-element.162), channel_id=1, source_target_pairs={{0,1},{1,0},{2,5},{3,4},{4,3},{5,2},{6,7},{7,6},{8,9},{9,8},{10,13... | collective-permute-start | bytes 1253384 | tf_op jit(solution)/shard_map/ppermute | solution.py:924
  8.1 17.1 %collective-permute-start.2 = (bf16[304,768]{1,0:T(8,128)(2,1)S(1)}, bf16[304,768]{1,0:T(8,128)(2,1)S(1)}, u32[]{:S(2)}, u32[]{:S(2)}) collective-permute-start(bf16[304,768]{1,0:T(8,128)(2,1)S(1)} %get-tuple-element.163.refs_0_), channel_id=1, source_target_pairs={{0,24},{4,28},{8,16},{12,20},{16,8},{20,12},{24,0},{28,4},{1,25},{... | collective-permute-start | bytes 1400840 | tf_op jit(solution)/shard_map/ppermute | solution.py:672
  10.5 21.9 %collective-permute-start.1 = (bf16[304,768]{1,0:T(8,128)(2,1)S(1)}, bf16[304,768]{1,0:T(8,128)(2,1)S(1)}, u32[]{:S(2)}, u32[]{:S(2)}) collective-permute-start(bf16[304,768]{1,0:T(8,128)(2,1)S(1)} %get-tuple-element.163.refs_0_), channel_id=1, source_target_pairs={{0,16},{4,20},{8,24},{12,28},{16,0},{20,4},{24,8},{28,12},{1,17},{... | collective-permute-start | bytes 1400840 | tf_op jit(solution)/shard_map/ppermute | solution.py:672
  11.0 21.4 %collective-permute-start = (bf16[304,768]{1,0:T(8,128)(2,1)S(1)}, bf16[304,768]{1,0:T(8,128)(2,1)S(1)}, u32[]{:S(2)}, u32[]{:S(2)}) collective-permute-start(bf16[304,768]{1,0:T(8,128)(2,1)S(1)} %get-tuple-element.163.refs_0_), channel_id=1, source_target_pairs={{0,8},{4,12},{8,0},{12,4},{16,24},{20,28},{24,16},{28,20},{1,9},{5... | collective-permute-start | bytes 1400840 | tf_op jit(solution)/shard_map/ppermute | solution.py:672
  11.6 20.9 %collective-permute-start.5 = (bf16[272,768]{1,0:T(8,128)(2,1)S(1)}, bf16[272,768]{1,0:T(8,128)(2,1)S(1)}, u32[]{:S(2)}, u32[]{:S(2)}) collective-permute-start(bf16[272,768]{1,0:T(8,128)(2,1)S(1)} %collective-permute-done.3.refs_8_), channel_id=1, source_target_pairs={{0,4},{4,0},{8,12},{12,8},{16,20},{20,16},{24,28},{28,24},{1,5},{5... | collective-permute-start | bytes 1253384 | tf_op jit(solution)/shard_map/ppermute | solution.py:672
  34.1 28.5 %collective-permute-start.13 = (bf16[96,3840]{1,0:T(8,128)(2,1)S(1)}, bf16[96,3840]{1,0:T(8,128)(2,1)}, u32[]{:S(2)}, u32[]{:S(2)}) collective-permute-start(bf16[96,3840]{1,0:T(8,128)(2,1)S(1)} %pad_maximum_fusion.refs_0_), channel_id=1, source_target_pairs={{0,24},{4,28},{8,16},{12,20},{16,8},{20,12},{24,0},{28,4},{1,25},{... | collective-permute-start | bytes 2211848 | tf_op jit(solution)/shard_map/ppermute | solution.py:672
  35.7 33.8 %collective-permute-start.12 = (bf16[96,3840]{1,0:T(8,128)(2,1)S(1)}, bf16[96,3840]{1,0:T(8,128)(2,1)}, u32[]{:S(2)}, u32[]{:S(2)}) collective-permute-start(bf16[96,3840]{1,0:T(8,128)(2,1)S(1)} %pad_maximum_fusion.refs_0_), channel_id=1, source_target_pairs={{0,16},{4,20},{8,24},{12,28},{16,0},{20,4},{24,8},{28,12},{1,17},{... | collective-permute-start | bytes 2211848 | tf_op jit(solution)/shard_map/ppermute | solution.py:672
  37.1 32.5 %collective-permute-start.11 = (bf16[96,3840]{1,0:T(8,128)(2,1)S(1)}, bf16[96,3840]{1,0:T(8,128)(2,1)}, u32[]{:S(2)}, u32[]{:S(2)}) collective-permute-start(bf16[96,3840]{1,0:T(8,128)(2,1)S(1)} %pad_maximum_fusion.refs_0_), channel_id=1, source_target_pairs={{0,8},{4,12},{8,0},{12,4},{16,24},{20,28},{24,16},{28,20},{1,9},{5... | collective-permute-start | bytes 2211848 | tf_op jit(solution)/shard_map/ppermute | solution.py:672
  39.5 32.0 %collective-permute-start.16 = (bf16[96,3840]{1,0:T(8,128)(2,1)S(1)}, bf16[96,3840]{1,0:T(8,128)(2,1)}, u32[]{:S(2)}, u32[]{:S(2)}) collective-permute-start(bf16[96,3840]{1,0:T(8,128)(2,1)S(1)} %pad_maximum_fusion.refs_0_), channel_id=1, source_target_pairs={{0,4},{4,0},{8,12},{12,8},{16,20},{20,16},{24,28},{28,24},{1,5},{5... | collective-permute-start | bytes 2211848 | tf_op jit(solution)/shard_map/ppermute | solution.py:672
  70.1 16.0 %collective-permute-start.15 = (bf16[384,768]{1,0:T(8,128)(2,1)}, bf16[384,768]{1,0:T(8,128)(2,1)S(1)}, u32[]{:S(2)}, u32[]{:S(2)}) collective-permute-start(bf16[384,768]{1,0:T(8,128)(2,1)} %refs_0_.2), channel_id=1, source_target_pairs={{0,16},{4,20},{8,24},{12,28},{16,0},{20,4},{24,8},{28,12},{1,17},{... | collective-permute-start | bytes 1769480 | tf_op jit(solution)/shard_map/ppermute | solution.py:672
  71.5 15.7 %collective-permute-start.14 = (bf16[384,768]{1,0:T(8,128)(2,1)}, bf16[384,768]{1,0:T(8,128)(2,1)S(1)}, u32[]{:S(2)}, u32[]{:S(2)}) collective-permute-start(bf16[384,768]{1,0:T(8,128)(2,1)} %refs_0_.2), channel_id=1, source_target_pairs={{0,8},{4,12},{8,0},{12,4},{16,24},{20,28},{24,16},{28,20},{1,9},{5... | collective-permute-start | bytes 1769480 | tf_op jit(solution)/shard_map/ppermute | solution.py:672
  72.4 16.9 %collective-permute-start.28 = (bf16[256,768]{1,0:T(8,128)(2,1)S(1)}, bf16[256,768]{1,0:T(8,128)(2,1)S(1)}, u32[]{:S(2)}, u32[]{:S(2)}) collective-permute-start(bf16[256,768]{1,0:T(8,128)(2,1)S(1)} %get-tuple-element.301), channel_id=1, source_target_pairs={{0,1},{1,0},{2,5},{3,4},{4,3},{5,2},{6,7},{7,6},{8,9},{9,8},{10,13... | collective-permute-start | bytes 1179656 | tf_op jit(solution)/shard_map/ppermute | solution.py:701
  73.2 16.6 %collective-permute-start.27 = (bf16[256,768]{1,0:T(8,128)(2,1)S(1)}, bf16[256,768]{1,0:T(8,128)(2,1)S(1)}, u32[]{:S(2)}, u32[]{:S(2)}) collective-permute-start(bf16[256,768]{1,0:T(8,128)(2,1)S(1)} %get-tuple-element.302), channel_id=1, source_target_pairs={{0,0},{1,1},{2,4},{3,5},{4,2},{5,3},{6,6},{7,7},{8,8},{9,9},{10,12... | collective-permute-start | bytes 1179656 | tf_op jit(solution)/shard_map/ppermute | solution.py:701
  123.4 28.3 %collective-permute-start.32 = (bf16[2,96,3072]{2,1,0:T(8,128)(2,1)S(1)}, bf16[2,96,3072]{2,1,0:T(8,128)(2,1)S(1)}, u32[]{:S(2)}, u32[]{:S(2)}) collective-permute-start(bf16[2,96,3072]{2,1,0:T(8,128)(2,1)S(1)} %get-tuple-element.202), channel_id=1, source_target_pairs={{0,16},{4,20},{8,24},{12,28},{16,0},{20,4},{24,8},{28,12},{1,17},{... | collective-permute-start | bytes 3538952 | tf_op jit(solution)/shard_map/ppermute | solution.py:672
  124.2 28.0 %collective-permute-start.31 = (bf16[2,384,768]{2,1,0:T(8,128)(2,1)S(1)}, bf16[2,384,768]{2,1,0:T(8,128)(2,1)S(1)}, u32[]{:S(2)}, u32[]{:S(2)}) collective-permute-start(bf16[2,384,768]{2,1,0:T(8,128)(2,1)S(1)} %get-tuple-element.198), channel_id=1, source_target_pairs={{0,8},{4,12},{8,0},{12,4},{16,24},{20,28},{24,16},{28,20},{1,9},{5... | collective-permute-start | bytes 3538952 | tf_op jit(solution)/shard_map/ppermute | solution.py:672
  133.2 11.7 %collective-permute-start.33 = (bf16[4,96,768]{2,1,0:T(8,128)(2,1)S(1)}, bf16[4,96,768]{2,1,0:T(8,128)(2,1)S(1)}, u32[]{:S(2)}, u32[]{:S(2)}) collective-permute-start(bf16[4,96,768]{2,1,0:T(8,128)(2,1)S(1)} %get-tuple-element.226), channel_id=1, source_target_pairs={{0,4},{4,0},{8,12},{12,8},{16,20},{20,16},{24,28},{28,24},{1,5},{5... | collective-permute-start | bytes 1769480 | tf_op jit(solution)/shard_map/ppermute | solution.py:672
  133.2 20.4 %collective-permute-start.34 = (bf16[256,768]{1,0:T(8,128)(2,1)S(1)}, bf16[256,768]{1,0:T(8,128)(2,1)S(1)}, u32[]{:S(2)}, u32[]{:S(2)}) collective-permute-start(bf16[256,768]{1,0:T(8,128)(2,1)S(1)} %broadcast_select_fusion.2), channel_id=1, source_target_pairs={{1,0},{0,1},{5,2},{4,3},{3,4},{2,5},{7,6},{6,7},{9,8},{8,9},{13,10... | collective-permute-start | bytes 1179656 | tf_op jit(solution)/shard_map/ppermute | solution.py:716
  133.4 20.2 %collective-permute-start.35 = (bf16[256,768]{1,0:T(8,128)(2,1)S(1)}, bf16[256,768]{1,0:T(8,128)(2,1)S(1)}, u32[]{:S(2)}, u32[]{:S(2)}) collective-permute-start(bf16[256,768]{1,0:T(8,128)(2,1)S(1)} %broadcast_select_fusion.3), channel_id=1, source_target_pairs={{0,0},{1,1},{4,2},{5,3},{2,4},{3,5},{6,6},{7,7},{8,8},{9,9},{12,10... | collective-permute-start | bytes 1179656 | tf_op jit(solution)/shard_map/ppermute | solution.py:716
  155.1 19.0 %collective-permute-start.38 = (bf16[1,384,768]{2,1,0:T(8,128)(2,1)S(1)}, bf16[1,384,768]{2,1,0:T(8,128)(2,1)S(1)}, u32[]{:S(2)}, u32[]{:S(2)}) collective-permute-start(bf16[1,384,768]{2,1,0:T(8,128)(2,1)S(1)} %get-tuple-element.227), channel_id=1, source_target_pairs={{0,16},{4,20},{8,24},{12,28},{16,0},{20,4},{24,8},{28,12},{1,17},{... | collective-permute-start | bytes 1769480 | tf_op jit(solution)/shard_map/ppermute | solution.py:672
  156.4 17.7 %collective-permute-start.39 = (bf16[1,96,3072]{2,1,0:T(8,128)(2,1)S(1)}, bf16[1,96,3072]{2,1,0:T(8,128)(2,1)S(1)}, u32[]{:S(2)}, u32[]{:S(2)}) collective-permute-start(bf16[1,96,3072]{2,1,0:T(8,128)(2,1)S(1)} %get-tuple-element.228), channel_id=1, source_target_pairs={{0,8},{4,12},{8,0},{12,4},{16,24},{20,28},{24,16},{28,20},{1,9},{5... | collective-permute-start | bytes 1769480 | tf_op jit(solution)/shard_map/ppermute | solution.py:672
  161.3 15.3 %collective-permute-start.40 = (bf16[2,96,1280]{2,1,0:T(8,128)(2,1)S(1)}, bf16[2,96,1280]{2,1,0:T(8,128)(2,1)S(1)}, u32[]{:S(2)}, u32[]{:S(2)}) collective-permute-start(bf16[2,96,1280]{2,1,0:T(8,128)(2,1)S(1)} %get-tuple-element.253), channel_id=1, source_target_pairs={{0,4},{4,0},{8,12},{12,8},{16,20},{20,16},{24,28},{28,24},{1,5},{5... | collective-permute-start | bytes 1474568 | tf_op jit(solution)/shard_map/ppermute | solution.py:672
  161.4 15.2 %collective-permute-start.41 = (bf16[2,96,1280]{2,1,0:T(8,128)(2,1)S(1)}, bf16[2,96,1280]{2,1,0:T(8,128)(2,1)S(1)}, u32[]{:S(2)}, u32[]{:S(2)}) collective-permute-start(bf16[2,96,1280]{2,1,0:T(8,128)(2,1)S(1)} %get-tuple-element.254), channel_id=1, source_target_pairs={{0,4},{4,0},{8,12},{12,8},{16,20},{20,16},{24,28},{28,24},{1,5},{5... | collective-permute-start | bytes 1474568 | tf_op jit(solution)/shard_map/ppermute | solution.py:672
  161.9 14.7 %collective-permute-start.42 = (bf16[2,96,768]{2,1,0:T(8,128)(2,1)S(1)}, bf16[2,96,768]{2,1,0:T(8,128)(2,1)S(1)}, u32[]{:S(2)}, u32[]{:S(2)}) collective-permute-start(bf16[2,96,768]{2,1,0:T(8,128)(2,1)S(1)} %get-tuple-element.229), channel_id=1, source_target_pairs={{0,16},{4,20},{8,24},{12,28},{16,0},{20,4},{24,8},{28,12},{1,17},{... | collective-permute-start | bytes 884744 | tf_op jit(solution)/shard_map/ppermute | solution.py:672
  178.1 15.3 %collective-permute-start.46 = (bf16[2,24,6144]{2,1,0:T(8,128)(2,1)S(1)}, bf16[2,24,6144]{2,1,0:T(8,128)(2,1)S(1)}, u32[]{:S(2)}, u32[]{:S(2)}) collective-permute-start(bf16[2,24,6144]{2,1,0:T(8,128)(2,1)S(1)} %get-tuple-element.250), channel_id=1, source_target_pairs={{0,1},{1,0},{2,3},{3,2},{4,5},{5,4},{6,7},{7,6},{8,9},{9,8},{10,11... | collective-permute-start | bytes 1769480 | tf_op jit(solution)/shard_map/ppermute | solution.py:676
  178.8 12.9 %collective-permute-start.45 = (bf16[2,96,1280]{2,1,0:T(8,128)(2,1)S(1)}, bf16[2,96,1280]{2,1,0:T(8,128)(2,1)S(1)}, u32[]{:S(2)}, u32[]{:S(2)}) collective-permute-start(bf16[2,96,1280]{2,1,0:T(8,128)(2,1)S(1)} %get-tuple-element.256), channel_id=1, source_target_pairs={{0,8},{4,12},{8,0},{12,4},{16,24},{20,28},{24,16},{28,20},{1,9},{5... | collective-permute-start | bytes 1474568 | tf_op jit(solution)/shard_map/ppermute | solution.py:672
  194.9 12.4 %collective-permute-start.49 = (bf16[2,96,1280]{2,1,0:T(8,128)(2,1)S(1)}, bf16[2,96,1280]{2,1,0:T(8,128)(2,1)S(1)}, u32[]{:S(2)}, u32[]{:S(2)}) collective-permute-start(bf16[2,96,1280]{2,1,0:T(8,128)(2,1)S(1)} %get-tuple-element.275), channel_id=1, source_target_pairs={{0,8},{4,12},{8,0},{12,4},{16,24},{20,28},{24,16},{28,20},{1,9},{5... | collective-permute-start | bytes 1474568 | tf_op jit(solution)/shard_map/ppermute | solution.py:672
  196.2 13.8 %collective-permute-start.50 = (bf16[256,768]{1,0:T(8,128)(2,1)S(1)}, bf16[256,768]{1,0:T(8,128)(2,1)S(1)}, u32[]{:S(2)}, u32[]{:S(2)}) collective-permute-start(bf16[256,768]{1,0:T(8,128)(2,1)S(1)} %broadcast_select_fusion), channel_id=1, source_target_pairs={{1,0},{0,1},{5,2},{4,3},{3,4},{2,5},{7,6},{6,7},{9,8},{8,9},{13,10... | collective-permute-start | bytes 1179656 | tf_op jit(solution)/shard_map/ppermute | solution.py:716
  196.5 13.4 %collective-permute-start.51 = (bf16[256,768]{1,0:T(8,128)(2,1)S(1)}, bf16[256,768]{1,0:T(8,128)(2,1)S(1)}, u32[]{:S(2)}, u32[]{:S(2)}) collective-permute-start(bf16[256,768]{1,0:T(8,128)(2,1)S(1)} %broadcast_select_fusion.1), channel_id=1, source_target_pairs={{0,0},{1,1},{4,2},{5,3},{2,4},{3,5},{6,6},{7,7},{8,8},{9,9},{12,10... | collective-permute-start | bytes 1179656 | tf_op jit(solution)/shard_map/ppermute | solution.py:716
  197.2 17.3 %collective-permute-start.52 = (bf16[1,96,1280]{2,1,0:T(8,128)(2,1)S(1)}, bf16[1,96,1280]{2,1,0:T(8,128)(2,1)S(1)}, u32[]{:S(2)}, u32[]{:S(2)}) collective-permute-start(bf16[1,96,1280]{2,1,0:T(8,128)(2,1)S(1)} %get-tuple-element.267), channel_id=1, source_target_pairs={{0,16},{4,20},{8,24},{12,28},{16,0},{20,4},{24,8},{28,12},{1,17},{... | collective-permute-start | bytes 737288 | tf_op jit(solution)/shard_map/ppermute | solution.py:672
  215.2 12.9 %collective-permute-start.55 = (bf16[2,24,3328]{2,1,0:T(8,128)(2,1)S(1)}, bf16[2,24,3328]{2,1,0:T(8,128)(2,1)S(1)}, u32[]{:S(2)}, u32[]{:S(2)}) collective-permute-start(bf16[2,24,3328]{2,1,0:T(8,128)(2,1)S(1)} %get-tuple-element.284), channel_id=1, source_target_pairs={{0,1},{1,0},{2,3},{3,2},{4,5},{5,4},{6,7},{7,6},{8,9},{9,8},{10,11... | collective-permute-start | bytes 958472 | tf_op jit(solution)/shard_map/ppermute | solution.py:676
  215.9 21.2 %collective-permute-start.56 = (bf16[1,24,6144]{2,1,0:T(8,128)(2,1)S(1)}, bf16[1,24,6144]{2,1,0:T(8,128)(2,1)S(1)}, u32[]{:S(2)}, u32[]{:S(2)}) collective-permute-start(bf16[1,24,6144]{2,1,0:T(8,128)(2,1)S(1)} %get-tuple-element.270), channel_id=1, source_target_pairs={{0,2},{1,3},{2,0},{3,1},{4,6},{5,7},{6,4},{7,5},{8,10},{9,11},{10,... | collective-permute-start | bytes 884744 | tf_op jit(solution)/shard_map/ppermute | solution.py:676
  228.7 11.5 %collective-permute-start.57 = (bf16[1,24,3328]{2,1,0:T(8,128)(2,1)S(1)}, bf16[1,24,3328]{2,1,0:T(8,128)(2,1)S(1)}, u32[]{:S(2)}, u32[]{:S(2)}) collective-permute-start(bf16[1,24,3328]{2,1,0:T(8,128)(2,1)S(1)} %get-tuple-element.287), channel_id=1, source_target_pairs={{0,2},{1,3},{2,0},{3,1},{4,6},{5,7},{6,4},{7,5},{8,10},{9,11},{10,... | collective-permute-start | bytes 479240 | tf_op jit(solution)/shard_map/ppermute | solution.py:676
  (54 other events, 488.5 us)

commit v4 on v3

--- a/solution.py
+++ b/solution.py
@@ -553,12 +553,13 @@
 
 
 def fold_body(plans, scalars, *refs):
-    places = [0]
-    for *_, count in plans:
+    places, outs = [0], [0]
+    for *_, count, sends in plans:
         places.append(places[-1] + 1 + count)
-    for item, (outer, inner, bit, count) in enumerate(plans):
+        outs.append(outs[-1] + 1 + sends)
+    for item, (outer, inner, bit, count, sends) in enumerate(plans):
         keep, *gots = refs[places[item] : places[item + 1]]
-        send, left = refs[places[-1] + 2 * item : places[-1] + 2 * item + 2]
+        *sent, left = refs[places[-1] + outs[item] : places[-1] + outs[item + 1]]
         mine = scalars[bit]
         rows = keep.shape[1]
         stripe = STRIPE if rows % STRIPE == 0 else rows
@@ -568,23 +569,37 @@
             span = step_of(k, stripe) if stripe != rows else slice(None)
             for i in range(outer):
                 for j in range(inner):
-                    for target, side in ((send, 1 - mine), (left, mine)):
+                    for away, side in ((True, 1 - mine), (False, mine)):
                         place = (2 * i + side) * inner + j
-                        got = gots[0][place, span, :] if count == 1 else gots[i][side * inner + j, span, :]
+                        if count == 1:
+                            got = gots[0][place, span, :]
+                        elif outer == 1:
+                            got = jnp.where(side == 0, gots[0][j, span, :], gots[1][j, span, :])
+                        else:
+                            got = gots[i][side * inner + j, span, :]
                         value = keep[place, span, :].astype(jnp.float32) + got.astype(jnp.float32)
-                        target[i * inner + j, span, :] = value.astype(target.dtype)
+                        if away and sends == 2:
+                            sent[i][j, span, :] = value.astype(sent[i].dtype)
+                        else:
+                            target = sent[0] if away else left
+                            target[i * inner + j, span, :] = value.astype(target.dtype)
 
 
 def fold(scalars, items):
     outs, plans, given = [], [], []
-    for keep, got, (outer, inner, bit) in items:
+    for keep, got, (outer, inner, bit, *more) in items:
         gots = got if isinstance(got, tuple) else (got,)
+        sends = 2 if more else 1
         shape = (keep.shape[0] // 2,) + keep.shape[1:]
-        outs += [array(jnp.bfloat16, *shape), array(keep.dtype, *shape)]
-        plans.append((outer, inner, bit, len(gots)))
+        outs += [array(jnp.bfloat16, shape[0] // sends, *shape[1:])] * sends + [array(keep.dtype, *shape)]
+        plans.append((outer, inner, bit, len(gots), sends))
         given += [keep, *gots]
-    got = whole_call(functools.partial(fold_body, plans), "fold", scalars, [], given, outs, [], [])
-    return [(got[2 * i], got[2 * i + 1]) for i in range(len(items))]
+    got = list(whole_call(functools.partial(fold_body, plans), "fold", scalars, [], given, outs, [], []))
+    result = []
+    for *_, sends in plans:
+        sent = tuple(got.pop(0) for _ in range(sends))
+        result.append((sent if sends == 2 else sent[0], got.pop(0)))
+    return result
 
 
 def merge_body(shapes, scalars, *refs):
@@ -630,32 +645,31 @@
     )
 
 
-def last_qkv_body(scalars, keep, got, query_ref, key_ref, value_ref, out_ref, small_ref, late_ref, wide_ref, turned):
+def last_qkv_body(scalars, keep, got, more_keep, more_got, query_ref, key_ref, value_ref, out_ref, small_ref, late_ref, wide_ref, turned):
     low = keep.shape[1]
     width = query_ref.shape[1]
     half = width // 2
-    second = 3 * half + LANES
-    third = 2 * second
-
-    def total(first, size):
-        return keep[0, :, first : first + size] + got[0, :, first : first + size].astype(jnp.float32)
-
+
+    def total(pair, first, size):
+        return pair[0][0, :, first : first + size] + pair[1][0, :, first : first + size].astype(jnp.float32)
+
+    one, two = (keep, got), (more_keep, more_got)
     for i, ref in enumerate((query_ref, key_ref, value_ref)):
-        ref[:, :half] = total(i * half, half)
-        ref[:, half:] = total(second + i * half, half)
-    out_ref[...] = total(third, width)
-    wide_ref[...] = total(3 * half, LANES)[0:1, :]
-    for ref, first in ((small_ref, 3 * half), (late_ref, second + 3 * half)):
+        ref[:, :half] = total(one, i * half, half)
+        ref[:, half:] = total(two, i * half, half)
+    out_ref[...] = total(one, 3 * half + LANES, width)
+    wide_ref[...] = total(one, 3 * half, LANES)[0:1, :]
+    for ref, pair in ((small_ref, one), (late_ref, two)):
         turned[...] = jnp.zeros_like(turned)
-        turned[:low, :] = total(first, LANES)
+        turned[:low, :] = total(pair, 3 * half, LANES)
         ref[...] = turned[...].T[: ref.shape[0], :]
 
 
-def last_qkv(scalars, keep, got, width):
+def last_qkv(scalars, keep, got, more_keep, more_got, width):
     low = keep.shape[1]
     f32 = jnp.float32
     return whole_call(
-        last_qkv_body, "last_qkv", scalars, [], [keep, got],
+        last_qkv_body, "last_qkv", scalars, [], [keep, got, more_keep, more_got],
         [array(f32, low, width)] * 4 + [array(f32, 24, LANES), array(f32, 8, LANES), array(f32, 1, LANES)], [], [pltpu.VMEM((LANES, LANES), f32)],
     )
 
@@ -1010,19 +1024,24 @@
         one_got = swap_dp(order.mark(send), 4)
         ((send, ff_keep),) = fold(order.gate(scalars), [(ff_keep, ff_got, (1, 1, 5))])
         ff_got = swap_seq(order.mark(send), 2)
-        ((send, two_keep),) = fold(order.gate(scalars), [(two_keep, two_got, (2, 1, 2))])
-        two_got = swap_dp(order.mark(send), 2)
+        ((sent, two_keep),) = fold(order.gate(scalars), [(two_keep, two_got, (2, 1, 2, True))])
+        two_got = tuple(swap_dp(x, 2) for x in order.mark(*sent))
+        send, keep = merge(order.gate(scalars), [(one_keep, one_got), (out_keep, out_got)], share)
+        got = swap_seq(order.mark(send), 1)
         ((send, two_keep),) = fold(order.gate(scalars), [(two_keep, two_got, (1, 1, 3))])
         two_got = swap_dp(order.mark(send), 4)
     input_grad = order.mark(both_sequences(order, in_pieces).astype(jnp.float32))
     if direct:
-        send, keep = merge(order.gate(scalars), [(one_keep, one_got), (two_keep, two_got), (out_keep, out_got)], share)
-        got = swap_seq(order.mark(send), 1)
         ((send, keep),) = fold(order.gate(scalars), [(keep, got, (1, 1, 5))])
         got = swap_seq(order.mark(send), 2)
+        send, two_keep = merge(order.gate(scalars), [(two_keep, two_got)], share)
+        two_got = swap_seq(order.mark(send), 1)
+        ((send, two_keep),) = fold(order.gate(scalars), [(two_keep, two_got, (1, 1, 5))])
+        two_got = swap_seq(order.mark(send), 2)
         down_grad, up_grad = order.mark(*last_ff(order.gate(scalars), ff_keep, ff_got, width))
-    if direct:
-        query_grad, key_grad, value_grad, out_grad, small, late, line = last_qkv(order.gate(scalars), keep, got, width)
+        query_grad, key_grad, value_grad, out_grad, small, late, line = last_qkv(
+            order.gate(scalars), keep, got, two_keep, two_got, width
+        )
         up_bias_grad = line[0, LANES - inner_width // devices :]
     ob, g1, s1 = [small[i, :share] for i in (0, 1, 2)]
     db, g2, s2 = [small[i, :share] for i in (8, 9, 10)]

time: 243 us -> 240 us (0.988)
    ppermute x46 -> x47, waiting for transfers between devices: 57.4 us -> 48.7 us  [swap_dp(): lax.ppermute(value, 'dp', [(i, i ^ mask) for i in range(lax.axis_size('dp...]
    ppermute x4 -> x6, waiting for transfers between devices: 18.2 us -> 25.2 us  [swap_seq(): lax.ppermute(value, 'seq', [(i, i ^ mask) for i in range(lax.axis_size('s...]
    ppermute x4 -> x6, starting transfers between devices: 6.45 us -> 2.46 us  [swap_seq(): lax.ppermute(value, 'seq', [(i, i ^ mask) for i in range(lax.axis_size('s...]
    ppermute x46 -> x47, starting transfers between devices: 42.7 us -> 44.2 us  [swap_dp(): lax.ppermute(value, 'dp', [(i, i ^ mask) for i in range(lax.axis_size('dp...]
    pallas_call x23 -> x25, Pallas kernels: 99.4 us -> 101 us  [whole_call(): pl.pallas_call(body, in_specs=[pl.BlockSpec(memory_space=pltpu.SMEM)] + [...]
  transfers between devices with their start and end apart: 58 -> 61, of which waited for: 25 -> 26; matrix products, arithmetic and copies ran while one was open for 1% -> 1% of each run, Pallas kernels for 34% -> 35%
where the time goes in v4:
time: 240 us
  Pallas kernels  101 us (42%)
  waiting for transfers between devices  74 us (31%)
  starting transfers between devices  53.8 us (22%)
  local copies, waits for them, and re-layouts  6.5 us (3%)
  other arithmetic  3.81 us (2%)
    pallas_call x25, Pallas kernels, whole_call(): pl.pallas_call(body, in_specs=[pl.BlockSpec(memory_space=pltpu.SMEM)] + [...  101 us
    ppermute x47, waiting for transfers between devices, swap_dp(): lax.ppermute(value, 'dp', [(i, i ^ mask) for i in range(lax.axis_size('dp...  48.7 us
    ppermute x47, starting transfers between devices, swap_dp(): lax.ppermute(value, 'dp', [(i, i ^ mask) for i in range(lax.axis_size('dp...  44.2 us
    ppermute x6, waiting for transfers between devices, swap_seq(): lax.ppermute(value, 'seq', [(i, i ^ mask) for i in range(lax.axis_size('s...  25.2 us
  transfers between devices with their start and end apart: 61, of which 26 were waited for; matrix products, arithmetic and copies ran while one was open for 1% of the time, Pallas kernels for 35%

profile of v4, /device:TPU:0, one launch (start us, length us, event | category | flops | bytes accessed | tf_op | source)
XLA Modules:
  0.0 240.0 jit_solution(13018907250336023093)
XLA Ops:
  2.1 2.2 pack.1
  5.0 3.1 %collective-permute-start.4 = (bf16[272,768]{1,0:T(8,128)(2,1)S(1)}, bf16[272,768]{1,0:T(8,128)(2,1)S(1)}, u32[]{:S(2)}, u32[]{:S(2)}) collective-permute-start(bf16[272,768]{1,0:T(8,128)(2,1)S(1)} %get-tuple-element.169), channel_id=1, source_target_pairs={{0,1},{1,0},{2,5},{3,4},{4,3},{5,2},{6,7},{7,6},{8,9},{9,8},{10,13... | collective-permute-start | bytes 1253384 | tf_op jit(solution)/shard_map/ppermute | solution.py:938
  8.1 2.4 %collective-permute-start.2 = (bf16[304,768]{1,0:T(8,128)(2,1)S(1)}, bf16[304,768]{1,0:T(8,128)(2,1)S(1)}, u32[]{:S(2)}, u32[]{:S(2)}) collective-permute-start(bf16[304,768]{1,0:T(8,128)(2,1)S(1)} %get-tuple-element.170.refs_0_), channel_id=1, source_target_pairs={{0,24},{4,28},{8,16},{12,20},{16,8},{20,12},{24,0},{28,4},{1,25},{... | collective-permute-start | bytes 1400840 | tf_op jit(solution)/shard_map/ppermute | solution.py:686
  11.6 13.5 %collective-permute-start.5 = (bf16[272,768]{1,0:T(8,128)(2,1)S(1)}, bf16[272,768]{1,0:T(8,128)(2,1)S(1)}, u32[]{:S(2)}, u32[]{:S(2)}) collective-permute-start(bf16[272,768]{1,0:T(8,128)(2,1)S(1)} %collective-permute-done.3.refs_8_), channel_id=1, source_target_pairs={{0,4},{4,0},{8,12},{12,8},{16,20},{20,16},{24,28},{28,24},{1,5},{5... | collective-permute-start | bytes 1253384 | tf_op jit(solution)/shard_map/ppermute | solution.py:686
  25.2 7.3 %collective-permute-done.1.refs_4_ = bf16[304,768]{1,0:T(8,128)(2,1)S(1)} collective-permute-done((bf16[304,768]{1,0:T(8,128)(2,1)S(1)}, bf16[304,768]{1,0:T(8,128)(2,1)S(1)}, u32[]{:S(2)}, u32[]{:S(2)}) %collective-permute-start.1) | collective-permute-done | bytes 466976 | tf_op jit(solution)/shard_map/ppermute | solution.py:686
  34.1 1.6 collective-permute-start.13
  41.0 20.7 %project.1 = (bf16[512,768]{1,0:T(8,128)(2,1)S(1)}, f32[2,8,512]{2,1,0:T(8,128)S(1)}, bf16[512,768]{1,0:T(8,128)(2,1)S(1)}, f32[16,768]{1,0:T(8,128)S(1)}, f32[1...) custom-call(s32[8]{0:T(128)S(1)} %stack.57.scalars, ...), custom_call_target="tpu_custom_call" | custom-call | flops 1 | bytes 1 | tf_op jit(solution)/shard_map/project/pallas_call | solution.py:422
  62.7 6.8 %collective-permute-done.12.refs_4_ = bf16[96,3840]{1,0:T(8,128)(2,1)} collective-permute-done((bf16[96,3840]{1,0:T(8,128)(2,1)S(1)}, bf16[96,3840]{1,0:T(8,128)(2,1)}, u32[]{:S(2)}, u32[]{:S(2)}) %collective-permute-start.12) | collective-permute-done | bytes 737312 | tf_op jit(solution)/shard_map/ppermute | solution.py:686
  70.1 1.4 collective-permute-start.15
  74.2 10.7 %widen.1 = (f32[512,768]{1,0:T(8,128)S(1)}, f32[512,128]{1,0:T(8,128)S(1)}, bf16[512,768]{1,0:T(8,128)(2,1)S(1)}, bf16[512,3072]{1,0:T(8,128)(2,1)S(1)}, bf16[51...) custom-call(s32[8]{0:T(128)S(1)} %stack.57.scalars, ...), custom_call_target="tpu_custom_call" | custom-call | flops 1 | bytes 1 | tf_op jit(solution)/shard_map/widen/pallas_call | solution.py:422
  89.8 2.2 collective-permute-start.22
  92.0 4.5 %collective-permute-done.25.refs_8_ = bf16[192,768]{1,0:T(8,128)(2,1)S(1)} collective-permute-done((bf16[192,768]{1,0:T(8,128)(2,1)S(1)}, bf16[192,768]{1,0:T(8,128)(2,1)S(1)}, u32[]{:S(2)}, u32[]{:S(2)}) %collective-permute-start.25) | collective-permute-done | bytes 294944 | tf_op jit(solution)/shard_map/ppermute | solution.py:686
  100.6 10.3 %narrow.1 = (bf16[512,768]{1,0:T(8,128)(2,1)S(1)}, f32[512,768]{1,0:T(8,128)S(1)}, bf16[512,768]{1,0:T(8,128)(2,1)S(1)}, f32[8,768]{1,0:T(8,128)S(1)}, bf16[4,38...) custom-call(s32[8]{0:T(128)S(1)} %stack.57.scalars, ...), custom_call_target="tpu_custom_call" | custom-call | flops 1 | bytes 1 | tf_op jit(solution)/shard_map/narrow/pallas_call | solution.py:422
  111.2 6.5 %inner_back.1 = (bf16[512,3072]{1,0:T(8,128)(2,1)S(1)}, f32[1,3072]{1,0:T(1,128)S(1)}, bf16[4,96,3072]{2,1,0:T(8,128)(2,1)S(1)}, bf16[4,96,3072]{2,1,0:T(8,128)(2,1)S(1)}) custom-call(s32[8]{0:T(128)S(1)} %stack.57.scalars, bf16[512,768]{1,0:T(8,128)(2,1)S(1)} %get-tuple-element.197.low, bf16[3072,768]{1,0:T(8,128)(2,1)S(1)} %get-tuple-element.198.wd, ...), custom_call_target="tpu_custom_call" | custom-call | flops 1 | bytes 1 | tf_op jit(solution)/shard_map/inner_back/pallas_call | solution.py:422
  119.4 3.0 %collective-permute-done.30.refs_1_ = bf16[4,96,3072]{2,1,0:T(8,128)(2,1)S(1)} collective-permute-done((bf16[4,96,3072]{2,1,0:T(8,128)(2,1)S(1)}, bf16[4,96,3072]{2,1,0:T(8,128)(2,1)S(1)}, u32[]{:S(2)}, u32[]{:S(2)}) %collective-permute-start.30) | collective-permute-done | bytes 2359328 | tf_op jit(solution)/shard_map/ppermute | solution.py:686
  125.5 6.7 %outer_back.1 = (f32[512,768]{1,0:T(8,128)S(1)}, bf16[512,768]{1,0:T(8,128)(2,1)S(1)}, f32[8,768]{1,0:T(8,128)S(1)}, bf16[4,96,768]{2,1,0:T(8,128)(2,1)S(1)}, bf16[4,96,768]{2,1,0:T(8,128)(2,1)S(1)}) custom-call(s32[8]{0:T(128)S(1)} %stack.57.scalars, bf16[512,3072]{1,0:T(8,128)(2,1)S(1)} %get-tuple-element.201.grad, ...), custom_call_target="tpu_custom_call" | custom-call | flops 1 | bytes 1 | tf_op jit(solution)/shard_map/outer_back/pallas_call | solution.py:422
  134.0 10.8 %attend_back.2 = (bf16[512,384]{1,0:T(8,128)(2,1)S(1)}, f32[512,384]{1,0:T(8,128)S(1)}, f32[512,384]{1,0:T(8,128)S(1)}, bf16[512,384]{1,0:T(8,128)(2,1)S(1)}, bf16[512,384]{1,0:T(8,128)(2,1)S(1)}) custom-call(s32[8]{0:T(128)S(1)} %stack.57.scalars, bf16[512,768]{1,0:T(8,128)(2,1)} %get-tuple-element.217.refs_0_, ...), custom_call_target="tpu_custom_call" | custom-call | flops 1 | bytes 1 | tf_op jit(solution)/shard_map/attend_back/pallas_call | solution.py:422
  144.9 6.9 %collective-permute-done.32.refs_3_ = bf16[2,96,3072]{2,1,0:T(8,128)(2,1)S(1)} collective-permute-done((bf16[2,96,3072]{2,1,0:T(8,128)(2,1)S(1)}, bf16[2,96,3072]{2,1,0:T(8,128)(2,1)S(1)}, u32[]{:S(2)}, u32[]{:S(2)}) %collective-permute-start.32) | collective-permute-done | bytes 1179680 | tf_op jit(solution)/shard_map/ppermute | solution.py:686
  157.0 4.3 %qkv_back.2 = (bf16[2,96,1280]{2,1,0:T(8,128)(2,1)S(1)}, bf16[2,96,1280]{2,1,0:T(8,128)(2,1)S(1)}, bf16[4,96,1280]{2,1,0:T(8,128)(2,1)S(1)}, f32[512,768]{1,0:T(8,128)S(1)}, f32[8,384]{1,0:T(8,128)S(1)}) custom-call(s32[8]{0:T(128)S(1)} %stack.57.scalars, bf16[512,384]{1,0:T(8,128)(2,1)S(1)} %get-tuple-element.224.refs_0_, ...), custom_call_target="tpu_custom_call" | custom-call | flops 1 | bytes 1 | tf_op jit(solution)/shard_map/qkv_back/pallas_call | solution.py:422
  163.2 10.8 %attend_back.3 = (bf16[512,384]{1,0:T(8,128)(2,1)S(1)}, f32[512,384]{1,0:T(8,128)S(1)}, f32[512,384]{1,0:T(8,128)S(1)}, bf16[512,384]{1,0:T(8,128)(2,1)S(1)}, bf16[512,384]{1,0:T(8,128)(2,1)S(1)}) custom-call(s32[8]{0:T(128)S(1)} %stack.57.scalars, bf16[512,768]{1,0:T(8,128)(2,1)} %get-tuple-element.217.refs_0_, ...), custom_call_target="tpu_custom_call" | custom-call | flops 1 | bytes 1 | tf_op jit(solution)/shard_map/attend_back/pallas_call | solution.py:422
  174.9 1.7 collective-permute-done.42.refs_4_
  179.4 1.4 collective-permute-start.50
  180.8 4.3 %qkv_back.3 = (bf16[2,96,1280]{2,1,0:T(8,128)(2,1)S(1)}, bf16[2,96,1280]{2,1,0:T(8,128)(2,1)S(1)}, bf16[4,96,1280]{2,1,0:T(8,128)(2,1)S(1)}, bf16[512,768]{1,0:T(8,128)(2,1)S(1)}, f32[8,384]{1,0:T(8,128)}) custom-call(s32[8]{0:T(128)S(1)} %stack.57.scalars, bf16[512,384]{1,0:T(8,128)(2,1)S(1)} %get-tuple-element.249.refs_0_, ...), custom_call_target="tpu_custom_call" | custom-call | flops 1 | bytes 1 | tf_op jit(solution)/shard_map/qkv_back/pallas_call | solution.py:422
  185.8 7.6 %collective-permute-done.46.refs_1_ = bf16[2,24,6144]{2,1,0:T(8,128)(2,1)S(1)} collective-permute-done((bf16[2,24,6144]{2,1,0:T(8,128)(2,1)S(1)}, bf16[2,24,6144]{2,1,0:T(8,128)(2,1)S(1)}, u32[]{:S(2)}, u32[]{:S(2)}) %collective-permute-start.46) | collective-permute-done | bytes 589856 | tf_op jit(solution)/shard_map/ppermute | solution.py:690
  200.0 3.7 %collective-permute-done.49 = bf16[1,96,1280]{2,1,0:T(8,128)(2,1)S(1)} collective-permute-done((bf16[1,96,1280]{2,1,0:T(8,128)(2,1)S(1)}, bf16[1,96,1280]{2,1,0:T(8,128)(2,1)S(1)}, u32[]{:S(2)}, u32[]{:S(2)}) %collective-permute-start.49) | collective-permute-done | bytes 245792 | tf_op jit(solution)/shard_map/ppermute | solution.py:686
  204.4 1.8 collective-permute-done.51.refs_1_
  206.2 5.3 %collective-permute-done.52.refs_2_ = bf16[1,96,1280]{2,1,0:T(8,128)(2,1)S(1)} collective-permute-done((bf16[1,96,1280]{2,1,0:T(8,128)(2,1)S(1)}, bf16[1,96,1280]{2,1,0:T(8,128)(2,1)S(1)}, u32[]{:S(2)}, u32[]{:S(2)}) %collective-permute-start.52) | collective-permute-done | bytes 245792 | tf_op jit(solution)/shard_map/ppermute | solution.py:686
  212.1 1.5 collective-permute-start.56
  215.3 5.2 %collective-permute-done.55.refs_1_ = bf16[2,24,2048]{2,1,0:T(8,128)(2,1)S(1)} collective-permute-done((bf16[2,24,2048]{2,1,0:T(8,128)(2,1)S(1)}, bf16[2,24,2048]{2,1,0:T(8,128)(2,1)S(1)}, u32[]{:S(2)}, u32[]{:S(2)}) %collective-permute-start.55) | collective-permute-done | bytes 196640 | tf_op jit(solution)/shard_map/ppermute | solution.py:690
  223.1 5.7 %collective-permute-done.57.refs_1_ = bf16[2,24,1280]{2,1,0:T(8,128)(2,1)S(1)} collective-permute-done((bf16[2,24,1280]{2,1,0:T(8,128)(2,1)S(1)}, bf16[2,24,1280]{2,1,0:T(8,128)(2,1)S(1)}, u32[]{:S(2)}, u32[]{:S(2)}) %collective-permute-start.57) | collective-permute-done | bytes 122912 | tf_op jit(solution)/shard_map/ppermute | solution.py:690
  229.4 3.6 %collective-permute-done.58.got = bf16[1,24,6144]{2,1,0:T(8,128)(2,1)S(1)} collective-permute-done((bf16[1,24,6144]{2,1,0:T(8,128)(2,1)S(1)}, bf16[1,24,6144]{2,1,0:T(8,128)(2,1)S(1)}, u32[]{:S(2)}, u32[]{:S(2)}) %collective-permute-start.58) | collective-permute-done | bytes 294944 | tf_op jit(solution)/shard_map/ppermute | solution.py:690
  234.4 2.0 collective-permute-done.59.got
  (186 shorter events, 59.1 us)
Async XLA Ops:
  5.0 20.1 %collective-permute-start.4 = (bf16[272,768]{1,0:T(8,128)(2,1)S(1)}, bf16[272,768]{1,0:T(8,128)(2,1)S(1)}, u32[]{:S(2)}, u32[]{:S(2)}) collective-permute-start(bf16[272,768]{1,0:T(8,128)(2,1)S(1)} %get-tuple-element.169), channel_id=1, source_target_pairs={{0,1},{1,0},{2,5},{3,4},{4,3},{5,2},{6,7},{7,6},{8,9},{9,8},{10,13... | collective-permute-start | bytes 1253384 | tf_op jit(solution)/shard_map/ppermute | solution.py:938
  8.1 17.1 %collective-permute-start.2 = (bf16[304,768]{1,0:T(8,128)(2,1)S(1)}, bf16[304,768]{1,0:T(8,128)(2,1)S(1)}, u32[]{:S(2)}, u32[]{:S(2)}) collective-permute-start(bf16[304,768]{1,0:T(8,128)(2,1)S(1)} %get-tuple-element.170.refs_0_), channel_id=1, source_target_pairs={{0,24},{4,28},{8,16},{12,20},{16,8},{20,12},{24,0},{28,4},{1,25},{... | collective-permute-start | bytes 1400840 | tf_op jit(solution)/shard_map/ppermute | solution.py:686
  10.5 21.9 %collective-permute-start.1 = (bf16[304,768]{1,0:T(8,128)(2,1)S(1)}, bf16[304,768]{1,0:T(8,128)(2,1)S(1)}, u32[]{:S(2)}, u32[]{:S(2)}) collective-permute-start(bf16[304,768]{1,0:T(8,128)(2,1)S(1)} %get-tuple-element.170.refs_0_), channel_id=1, source_target_pairs={{0,16},{4,20},{8,24},{12,28},{16,0},{20,4},{24,8},{28,12},{1,17},{... | collective-permute-start | bytes 1400840 | tf_op jit(solution)/shard_map/ppermute | solution.py:686
  11.0 21.4 %collective-permute-start = (bf16[304,768]{1,0:T(8,128)(2,1)S(1)}, bf16[304,768]{1,0:T(8,128)(2,1)S(1)}, u32[]{:S(2)}, u32[]{:S(2)}) collective-permute-start(bf16[304,768]{1,0:T(8,128)(2,1)S(1)} %get-tuple-element.170.refs_0_), channel_id=1, source_target_pairs={{0,8},{4,12},{8,0},{12,4},{16,24},{20,28},{24,16},{28,20},{1,9},{5... | collective-permute-start | bytes 1400840 | tf_op jit(solution)/shard_map/ppermute | solution.py:686
  11.6 20.9 %collective-permute-start.5 = (bf16[272,768]{1,0:T(8,128)(2,1)S(1)}, bf16[272,768]{1,0:T(8,128)(2,1)S(1)}, u32[]{:S(2)}, u32[]{:S(2)}) collective-permute-start(bf16[272,768]{1,0:T(8,128)(2,1)S(1)} %collective-permute-done.3.refs_8_), channel_id=1, source_target_pairs={{0,4},{4,0},{8,12},{12,8},{16,20},{20,16},{24,28},{28,24},{1,5},{5... | collective-permute-start | bytes 1253384 | tf_op jit(solution)/shard_map/ppermute | solution.py:686
  34.1 28.6 %collective-permute-start.13 = (bf16[96,3840]{1,0:T(8,128)(2,1)S(1)}, bf16[96,3840]{1,0:T(8,128)(2,1)}, u32[]{:S(2)}, u32[]{:S(2)}) collective-permute-start(bf16[96,3840]{1,0:T(8,128)(2,1)S(1)} %pad_maximum_fusion.refs_0_), channel_id=1, source_target_pairs={{0,24},{4,28},{8,16},{12,20},{16,8},{20,12},{24,0},{28,4},{1,25},{... | collective-permute-start | bytes 2211848 | tf_op jit(solution)/shard_map/ppermute | solution.py:686
  35.7 33.8 %collective-permute-start.12 = (bf16[96,3840]{1,0:T(8,128)(2,1)S(1)}, bf16[96,3840]{1,0:T(8,128)(2,1)}, u32[]{:S(2)}, u32[]{:S(2)}) collective-permute-start(bf16[96,3840]{1,0:T(8,128)(2,1)S(1)} %pad_maximum_fusion.refs_0_), channel_id=1, source_target_pairs={{0,16},{4,20},{8,24},{12,28},{16,0},{20,4},{24,8},{28,12},{1,17},{... | collective-permute-start | bytes 2211848 | tf_op jit(solution)/shard_map/ppermute | solution.py:686
  37.1 32.5 %collective-permute-start.11 = (bf16[96,3840]{1,0:T(8,128)(2,1)S(1)}, bf16[96,3840]{1,0:T(8,128)(2,1)}, u32[]{:S(2)}, u32[]{:S(2)}) collective-permute-start(bf16[96,3840]{1,0:T(8,128)(2,1)S(1)} %pad_maximum_fusion.refs_0_), channel_id=1, source_target_pairs={{0,8},{4,12},{8,0},{12,4},{16,24},{20,28},{24,16},{28,20},{1,9},{5... | collective-permute-start | bytes 2211848 | tf_op jit(solution)/shard_map/ppermute | solution.py:686
  39.5 32.0 %collective-permute-start.16 = (bf16[96,3840]{1,0:T(8,128)(2,1)S(1)}, bf16[96,3840]{1,0:T(8,128)(2,1)}, u32[]{:S(2)}, u32[]{:S(2)}) collective-permute-start(bf16[96,3840]{1,0:T(8,128)(2,1)S(1)} %pad_maximum_fusion.refs_0_), channel_id=1, source_target_pairs={{0,4},{4,0},{8,12},{12,8},{16,20},{20,16},{24,28},{28,24},{1,5},{5... | collective-permute-start | bytes 2211848 | tf_op jit(solution)/shard_map/ppermute | solution.py:686
  70.1 16.0 %collective-permute-start.15 = (bf16[384,768]{1,0:T(8,128)(2,1)}, bf16[384,768]{1,0:T(8,128)(2,1)S(1)}, u32[]{:S(2)}, u32[]{:S(2)}) collective-permute-start(bf16[384,768]{1,0:T(8,128)(2,1)} %refs_0_.2), channel_id=1, source_target_pairs={{0,16},{4,20},{8,24},{12,28},{16,0},{20,4},{24,8},{28,12},{1,17},{... | collective-permute-start | bytes 1769480 | tf_op jit(solution)/shard_map/ppermute | solution.py:686
  71.5 15.7 %collective-permute-start.14 = (bf16[384,768]{1,0:T(8,128)(2,1)}, bf16[384,768]{1,0:T(8,128)(2,1)S(1)}, u32[]{:S(2)}, u32[]{:S(2)}) collective-permute-start(bf16[384,768]{1,0:T(8,128)(2,1)} %refs_0_.2), channel_id=1, source_target_pairs={{0,8},{4,12},{8,0},{12,4},{16,24},{20,28},{24,16},{28,20},{1,9},{5... | collective-permute-start | bytes 1769480 | tf_op jit(solution)/shard_map/ppermute | solution.py:686
  72.4 16.9 %collective-permute-start.28 = (bf16[256,768]{1,0:T(8,128)(2,1)S(1)}, bf16[256,768]{1,0:T(8,128)(2,1)S(1)}, u32[]{:S(2)}, u32[]{:S(2)}) collective-permute-start(bf16[256,768]{1,0:T(8,128)(2,1)S(1)} %get-tuple-element.315), channel_id=1, source_target_pairs={{0,1},{1,0},{2,5},{3,4},{4,3},{5,2},{6,7},{7,6},{8,9},{9,8},{10,13... | collective-permute-start | bytes 1179656 | tf_op jit(solution)/shard_map/ppermute | solution.py:715
  73.2 16.6 %collective-permute-start.27 = (bf16[256,768]{1,0:T(8,128)(2,1)S(1)}, bf16[256,768]{1,0:T(8,128)(2,1)S(1)}, u32[]{:S(2)}, u32[]{:S(2)}) collective-permute-start(bf16[256,768]{1,0:T(8,128)(2,1)S(1)} %get-tuple-element.316), channel_id=1, source_target_pairs={{0,0},{1,1},{2,4},{3,5},{4,2},{5,3},{6,6},{7,7},{8,8},{9,9},{10,12... | collective-permute-start | bytes 1179656 | tf_op jit(solution)/shard_map/ppermute | solution.py:715
  123.4 28.3 %collective-permute-start.32 = (bf16[2,96,3072]{2,1,0:T(8,128)(2,1)S(1)}, bf16[2,96,3072]{2,1,0:T(8,128)(2,1)S(1)}, u32[]{:S(2)}, u32[]{:S(2)}) collective-permute-start(bf16[2,96,3072]{2,1,0:T(8,128)(2,1)S(1)} %get-tuple-element.209), channel_id=1, source_target_pairs={{0,16},{4,20},{8,24},{12,28},{16,0},{20,4},{24,8},{28,12},{1,17},{... | collective-permute-start | bytes 3538952 | tf_op jit(solution)/shard_map/ppermute | solution.py:686
  124.2 27.9 %collective-permute-start.31 = (bf16[2,384,768]{2,1,0:T(8,128)(2,1)S(1)}, bf16[2,384,768]{2,1,0:T(8,128)(2,1)S(1)}, u32[]{:S(2)}, u32[]{:S(2)}) collective-permute-start(bf16[2,384,768]{2,1,0:T(8,128)(2,1)S(1)} %get-tuple-element.205), channel_id=1, source_target_pairs={{0,8},{4,12},{8,0},{12,4},{16,24},{20,28},{24,16},{28,20},{1,9},{5... | collective-permute-start | bytes 3538952 | tf_op jit(solution)/shard_map/ppermute | solution.py:686
  133.1 11.7 %collective-permute-start.33 = (bf16[4,96,768]{2,1,0:T(8,128)(2,1)S(1)}, bf16[4,96,768]{2,1,0:T(8,128)(2,1)S(1)}, u32[]{:S(2)}, u32[]{:S(2)}) collective-permute-start(bf16[4,96,768]{2,1,0:T(8,128)(2,1)S(1)} %get-tuple-element.233), channel_id=1, source_target_pairs={{0,4},{4,0},{8,12},{12,8},{16,20},{20,16},{24,28},{28,24},{1,5},{5... | collective-permute-start | bytes 1769480 | tf_op jit(solution)/shard_map/ppermute | solution.py:686
  133.1 20.4 %collective-permute-start.34 = (bf16[256,768]{1,0:T(8,128)(2,1)S(1)}, bf16[256,768]{1,0:T(8,128)(2,1)S(1)}, u32[]{:S(2)}, u32[]{:S(2)}) collective-permute-start(bf16[256,768]{1,0:T(8,128)(2,1)S(1)} %broadcast_select_fusion.2), channel_id=1, source_target_pairs={{1,0},{0,1},{5,2},{4,3},{3,4},{2,5},{7,6},{6,7},{9,8},{8,9},{13,10... | collective-permute-start | bytes 1179656 | tf_op jit(solution)/shard_map/ppermute | solution.py:730
  133.4 20.2 %collective-permute-start.35 = (bf16[256,768]{1,0:T(8,128)(2,1)S(1)}, bf16[256,768]{1,0:T(8,128)(2,1)S(1)}, u32[]{:S(2)}, u32[]{:S(2)}) collective-permute-start(bf16[256,768]{1,0:T(8,128)(2,1)S(1)} %broadcast_select_fusion.3), channel_id=1, source_target_pairs={{0,0},{1,1},{4,2},{5,3},{2,4},{3,5},{6,6},{7,7},{8,8},{9,9},{12,10... | collective-permute-start | bytes 1179656 | tf_op jit(solution)/shard_map/ppermute | solution.py:730
  155.1 19.0 %collective-permute-start.38 = (bf16[1,384,768]{2,1,0:T(8,128)(2,1)S(1)}, bf16[1,384,768]{2,1,0:T(8,128)(2,1)S(1)}, u32[]{:S(2)}, u32[]{:S(2)}) collective-permute-start(bf16[1,384,768]{2,1,0:T(8,128)(2,1)S(1)} %get-tuple-element.234), channel_id=1, source_target_pairs={{0,16},{4,20},{8,24},{12,28},{16,0},{20,4},{24,8},{28,12},{1,17},{... | collective-permute-start | bytes 1769480 | tf_op jit(solution)/shard_map/ppermute | solution.py:686
  156.4 17.7 %collective-permute-start.39 = (bf16[1,96,3072]{2,1,0:T(8,128)(2,1)S(1)}, bf16[1,96,3072]{2,1,0:T(8,128)(2,1)S(1)}, u32[]{:S(2)}, u32[]{:S(2)}) collective-permute-start(bf16[1,96,3072]{2,1,0:T(8,128)(2,1)S(1)} %get-tuple-element.235), channel_id=1, source_target_pairs={{0,8},{4,12},{8,0},{12,4},{16,24},{20,28},{24,16},{28,20},{1,9},{5... | collective-permute-start | bytes 1769480 | tf_op jit(solution)/shard_map/ppermute | solution.py:686
  161.3 15.3 %collective-permute-start.40 = (bf16[2,96,1280]{2,1,0:T(8,128)(2,1)S(1)}, bf16[2,96,1280]{2,1,0:T(8,128)(2,1)S(1)}, u32[]{:S(2)}, u32[]{:S(2)}) collective-permute-start(bf16[2,96,1280]{2,1,0:T(8,128)(2,1)S(1)} %get-tuple-element.260), channel_id=1, source_target_pairs={{0,4},{4,0},{8,12},{12,8},{16,20},{20,16},{24,28},{28,24},{1,5},{5... | collective-permute-start | bytes 1474568 | tf_op jit(solution)/shard_map/ppermute | solution.py:686
  161.4 15.2 %collective-permute-start.41 = (bf16[2,96,1280]{2,1,0:T(8,128)(2,1)S(1)}, bf16[2,96,1280]{2,1,0:T(8,128)(2,1)S(1)}, u32[]{:S(2)}, u32[]{:S(2)}) collective-permute-start(bf16[2,96,1280]{2,1,0:T(8,128)(2,1)S(1)} %get-tuple-element.261), channel_id=1, source_target_pairs={{0,4},{4,0},{8,12},{12,8},{16,20},{20,16},{24,28},{28,24},{1,5},{5... | collective-permute-start | bytes 1474568 | tf_op jit(solution)/shard_map/ppermute | solution.py:686
  161.9 14.7 %collective-permute-start.42 = (bf16[2,96,768]{2,1,0:T(8,128)(2,1)S(1)}, bf16[2,96,768]{2,1,0:T(8,128)(2,1)S(1)}, u32[]{:S(2)}, u32[]{:S(2)}) collective-permute-start(bf16[2,96,768]{2,1,0:T(8,128)(2,1)S(1)} %get-tuple-element.236), channel_id=1, source_target_pairs={{0,16},{4,20},{8,24},{12,28},{16,0},{20,4},{24,8},{28,12},{1,17},{... | collective-permute-start | bytes 884744 | tf_op jit(solution)/shard_map/ppermute | solution.py:686
  178.1 15.3 %collective-permute-start.46 = (bf16[2,24,6144]{2,1,0:T(8,128)(2,1)S(1)}, bf16[2,24,6144]{2,1,0:T(8,128)(2,1)S(1)}, u32[]{:S(2)}, u32[]{:S(2)}) collective-permute-start(bf16[2,24,6144]{2,1,0:T(8,128)(2,1)S(1)} %get-tuple-element.257), channel_id=1, source_target_pairs={{0,1},{1,0},{2,3},{3,2},{4,5},{5,4},{6,7},{7,6},{8,9},{9,8},{10,11... | collective-permute-start | bytes 1769480 | tf_op jit(solution)/shard_map/ppermute | solution.py:690
  178.8 15.3 %collective-permute-start.45 = (bf16[2,96,1280]{2,1,0:T(8,128)(2,1)S(1)}, bf16[2,96,1280]{2,1,0:T(8,128)(2,1)S(1)}, u32[]{:S(2)}, u32[]{:S(2)}) collective-permute-start(bf16[2,96,1280]{2,1,0:T(8,128)(2,1)S(1)} %get-tuple-element.263), channel_id=1, source_target_pairs={{0,8},{4,12},{8,0},{12,4},{16,24},{20,28},{24,16},{28,20},{1,9},{5... | collective-permute-start | bytes 1474568 | tf_op jit(solution)/shard_map/ppermute | solution.py:686
  179.4 19.9 %collective-permute-start.50 = (bf16[1,96,768]{2,1,0:T(8,128)(2,1)S(1)}, bf16[1,96,768]{2,1,0:T(8,128)(2,1)S(1)}, u32[]{:S(2)}, u32[]{:S(2)}) collective-permute-start(bf16[1,96,768]{2,1,0:T(8,128)(2,1)S(1)} %get-tuple-element.264), channel_id=1, source_target_pairs={{0,8},{4,12},{8,0},{12,4},{16,24},{20,28},{24,16},{28,20},{1,9},{5... | collective-permute-start | bytes 442376 | tf_op jit(solution)/shard_map/ppermute | solution.py:686
  185.2 11.9 %collective-permute-start.48 = (bf16[2,96,1280]{2,1,0:T(8,128)(2,1)S(1)}, bf16[2,96,1280]{2,1,0:T(8,128)(2,1)S(1)}, u32[]{:S(2)}, u32[]{:S(2)}) collective-permute-start(bf16[2,96,1280]{2,1,0:T(8,128)(2,1)S(1)} %get-tuple-element.281), channel_id=1, source_target_pairs={{0,4},{4,0},{8,12},{12,8},{16,20},{20,16},{24,28},{28,24},{1,5},{5... | collective-permute-start | bytes 1474568 | tf_op jit(solution)/shard_map/ppermute | solution.py:686
  193.4 20.6 %collective-permute-start.53 = (bf16[256,768]{1,0:T(8,128)(2,1)S(1)}, bf16[256,768]{1,0:T(8,128)(2,1)S(1)}, u32[]{:S(2)}, u32[]{:S(2)}) collective-permute-start(bf16[256,768]{1,0:T(8,128)(2,1)S(1)} %broadcast_select_fusion), channel_id=1, source_target_pairs={{1,0},{0,1},{5,2},{4,3},{3,4},{2,5},{7,6},{6,7},{9,8},{8,9},{13,10... | collective-permute-start | bytes 1179656 | tf_op jit(solution)/shard_map/ppermute | solution.py:730
  194.1 20.0 %collective-permute-start.54 = (bf16[256,768]{1,0:T(8,128)(2,1)S(1)}, bf16[256,768]{1,0:T(8,128)(2,1)S(1)}, u32[]{:S(2)}, u32[]{:S(2)}) collective-permute-start(bf16[256,768]{1,0:T(8,128)(2,1)S(1)} %broadcast_select_fusion.1), channel_id=1, source_target_pairs={{0,0},{1,1},{4,2},{5,3},{2,4},{3,5},{6,6},{7,7},{8,8},{9,9},{12,10... | collective-permute-start | bytes 1179656 | tf_op jit(solution)/shard_map/ppermute | solution.py:730
  199.3 12.2 %collective-permute-start.52 = (bf16[1,96,1280]{2,1,0:T(8,128)(2,1)S(1)}, bf16[1,96,1280]{2,1,0:T(8,128)(2,1)S(1)}, u32[]{:S(2)}, u32[]{:S(2)}) collective-permute-start(bf16[1,96,1280]{2,1,0:T(8,128)(2,1)S(1)} %get-tuple-element.283), channel_id=1, source_target_pairs={{0,8},{4,12},{8,0},{12,4},{16,24},{20,28},{24,16},{28,20},{1,9},{5... | collective-permute-start | bytes 737288 | tf_op jit(solution)/shard_map/ppermute | solution.py:686
  214.0 19.0 %collective-permute-start.58 = (bf16[1,24,6144]{2,1,0:T(8,128)(2,1)S(1)}, bf16[1,24,6144]{2,1,0:T(8,128)(2,1)S(1)}, u32[]{:S(2)}, u32[]{:S(2)}) collective-permute-start(bf16[1,24,6144]{2,1,0:T(8,128)(2,1)S(1)} %get-tuple-element.277), channel_id=1, source_target_pairs={{0,2},{1,3},{2,0},{3,1},{4,6},{5,7},{6,4},{7,5},{8,10},{9,11},{10,... | collective-permute-start | bytes 884744 | tf_op jit(solution)/shard_map/ppermute | solution.py:690
  223.1 13.4 %collective-permute-start.59 = (bf16[1,24,2048]{2,1,0:T(8,128)(2,1)S(1)}, bf16[1,24,2048]{2,1,0:T(8,128)(2,1)S(1)}, u32[]{:S(2)}, u32[]{:S(2)}) collective-permute-start(bf16[1,24,2048]{2,1,0:T(8,128)(2,1)S(1)} %get-tuple-element.294), channel_id=1, source_target_pairs={{0,2},{1,3},{2,0},{3,1},{4,6},{5,7},{6,4},{7,5},{8,10},{9,11},{10,... | collective-permute-start | bytes 294920 | tf_op jit(solution)/shard_map/ppermute | solution.py:690
  (57 other events, 517.5 us)

commit v5 on v4

--- a/solution.py
+++ b/solution.py
@@ -225,6 +225,11 @@
 def parts_of(refs):
     if len(refs) == PARTS:
         return [(i, 0, ref) for i, ref in enumerate(refs)]
+    if len(refs) == 6:
+        own, own_far, near_x, near_y, near_d, far = refs
+        rows = own.shape[0]
+        other = [far.at[i * rows : (i + 1) * rows, :] for i in range(3)]
+        return [(i, 0, ref) for i, ref in enumerate((own, own_far, near_x, other[0], near_y, other[1], near_d, other[2]))]
     pieces = [(i, 0, ref) for i, ref in enumerate(refs[:6])]
     for i in range(2):
         top, bottom = refs[6 + i], refs[8 + i]
@@ -810,11 +815,13 @@
 
 def project_body(sizes, scalars, *refs):
     rows, wide, vectors, qblock, chunk, lanes, shards = sizes
-    pieces, hidden = parts_of(refs[:shards]), refs[shards : shards + 4]
+    pieces, hidden = parts_of(refs[:shards]), list(refs[shards : shards + 3])
+    size = hidden[0].shape[0]
+    hidden = hidden[:2] + [hidden[2].at[:size, :], hidden[2].at[size:, :]]
     (
         attended, lse, tokens, vec_ref, up_ref, segments, ordered, query_out, keys_out, values_out, keys_far_out, values_far_out, weights_out,
         query, keys, values, keys_far, values_far, far, held, small, turned, ids, sems, hidden_sems, out_sems, kall, vt, tiles,
-    ) = refs[shards + 4 :]
+    ) = refs[shards + 3 :]
     count, width = tokens.shape
     block = count // 2
     half = width // 2
@@ -939,10 +946,12 @@
     out_up, down_part = lax.optimization_barrier(
         (jnp.concatenate([out_weight, up_weight], axis=1), down_weight, *near[1:4])
     )[:2]
-    hidden += [swap_dp(piece, 1) for piece in hidden]
+    hidden.append(swap_dp(jnp.concatenate(hidden), 1))
     if direct:
-        near = list(lax.optimization_barrier((*near, *hidden))[:4])
-    shards = both_cores(near) if direct else near
+        own_far, *arrived = lax.optimization_barrier((swap_dp(part, 1), *near[1:4]))
+        shards = [part, own_far, *arrived, swap_dp(jnp.concatenate(arrived), 1)]
+    else:
+        shards = near
     out_up_near = near_shards(out_up)
     attended, lse, tokens, vec, up_add, segments, ordered, query, keys, values, keys_other, values_other, w_qkv = project(
         scalars, shards, hidden, width // PARTS, inner_width // PARTS, len(vectors), qblock, chunk, pairs * LANES
@@ -967,12 +976,13 @@
     if direct:
         ((send, down_keep),) = fold(order.gate(scalars), [(down_keep, down_got, (2, 1, 2))])
         down_got = swap_dp(order.mark(send), 2)
+    sum_one_grad, attended_grad, sums_one, out_send, out_keep = outer_back(
+        order.gate(scalars), inner_grad, wu, sum_two_grad, normal_one, scale_one, vec, wo, attended
+    )
+    order.mark(attended_grad)
+    if direct:
         ((send, up_keep),) = fold(order.gate(scalars), [(up_keep, up_got, (1, 2, 3))])
         up_got = swap_dp(order.mark(send), 4)
-    sum_one_grad, attended_grad, sums_one, out_send, out_keep = outer_back(
-        order.gate(scalars), inner_grad, wu, sum_two_grad, normal_one, scale_one, vec, wo, attended
-    )
-    order.mark(attended_grad)
     out_got = swap(out_send)
 
     def attend(side):
@@ -981,12 +991,11 @@
 
     dq, dk, dv, *far = attend(0)
     if direct:
-        (send, down_keep), (other, up_keep), (third, out_keep) = fold(
-            order.gate(scalars),
-            [(down_keep, down_got, (1, 1, 3)), (up_keep, up_got, (1, 1, 2)), (out_keep, out_got, (1, 2, 3))],
+        (send, down_keep), (third, out_keep) = fold(
+            order.gate(scalars), [(down_keep, down_got, (1, 1, 3)), (out_keep, out_got, (1, 2, 3))]
         )
-        order.mark(send, other, third)
-        down_got, up_got, out_got = swap_dp(send, 4), swap_dp(other, 2), swap_dp(third, 4)
+        order.mark(send, third)
+        down_got, out_got = swap_dp(send, 4), swap_dp(third, 4)
     layer_out = order.mark(both_sequences(order, out_pieces))
     one_low, one_high, one_keep, gradient, sums_first = qkv_back(
         0, order.gate(scalars), dq, dk, dv, *[swap_dp(x, 1) for x in order.gate(far)], ordered, w_qkv, sum_one_grad,
@@ -994,6 +1003,9 @@
     )
     order.mark(gradient)
     one_got = (swap(one_low), swap(one_high))
+    if direct:
+        ((send, up_keep),) = fold(order.gate(scalars), [(up_keep, up_got, (1, 1, 2))])
+        up_got = swap_dp(order.mark(send), 2)
     dq, dk, dv, *far = attend(1)
     if direct:
         send, ff_keep = merge(order.gate(scalars), [(down_keep, down_got), (up_keep, up_got)], share)

time: 240 us -> 239 us (level)
  Pallas kernels: 101 us -> 92.7 us
  starting transfers between devices: 53.8 us -> 61.3 us
    ppermute x6, waiting for transfers between devices: 25.2 us -> 12.5 us  [swap_seq(): lax.ppermute(value, 'seq', [(i, i ^ mask) for i in range(lax.axis_size('s...]
    ppermute x47 -> x44, waiting for transfers between devices: 48.7 us -> 59.2 us  [swap_dp(): lax.ppermute(value, 'dp', [(i, i ^ mask) for i in range(lax.axis_size('dp...]
    pallas_call x25 -> x26, Pallas kernels: 101 us -> 92.7 us  [whole_call(): pl.pallas_call(body, in_specs=[pl.BlockSpec(memory_space=pltpu.SMEM)] + [...]
    ppermute x6, starting transfers between devices: 2.46 us -> 10.3 us  [swap_seq(): lax.ppermute(value, 'seq', [(i, i ^ mask) for i in range(lax.axis_size('s...]
    ppermute x47 -> x44, starting transfers between devices: 44.2 us -> 39.4 us  [swap_dp(): lax.ppermute(value, 'dp', [(i, i ^ mask) for i in range(lax.axis_size('dp...]
    ppermute x2, starting transfers between devices: 1.15 us -> 4.32 us  [to_sequences(): got.append(lax.ppermute(piece, AXES, spread_pairs(first)))]
    unnamed x56 -> x52, local copies, waits for them, and re-layouts: 3.95 us -> 5.68 us
  transfers between devices with their start and end apart: 61 -> 58, of which waited for: 26 -> 18; matrix products, arithmetic and copies ran while one was open for 1% -> 1% of each run, Pallas kernels for 35% -> 33%
where the time goes in v5:
time: 239 us; the launch traced here: 238 us
  Pallas kernels  92.7 us (39%)
  waiting for transfers between devices  71.7 us (30%)
  starting transfers between devices  61.3 us (26%)
  local copies, waits for them, and re-layouts  8.18 us (3%)
  other arithmetic  3.02 us (1%)
    pallas_call x26, Pallas kernels, whole_call(): pl.pallas_call(body, in_specs=[pl.BlockSpec(memory_space=pltpu.SMEM)] + [...  92.7 us
    ppermute x44, waiting for transfers between devices, swap_dp(): lax.ppermute(value, 'dp', [(i, i ^ mask) for i in range(lax.axis_size('dp...  59.2 us
    ppermute x44, starting transfers between devices, swap_dp(): lax.ppermute(value, 'dp', [(i, i ^ mask) for i in range(lax.axis_size('dp...  39.4 us
    ppermute x6, waiting for transfers between devices, swap_seq(): lax.ppermute(value, 'seq', [(i, i ^ mask) for i in range(lax.axis_size('s...  12.5 us
    ppermute x6, starting transfers between devices, swap_seq(): lax.ppermute(value, 'seq', [(i, i ^ mask) for i in range(lax.axis_size('s...  10.3 us
    unnamed x52, local copies, waits for them, and re-layouts  5.68 us
  transfers between devices with their start and end apart: 58, of which 18 were waited for; matrix products, arithmetic and copies ran while one was open for 1% of the time, Pallas kernels for 33%

profile of v5, /device:TPU:0, one launch (start us, length us, event | category | flops | bytes accessed | tf_op | source)
XLA Modules:
  0.0 238.3 jit_solution(8333140307286599815)
XLA Ops:
  2.0 2.2 pack.1
  4.8 3.5 %collective-permute-start.2 = (bf16[304,768]{1,0:T(8,128)(2,1)S(1)}, bf16[304,768]{1,0:T(8,128)(2,1)S(1)}, u32[]{:S(2)}, u32[]{:S(2)}) collective-permute-start(bf16[304,768]{1,0:T(8,128)(2,1)S(1)} %get-tuple-element.167.refs_0_), channel_id=1, source_target_pairs={{0,24},{4,28},{8,16},{12,20},{16,8},{20,12},{24,0},{28,4},{1,25},{... | collective-permute-start | bytes 1400840 | tf_op jit(solution)/shard_map/ppermute | solution.py:691
  9.7 2.0 collective-permute-start.6
  11.7 8.2 %collective-permute-done.2.refs_4_ = bf16[304,768]{1,0:T(8,128)(2,1)S(1)} collective-permute-done((bf16[304,768]{1,0:T(8,128)(2,1)S(1)}, bf16[304,768]{1,0:T(8,128)(2,1)S(1)}, u32[]{:S(2)}, u32[]{:S(2)}) %collective-permute-start.2) | collective-permute-done | bytes 466976 | tf_op jit(solution)/shard_map/ppermute | solution.py:691
  19.9 9.7 %collective-permute-done.1.refs_3_ = bf16[304,768]{1,0:T(8,128)(2,1)S(1)} collective-permute-done((bf16[304,768]{1,0:T(8,128)(2,1)S(1)}, bf16[304,768]{1,0:T(8,128)(2,1)S(1)}, u32[]{:S(2)}, u32[]{:S(2)}) %collective-permute-start.1) | collective-permute-done | bytes 466976 | tf_op jit(solution)/shard_map/ppermute | solution.py:691
  36.5 17.1 %project.1 = (bf16[512,768]{1,0:T(8,128)(2,1)S(1)}, f32[2,8,512]{2,1,0:T(8,128)S(1)}, bf16[512,768]{1,0:T(8,128)(2,1)S(1)}, f32[16,768]{1,0:T(8,128)S(1)}, f32[1...) custom-call(s32[8]{0:T(128)S(1)} %stack.57.scalars, ...), custom_call_target="tpu_custom_call" | custom-call | flops 1 | bytes 1 | tf_op jit(solution)/shard_map/project/pallas_call | solution.py:427
  54.6 12.1 %collective-permute-done.9.refs_4_ = bf16[96,3840]{1,0:T(8,128)(2,1)} collective-permute-done((bf16[96,3840]{1,0:T(8,128)(2,1)S(1)}, bf16[96,3840]{1,0:T(8,128)(2,1)}, u32[]{:S(2)}, u32[]{:S(2)}) %collective-permute-start.9) | collective-permute-done | bytes 737312 | tf_op jit(solution)/shard_map/ppermute | solution.py:691
  69.4 3.5 %collective-permute-start.25 = (bf16[256,768]{1,0:T(8,128)(2,1)S(1)}, bf16[256,768]{1,0:T(8,128)(2,1)S(1)}, u32[]{:S(2)}, u32[]{:S(2)}) collective-permute-start(bf16[256,768]{1,0:T(8,128)(2,1)S(1)} %get-tuple-element.317), channel_id=1, source_target_pairs={{0,1},{1,0},{2,5},{3,4},{4,3},{5,2},{6,7},{7,6},{8,9},{9,8},{10,13... | collective-permute-start | bytes 1179656 | tf_op jit(solution)/shard_map/ppermute | solution.py:720
  73.7 10.7 %widen.1 = (f32[512,768]{1,0:T(8,128)S(1)}, f32[512,128]{1,0:T(8,128)S(1)}, bf16[512,768]{1,0:T(8,128)(2,1)S(1)}, bf16[512,3072]{1,0:T(8,128)(2,1)S(1)}, bf16[51...) custom-call(s32[8]{0:T(128)S(1)} %stack.57.scalars, ...), custom_call_target="tpu_custom_call" | custom-call | flops 1 | bytes 1 | tf_op jit(solution)/shard_map/widen/pallas_call | solution.py:427
  86.5 3.7 %collective-permute-start.17 = (bf16[384,768]{1,0:T(8,128)(2,1)S(1)}, bf16[384,768]{1,0:T(8,128)(2,1)S(1)}, u32[]{:S(2)}, u32[]{:S(2)}) collective-permute-start(bf16[384,768]{1,0:T(8,128)(2,1)S(1)} %copy-done.15), channel_id=1, source_target_pairs={{0,4},{4,0},{8,12},{12,8},{16,20},{20,16},{24,28},{28,24},{1,5},{5... | collective-permute-start | bytes 1769480 | tf_op jit(solution)/shard_map/ppermute | solution.py:691
  91.5 2.8 %collective-permute-start.23 = (bf16[192,768]{1,0:T(8,128)(2,1)S(1)}, bf16[192,768]{1,0:T(8,128)(2,1)S(1)}, u32[]{:S(2)}, u32[]{:S(2)}) collective-permute-start(bf16[192,768]{1,0:T(8,128)(2,1)S(1)} %collective-permute-done.22.refs_8_), channel_id=1, source_target_pairs={{0,4},{4,0},{8,12},{12,8},{16,20},{20,16},{24,28},{28,24},{1,5},{5... | collective-permute-start | bytes 884744 | tf_op jit(solution)/shard_map/ppermute | solution.py:691
  98.1 10.4 %narrow.1 = (bf16[512,768]{1,0:T(8,128)(2,1)S(1)}, f32[512,768]{1,0:T(8,128)S(1)}, bf16[512,768]{1,0:T(8,128)(2,1)S(1)}, f32[8,768]{1,0:T(8,128)S(1)}, bf16[4,38...) custom-call(s32[8]{0:T(128)S(1)} %stack.57.scalars, ...), custom_call_target="tpu_custom_call" | custom-call | flops 1 | bytes 1 | tf_op jit(solution)/shard_map/narrow/pallas_call | solution.py:427
  109.0 6.5 %inner_back.1 = (bf16[512,3072]{1,0:T(8,128)(2,1)S(1)}, f32[1,3072]{1,0:T(1,128)S(1)}, bf16[4,96,3072]{2,1,0:T(8,128)(2,1)S(1)}, bf16[4,96,3072]{2,1,0:T(8,128)(2,1)S(1)}) custom-call(s32[8]{0:T(128)S(1)} %stack.57.scalars, bf16[512,768]{1,0:T(8,128)(2,1)S(1)} %get-tuple-element.198.low, bf16[3072,768]{1,0:T(8,128)(2,1)S(1)} %get-tuple-element.199.wd, ...), custom_call_target="tpu_custom_call" | custom-call | flops 1 | bytes 1 | tf_op jit(solution)/shard_map/inner_back/pallas_call | solution.py:427
  117.7 6.6 %outer_back.1 = (f32[512,768]{1,0:T(8,128)S(1)}, bf16[512,768]{1,0:T(8,128)(2,1)S(1)}, f32[8,768]{1,0:T(8,128)S(1)}, bf16[4,96,768]{2,1,0:T(8,128)(2,1)S(1)}, bf16[4,96,768]{2,1,0:T(8,128)(2,1)S(1)}) custom-call(s32[8]{0:T(128)S(1)} %stack.57.scalars, bf16[512,3072]{1,0:T(8,128)(2,1)S(1)} %get-tuple-element.202.grad, ...), custom_call_target="tpu_custom_call" | custom-call | flops 1 | bytes 1 | tf_op jit(solution)/shard_map/outer_back/pallas_call | solution.py:427
  127.8 2.8 %collective-permute-start.30 = (bf16[256,768]{1,0:T(8,128)(2,1)S(1)}, bf16[256,768]{1,0:T(8,128)(2,1)S(1)}, u32[]{:S(2)}, u32[]{:S(2)}) collective-permute-start(bf16[256,768]{1,0:T(8,128)(2,1)S(1)} %broadcast_select_fusion.2), channel_id=1, source_target_pairs={{1,0},{0,1},{5,2},{4,3},{3,4},{2,5},{7,6},{6,7},{9,8},{8,9},{13,10... | collective-permute-start | bytes 1179656 | tf_op jit(solution)/shard_map/ppermute | solution.py:735
  131.3 8.4 %attend_back.2 = (bf16[512,384]{1,0:T(8,128)(2,1)S(1)}, f32[512,384]{1,0:T(8,128)S(1)}, f32[512,384]{1,0:T(8,128)S(1)}, bf16[512,384]{1,0:T(8,128)(2,1)S(1)}, bf16[512,384]{1,0:T(8,128)(2,1)S(1)}) custom-call(s32[8]{0:T(128)S(1)} %stack.57.scalars, bf16[512,768]{1,0:T(8,128)(2,1)} %get-tuple-element.218.refs_0_, ...), custom_call_target="tpu_custom_call" | custom-call | flops 1 | bytes 1 | tf_op jit(solution)/shard_map/attend_back/pallas_call | solution.py:427
  139.7 5.5 %collective-permute-done.28.refs_1_ = bf16[2,384,768]{2,1,0:T(8,128)(2,1)S(1)} collective-permute-done((bf16[2,384,768]{2,1,0:T(8,128)(2,1)S(1)}, bf16[2,384,768]{2,1,0:T(8,128)(2,1)S(1)}, u32[]{:S(2)}, u32[]{:S(2)}) %collective-permute-start.28) | collective-permute-done | bytes 1179680 | tf_op jit(solution)/shard_map/ppermute | solution.py:691
  147.3 3.8 %collective-permute-start.32 = (bf16[512,384]{1,0:T(8,128)(2,1)S(1)}, bf16[512,384]{1,0:T(8,128)(2,1)S(1)}, u32[]{:S(2)}, u32[]{:S(2)}) collective-permute-start(bf16[512,384]{1,0:T(8,128)(2,1)S(1)} %get-tuple-element.238), channel_id=1, source_target_pairs={{0,4},{4,0},{8,12},{12,8},{16,20},{20,16},{24,28},{28,24},{1,5},{5... | collective-permute-start | bytes 1179656 | tf_op jit(solution)/shard_map/ppermute | solution.py:691
  153.0 4.3 %qkv_back.2 = (bf16[2,96,1280]{2,1,0:T(8,128)(2,1)S(1)}, bf16[2,96,1280]{2,1,0:T(8,128)(2,1)S(1)}, bf16[4,96,1280]{2,1,0:T(8,128)(2,1)S(1)}, f32[512,768]{1,0:T(8,128)S(1)}, f32[8,384]{1,0:T(8,128)S(1)}) custom-call(s32[8]{0:T(128)S(1)} %stack.57.scalars, bf16[512,384]{1,0:T(8,128)(2,1)S(1)} %get-tuple-element.225.refs_0_, ...), custom_call_target="tpu_custom_call" | custom-call | flops 1 | bytes 1 | tf_op jit(solution)/shard_map/qkv_back/pallas_call | solution.py:427
  159.2 1.6 collective-permute-start.39
  160.8 8.4 %attend_back.3 = (bf16[512,384]{1,0:T(8,128)(2,1)S(1)}, f32[512,384]{1,0:T(8,128)S(1)}, f32[512,384]{1,0:T(8,128)S(1)}, bf16[512,384]{1,0:T(8,128)(2,1)S(1)}, bf16[512,384]{1,0:T(8,128)(2,1)S(1)}) custom-call(s32[8]{0:T(128)S(1)} %stack.57.scalars, bf16[512,768]{1,0:T(8,128)(2,1)} %get-tuple-element.218.refs_0_, ...), custom_call_target="tpu_custom_call" | custom-call | flops 1 | bytes 1 | tf_op jit(solution)/shard_map/attend_back/pallas_call | solution.py:427
  169.3 4.6 %collective-permute-done.36 = bf16[1,96,3072]{2,1,0:T(8,128)(2,1)S(1)} collective-permute-done((bf16[1,96,3072]{2,1,0:T(8,128)(2,1)S(1)}, bf16[1,96,3072]{2,1,0:T(8,128)(2,1)S(1)}, u32[]{:S(2)}, u32[]{:S(2)}) %collective-permute-start.36) | collective-permute-done | bytes 589856 | tf_op jit(solution)/shard_map/ppermute | solution.py:691
  179.8 4.3 %qkv_back.3 = (bf16[2,96,1280]{2,1,0:T(8,128)(2,1)S(1)}, bf16[2,96,1280]{2,1,0:T(8,128)(2,1)S(1)}, bf16[4,96,1280]{2,1,0:T(8,128)(2,1)S(1)}, bf16[512,768]{1,0:T(8,128)(2,1)S(1)}, f32[8,384]{1,0:T(8,128)}) custom-call(s32[8]{0:T(128)S(1)} %stack.57.scalars, bf16[512,384]{1,0:T(8,128)(2,1)S(1)} %get-tuple-element.251.refs_0_, ...), custom_call_target="tpu_custom_call" | custom-call | flops 1 | bytes 1 | tf_op jit(solution)/shard_map/qkv_back/pallas_call | solution.py:427
  184.8 7.1 %collective-permute-done.42.refs_1_ = bf16[2,96,1280]{2,1,0:T(8,128)(2,1)S(1)} collective-permute-done((bf16[2,96,1280]{2,1,0:T(8,128)(2,1)S(1)}, bf16[2,96,1280]{2,1,0:T(8,128)(2,1)S(1)}, u32[]{:S(2)}, u32[]{:S(2)}) %collective-permute-start.42) | collective-permute-done | bytes 491552 | tf_op jit(solution)/shard_map/ppermute | solution.py:691
  197.9 2.6 %collective-permute-done.46 = bf16[1,96,1280]{2,1,0:T(8,128)(2,1)S(1)} collective-permute-done((bf16[1,96,1280]{2,1,0:T(8,128)(2,1)S(1)}, bf16[1,96,1280]{2,1,0:T(8,128)(2,1)S(1)}, u32[]{:S(2)}, u32[]{:S(2)}) %collective-permute-start.46) | collective-permute-done | bytes 245792 | tf_op jit(solution)/shard_map/ppermute | solution.py:691
  201.1 1.6 collective-permute-done.48.refs_1_
  202.7 5.3 %collective-permute-done.49.refs_2_ = bf16[1,96,1280]{2,1,0:T(8,128)(2,1)S(1)} collective-permute-done((bf16[1,96,1280]{2,1,0:T(8,128)(2,1)S(1)}, bf16[1,96,1280]{2,1,0:T(8,128)(2,1)S(1)}, u32[]{:S(2)}, u32[]{:S(2)}) %collective-permute-start.49) | collective-permute-done | bytes 245792 | tf_op jit(solution)/shard_map/ppermute | solution.py:691
  208.7 1.6 collective-permute-start.53
  210.3 2.8 %collective-permute-start.52 = (bf16[2,24,2048]{2,1,0:T(8,128)(2,1)S(1)}, bf16[2,24,2048]{2,1,0:T(8,128)(2,1)S(1)}, u32[]{:S(2)}, u32[]{:S(2)}) collective-permute-start(bf16[2,24,2048]{2,1,0:T(8,128)(2,1)S(1)} %get-tuple-element.289), channel_id=1, source_target_pairs={{0,1},{1,0},{2,3},{3,2},{4,5},{5,4},{6,7},{7,6},{8,9},{9,8},{10,11... | collective-permute-start | bytes 589832 | tf_op jit(solution)/shard_map/ppermute | solution.py:695
  214.4 5.2 %collective-permute-done.52.refs_1_ = bf16[2,24,2048]{2,1,0:T(8,128)(2,1)S(1)} collective-permute-done((bf16[2,24,2048]{2,1,0:T(8,128)(2,1)S(1)}, bf16[2,24,2048]{2,1,0:T(8,128)(2,1)S(1)}, u32[]{:S(2)}, u32[]{:S(2)}) %collective-permute-start.52) | collective-permute-done | bytes 196640 | tf_op jit(solution)/shard_map/ppermute | solution.py:695
  222.2 3.1 %collective-permute-start.56 = (bf16[1,24,2048]{2,1,0:T(8,128)(2,1)S(1)}, bf16[1,24,2048]{2,1,0:T(8,128)(2,1)S(1)}, u32[]{:S(2)}, u32[]{:S(2)}) collective-permute-start(bf16[1,24,2048]{2,1,0:T(8,128)(2,1)S(1)} %get-tuple-element.296), channel_id=1, source_target_pairs={{0,2},{1,3},{2,0},{3,1},{4,6},{5,7},{6,4},{7,5},{8,10},{9,11},{10,... | collective-permute-start | bytes 294920 | tf_op jit(solution)/shard_map/ppermute | solution.py:695
  225.3 3.3 %collective-permute-done.54.refs_1_ = bf16[2,24,1280]{2,1,0:T(8,128)(2,1)S(1)} collective-permute-done((bf16[2,24,1280]{2,1,0:T(8,128)(2,1)S(1)}, bf16[2,24,1280]{2,1,0:T(8,128)(2,1)S(1)}, u32[]{:S(2)}, u32[]{:S(2)}) %collective-permute-start.54) | collective-permute-done | bytes 122912 | tf_op jit(solution)/shard_map/ppermute | solution.py:695
  (179 shorter events, 61.6 us)
Async XLA Ops:
  4.8 15.1 %collective-permute-start.2 = (bf16[304,768]{1,0:T(8,128)(2,1)S(1)}, bf16[304,768]{1,0:T(8,128)(2,1)S(1)}, u32[]{:S(2)}, u32[]{:S(2)}) collective-permute-start(bf16[304,768]{1,0:T(8,128)(2,1)S(1)} %get-tuple-element.167.refs_0_), channel_id=1, source_target_pairs={{0,24},{4,28},{8,16},{12,20},{16,8},{20,12},{24,0},{28,4},{1,25},{... | collective-permute-start | bytes 1400840 | tf_op jit(solution)/shard_map/ppermute | solution.py:691
  8.3 21.3 %collective-permute-start.1 = (bf16[304,768]{1,0:T(8,128)(2,1)S(1)}, bf16[304,768]{1,0:T(8,128)(2,1)S(1)}, u32[]{:S(2)}, u32[]{:S(2)}) collective-permute-start(bf16[304,768]{1,0:T(8,128)(2,1)S(1)} %get-tuple-element.167.refs_0_), channel_id=1, source_target_pairs={{0,16},{4,20},{8,24},{12,28},{16,0},{20,4},{24,8},{28,12},{1,17},{... | collective-permute-start | bytes 1400840 | tf_op jit(solution)/shard_map/ppermute | solution.py:691
  8.8 21.1 %collective-permute-start = (bf16[304,768]{1,0:T(8,128)(2,1)S(1)}, bf16[304,768]{1,0:T(8,128)(2,1)S(1)}, u32[]{:S(2)}, u32[]{:S(2)}) collective-permute-start(bf16[304,768]{1,0:T(8,128)(2,1)S(1)} %get-tuple-element.167.refs_0_), channel_id=1, source_target_pairs={{0,8},{4,12},{8,0},{12,4},{16,24},{20,28},{24,16},{28,20},{1,9},{5... | collective-permute-start | bytes 1400840 | tf_op jit(solution)/shard_map/ppermute | solution.py:691
  8.9 21.1 %collective-permute-start.5 = (bf16[272,768]{1,0:T(8,128)(2,1)S(1)}, bf16[272,768]{1,0:T(8,128)(2,1)S(1)}, u32[]{:S(2)}, u32[]{:S(2)}) collective-permute-start(bf16[272,768]{1,0:T(8,128)(2,1)S(1)} %get-tuple-element.173), channel_id=1, source_target_pairs={{0,0},{1,1},{2,4},{3,5},{4,2},{5,3},{6,6},{7,7},{8,8},{9,9},{10,12... | collective-permute-start | bytes 1253384 | tf_op jit(solution)/shard_map/ppermute | solution.py:945
  9.7 20.4 %collective-permute-start.6 = (bf16[272,768]{1,0:T(8,128)(2,1)S(1)}, bf16[272,768]{1,0:T(8,128)(2,1)S(1)}, u32[]{:S(2)}, u32[]{:S(2)}) collective-permute-start(bf16[272,768]{1,0:T(8,128)(2,1)S(1)} %get-tuple-element.174), channel_id=1, source_target_pairs={{0,1},{1,0},{2,5},{3,4},{4,3},{5,2},{6,7},{7,6},{8,9},{9,8},{10,13... | collective-permute-start | bytes 1253384 | tf_op jit(solution)/shard_map/ppermute | solution.py:945
  31.0 23.6 %collective-permute-start.10 = (bf16[96,3840]{1,0:T(8,128)(2,1)S(1)}, bf16[96,3840]{1,0:T(8,128)(2,1)}, u32[]{:S(2)}, u32[]{:S(2)}) collective-permute-start(bf16[96,3840]{1,0:T(8,128)(2,1)S(1)} %pad_maximum_fusion.2.refs_0_), channel_id=1, source_target_pairs={{0,24},{4,28},{8,16},{12,20},{16,8},{20,12},{24,0},{28,4},{1,25},{... | collective-permute-start | bytes 2211848 | tf_op jit(solution)/shard_map/ppermute | solution.py:691
  32.5 34.2 %collective-permute-start.9 = (bf16[96,3840]{1,0:T(8,128)(2,1)S(1)}, bf16[96,3840]{1,0:T(8,128)(2,1)}, u32[]{:S(2)}, u32[]{:S(2)}) collective-permute-start(bf16[96,3840]{1,0:T(8,128)(2,1)S(1)} %pad_maximum_fusion.2.refs_0_), channel_id=1, source_target_pairs={{0,16},{4,20},{8,24},{12,28},{16,0},{20,4},{24,8},{28,12},{1,17},{... | collective-permute-start | bytes 2211848 | tf_op jit(solution)/shard_map/ppermute | solution.py:691
  33.9 32.8 %collective-permute-start.8 = (bf16[96,3840]{1,0:T(8,128)(2,1)S(1)}, bf16[96,3840]{1,0:T(8,128)(2,1)}, u32[]{:S(2)}, u32[]{:S(2)}) collective-permute-start(bf16[96,3840]{1,0:T(8,128)(2,1)S(1)} %pad_maximum_fusion.2.refs_0_), channel_id=1, source_target_pairs={{0,8},{4,12},{8,0},{12,4},{16,24},{20,28},{24,16},{28,20},{1,9},{5... | collective-permute-start | bytes 2211848 | tf_op jit(solution)/shard_map/ppermute | solution.py:691
  34.5 34.2 %collective-permute-start.13 = (bf16[96,3840]{1,0:T(8,128)(2,1)S(1)}, bf16[96,3840]{1,0:T(8,128)(2,1)}, u32[]{:S(2)}, u32[]{:S(2)}) collective-permute-start(bf16[96,3840]{1,0:T(8,128)(2,1)S(1)} %pad_maximum_fusion.2.refs_0_), channel_id=1, source_target_pairs={{0,4},{4,0},{8,12},{12,8},{16,20},{20,16},{24,28},{28,24},{1,5},{5... | collective-permute-start | bytes 2211848 | tf_op jit(solution)/shard_map/ppermute | solution.py:691
  67.2 17.2 %collective-permute-start.12 = (bf16[384,768]{1,0:T(8,128)(2,1)}, bf16[384,768]{1,0:T(8,128)(2,1)S(1)}, u32[]{:S(2)}, u32[]{:S(2)}) collective-permute-start(bf16[384,768]{1,0:T(8,128)(2,1)} %refs_0_.2), channel_id=1, source_target_pairs={{0,16},{4,20},{8,24},{12,28},{16,0},{20,4},{24,8},{28,12},{1,17},{... | collective-permute-start | bytes 1769480 | tf_op jit(solution)/shard_map/ppermute | solution.py:691
  68.7 15.8 %collective-permute-start.11 = (bf16[384,768]{1,0:T(8,128)(2,1)}, bf16[384,768]{1,0:T(8,128)(2,1)S(1)}, u32[]{:S(2)}, u32[]{:S(2)}) collective-permute-start(bf16[384,768]{1,0:T(8,128)(2,1)} %refs_0_.2), channel_id=1, source_target_pairs={{0,8},{4,12},{8,0},{12,4},{16,24},{20,28},{24,16},{28,20},{1,9},{5... | collective-permute-start | bytes 1769480 | tf_op jit(solution)/shard_map/ppermute | solution.py:691
  69.4 20.8 %collective-permute-start.25 = (bf16[256,768]{1,0:T(8,128)(2,1)S(1)}, bf16[256,768]{1,0:T(8,128)(2,1)S(1)}, u32[]{:S(2)}, u32[]{:S(2)}) collective-permute-start(bf16[256,768]{1,0:T(8,128)(2,1)S(1)} %get-tuple-element.317), channel_id=1, source_target_pairs={{0,1},{1,0},{2,5},{3,4},{4,3},{5,2},{6,7},{7,6},{8,9},{9,8},{10,13... | collective-permute-start | bytes 1179656 | tf_op jit(solution)/shard_map/ppermute | solution.py:720
  72.8 17.4 %collective-permute-start.24 = (bf16[256,768]{1,0:T(8,128)(2,1)S(1)}, bf16[256,768]{1,0:T(8,128)(2,1)S(1)}, u32[]{:S(2)}, u32[]{:S(2)}) collective-permute-start(bf16[256,768]{1,0:T(8,128)(2,1)S(1)} %get-tuple-element.318), channel_id=1, source_target_pairs={{0,0},{1,1},{2,4},{3,5},{4,2},{5,3},{6,6},{7,7},{8,8},{9,9},{10,12... | collective-permute-start | bytes 1179656 | tf_op jit(solution)/shard_map/ppermute | solution.py:720
  116.9 28.3 %collective-permute-start.28 = (bf16[2,384,768]{2,1,0:T(8,128)(2,1)S(1)}, bf16[2,384,768]{2,1,0:T(8,128)(2,1)S(1)}, u32[]{:S(2)}, u32[]{:S(2)}) collective-permute-start(bf16[2,384,768]{2,1,0:T(8,128)(2,1)S(1)} %get-tuple-element.206), channel_id=1, source_target_pairs={{0,8},{4,12},{8,0},{12,4},{16,24},{20,28},{24,16},{28,20},{1,9},{5... | collective-permute-start | bytes 3538952 | tf_op jit(solution)/shard_map/ppermute | solution.py:691
  126.4 30.9 %collective-permute-start.34 = (bf16[2,96,3072]{2,1,0:T(8,128)(2,1)S(1)}, bf16[2,96,3072]{2,1,0:T(8,128)(2,1)S(1)}, u32[]{:S(2)}, u32[]{:S(2)}) collective-permute-start(bf16[2,96,3072]{2,1,0:T(8,128)(2,1)S(1)} %get-tuple-element.216), channel_id=1, source_target_pairs={{0,16},{4,20},{8,24},{12,28},{16,0},{20,4},{24,8},{28,12},{1,17},{... | collective-permute-start | bytes 3538952 | tf_op jit(solution)/shard_map/ppermute | solution.py:691
  127.8 11.9 %collective-permute-start.29 = (bf16[4,96,768]{2,1,0:T(8,128)(2,1)S(1)}, bf16[4,96,768]{2,1,0:T(8,128)(2,1)S(1)}, u32[]{:S(2)}, u32[]{:S(2)}) collective-permute-start(bf16[4,96,768]{2,1,0:T(8,128)(2,1)S(1)} %get-tuple-element.233), channel_id=1, source_target_pairs={{0,4},{4,0},{8,12},{12,8},{16,20},{20,16},{24,28},{28,24},{1,5},{5... | collective-permute-start | bytes 1769480 | tf_op jit(solution)/shard_map/ppermute | solution.py:691
  127.8 18.5 %collective-permute-start.30 = (bf16[256,768]{1,0:T(8,128)(2,1)S(1)}, bf16[256,768]{1,0:T(8,128)(2,1)S(1)}, u32[]{:S(2)}, u32[]{:S(2)}) collective-permute-start(bf16[256,768]{1,0:T(8,128)(2,1)S(1)} %broadcast_select_fusion.2), channel_id=1, source_target_pairs={{1,0},{0,1},{5,2},{4,3},{3,4},{2,5},{7,6},{6,7},{9,8},{8,9},{13,10... | collective-permute-start | bytes 1179656 | tf_op jit(solution)/shard_map/ppermute | solution.py:735
  130.6 15.7 %collective-permute-start.31 = (bf16[256,768]{1,0:T(8,128)(2,1)S(1)}, bf16[256,768]{1,0:T(8,128)(2,1)S(1)}, u32[]{:S(2)}, u32[]{:S(2)}) collective-permute-start(bf16[256,768]{1,0:T(8,128)(2,1)S(1)} %broadcast_select_fusion.3), channel_id=1, source_target_pairs={{0,0},{1,1},{4,2},{5,3},{2,4},{3,5},{6,6},{7,7},{8,8},{9,9},{12,10... | collective-permute-start | bytes 1179656 | tf_op jit(solution)/shard_map/ppermute | solution.py:735
  151.1 18.2 %collective-permute-start.35 = (bf16[1,384,768]{2,1,0:T(8,128)(2,1)S(1)}, bf16[1,384,768]{2,1,0:T(8,128)(2,1)S(1)}, u32[]{:S(2)}, u32[]{:S(2)}) collective-permute-start(bf16[1,384,768]{2,1,0:T(8,128)(2,1)S(1)} %get-tuple-element.234), channel_id=1, source_target_pairs={{0,16},{4,20},{8,24},{12,28},{16,0},{20,4},{24,8},{28,12},{1,17},{... | collective-permute-start | bytes 1769480 | tf_op jit(solution)/shard_map/ppermute | solution.py:691
  158.2 15.7 %collective-permute-start.36 = (bf16[1,96,3072]{2,1,0:T(8,128)(2,1)S(1)}, bf16[1,96,3072]{2,1,0:T(8,128)(2,1)S(1)}, u32[]{:S(2)}, u32[]{:S(2)}) collective-permute-start(bf16[1,96,3072]{2,1,0:T(8,128)(2,1)S(1)} %get-tuple-element.249), channel_id=1, source_target_pairs={{0,8},{4,12},{8,0},{12,4},{16,24},{20,28},{24,16},{28,20},{1,9},{5... | collective-permute-start | bytes 1769480 | tf_op jit(solution)/shard_map/ppermute | solution.py:691
  158.7 15.9 %collective-permute-start.37 = (bf16[2,96,1280]{2,1,0:T(8,128)(2,1)S(1)}, bf16[2,96,1280]{2,1,0:T(8,128)(2,1)S(1)}, u32[]{:S(2)}, u32[]{:S(2)}) collective-permute-start(bf16[2,96,1280]{2,1,0:T(8,128)(2,1)S(1)} %get-tuple-element.262), channel_id=1, source_target_pairs={{0,4},{4,0},{8,12},{12,8},{16,20},{20,16},{24,28},{28,24},{1,5},{5... | collective-permute-start | bytes 1474568 | tf_op jit(solution)/shard_map/ppermute | solution.py:691
  158.8 15.8 %collective-permute-start.38 = (bf16[2,96,1280]{2,1,0:T(8,128)(2,1)S(1)}, bf16[2,96,1280]{2,1,0:T(8,128)(2,1)S(1)}, u32[]{:S(2)}, u32[]{:S(2)}) collective-permute-start(bf16[2,96,1280]{2,1,0:T(8,128)(2,1)S(1)} %get-tuple-element.263), channel_id=1, source_target_pairs={{0,4},{4,0},{8,12},{12,8},{16,20},{20,16},{24,28},{28,24},{1,5},{5... | collective-permute-start | bytes 1474568 | tf_op jit(solution)/shard_map/ppermute | solution.py:691
  159.2 15.4 %collective-permute-start.39 = (bf16[2,96,768]{2,1,0:T(8,128)(2,1)S(1)}, bf16[2,96,768]{2,1,0:T(8,128)(2,1)S(1)}, u32[]{:S(2)}, u32[]{:S(2)}) collective-permute-start(bf16[2,96,768]{2,1,0:T(8,128)(2,1)S(1)} %get-tuple-element.235), channel_id=1, source_target_pairs={{0,16},{4,20},{8,24},{12,28},{16,0},{20,4},{24,8},{28,12},{1,17},{... | collective-permute-start | bytes 884744 | tf_op jit(solution)/shard_map/ppermute | solution.py:691
  176.1 16.1 %collective-permute-start.43 = (bf16[2,24,6144]{2,1,0:T(8,128)(2,1)S(1)}, bf16[2,24,6144]{2,1,0:T(8,128)(2,1)S(1)}, u32[]{:S(2)}, u32[]{:S(2)}) collective-permute-start(bf16[2,24,6144]{2,1,0:T(8,128)(2,1)S(1)} %get-tuple-element.259), channel_id=1, source_target_pairs={{0,1},{1,0},{2,3},{3,2},{4,5},{5,4},{6,7},{7,6},{8,9},{9,8},{10,11... | collective-permute-start | bytes 1769480 | tf_op jit(solution)/shard_map/ppermute | solution.py:695
  177.7 14.1 %collective-permute-start.42 = (bf16[2,96,1280]{2,1,0:T(8,128)(2,1)S(1)}, bf16[2,96,1280]{2,1,0:T(8,128)(2,1)S(1)}, u32[]{:S(2)}, u32[]{:S(2)}) collective-permute-start(bf16[2,96,1280]{2,1,0:T(8,128)(2,1)S(1)} %get-tuple-element.265), channel_id=1, source_target_pairs={{0,8},{4,12},{8,0},{12,4},{16,24},{20,28},{24,16},{28,20},{1,9},{5... | collective-permute-start | bytes 1474568 | tf_op jit(solution)/shard_map/ppermute | solution.py:691
  179.0 18.4 %collective-permute-start.47 = (bf16[1,96,768]{2,1,0:T(8,128)(2,1)S(1)}, bf16[1,96,768]{2,1,0:T(8,128)(2,1)S(1)}, u32[]{:S(2)}, u32[]{:S(2)}) collective-permute-start(bf16[1,96,768]{2,1,0:T(8,128)(2,1)S(1)} %get-tuple-element.266), channel_id=1, source_target_pairs={{0,8},{4,12},{8,0},{12,4},{16,24},{20,28},{24,16},{28,20},{1,9},{5... | collective-permute-start | bytes 442376 | tf_op jit(solution)/shard_map/ppermute | solution.py:691
  184.2 10.8 %collective-permute-start.45 = (bf16[2,96,1280]{2,1,0:T(8,128)(2,1)S(1)}, bf16[2,96,1280]{2,1,0:T(8,128)(2,1)S(1)}, u32[]{:S(2)}, u32[]{:S(2)}) collective-permute-start(bf16[2,96,1280]{2,1,0:T(8,128)(2,1)S(1)} %get-tuple-element.283), channel_id=1, source_target_pairs={{0,4},{4,0},{8,12},{12,8},{16,20},{20,16},{24,28},{28,24},{1,5},{5... | collective-permute-start | bytes 1474568 | tf_op jit(solution)/shard_map/ppermute | solution.py:691
  191.9 21.3 %collective-permute-start.50 = (bf16[256,768]{1,0:T(8,128)(2,1)S(1)}, bf16[256,768]{1,0:T(8,128)(2,1)S(1)}, u32[]{:S(2)}, u32[]{:S(2)}) collective-permute-start(bf16[256,768]{1,0:T(8,128)(2,1)S(1)} %broadcast_select_fusion), channel_id=1, source_target_pairs={{1,0},{0,1},{5,2},{4,3},{3,4},{2,5},{7,6},{6,7},{9,8},{8,9},{13,10... | collective-permute-start | bytes 1179656 | tf_op jit(solution)/shard_map/ppermute | solution.py:735
  192.3 20.9 %collective-permute-start.51 = (bf16[256,768]{1,0:T(8,128)(2,1)S(1)}, bf16[256,768]{1,0:T(8,128)(2,1)S(1)}, u32[]{:S(2)}, u32[]{:S(2)}) collective-permute-start(bf16[256,768]{1,0:T(8,128)(2,1)S(1)} %broadcast_select_fusion.1), channel_id=1, source_target_pairs={{0,0},{1,1},{4,2},{5,3},{2,4},{3,5},{6,6},{7,7},{8,8},{9,9},{12,10... | collective-permute-start | bytes 1179656 | tf_op jit(solution)/shard_map/ppermute | solution.py:735
  208.7 11.5 %collective-permute-start.53 = (bf16[1,96,1280]{2,1,0:T(8,128)(2,1)S(1)}, bf16[1,96,1280]{2,1,0:T(8,128)(2,1)S(1)}, u32[]{:S(2)}, u32[]{:S(2)}) collective-permute-start(bf16[1,96,1280]{2,1,0:T(8,128)(2,1)S(1)} %get-tuple-element.292), channel_id=1, source_target_pairs={{0,16},{4,20},{8,24},{12,28},{16,0},{20,4},{24,8},{28,12},{1,17},{... | collective-permute-start | bytes 737288 | tf_op jit(solution)/shard_map/ppermute | solution.py:691
  213.1 18.6 %collective-permute-start.55 = (bf16[1,24,6144]{2,1,0:T(8,128)(2,1)S(1)}, bf16[1,24,6144]{2,1,0:T(8,128)(2,1)S(1)}, u32[]{:S(2)}, u32[]{:S(2)}) collective-permute-start(bf16[1,24,6144]{2,1,0:T(8,128)(2,1)S(1)} %get-tuple-element.279), channel_id=1, source_target_pairs={{0,2},{1,3},{2,0},{3,1},{4,6},{5,7},{6,4},{7,5},{8,10},{9,11},{10,... | collective-permute-start | bytes 884744 | tf_op jit(solution)/shard_map/ppermute | solution.py:695
  222.2 12.3 %collective-permute-start.56 = (bf16[1,24,2048]{2,1,0:T(8,128)(2,1)S(1)}, bf16[1,24,2048]{2,1,0:T(8,128)(2,1)S(1)}, u32[]{:S(2)}, u32[]{:S(2)}) collective-permute-start(bf16[1,24,2048]{2,1,0:T(8,128)(2,1)S(1)} %get-tuple-element.296), channel_id=1, source_target_pairs={{0,2},{1,3},{2,0},{3,1},{4,6},{5,7},{6,4},{7,5},{8,10},{9,11},{10,... | collective-permute-start | bytes 294920 | tf_op jit(solution)/shard_map/ppermute | solution.py:695
  (52 other events, 445.5 us)

commit v6 on v5

--- a/solution.py
+++ b/solution.py
@@ -786,7 +786,7 @@
             part[i * rows : (i + 1) * rows, :] = ref[...]
         lines[...] = jnp.zeros_like(lines)
         for i, ref in enumerate(vectors):
-            lines[i : i + 1, : ref.shape[1]] = ref[...].astype(jnp.float32)
+            lines[i, : ref.shape[-1]] = (ref[...] if len(ref.shape) == 1 else ref[0]).astype(jnp.float32)
         part[3 * rows :, :] = lines[...].astype(jnp.bfloat16)
     odd = scalars[7]
     block, half = hidden.shape[1], ids.shape[1] // 2
@@ -802,7 +802,7 @@
     piece = array(jnp.bfloat16, hidden.shape[1] + 16, hidden.shape[2])
     if lax.axis_size("dp") == PARTS:
         rows, width = weights[0].shape
-        given = weights + [v[None, :] for v in vectors]
+        given = weights + [v[None, :] for v in vectors[:-1]] + vectors[-1:]
         return whole_call(
             functools.partial(pack_body, len(given)), "pack", scalars, [], [Far(x) for x in given + [hidden, ids]],
             [piece, piece, array(jnp.bfloat16, 3 * rows + 16, width)], [], [pltpu.VMEM((16, width), jnp.float32)],

time: 239 us -> 237 us (level)
  waiting for transfers between devices: 71.7 us -> 63.4 us
  Pallas kernels: 92.7 us -> 101 us
    pallas_call x26, Pallas kernels: 92.7 us -> 101 us  [whole_call(): pl.pallas_call(body, in_specs=[pl.BlockSpec(memory_space=pltpu.SMEM)] + [...]
    ppermute x44, waiting for transfers between devices: 59.2 us -> 50.9 us  [swap_dp(): lax.ppermute(value, 'dp', [(i, i ^ mask) for i in range(lax.axis_size('dp...]
  transfers between devices with their start and end apart: 58 -> 58, of which waited for: 18 -> 18; matrix products, arithmetic and copies ran while one was open for 1% -> 1% of each run, Pallas kernels for 33% -> 36%
where the time goes in v6:
time: 237 us
  Pallas kernels  101 us (43%)
  waiting for transfers between devices  63.4 us (27%)
  starting transfers between devices  61.3 us (26%)
  local copies, waits for them, and re-layouts  6.94 us (3%)
  other arithmetic  3.02 us (1%)
    pallas_call x26, Pallas kernels, whole_call(): pl.pallas_call(body, in_specs=[pl.BlockSpec(memory_space=pltpu.SMEM)] + [...  101 us
    ppermute x44, waiting for transfers between devices, swap_dp(): lax.ppermute(value, 'dp', [(i, i ^ mask) for i in range(lax.axis_size('dp...  50.9 us
    ppermute x44, starting transfers between devices, swap_dp(): lax.ppermute(value, 'dp', [(i, i ^ mask) for i in range(lax.axis_size('dp...  39.4 us
    ppermute x6, waiting for transfers between devices, swap_seq(): lax.ppermute(value, 'seq', [(i, i ^ mask) for i in range(lax.axis_size('s...  12.4 us
    ppermute x6, starting transfers between devices, swap_seq(): lax.ppermute(value, 'seq', [(i, i ^ mask) for i in range(lax.axis_size('s...  10.3 us
    unnamed x52, local copies, waits for them, and re-layouts  5.68 us
  transfers between devices with their start and end apart: 58, of which 18 were waited for; matrix products, arithmetic and copies ran while one was open for 1% of the time, Pallas kernels for 36%

profile of v6, /device:TPU:0, one launch (start us, length us, event | category | flops | bytes accessed | tf_op | source)
XLA Modules:
  0.0 237.1 jit_solution(2487556374889302323)
XLA Ops:
  0.8 2.2 pack.1
  3.5 3.5 %collective-permute-start.2 = (bf16[304,768]{1,0:T(8,128)(2,1)S(1)}, bf16[304,768]{1,0:T(8,128)(2,1)S(1)}, u32[]{:S(2)}, u32[]{:S(2)}) collective-permute-start(bf16[304,768]{1,0:T(8,128)(2,1)S(1)} %get-tuple-element.167.refs_0_), channel_id=1, source_target_pairs={{0,24},{4,28},{8,16},{12,20},{16,8},{20,12},{24,0},{28,4},{1,25},{... | collective-permute-start | bytes 1400840 | tf_op jit(solution)/shard_map/ppermute | solution.py:691
  8.4 2.0 collective-permute-start.6
  10.5 8.2 %collective-permute-done.2.refs_4_ = bf16[304,768]{1,0:T(8,128)(2,1)S(1)} collective-permute-done((bf16[304,768]{1,0:T(8,128)(2,1)S(1)}, bf16[304,768]{1,0:T(8,128)(2,1)S(1)}, u32[]{:S(2)}, u32[]{:S(2)}) %collective-permute-start.2) | collective-permute-done | bytes 466976 | tf_op jit(solution)/shard_map/ppermute | solution.py:691
  18.6 9.7 %collective-permute-done.1.refs_3_ = bf16[304,768]{1,0:T(8,128)(2,1)S(1)} collective-permute-done((bf16[304,768]{1,0:T(8,128)(2,1)S(1)}, bf16[304,768]{1,0:T(8,128)(2,1)S(1)}, u32[]{:S(2)}, u32[]{:S(2)}) %collective-permute-start.1) | collective-permute-done | bytes 466976 | tf_op jit(solution)/shard_map/ppermute | solution.py:691
  35.3 20.6 %project.1 = (bf16[512,768]{1,0:T(8,128)(2,1)S(1)}, f32[2,8,512]{2,1,0:T(8,128)S(1)}, bf16[512,768]{1,0:T(8,128)(2,1)S(1)}, f32[16,768]{1,0:T(8,128)S(1)}, f32[1...) custom-call(s32[8]{0:T(128)S(1)} %stack.57.scalars, ...), custom_call_target="tpu_custom_call" | custom-call | flops 1 | bytes 1 | tf_op jit(solution)/shard_map/project/pallas_call | solution.py:427
  56.8 8.6 %collective-permute-done.9.refs_4_ = bf16[96,3840]{1,0:T(8,128)(2,1)} collective-permute-done((bf16[96,3840]{1,0:T(8,128)(2,1)S(1)}, bf16[96,3840]{1,0:T(8,128)(2,1)}, u32[]{:S(2)}, u32[]{:S(2)}) %collective-permute-start.9) | collective-permute-done | bytes 737312 | tf_op jit(solution)/shard_map/ppermute | solution.py:691
  68.1 3.5 %collective-permute-start.25 = (bf16[256,768]{1,0:T(8,128)(2,1)S(1)}, bf16[256,768]{1,0:T(8,128)(2,1)S(1)}, u32[]{:S(2)}, u32[]{:S(2)}) collective-permute-start(bf16[256,768]{1,0:T(8,128)(2,1)S(1)} %get-tuple-element.317), channel_id=1, source_target_pairs={{0,1},{1,0},{2,5},{3,4},{4,3},{5,2},{6,7},{7,6},{8,9},{9,8},{10,13... | collective-permute-start | bytes 1179656 | tf_op jit(solution)/shard_map/ppermute | solution.py:720
  72.5 10.7 %widen.1 = (f32[512,768]{1,0:T(8,128)S(1)}, f32[512,128]{1,0:T(8,128)S(1)}, bf16[512,768]{1,0:T(8,128)(2,1)S(1)}, bf16[512,3072]{1,0:T(8,128)(2,1)S(1)}, bf16[51...) custom-call(s32[8]{0:T(128)S(1)} %stack.57.scalars, ...), custom_call_target="tpu_custom_call" | custom-call | flops 1 | bytes 1 | tf_op jit(solution)/shard_map/widen/pallas_call | solution.py:427
  85.3 3.7 %collective-permute-start.17 = (bf16[384,768]{1,0:T(8,128)(2,1)S(1)}, bf16[384,768]{1,0:T(8,128)(2,1)S(1)}, u32[]{:S(2)}, u32[]{:S(2)}) collective-permute-start(bf16[384,768]{1,0:T(8,128)(2,1)S(1)} %copy-done.15), channel_id=1, source_target_pairs={{0,4},{4,0},{8,12},{12,8},{16,20},{20,16},{24,28},{28,24},{1,5},{5... | collective-permute-start | bytes 1769480 | tf_op jit(solution)/shard_map/ppermute | solution.py:691
  90.3 2.8 %collective-permute-start.23 = (bf16[192,768]{1,0:T(8,128)(2,1)S(1)}, bf16[192,768]{1,0:T(8,128)(2,1)S(1)}, u32[]{:S(2)}, u32[]{:S(2)}) collective-permute-start(bf16[192,768]{1,0:T(8,128)(2,1)S(1)} %collective-permute-done.22.refs_8_), channel_id=1, source_target_pairs={{0,4},{4,0},{8,12},{12,8},{16,20},{20,16},{24,28},{28,24},{1,5},{5... | collective-permute-start | bytes 884744 | tf_op jit(solution)/shard_map/ppermute | solution.py:691
  96.9 10.4 %narrow.1 = (bf16[512,768]{1,0:T(8,128)(2,1)S(1)}, f32[512,768]{1,0:T(8,128)S(1)}, bf16[512,768]{1,0:T(8,128)(2,1)S(1)}, f32[8,768]{1,0:T(8,128)S(1)}, bf16[4,38...) custom-call(s32[8]{0:T(128)S(1)} %stack.57.scalars, ...), custom_call_target="tpu_custom_call" | custom-call | flops 1 | bytes 1 | tf_op jit(solution)/shard_map/narrow/pallas_call | solution.py:427
  107.8 6.5 %inner_back.1 = (bf16[512,3072]{1,0:T(8,128)(2,1)S(1)}, f32[1,3072]{1,0:T(1,128)S(1)}, bf16[4,96,3072]{2,1,0:T(8,128)(2,1)S(1)}, bf16[4,96,3072]{2,1,0:T(8,128)(2,1)S(1)}) custom-call(s32[8]{0:T(128)S(1)} %stack.57.scalars, bf16[512,768]{1,0:T(8,128)(2,1)S(1)} %get-tuple-element.198.low, bf16[3072,768]{1,0:T(8,128)(2,1)S(1)} %get-tuple-element.199.wd, ...), custom_call_target="tpu_custom_call" | custom-call | flops 1 | bytes 1 | tf_op jit(solution)/shard_map/inner_back/pallas_call | solution.py:427
  116.5 6.6 %outer_back.1 = (f32[512,768]{1,0:T(8,128)S(1)}, bf16[512,768]{1,0:T(8,128)(2,1)S(1)}, f32[8,768]{1,0:T(8,128)S(1)}, bf16[4,96,768]{2,1,0:T(8,128)(2,1)S(1)}, bf16[4,96,768]{2,1,0:T(8,128)(2,1)S(1)}) custom-call(s32[8]{0:T(128)S(1)} %stack.57.scalars, bf16[512,3072]{1,0:T(8,128)(2,1)S(1)} %get-tuple-element.202.grad, ...), custom_call_target="tpu_custom_call" | custom-call | flops 1 | bytes 1 | tf_op jit(solution)/shard_map/outer_back/pallas_call | solution.py:427
  126.6 2.8 %collective-permute-start.30 = (bf16[256,768]{1,0:T(8,128)(2,1)S(1)}, bf16[256,768]{1,0:T(8,128)(2,1)S(1)}, u32[]{:S(2)}, u32[]{:S(2)}) collective-permute-start(bf16[256,768]{1,0:T(8,128)(2,1)S(1)} %broadcast_select_fusion.2), channel_id=1, source_target_pairs={{1,0},{0,1},{5,2},{4,3},{3,4},{2,5},{7,6},{6,7},{9,8},{8,9},{13,10... | collective-permute-start | bytes 1179656 | tf_op jit(solution)/shard_map/ppermute | solution.py:735
  130.0 10.8 %attend_back.2 = (bf16[512,384]{1,0:T(8,128)(2,1)S(1)}, f32[512,384]{1,0:T(8,128)S(1)}, f32[512,384]{1,0:T(8,128)S(1)}, bf16[512,384]{1,0:T(8,128)(2,1)S(1)}, bf16[512,384]{1,0:T(8,128)(2,1)S(1)}) custom-call(s32[8]{0:T(128)S(1)} %stack.57.scalars, bf16[512,768]{1,0:T(8,128)(2,1)} %get-tuple-element.218.refs_0_, ...), custom_call_target="tpu_custom_call" | custom-call | flops 1 | bytes 1 | tf_op jit(solution)/shard_map/attend_back/pallas_call | solution.py:427
  140.8 3.1 %collective-permute-done.28.refs_1_ = bf16[2,384,768]{2,1,0:T(8,128)(2,1)S(1)} collective-permute-done((bf16[2,384,768]{2,1,0:T(8,128)(2,1)S(1)}, bf16[2,384,768]{2,1,0:T(8,128)(2,1)S(1)}, u32[]{:S(2)}, u32[]{:S(2)}) %collective-permute-start.28) | collective-permute-done | bytes 1179680 | tf_op jit(solution)/shard_map/ppermute | solution.py:691
  146.1 3.8 %collective-permute-start.32 = (bf16[512,384]{1,0:T(8,128)(2,1)S(1)}, bf16[512,384]{1,0:T(8,128)(2,1)S(1)}, u32[]{:S(2)}, u32[]{:S(2)}) collective-permute-start(bf16[512,384]{1,0:T(8,128)(2,1)S(1)} %get-tuple-element.238), channel_id=1, source_target_pairs={{0,4},{4,0},{8,12},{12,8},{16,20},{20,16},{24,28},{28,24},{1,5},{5... | collective-permute-start | bytes 1179656 | tf_op jit(solution)/shard_map/ppermute | solution.py:691
  151.7 4.3 %qkv_back.2 = (bf16[2,96,1280]{2,1,0:T(8,128)(2,1)S(1)}, bf16[2,96,1280]{2,1,0:T(8,128)(2,1)S(1)}, bf16[4,96,1280]{2,1,0:T(8,128)(2,1)S(1)}, f32[512,768]{1,0:T(8,128)S(1)}, f32[8,384]{1,0:T(8,128)S(1)}) custom-call(s32[8]{0:T(128)S(1)} %stack.57.scalars, bf16[512,384]{1,0:T(8,128)(2,1)S(1)} %get-tuple-element.225.refs_0_, ...), custom_call_target="tpu_custom_call" | custom-call | flops 1 | bytes 1 | tf_op jit(solution)/shard_map/qkv_back/pallas_call | solution.py:427
  159.6 10.8 %attend_back.3 = (bf16[512,384]{1,0:T(8,128)(2,1)S(1)}, f32[512,384]{1,0:T(8,128)S(1)}, f32[512,384]{1,0:T(8,128)S(1)}, bf16[512,384]{1,0:T(8,128)(2,1)S(1)}, bf16[512,384]{1,0:T(8,128)(2,1)S(1)}) custom-call(s32[8]{0:T(128)S(1)} %stack.57.scalars, bf16[512,768]{1,0:T(8,128)(2,1)} %get-tuple-element.218.refs_0_, ...), custom_call_target="tpu_custom_call" | custom-call | flops 1 | bytes 1 | tf_op jit(solution)/shard_map/attend_back/pallas_call | solution.py:427
  170.4 2.2 collective-permute-done.36
  174.9 1.6 collective-permute-start.43
  178.5 4.3 %qkv_back.3 = (bf16[2,96,1280]{2,1,0:T(8,128)(2,1)S(1)}, bf16[2,96,1280]{2,1,0:T(8,128)(2,1)S(1)}, bf16[4,96,1280]{2,1,0:T(8,128)(2,1)S(1)}, bf16[512,768]{1,0:T(8,128)(2,1)S(1)}, f32[8,384]{1,0:T(8,128)}) custom-call(s32[8]{0:T(128)S(1)} %stack.57.scalars, bf16[512,384]{1,0:T(8,128)(2,1)S(1)} %get-tuple-element.251.refs_0_, ...), custom_call_target="tpu_custom_call" | custom-call | flops 1 | bytes 1 | tf_op jit(solution)/shard_map/qkv_back/pallas_call | solution.py:427
  183.5 7.1 %collective-permute-done.42.refs_1_ = bf16[2,96,1280]{2,1,0:T(8,128)(2,1)S(1)} collective-permute-done((bf16[2,96,1280]{2,1,0:T(8,128)(2,1)S(1)}, bf16[2,96,1280]{2,1,0:T(8,128)(2,1)S(1)}, u32[]{:S(2)}, u32[]{:S(2)}) %collective-permute-start.42) | collective-permute-done | bytes 491552 | tf_op jit(solution)/shard_map/ppermute | solution.py:691
  194.5 1.6 collective-permute-start.48
  196.6 2.5 %collective-permute-done.46 = bf16[1,96,1280]{2,1,0:T(8,128)(2,1)S(1)} collective-permute-done((bf16[1,96,1280]{2,1,0:T(8,128)(2,1)S(1)}, bf16[1,96,1280]{2,1,0:T(8,128)(2,1)S(1)}, u32[]{:S(2)}, u32[]{:S(2)}) %collective-permute-start.46) | collective-permute-done | bytes 245792 | tf_op jit(solution)/shard_map/ppermute | solution.py:691
  199.8 1.6 collective-permute-done.48.refs_1_
  201.5 5.3 %collective-permute-done.49.refs_2_ = bf16[1,96,1280]{2,1,0:T(8,128)(2,1)S(1)} collective-permute-done((bf16[1,96,1280]{2,1,0:T(8,128)(2,1)S(1)}, bf16[1,96,1280]{2,1,0:T(8,128)(2,1)S(1)}, u32[]{:S(2)}, u32[]{:S(2)}) %collective-permute-start.49) | collective-permute-done | bytes 245792 | tf_op jit(solution)/shard_map/ppermute | solution.py:691
  209.0 2.9 %collective-permute-start.52 = (bf16[2,24,2048]{2,1,0:T(8,128)(2,1)S(1)}, bf16[2,24,2048]{2,1,0:T(8,128)(2,1)S(1)}, u32[]{:S(2)}, u32[]{:S(2)}) collective-permute-start(bf16[2,24,2048]{2,1,0:T(8,128)(2,1)S(1)} %get-tuple-element.289), channel_id=1, source_target_pairs={{0,1},{1,0},{2,3},{3,2},{4,5},{5,4},{6,7},{7,6},{8,9},{9,8},{10,11... | collective-permute-start | bytes 589832 | tf_op jit(solution)/shard_map/ppermute | solution.py:695
  213.2 5.2 %collective-permute-done.52.refs_1_ = bf16[2,24,2048]{2,1,0:T(8,128)(2,1)S(1)} collective-permute-done((bf16[2,24,2048]{2,1,0:T(8,128)(2,1)S(1)}, bf16[2,24,2048]{2,1,0:T(8,128)(2,1)S(1)}, u32[]{:S(2)}, u32[]{:S(2)}) %collective-permute-start.52) | collective-permute-done | bytes 196640 | tf_op jit(solution)/shard_map/ppermute | solution.py:695
  220.9 3.1 %collective-permute-start.56 = (bf16[1,24,2048]{2,1,0:T(8,128)(2,1)S(1)}, bf16[1,24,2048]{2,1,0:T(8,128)(2,1)S(1)}, u32[]{:S(2)}, u32[]{:S(2)}) collective-permute-start(bf16[1,24,2048]{2,1,0:T(8,128)(2,1)S(1)} %get-tuple-element.296), channel_id=1, source_target_pairs={{0,2},{1,3},{2,0},{3,1},{4,6},{5,7},{6,4},{7,5},{8,10},{9,11},{10,... | collective-permute-start | bytes 294920 | tf_op jit(solution)/shard_map/ppermute | solution.py:695
  224.1 3.2 %collective-permute-done.54.refs_1_ = bf16[2,24,1280]{2,1,0:T(8,128)(2,1)S(1)} collective-permute-done((bf16[2,24,1280]{2,1,0:T(8,128)(2,1)S(1)}, bf16[2,24,1280]{2,1,0:T(8,128)(2,1)S(1)}, u32[]{:S(2)}, u32[]{:S(2)}) %collective-permute-start.54) | collective-permute-done | bytes 122912 | tf_op jit(solution)/shard_map/ppermute | solution.py:695
  (178 shorter events, 60.4 us)
Async XLA Ops:
  3.5 15.1 %collective-permute-start.2 = (bf16[304,768]{1,0:T(8,128)(2,1)S(1)}, bf16[304,768]{1,0:T(8,128)(2,1)S(1)}, u32[]{:S(2)}, u32[]{:S(2)}) collective-permute-start(bf16[304,768]{1,0:T(8,128)(2,1)S(1)} %get-tuple-element.167.refs_0_), channel_id=1, source_target_pairs={{0,24},{4,28},{8,16},{12,20},{16,8},{20,12},{24,0},{28,4},{1,25},{... | collective-permute-start | bytes 1400840 | tf_op jit(solution)/shard_map/ppermute | solution.py:691
  7.0 21.3 %collective-permute-start.1 = (bf16[304,768]{1,0:T(8,128)(2,1)S(1)}, bf16[304,768]{1,0:T(8,128)(2,1)S(1)}, u32[]{:S(2)}, u32[]{:S(2)}) collective-permute-start(bf16[304,768]{1,0:T(8,128)(2,1)S(1)} %get-tuple-element.167.refs_0_), channel_id=1, source_target_pairs={{0,16},{4,20},{8,24},{12,28},{16,0},{20,4},{24,8},{28,12},{1,17},{... | collective-permute-start | bytes 1400840 | tf_op jit(solution)/shard_map/ppermute | solution.py:691
  7.5 21.1 %collective-permute-start = (bf16[304,768]{1,0:T(8,128)(2,1)S(1)}, bf16[304,768]{1,0:T(8,128)(2,1)S(1)}, u32[]{:S(2)}, u32[]{:S(2)}) collective-permute-start(bf16[304,768]{1,0:T(8,128)(2,1)S(1)} %get-tuple-element.167.refs_0_), channel_id=1, source_target_pairs={{0,8},{4,12},{8,0},{12,4},{16,24},{20,28},{24,16},{28,20},{1,9},{5... | collective-permute-start | bytes 1400840 | tf_op jit(solution)/shard_map/ppermute | solution.py:691
  7.7 21.1 %collective-permute-start.5 = (bf16[272,768]{1,0:T(8,128)(2,1)S(1)}, bf16[272,768]{1,0:T(8,128)(2,1)S(1)}, u32[]{:S(2)}, u32[]{:S(2)}) collective-permute-start(bf16[272,768]{1,0:T(8,128)(2,1)S(1)} %get-tuple-element.173), channel_id=1, source_target_pairs={{0,0},{1,1},{2,4},{3,5},{4,2},{5,3},{6,6},{7,7},{8,8},{9,9},{10,12... | collective-permute-start | bytes 1253384 | tf_op jit(solution)/shard_map/ppermute | solution.py:945
  8.4 20.4 %collective-permute-start.6 = (bf16[272,768]{1,0:T(8,128)(2,1)S(1)}, bf16[272,768]{1,0:T(8,128)(2,1)S(1)}, u32[]{:S(2)}, u32[]{:S(2)}) collective-permute-start(bf16[272,768]{1,0:T(8,128)(2,1)S(1)} %get-tuple-element.174), channel_id=1, source_target_pairs={{0,1},{1,0},{2,5},{3,4},{4,3},{5,2},{6,7},{7,6},{8,9},{9,8},{10,13... | collective-permute-start | bytes 1253384 | tf_op jit(solution)/shard_map/ppermute | solution.py:945
  29.8 27.1 %collective-permute-start.10 = (bf16[96,3840]{1,0:T(8,128)(2,1)S(1)}, bf16[96,3840]{1,0:T(8,128)(2,1)}, u32[]{:S(2)}, u32[]{:S(2)}) collective-permute-start(bf16[96,3840]{1,0:T(8,128)(2,1)S(1)} %pad_maximum_fusion.2.refs_0_), channel_id=1, source_target_pairs={{0,24},{4,28},{8,16},{12,20},{16,8},{20,12},{24,0},{28,4},{1,25},{... | collective-permute-start | bytes 2211848 | tf_op jit(solution)/shard_map/ppermute | solution.py:691
  31.3 34.2 %collective-permute-start.9 = (bf16[96,3840]{1,0:T(8,128)(2,1)S(1)}, bf16[96,3840]{1,0:T(8,128)(2,1)}, u32[]{:S(2)}, u32[]{:S(2)}) collective-permute-start(bf16[96,3840]{1,0:T(8,128)(2,1)S(1)} %pad_maximum_fusion.2.refs_0_), channel_id=1, source_target_pairs={{0,16},{4,20},{8,24},{12,28},{16,0},{20,4},{24,8},{28,12},{1,17},{... | collective-permute-start | bytes 2211848 | tf_op jit(solution)/shard_map/ppermute | solution.py:691
  32.7 32.8 %collective-permute-start.8 = (bf16[96,3840]{1,0:T(8,128)(2,1)S(1)}, bf16[96,3840]{1,0:T(8,128)(2,1)}, u32[]{:S(2)}, u32[]{:S(2)}) collective-permute-start(bf16[96,3840]{1,0:T(8,128)(2,1)S(1)} %pad_maximum_fusion.2.refs_0_), channel_id=1, source_target_pairs={{0,8},{4,12},{8,0},{12,4},{16,24},{20,28},{24,16},{28,20},{1,9},{5... | collective-permute-start | bytes 2211848 | tf_op jit(solution)/shard_map/ppermute | solution.py:691
  33.2 34.2 %collective-permute-start.13 = (bf16[96,3840]{1,0:T(8,128)(2,1)S(1)}, bf16[96,3840]{1,0:T(8,128)(2,1)}, u32[]{:S(2)}, u32[]{:S(2)}) collective-permute-start(bf16[96,3840]{1,0:T(8,128)(2,1)S(1)} %pad_maximum_fusion.2.refs_0_), channel_id=1, source_target_pairs={{0,4},{4,0},{8,12},{12,8},{16,20},{20,16},{24,28},{28,24},{1,5},{5... | collective-permute-start | bytes 2211848 | tf_op jit(solution)/shard_map/ppermute | solution.py:691
  66.0 17.2 %collective-permute-start.12 = (bf16[384,768]{1,0:T(8,128)(2,1)}, bf16[384,768]{1,0:T(8,128)(2,1)S(1)}, u32[]{:S(2)}, u32[]{:S(2)}) collective-permute-start(bf16[384,768]{1,0:T(8,128)(2,1)} %refs_0_.2), channel_id=1, source_target_pairs={{0,16},{4,20},{8,24},{12,28},{16,0},{20,4},{24,8},{28,12},{1,17},{... | collective-permute-start | bytes 1769480 | tf_op jit(solution)/shard_map/ppermute | solution.py:691
  67.5 15.8 %collective-permute-start.11 = (bf16[384,768]{1,0:T(8,128)(2,1)}, bf16[384,768]{1,0:T(8,128)(2,1)S(1)}, u32[]{:S(2)}, u32[]{:S(2)}) collective-permute-start(bf16[384,768]{1,0:T(8,128)(2,1)} %refs_0_.2), channel_id=1, source_target_pairs={{0,8},{4,12},{8,0},{12,4},{16,24},{20,28},{24,16},{28,20},{1,9},{5... | collective-permute-start | bytes 1769480 | tf_op jit(solution)/shard_map/ppermute | solution.py:691
  68.1 20.8 %collective-permute-start.25 = (bf16[256,768]{1,0:T(8,128)(2,1)S(1)}, bf16[256,768]{1,0:T(8,128)(2,1)S(1)}, u32[]{:S(2)}, u32[]{:S(2)}) collective-permute-start(bf16[256,768]{1,0:T(8,128)(2,1)S(1)} %get-tuple-element.317), channel_id=1, source_target_pairs={{0,1},{1,0},{2,5},{3,4},{4,3},{5,2},{6,7},{7,6},{8,9},{9,8},{10,13... | collective-permute-start | bytes 1179656 | tf_op jit(solution)/shard_map/ppermute | solution.py:720
  71.6 17.4 %collective-permute-start.24 = (bf16[256,768]{1,0:T(8,128)(2,1)S(1)}, bf16[256,768]{1,0:T(8,128)(2,1)S(1)}, u32[]{:S(2)}, u32[]{:S(2)}) collective-permute-start(bf16[256,768]{1,0:T(8,128)(2,1)S(1)} %get-tuple-element.318), channel_id=1, source_target_pairs={{0,0},{1,1},{2,4},{3,5},{4,2},{5,3},{6,6},{7,7},{8,8},{9,9},{10,12... | collective-permute-start | bytes 1179656 | tf_op jit(solution)/shard_map/ppermute | solution.py:720
  115.7 28.3 %collective-permute-start.28 = (bf16[2,384,768]{2,1,0:T(8,128)(2,1)S(1)}, bf16[2,384,768]{2,1,0:T(8,128)(2,1)S(1)}, u32[]{:S(2)}, u32[]{:S(2)}) collective-permute-start(bf16[2,384,768]{2,1,0:T(8,128)(2,1)S(1)} %get-tuple-element.206), channel_id=1, source_target_pairs={{0,8},{4,12},{8,0},{12,4},{16,24},{20,28},{24,16},{28,20},{1,9},{5... | collective-permute-start | bytes 3538952 | tf_op jit(solution)/shard_map/ppermute | solution.py:691
  125.2 30.9 %collective-permute-start.34 = (bf16[2,96,3072]{2,1,0:T(8,128)(2,1)S(1)}, bf16[2,96,3072]{2,1,0:T(8,128)(2,1)S(1)}, u32[]{:S(2)}, u32[]{:S(2)}) collective-permute-start(bf16[2,96,3072]{2,1,0:T(8,128)(2,1)S(1)} %get-tuple-element.216), channel_id=1, source_target_pairs={{0,16},{4,20},{8,24},{12,28},{16,0},{20,4},{24,8},{28,12},{1,17},{... | collective-permute-start | bytes 3538952 | tf_op jit(solution)/shard_map/ppermute | solution.py:691
  126.6 14.3 %collective-permute-start.29 = (bf16[4,96,768]{2,1,0:T(8,128)(2,1)S(1)}, bf16[4,96,768]{2,1,0:T(8,128)(2,1)S(1)}, u32[]{:S(2)}, u32[]{:S(2)}) collective-permute-start(bf16[4,96,768]{2,1,0:T(8,128)(2,1)S(1)} %get-tuple-element.233), channel_id=1, source_target_pairs={{0,4},{4,0},{8,12},{12,8},{16,20},{20,16},{24,28},{28,24},{1,5},{5... | collective-permute-start | bytes 1769480 | tf_op jit(solution)/shard_map/ppermute | solution.py:691
  126.6 18.5 %collective-permute-start.30 = (bf16[256,768]{1,0:T(8,128)(2,1)S(1)}, bf16[256,768]{1,0:T(8,128)(2,1)S(1)}, u32[]{:S(2)}, u32[]{:S(2)}) collective-permute-start(bf16[256,768]{1,0:T(8,128)(2,1)S(1)} %broadcast_select_fusion.2), channel_id=1, source_target_pairs={{1,0},{0,1},{5,2},{4,3},{3,4},{2,5},{7,6},{6,7},{9,8},{8,9},{13,10... | collective-permute-start | bytes 1179656 | tf_op jit(solution)/shard_map/ppermute | solution.py:735
  129.3 15.7 %collective-permute-start.31 = (bf16[256,768]{1,0:T(8,128)(2,1)S(1)}, bf16[256,768]{1,0:T(8,128)(2,1)S(1)}, u32[]{:S(2)}, u32[]{:S(2)}) collective-permute-start(bf16[256,768]{1,0:T(8,128)(2,1)S(1)} %broadcast_select_fusion.3), channel_id=1, source_target_pairs={{0,0},{1,1},{4,2},{5,3},{2,4},{3,5},{6,6},{7,7},{8,8},{9,9},{12,10... | collective-permute-start | bytes 1179656 | tf_op jit(solution)/shard_map/ppermute | solution.py:735
  149.8 20.6 %collective-permute-start.35 = (bf16[1,384,768]{2,1,0:T(8,128)(2,1)S(1)}, bf16[1,384,768]{2,1,0:T(8,128)(2,1)S(1)}, u32[]{:S(2)}, u32[]{:S(2)}) collective-permute-start(bf16[1,384,768]{2,1,0:T(8,128)(2,1)S(1)} %get-tuple-element.234), channel_id=1, source_target_pairs={{0,16},{4,20},{8,24},{12,28},{16,0},{20,4},{24,8},{28,12},{1,17},{... | collective-permute-start | bytes 1769480 | tf_op jit(solution)/shard_map/ppermute | solution.py:691
  156.9 15.7 %collective-permute-start.36 = (bf16[1,96,3072]{2,1,0:T(8,128)(2,1)S(1)}, bf16[1,96,3072]{2,1,0:T(8,128)(2,1)S(1)}, u32[]{:S(2)}, u32[]{:S(2)}) collective-permute-start(bf16[1,96,3072]{2,1,0:T(8,128)(2,1)S(1)} %get-tuple-element.249), channel_id=1, source_target_pairs={{0,8},{4,12},{8,0},{12,4},{16,24},{20,28},{24,16},{28,20},{1,9},{5... | collective-permute-start | bytes 1769480 | tf_op jit(solution)/shard_map/ppermute | solution.py:691
  157.5 15.9 %collective-permute-start.37 = (bf16[2,96,1280]{2,1,0:T(8,128)(2,1)S(1)}, bf16[2,96,1280]{2,1,0:T(8,128)(2,1)S(1)}, u32[]{:S(2)}, u32[]{:S(2)}) collective-permute-start(bf16[2,96,1280]{2,1,0:T(8,128)(2,1)S(1)} %get-tuple-element.262), channel_id=1, source_target_pairs={{0,4},{4,0},{8,12},{12,8},{16,20},{20,16},{24,28},{28,24},{1,5},{5... | collective-permute-start | bytes 1474568 | tf_op jit(solution)/shard_map/ppermute | solution.py:691
  157.6 15.8 %collective-permute-start.38 = (bf16[2,96,1280]{2,1,0:T(8,128)(2,1)S(1)}, bf16[2,96,1280]{2,1,0:T(8,128)(2,1)S(1)}, u32[]{:S(2)}, u32[]{:S(2)}) collective-permute-start(bf16[2,96,1280]{2,1,0:T(8,128)(2,1)S(1)} %get-tuple-element.263), channel_id=1, source_target_pairs={{0,4},{4,0},{8,12},{12,8},{16,20},{20,16},{24,28},{28,24},{1,5},{5... | collective-permute-start | bytes 1474568 | tf_op jit(solution)/shard_map/ppermute | solution.py:691
  158.0 15.4 %collective-permute-start.39 = (bf16[2,96,768]{2,1,0:T(8,128)(2,1)S(1)}, bf16[2,96,768]{2,1,0:T(8,128)(2,1)S(1)}, u32[]{:S(2)}, u32[]{:S(2)}) collective-permute-start(bf16[2,96,768]{2,1,0:T(8,128)(2,1)S(1)} %get-tuple-element.235), channel_id=1, source_target_pairs={{0,16},{4,20},{8,24},{12,28},{16,0},{20,4},{24,8},{28,12},{1,17},{... | collective-permute-start | bytes 884744 | tf_op jit(solution)/shard_map/ppermute | solution.py:691
  174.9 16.1 %collective-permute-start.43 = (bf16[2,24,6144]{2,1,0:T(8,128)(2,1)S(1)}, bf16[2,24,6144]{2,1,0:T(8,128)(2,1)S(1)}, u32[]{:S(2)}, u32[]{:S(2)}) collective-permute-start(bf16[2,24,6144]{2,1,0:T(8,128)(2,1)S(1)} %get-tuple-element.259), channel_id=1, source_target_pairs={{0,1},{1,0},{2,3},{3,2},{4,5},{5,4},{6,7},{7,6},{8,9},{9,8},{10,11... | collective-permute-start | bytes 1769480 | tf_op jit(solution)/shard_map/ppermute | solution.py:695
  176.5 14.1 %collective-permute-start.42 = (bf16[2,96,1280]{2,1,0:T(8,128)(2,1)S(1)}, bf16[2,96,1280]{2,1,0:T(8,128)(2,1)S(1)}, u32[]{:S(2)}, u32[]{:S(2)}) collective-permute-start(bf16[2,96,1280]{2,1,0:T(8,128)(2,1)S(1)} %get-tuple-element.265), channel_id=1, source_target_pairs={{0,8},{4,12},{8,0},{12,4},{16,24},{20,28},{24,16},{28,20},{1,9},{5... | collective-permute-start | bytes 1474568 | tf_op jit(solution)/shard_map/ppermute | solution.py:691
  177.7 18.4 %collective-permute-start.47 = (bf16[1,96,768]{2,1,0:T(8,128)(2,1)S(1)}, bf16[1,96,768]{2,1,0:T(8,128)(2,1)S(1)}, u32[]{:S(2)}, u32[]{:S(2)}) collective-permute-start(bf16[1,96,768]{2,1,0:T(8,128)(2,1)S(1)} %get-tuple-element.266), channel_id=1, source_target_pairs={{0,8},{4,12},{8,0},{12,4},{16,24},{20,28},{24,16},{28,20},{1,9},{5... | collective-permute-start | bytes 442376 | tf_op jit(solution)/shard_map/ppermute | solution.py:691
  182.9 10.8 %collective-permute-start.45 = (bf16[2,96,1280]{2,1,0:T(8,128)(2,1)S(1)}, bf16[2,96,1280]{2,1,0:T(8,128)(2,1)S(1)}, u32[]{:S(2)}, u32[]{:S(2)}) collective-permute-start(bf16[2,96,1280]{2,1,0:T(8,128)(2,1)S(1)} %get-tuple-element.283), channel_id=1, source_target_pairs={{0,4},{4,0},{8,12},{12,8},{16,20},{20,16},{24,28},{28,24},{1,5},{5... | collective-permute-start | bytes 1474568 | tf_op jit(solution)/shard_map/ppermute | solution.py:691
  190.6 21.3 %collective-permute-start.50 = (bf16[256,768]{1,0:T(8,128)(2,1)S(1)}, bf16[256,768]{1,0:T(8,128)(2,1)S(1)}, u32[]{:S(2)}, u32[]{:S(2)}) collective-permute-start(bf16[256,768]{1,0:T(8,128)(2,1)S(1)} %broadcast_select_fusion), channel_id=1, source_target_pairs={{1,0},{0,1},{5,2},{4,3},{3,4},{2,5},{7,6},{6,7},{9,8},{8,9},{13,10... | collective-permute-start | bytes 1179656 | tf_op jit(solution)/shard_map/ppermute | solution.py:735
  191.0 20.9 %collective-permute-start.51 = (bf16[256,768]{1,0:T(8,128)(2,1)S(1)}, bf16[256,768]{1,0:T(8,128)(2,1)S(1)}, u32[]{:S(2)}, u32[]{:S(2)}) collective-permute-start(bf16[256,768]{1,0:T(8,128)(2,1)S(1)} %broadcast_select_fusion.1), channel_id=1, source_target_pairs={{0,0},{1,1},{4,2},{5,3},{2,4},{3,5},{6,6},{7,7},{8,8},{9,9},{12,10... | collective-permute-start | bytes 1179656 | tf_op jit(solution)/shard_map/ppermute | solution.py:735
  207.4 11.5 %collective-permute-start.53 = (bf16[1,96,1280]{2,1,0:T(8,128)(2,1)S(1)}, bf16[1,96,1280]{2,1,0:T(8,128)(2,1)S(1)}, u32[]{:S(2)}, u32[]{:S(2)}) collective-permute-start(bf16[1,96,1280]{2,1,0:T(8,128)(2,1)S(1)} %get-tuple-element.292), channel_id=1, source_target_pairs={{0,16},{4,20},{8,24},{12,28},{16,0},{20,4},{24,8},{28,12},{1,17},{... | collective-permute-start | bytes 737288 | tf_op jit(solution)/shard_map/ppermute | solution.py:691
  211.9 18.6 %collective-permute-start.55 = (bf16[1,24,6144]{2,1,0:T(8,128)(2,1)S(1)}, bf16[1,24,6144]{2,1,0:T(8,128)(2,1)S(1)}, u32[]{:S(2)}, u32[]{:S(2)}) collective-permute-start(bf16[1,24,6144]{2,1,0:T(8,128)(2,1)S(1)} %get-tuple-element.279), channel_id=1, source_target_pairs={{0,2},{1,3},{2,0},{3,1},{4,6},{5,7},{6,4},{7,5},{8,10},{9,11},{10,... | collective-permute-start | bytes 884744 | tf_op jit(solution)/shard_map/ppermute | solution.py:695
  220.9 12.3 %collective-permute-start.56 = (bf16[1,24,2048]{2,1,0:T(8,128)(2,1)S(1)}, bf16[1,24,2048]{2,1,0:T(8,128)(2,1)S(1)}, u32[]{:S(2)}, u32[]{:S(2)}) collective-permute-start(bf16[1,24,2048]{2,1,0:T(8,128)(2,1)S(1)} %get-tuple-element.296), channel_id=1, source_target_pairs={{0,2},{1,3},{2,0},{3,1},{4,6},{5,7},{6,4},{7,5},{8,10},{9,11},{10,... | collective-permute-start | bytes 294920 | tf_op jit(solution)/shard_map/ppermute | solution.py:695
  (52 other events, 445.4 us)

commit v7 on v6

--- a/solution.py
+++ b/solution.py
@@ -259,7 +259,7 @@
 
 
 BLOCK = 1024
-GELU_BLOCK = 256
+GELU_BLOCK = 512
 ROWS = 256
 
 

time: 237 us -> 237 us (level)
  transfers between devices with their start and end apart: 58 -> 58, of which waited for: 18 -> 20; matrix products, arithmetic and copies ran while one was open for 1% -> 1% of each run, Pallas kernels for 36% -> 36%
where the time goes in v7:
time: 237 us; the launch traced here: 236 us
  Pallas kernels  101 us (43%)
  waiting for transfers between devices  62.8 us (26%)
  starting transfers between devices  61.9 us (26%)
  local copies, waits for them, and re-layouts  6.93 us (3%)
  other arithmetic  3.02 us (1%)
    pallas_call x26, Pallas kernels, whole_call(): pl.pallas_call(body, in_specs=[pl.BlockSpec(memory_space=pltpu.SMEM)] + [...  101 us
    ppermute x44, waiting for transfers between devices, swap_dp(): lax.ppermute(value, 'dp', [(i, i ^ mask) for i in range(lax.axis_size('dp...  50.6 us
    ppermute x44, starting transfers between devices, swap_dp(): lax.ppermute(value, 'dp', [(i, i ^ mask) for i in range(lax.axis_size('dp...  38.7 us
    ppermute x6, waiting for transfers between devices, swap_seq(): lax.ppermute(value, 'seq', [(i, i ^ mask) for i in range(lax.axis_size('s...  12.2 us
    ppermute x6, starting transfers between devices, swap_seq(): lax.ppermute(value, 'seq', [(i, i ^ mask) for i in range(lax.axis_size('s...  11.4 us
    unnamed x52, local copies, waits for them, and re-layouts  5.68 us
  transfers between devices with their start and end apart: 58, of which 20 were waited for; matrix products, arithmetic and copies ran while one was open for 1% of the time, Pallas kernels for 36%

profile of v7, /device:TPU:0, one launch (start us, length us, event | category | flops | bytes accessed | tf_op | source)
XLA Modules:
  0.0 236.5 jit_solution(18374869239993974846)
XLA Ops:
  0.8 2.2 pack.1
  3.5 3.5 %collective-permute-start.2 = (bf16[304,768]{1,0:T(8,128)(2,1)S(1)}, bf16[304,768]{1,0:T(8,128)(2,1)S(1)}, u32[]{:S(2)}, u32[]{:S(2)}) collective-permute-start(bf16[304,768]{1,0:T(8,128)(2,1)S(1)} %get-tuple-element.167.refs_0_), channel_id=1, source_target_pairs={{0,24},{4,28},{8,16},{12,20},{16,8},{20,12},{24,0},{28,4},{1,25},{... | collective-permute-start | bytes 1400840 | tf_op jit(solution)/shard_map/ppermute | solution.py:691
  8.4 2.0 collective-permute-start.6
  10.5 8.2 %collective-permute-done.2.refs_4_ = bf16[304,768]{1,0:T(8,128)(2,1)S(1)} collective-permute-done((bf16[304,768]{1,0:T(8,128)(2,1)S(1)}, bf16[304,768]{1,0:T(8,128)(2,1)S(1)}, u32[]{:S(2)}, u32[]{:S(2)}) %collective-permute-start.2) | collective-permute-done | bytes 466976 | tf_op jit(solution)/shard_map/ppermute | solution.py:691
  18.6 9.7 %collective-permute-done.1.refs_3_ = bf16[304,768]{1,0:T(8,128)(2,1)S(1)} collective-permute-done((bf16[304,768]{1,0:T(8,128)(2,1)S(1)}, bf16[304,768]{1,0:T(8,128)(2,1)S(1)}, u32[]{:S(2)}, u32[]{:S(2)}) %collective-permute-start.1) | collective-permute-done | bytes 466976 | tf_op jit(solution)/shard_map/ppermute | solution.py:691
  35.3 20.6 %project.1 = (bf16[512,768]{1,0:T(8,128)(2,1)S(1)}, f32[2,8,512]{2,1,0:T(8,128)S(1)}, bf16[512,768]{1,0:T(8,128)(2,1)S(1)}, f32[16,768]{1,0:T(8,128)S(1)}, f32[1...) custom-call(s32[8]{0:T(128)S(1)} %stack.57.scalars, ...), custom_call_target="tpu_custom_call" | custom-call | flops 1 | bytes 1 | tf_op jit(solution)/shard_map/project/pallas_call | solution.py:427
  56.8 8.6 %collective-permute-done.9.refs_4_ = bf16[96,3840]{1,0:T(8,128)(2,1)} collective-permute-done((bf16[96,3840]{1,0:T(8,128)(2,1)S(1)}, bf16[96,3840]{1,0:T(8,128)(2,1)}, u32[]{:S(2)}, u32[]{:S(2)}) %collective-permute-start.9) | collective-permute-done | bytes 737312 | tf_op jit(solution)/shard_map/ppermute | solution.py:691
  68.1 3.5 %collective-permute-start.25 = (bf16[256,768]{1,0:T(8,128)(2,1)S(1)}, bf16[256,768]{1,0:T(8,128)(2,1)S(1)}, u32[]{:S(2)}, u32[]{:S(2)}) collective-permute-start(bf16[256,768]{1,0:T(8,128)(2,1)S(1)} %get-tuple-element.317), channel_id=1, source_target_pairs={{0,1},{1,0},{2,5},{3,4},{4,3},{5,2},{6,7},{7,6},{8,9},{9,8},{10,13... | collective-permute-start | bytes 1179656 | tf_op jit(solution)/shard_map/ppermute | solution.py:720
  72.5 10.2 %widen.1 = (f32[512,768]{1,0:T(8,128)S(1)}, f32[512,128]{1,0:T(8,128)S(1)}, bf16[512,768]{1,0:T(8,128)(2,1)S(1)}, bf16[512,3072]{1,0:T(8,128)(2,1)S(1)}, bf16[51...) custom-call(s32[8]{0:T(128)S(1)} %stack.57.scalars, ...), custom_call_target="tpu_custom_call" | custom-call | flops 1 | bytes 1 | tf_op jit(solution)/shard_map/widen/pallas_call | solution.py:427
  85.3 3.2 %collective-permute-start.17 = (bf16[384,768]{1,0:T(8,128)(2,1)S(1)}, bf16[384,768]{1,0:T(8,128)(2,1)S(1)}, u32[]{:S(2)}, u32[]{:S(2)}) collective-permute-start(bf16[384,768]{1,0:T(8,128)(2,1)S(1)} %copy-done.15), channel_id=1, source_target_pairs={{0,4},{4,0},{8,12},{12,8},{16,20},{20,16},{24,28},{28,24},{1,5},{5... | collective-permute-start | bytes 1769480 | tf_op jit(solution)/shard_map/ppermute | solution.py:691
  88.5 1.7 collective-permute-start.19
  90.4 2.5 %collective-permute-start.23 = (bf16[192,768]{1,0:T(8,128)(2,1)S(1)}, bf16[192,768]{1,0:T(8,128)(2,1)S(1)}, u32[]{:S(2)}, u32[]{:S(2)}) collective-permute-start(bf16[192,768]{1,0:T(8,128)(2,1)S(1)} %collective-permute-done.22.refs_8_), channel_id=1, source_target_pairs={{0,4},{4,0},{8,12},{12,8},{16,20},{20,16},{24,28},{28,24},{1,5},{5... | collective-permute-start | bytes 884744 | tf_op jit(solution)/shard_map/ppermute | solution.py:691
  96.3 10.4 %narrow.1 = (bf16[512,768]{1,0:T(8,128)(2,1)S(1)}, f32[512,768]{1,0:T(8,128)S(1)}, bf16[512,768]{1,0:T(8,128)(2,1)S(1)}, f32[8,768]{1,0:T(8,128)S(1)}, bf16[4,38...) custom-call(s32[8]{0:T(128)S(1)} %stack.57.scalars, ...), custom_call_target="tpu_custom_call" | custom-call | flops 1 | bytes 1 | tf_op jit(solution)/shard_map/narrow/pallas_call | solution.py:427
  107.3 6.5 %inner_back.1 = (bf16[512,3072]{1,0:T(8,128)(2,1)S(1)}, f32[1,3072]{1,0:T(1,128)S(1)}, bf16[4,96,3072]{2,1,0:T(8,128)(2,1)S(1)}, bf16[4,96,3072]{2,1,0:T(8,128)(2,1)S(1)}) custom-call(s32[8]{0:T(128)S(1)} %stack.57.scalars, bf16[512,768]{1,0:T(8,128)(2,1)S(1)} %get-tuple-element.198.low, bf16[3072,768]{1,0:T(8,128)(2,1)S(1)} %get-tuple-element.199.wd, ...), custom_call_target="tpu_custom_call" | custom-call | flops 1 | bytes 1 | tf_op jit(solution)/shard_map/inner_back/pallas_call | solution.py:427
  116.3 6.6 %outer_back.1 = (f32[512,768]{1,0:T(8,128)S(1)}, bf16[512,768]{1,0:T(8,128)(2,1)S(1)}, f32[8,768]{1,0:T(8,128)S(1)}, bf16[4,96,768]{2,1,0:T(8,128)(2,1)S(1)}, bf16[4,96,768]{2,1,0:T(8,128)(2,1)S(1)}) custom-call(s32[8]{0:T(128)S(1)} %stack.57.scalars, bf16[512,3072]{1,0:T(8,128)(2,1)S(1)} %get-tuple-element.202.grad, ...), custom_call_target="tpu_custom_call" | custom-call | flops 1 | bytes 1 | tf_op jit(solution)/shard_map/outer_back/pallas_call | solution.py:427
  126.0 3.1 %collective-permute-start.30 = (bf16[256,768]{1,0:T(8,128)(2,1)S(1)}, bf16[256,768]{1,0:T(8,128)(2,1)S(1)}, u32[]{:S(2)}, u32[]{:S(2)}) collective-permute-start(bf16[256,768]{1,0:T(8,128)(2,1)S(1)} %broadcast_select_fusion.2), channel_id=1, source_target_pairs={{1,0},{0,1},{5,2},{4,3},{3,4},{2,5},{7,6},{6,7},{9,8},{8,9},{13,10... | collective-permute-start | bytes 1179656 | tf_op jit(solution)/shard_map/ppermute | solution.py:735
  129.8 10.8 %attend_back.2 = (bf16[512,384]{1,0:T(8,128)(2,1)S(1)}, f32[512,384]{1,0:T(8,128)S(1)}, f32[512,384]{1,0:T(8,128)S(1)}, bf16[512,384]{1,0:T(8,128)(2,1)S(1)}, bf16[512,384]{1,0:T(8,128)(2,1)S(1)}) custom-call(s32[8]{0:T(128)S(1)} %stack.57.scalars, bf16[512,768]{1,0:T(8,128)(2,1)} %get-tuple-element.218.refs_0_, ...), custom_call_target="tpu_custom_call" | custom-call | flops 1 | bytes 1 | tf_op jit(solution)/shard_map/attend_back/pallas_call | solution.py:427
  140.6 2.8 %collective-permute-done.28.refs_1_ = bf16[2,384,768]{2,1,0:T(8,128)(2,1)S(1)} collective-permute-done((bf16[2,384,768]{2,1,0:T(8,128)(2,1)S(1)}, bf16[2,384,768]{2,1,0:T(8,128)(2,1)S(1)}, u32[]{:S(2)}, u32[]{:S(2)}) %collective-permute-start.28) | collective-permute-done | bytes 1179680 | tf_op jit(solution)/shard_map/ppermute | solution.py:691
  145.6 3.6 %collective-permute-start.32 = (bf16[512,384]{1,0:T(8,128)(2,1)S(1)}, bf16[512,384]{1,0:T(8,128)(2,1)S(1)}, u32[]{:S(2)}, u32[]{:S(2)}) collective-permute-start(bf16[512,384]{1,0:T(8,128)(2,1)S(1)} %get-tuple-element.238), channel_id=1, source_target_pairs={{0,4},{4,0},{8,12},{12,8},{16,20},{20,16},{24,28},{28,24},{1,5},{5... | collective-permute-start | bytes 1179656 | tf_op jit(solution)/shard_map/ppermute | solution.py:691
  151.1 4.3 %qkv_back.2 = (bf16[2,96,1280]{2,1,0:T(8,128)(2,1)S(1)}, bf16[2,96,1280]{2,1,0:T(8,128)(2,1)S(1)}, bf16[4,96,1280]{2,1,0:T(8,128)(2,1)S(1)}, f32[512,768]{1,0:T(8,128)S(1)}, f32[8,384]{1,0:T(8,128)S(1)}) custom-call(s32[8]{0:T(128)S(1)} %stack.57.scalars, bf16[512,384]{1,0:T(8,128)(2,1)S(1)} %get-tuple-element.225.refs_0_, ...), custom_call_target="tpu_custom_call" | custom-call | flops 1 | bytes 1 | tf_op jit(solution)/shard_map/qkv_back/pallas_call | solution.py:427
  158.9 10.8 %attend_back.3 = (bf16[512,384]{1,0:T(8,128)(2,1)S(1)}, f32[512,384]{1,0:T(8,128)S(1)}, f32[512,384]{1,0:T(8,128)S(1)}, bf16[512,384]{1,0:T(8,128)(2,1)S(1)}, bf16[512,384]{1,0:T(8,128)(2,1)S(1)}) custom-call(s32[8]{0:T(128)S(1)} %stack.57.scalars, bf16[512,768]{1,0:T(8,128)(2,1)} %get-tuple-element.218.refs_0_, ...), custom_call_target="tpu_custom_call" | custom-call | flops 1 | bytes 1 | tf_op jit(solution)/shard_map/attend_back/pallas_call | solution.py:427
  169.7 2.2 collective-permute-done.36
  174.2 1.7 collective-permute-start.43
  178.0 4.3 %qkv_back.3 = (bf16[2,96,1280]{2,1,0:T(8,128)(2,1)S(1)}, bf16[2,96,1280]{2,1,0:T(8,128)(2,1)S(1)}, bf16[4,96,1280]{2,1,0:T(8,128)(2,1)S(1)}, bf16[512,768]{1,0:T(8,128)(2,1)S(1)}, f32[8,384]{1,0:T(8,128)}) custom-call(s32[8]{0:T(128)S(1)} %stack.57.scalars, bf16[512,384]{1,0:T(8,128)(2,1)S(1)} %get-tuple-element.251.refs_0_, ...), custom_call_target="tpu_custom_call" | custom-call | flops 1 | bytes 1 | tf_op jit(solution)/shard_map/qkv_back/pallas_call | solution.py:427
  183.0 7.1 %collective-permute-done.42.refs_1_ = bf16[2,96,1280]{2,1,0:T(8,128)(2,1)S(1)} collective-permute-done((bf16[2,96,1280]{2,1,0:T(8,128)(2,1)S(1)}, bf16[2,96,1280]{2,1,0:T(8,128)(2,1)S(1)}, u32[]{:S(2)}, u32[]{:S(2)}) %collective-permute-start.42) | collective-permute-done | bytes 491552 | tf_op jit(solution)/shard_map/ppermute | solution.py:691
  198.7 2.4 %collective-permute-done.48.refs_1_ = bf16[1,96,1280]{2,1,0:T(8,128)(2,1)S(1)} collective-permute-done((bf16[1,96,1280]{2,1,0:T(8,128)(2,1)S(1)}, bf16[1,96,1280]{2,1,0:T(8,128)(2,1)S(1)}, u32[]{:S(2)}, u32[]{:S(2)}) %collective-permute-start.48) | collective-permute-done | bytes 245792 | tf_op jit(solution)/shard_map/ppermute | solution.py:691
  201.1 5.3 %collective-permute-done.49.refs_2_ = bf16[1,96,1280]{2,1,0:T(8,128)(2,1)S(1)} collective-permute-done((bf16[1,96,1280]{2,1,0:T(8,128)(2,1)S(1)}, bf16[1,96,1280]{2,1,0:T(8,128)(2,1)S(1)}, u32[]{:S(2)}, u32[]{:S(2)}) %collective-permute-start.49) | collective-permute-done | bytes 245792 | tf_op jit(solution)/shard_map/ppermute | solution.py:691
  207.8 3.0 %collective-permute-start.52 = (bf16[2,24,2048]{2,1,0:T(8,128)(2,1)S(1)}, bf16[2,24,2048]{2,1,0:T(8,128)(2,1)S(1)}, u32[]{:S(2)}, u32[]{:S(2)}) collective-permute-start(bf16[2,24,2048]{2,1,0:T(8,128)(2,1)S(1)} %get-tuple-element.289), channel_id=1, source_target_pairs={{0,1},{1,0},{2,3},{3,2},{4,5},{5,4},{6,7},{7,6},{8,9},{9,8},{10,11... | collective-permute-start | bytes 589832 | tf_op jit(solution)/shard_map/ppermute | solution.py:695
  212.4 5.7 %collective-permute-done.52.refs_1_ = bf16[2,24,2048]{2,1,0:T(8,128)(2,1)S(1)} collective-permute-done((bf16[2,24,2048]{2,1,0:T(8,128)(2,1)S(1)}, bf16[2,24,2048]{2,1,0:T(8,128)(2,1)S(1)}, u32[]{:S(2)}, u32[]{:S(2)}) %collective-permute-start.52) | collective-permute-done | bytes 196640 | tf_op jit(solution)/shard_map/ppermute | solution.py:695
  219.8 5.0 %collective-permute-start.56 = (bf16[1,24,2048]{2,1,0:T(8,128)(2,1)S(1)}, bf16[1,24,2048]{2,1,0:T(8,128)(2,1)S(1)}, u32[]{:S(2)}, u32[]{:S(2)}) collective-permute-start(bf16[1,24,2048]{2,1,0:T(8,128)(2,1)S(1)} %get-tuple-element.296), channel_id=1, source_target_pairs={{0,2},{1,3},{2,0},{3,1},{4,6},{5,7},{6,4},{7,5},{8,10},{9,11},{10,... | collective-permute-start | bytes 294920 | tf_op jit(solution)/shard_map/ppermute | solution.py:695
  224.8 2.8 %collective-permute-done.54.refs_1_ = bf16[2,24,1280]{2,1,0:T(8,128)(2,1)S(1)} collective-permute-done((bf16[2,24,1280]{2,1,0:T(8,128)(2,1)S(1)}, bf16[2,24,1280]{2,1,0:T(8,128)(2,1)S(1)}, u32[]{:S(2)}, u32[]{:S(2)}) %collective-permute-start.54) | collective-permute-done | bytes 122912 | tf_op jit(solution)/shard_map/ppermute | solution.py:695
  232.4 1.7 collective-permute-done.57.more_got
  (178 shorter events, 59.0 us)
Async XLA Ops:
  3.5 15.1 %collective-permute-start.2 = (bf16[304,768]{1,0:T(8,128)(2,1)S(1)}, bf16[304,768]{1,0:T(8,128)(2,1)S(1)}, u32[]{:S(2)}, u32[]{:S(2)}) collective-permute-start(bf16[304,768]{1,0:T(8,128)(2,1)S(1)} %get-tuple-element.167.refs_0_), channel_id=1, source_target_pairs={{0,24},{4,28},{8,16},{12,20},{16,8},{20,12},{24,0},{28,4},{1,25},{... | collective-permute-start | bytes 1400840 | tf_op jit(solution)/shard_map/ppermute | solution.py:691
  7.0 21.3 %collective-permute-start.1 = (bf16[304,768]{1,0:T(8,128)(2,1)S(1)}, bf16[304,768]{1,0:T(8,128)(2,1)S(1)}, u32[]{:S(2)}, u32[]{:S(2)}) collective-permute-start(bf16[304,768]{1,0:T(8,128)(2,1)S(1)} %get-tuple-element.167.refs_0_), channel_id=1, source_target_pairs={{0,16},{4,20},{8,24},{12,28},{16,0},{20,4},{24,8},{28,12},{1,17},{... | collective-permute-start | bytes 1400840 | tf_op jit(solution)/shard_map/ppermute | solution.py:691
  7.5 21.1 %collective-permute-start = (bf16[304,768]{1,0:T(8,128)(2,1)S(1)}, bf16[304,768]{1,0:T(8,128)(2,1)S(1)}, u32[]{:S(2)}, u32[]{:S(2)}) collective-permute-start(bf16[304,768]{1,0:T(8,128)(2,1)S(1)} %get-tuple-element.167.refs_0_), channel_id=1, source_target_pairs={{0,8},{4,12},{8,0},{12,4},{16,24},{20,28},{24,16},{28,20},{1,9},{5... | collective-permute-start | bytes 1400840 | tf_op jit(solution)/shard_map/ppermute | solution.py:691
  7.7 21.1 %collective-permute-start.5 = (bf16[272,768]{1,0:T(8,128)(2,1)S(1)}, bf16[272,768]{1,0:T(8,128)(2,1)S(1)}, u32[]{:S(2)}, u32[]{:S(2)}) collective-permute-start(bf16[272,768]{1,0:T(8,128)(2,1)S(1)} %get-tuple-element.173), channel_id=1, source_target_pairs={{0,0},{1,1},{2,4},{3,5},{4,2},{5,3},{6,6},{7,7},{8,8},{9,9},{10,12... | collective-permute-start | bytes 1253384 | tf_op jit(solution)/shard_map/ppermute | solution.py:945
  8.4 20.4 %collective-permute-start.6 = (bf16[272,768]{1,0:T(8,128)(2,1)S(1)}, bf16[272,768]{1,0:T(8,128)(2,1)S(1)}, u32[]{:S(2)}, u32[]{:S(2)}) collective-permute-start(bf16[272,768]{1,0:T(8,128)(2,1)S(1)} %get-tuple-element.174), channel_id=1, source_target_pairs={{0,1},{1,0},{2,5},{3,4},{4,3},{5,2},{6,7},{7,6},{8,9},{9,8},{10,13... | collective-permute-start | bytes 1253384 | tf_op jit(solution)/shard_map/ppermute | solution.py:945
  29.8 27.1 %collective-permute-start.10 = (bf16[96,3840]{1,0:T(8,128)(2,1)S(1)}, bf16[96,3840]{1,0:T(8,128)(2,1)}, u32[]{:S(2)}, u32[]{:S(2)}) collective-permute-start(bf16[96,3840]{1,0:T(8,128)(2,1)S(1)} %pad_maximum_fusion.2.refs_0_), channel_id=1, source_target_pairs={{0,24},{4,28},{8,16},{12,20},{16,8},{20,12},{24,0},{28,4},{1,25},{... | collective-permute-start | bytes 2211848 | tf_op jit(solution)/shard_map/ppermute | solution.py:691
  31.3 34.2 %collective-permute-start.9 = (bf16[96,3840]{1,0:T(8,128)(2,1)S(1)}, bf16[96,3840]{1,0:T(8,128)(2,1)}, u32[]{:S(2)}, u32[]{:S(2)}) collective-permute-start(bf16[96,3840]{1,0:T(8,128)(2,1)S(1)} %pad_maximum_fusion.2.refs_0_), channel_id=1, source_target_pairs={{0,16},{4,20},{8,24},{12,28},{16,0},{20,4},{24,8},{28,12},{1,17},{... | collective-permute-start | bytes 2211848 | tf_op jit(solution)/shard_map/ppermute | solution.py:691
  32.7 32.8 %collective-permute-start.8 = (bf16[96,3840]{1,0:T(8,128)(2,1)S(1)}, bf16[96,3840]{1,0:T(8,128)(2,1)}, u32[]{:S(2)}, u32[]{:S(2)}) collective-permute-start(bf16[96,3840]{1,0:T(8,128)(2,1)S(1)} %pad_maximum_fusion.2.refs_0_), channel_id=1, source_target_pairs={{0,8},{4,12},{8,0},{12,4},{16,24},{20,28},{24,16},{28,20},{1,9},{5... | collective-permute-start | bytes 2211848 | tf_op jit(solution)/shard_map/ppermute | solution.py:691
  33.2 34.2 %collective-permute-start.13 = (bf16[96,3840]{1,0:T(8,128)(2,1)S(1)}, bf16[96,3840]{1,0:T(8,128)(2,1)}, u32[]{:S(2)}, u32[]{:S(2)}) collective-permute-start(bf16[96,3840]{1,0:T(8,128)(2,1)S(1)} %pad_maximum_fusion.2.refs_0_), channel_id=1, source_target_pairs={{0,4},{4,0},{8,12},{12,8},{16,20},{20,16},{24,28},{28,24},{1,5},{5... | collective-permute-start | bytes 2211848 | tf_op jit(solution)/shard_map/ppermute | solution.py:691
  66.0 16.7 %collective-permute-start.12 = (bf16[384,768]{1,0:T(8,128)(2,1)}, bf16[384,768]{1,0:T(8,128)(2,1)S(1)}, u32[]{:S(2)}, u32[]{:S(2)}) collective-permute-start(bf16[384,768]{1,0:T(8,128)(2,1)} %refs_0_.2), channel_id=1, source_target_pairs={{0,16},{4,20},{8,24},{12,28},{16,0},{20,4},{24,8},{28,12},{1,17},{... | collective-permute-start | bytes 1769480 | tf_op jit(solution)/shard_map/ppermute | solution.py:691
  67.5 15.6 %collective-permute-start.11 = (bf16[384,768]{1,0:T(8,128)(2,1)}, bf16[384,768]{1,0:T(8,128)(2,1)S(1)}, u32[]{:S(2)}, u32[]{:S(2)}) collective-permute-start(bf16[384,768]{1,0:T(8,128)(2,1)} %refs_0_.2), channel_id=1, source_target_pairs={{0,8},{4,12},{8,0},{12,4},{16,24},{20,28},{24,16},{28,20},{1,9},{5... | collective-permute-start | bytes 1769480 | tf_op jit(solution)/shard_map/ppermute | solution.py:691
  68.1 20.3 %collective-permute-start.25 = (bf16[256,768]{1,0:T(8,128)(2,1)S(1)}, bf16[256,768]{1,0:T(8,128)(2,1)S(1)}, u32[]{:S(2)}, u32[]{:S(2)}) collective-permute-start(bf16[256,768]{1,0:T(8,128)(2,1)S(1)} %get-tuple-element.317), channel_id=1, source_target_pairs={{0,1},{1,0},{2,5},{3,4},{4,3},{5,2},{6,7},{7,6},{8,9},{9,8},{10,13... | collective-permute-start | bytes 1179656 | tf_op jit(solution)/shard_map/ppermute | solution.py:720
  71.6 16.9 %collective-permute-start.24 = (bf16[256,768]{1,0:T(8,128)(2,1)S(1)}, bf16[256,768]{1,0:T(8,128)(2,1)S(1)}, u32[]{:S(2)}, u32[]{:S(2)}) collective-permute-start(bf16[256,768]{1,0:T(8,128)(2,1)S(1)} %get-tuple-element.318), channel_id=1, source_target_pairs={{0,0},{1,1},{2,4},{3,5},{4,2},{5,3},{6,6},{7,7},{8,8},{9,9},{10,12... | collective-permute-start | bytes 1179656 | tf_op jit(solution)/shard_map/ppermute | solution.py:720
  115.1 28.3 %collective-permute-start.28 = (bf16[2,384,768]{2,1,0:T(8,128)(2,1)S(1)}, bf16[2,384,768]{2,1,0:T(8,128)(2,1)S(1)}, u32[]{:S(2)}, u32[]{:S(2)}) collective-permute-start(bf16[2,384,768]{2,1,0:T(8,128)(2,1)S(1)} %get-tuple-element.206), channel_id=1, source_target_pairs={{0,8},{4,12},{8,0},{12,4},{16,24},{20,28},{24,16},{28,20},{1,9},{5... | collective-permute-start | bytes 3538952 | tf_op jit(solution)/shard_map/ppermute | solution.py:691
  125.0 30.4 %collective-permute-start.34 = (bf16[2,96,3072]{2,1,0:T(8,128)(2,1)S(1)}, bf16[2,96,3072]{2,1,0:T(8,128)(2,1)S(1)}, u32[]{:S(2)}, u32[]{:S(2)}) collective-permute-start(bf16[2,96,3072]{2,1,0:T(8,128)(2,1)S(1)} %get-tuple-element.216), channel_id=1, source_target_pairs={{0,16},{4,20},{8,24},{12,28},{16,0},{20,4},{24,8},{28,12},{1,17},{... | collective-permute-start | bytes 3538952 | tf_op jit(solution)/shard_map/ppermute | solution.py:691
  126.0 14.6 %collective-permute-start.29 = (bf16[4,96,768]{2,1,0:T(8,128)(2,1)S(1)}, bf16[4,96,768]{2,1,0:T(8,128)(2,1)S(1)}, u32[]{:S(2)}, u32[]{:S(2)}) collective-permute-start(bf16[4,96,768]{2,1,0:T(8,128)(2,1)S(1)} %get-tuple-element.233), channel_id=1, source_target_pairs={{0,4},{4,0},{8,12},{12,8},{16,20},{20,16},{24,28},{28,24},{1,5},{5... | collective-permute-start | bytes 1769480 | tf_op jit(solution)/shard_map/ppermute | solution.py:691
  126.0 18.5 %collective-permute-start.30 = (bf16[256,768]{1,0:T(8,128)(2,1)S(1)}, bf16[256,768]{1,0:T(8,128)(2,1)S(1)}, u32[]{:S(2)}, u32[]{:S(2)}) collective-permute-start(bf16[256,768]{1,0:T(8,128)(2,1)S(1)} %broadcast_select_fusion.2), channel_id=1, source_target_pairs={{1,0},{0,1},{5,2},{4,3},{3,4},{2,5},{7,6},{6,7},{9,8},{8,9},{13,10... | collective-permute-start | bytes 1179656 | tf_op jit(solution)/shard_map/ppermute | solution.py:735
  129.1 15.4 %collective-permute-start.31 = (bf16[256,768]{1,0:T(8,128)(2,1)S(1)}, bf16[256,768]{1,0:T(8,128)(2,1)S(1)}, u32[]{:S(2)}, u32[]{:S(2)}) collective-permute-start(bf16[256,768]{1,0:T(8,128)(2,1)S(1)} %broadcast_select_fusion.3), channel_id=1, source_target_pairs={{0,0},{1,1},{4,2},{5,3},{2,4},{3,5},{6,6},{7,7},{8,8},{9,9},{12,10... | collective-permute-start | bytes 1179656 | tf_op jit(solution)/shard_map/ppermute | solution.py:735
  149.2 20.5 %collective-permute-start.35 = (bf16[1,384,768]{2,1,0:T(8,128)(2,1)S(1)}, bf16[1,384,768]{2,1,0:T(8,128)(2,1)S(1)}, u32[]{:S(2)}, u32[]{:S(2)}) collective-permute-start(bf16[1,384,768]{2,1,0:T(8,128)(2,1)S(1)} %get-tuple-element.234), channel_id=1, source_target_pairs={{0,16},{4,20},{8,24},{12,28},{16,0},{20,4},{24,8},{28,12},{1,17},{... | collective-permute-start | bytes 1769480 | tf_op jit(solution)/shard_map/ppermute | solution.py:691
  156.3 15.7 %collective-permute-start.36 = (bf16[1,96,3072]{2,1,0:T(8,128)(2,1)S(1)}, bf16[1,96,3072]{2,1,0:T(8,128)(2,1)S(1)}, u32[]{:S(2)}, u32[]{:S(2)}) collective-permute-start(bf16[1,96,3072]{2,1,0:T(8,128)(2,1)S(1)} %get-tuple-element.249), channel_id=1, source_target_pairs={{0,8},{4,12},{8,0},{12,4},{16,24},{20,28},{24,16},{28,20},{1,9},{5... | collective-permute-start | bytes 1769480 | tf_op jit(solution)/shard_map/ppermute | solution.py:691
  157.5 15.3 %collective-permute-start.37 = (bf16[2,96,1280]{2,1,0:T(8,128)(2,1)S(1)}, bf16[2,96,1280]{2,1,0:T(8,128)(2,1)S(1)}, u32[]{:S(2)}, u32[]{:S(2)}) collective-permute-start(bf16[2,96,1280]{2,1,0:T(8,128)(2,1)S(1)} %get-tuple-element.262), channel_id=1, source_target_pairs={{0,4},{4,0},{8,12},{12,8},{16,20},{20,16},{24,28},{28,24},{1,5},{5... | collective-permute-start | bytes 1474568 | tf_op jit(solution)/shard_map/ppermute | solution.py:691
  157.6 15.2 %collective-permute-start.38 = (bf16[2,96,1280]{2,1,0:T(8,128)(2,1)S(1)}, bf16[2,96,1280]{2,1,0:T(8,128)(2,1)S(1)}, u32[]{:S(2)}, u32[]{:S(2)}) collective-permute-start(bf16[2,96,1280]{2,1,0:T(8,128)(2,1)S(1)} %get-tuple-element.263), channel_id=1, source_target_pairs={{0,4},{4,0},{8,12},{12,8},{16,20},{20,16},{24,28},{28,24},{1,5},{5... | collective-permute-start | bytes 1474568 | tf_op jit(solution)/shard_map/ppermute | solution.py:691
  158.0 14.8 %collective-permute-start.39 = (bf16[2,96,768]{2,1,0:T(8,128)(2,1)S(1)}, bf16[2,96,768]{2,1,0:T(8,128)(2,1)S(1)}, u32[]{:S(2)}, u32[]{:S(2)}) collective-permute-start(bf16[2,96,768]{2,1,0:T(8,128)(2,1)S(1)} %get-tuple-element.235), channel_id=1, source_target_pairs={{0,16},{4,20},{8,24},{12,28},{16,0},{20,4},{24,8},{28,12},{1,17},{... | collective-permute-start | bytes 884744 | tf_op jit(solution)/shard_map/ppermute | solution.py:691
  174.2 16.1 %collective-permute-start.43 = (bf16[2,24,6144]{2,1,0:T(8,128)(2,1)S(1)}, bf16[2,24,6144]{2,1,0:T(8,128)(2,1)S(1)}, u32[]{:S(2)}, u32[]{:S(2)}) collective-permute-start(bf16[2,24,6144]{2,1,0:T(8,128)(2,1)S(1)} %get-tuple-element.259), channel_id=1, source_target_pairs={{0,1},{1,0},{2,3},{3,2},{4,5},{5,4},{6,7},{7,6},{8,9},{9,8},{10,11... | collective-permute-start | bytes 1769480 | tf_op jit(solution)/shard_map/ppermute | solution.py:695
  176.0 14.1 %collective-permute-start.42 = (bf16[2,96,1280]{2,1,0:T(8,128)(2,1)S(1)}, bf16[2,96,1280]{2,1,0:T(8,128)(2,1)S(1)}, u32[]{:S(2)}, u32[]{:S(2)}) collective-permute-start(bf16[2,96,1280]{2,1,0:T(8,128)(2,1)S(1)} %get-tuple-element.265), channel_id=1, source_target_pairs={{0,8},{4,12},{8,0},{12,4},{16,24},{20,28},{24,16},{28,20},{1,9},{5... | collective-permute-start | bytes 1474568 | tf_op jit(solution)/shard_map/ppermute | solution.py:691
  177.2 18.2 %collective-permute-start.47 = (bf16[1,96,768]{2,1,0:T(8,128)(2,1)S(1)}, bf16[1,96,768]{2,1,0:T(8,128)(2,1)S(1)}, u32[]{:S(2)}, u32[]{:S(2)}) collective-permute-start(bf16[1,96,768]{2,1,0:T(8,128)(2,1)S(1)} %get-tuple-element.266), channel_id=1, source_target_pairs={{0,8},{4,12},{8,0},{12,4},{16,24},{20,28},{24,16},{28,20},{1,9},{5... | collective-permute-start | bytes 442376 | tf_op jit(solution)/shard_map/ppermute | solution.py:691
  182.4 11.2 %collective-permute-start.45 = (bf16[2,96,1280]{2,1,0:T(8,128)(2,1)S(1)}, bf16[2,96,1280]{2,1,0:T(8,128)(2,1)S(1)}, u32[]{:S(2)}, u32[]{:S(2)}) collective-permute-start(bf16[2,96,1280]{2,1,0:T(8,128)(2,1)S(1)} %get-tuple-element.283), channel_id=1, source_target_pairs={{0,4},{4,0},{8,12},{12,8},{16,20},{20,16},{24,28},{28,24},{1,5},{5... | collective-permute-start | bytes 1474568 | tf_op jit(solution)/shard_map/ppermute | solution.py:691
  190.1 21.0 %collective-permute-start.50 = (bf16[256,768]{1,0:T(8,128)(2,1)S(1)}, bf16[256,768]{1,0:T(8,128)(2,1)S(1)}, u32[]{:S(2)}, u32[]{:S(2)}) collective-permute-start(bf16[256,768]{1,0:T(8,128)(2,1)S(1)} %broadcast_select_fusion), channel_id=1, source_target_pairs={{1,0},{0,1},{5,2},{4,3},{3,4},{2,5},{7,6},{6,7},{9,8},{8,9},{13,10... | collective-permute-start | bytes 1179656 | tf_op jit(solution)/shard_map/ppermute | solution.py:735
  190.4 20.7 %collective-permute-start.51 = (bf16[256,768]{1,0:T(8,128)(2,1)S(1)}, bf16[256,768]{1,0:T(8,128)(2,1)S(1)}, u32[]{:S(2)}, u32[]{:S(2)}) collective-permute-start(bf16[256,768]{1,0:T(8,128)(2,1)S(1)} %broadcast_select_fusion.1), channel_id=1, source_target_pairs={{0,0},{1,1},{4,2},{5,3},{2,4},{3,5},{6,6},{7,7},{8,8},{9,9},{12,10... | collective-permute-start | bytes 1179656 | tf_op jit(solution)/shard_map/ppermute | solution.py:735
  207.1 11.6 %collective-permute-start.53 = (bf16[1,96,1280]{2,1,0:T(8,128)(2,1)S(1)}, bf16[1,96,1280]{2,1,0:T(8,128)(2,1)S(1)}, u32[]{:S(2)}, u32[]{:S(2)}) collective-permute-start(bf16[1,96,1280]{2,1,0:T(8,128)(2,1)S(1)} %get-tuple-element.292), channel_id=1, source_target_pairs={{0,16},{4,20},{8,24},{12,28},{16,0},{20,4},{24,8},{28,12},{1,17},{... | collective-permute-start | bytes 737288 | tf_op jit(solution)/shard_map/ppermute | solution.py:691
  210.8 18.8 %collective-permute-start.55 = (bf16[1,24,6144]{2,1,0:T(8,128)(2,1)S(1)}, bf16[1,24,6144]{2,1,0:T(8,128)(2,1)S(1)}, u32[]{:S(2)}, u32[]{:S(2)}) collective-permute-start(bf16[1,24,6144]{2,1,0:T(8,128)(2,1)S(1)} %get-tuple-element.279), channel_id=1, source_target_pairs={{0,2},{1,3},{2,0},{3,1},{4,6},{5,7},{6,4},{7,5},{8,10},{9,11},{10,... | collective-permute-start | bytes 884744 | tf_op jit(solution)/shard_map/ppermute | solution.py:695
  219.8 12.6 %collective-permute-start.56 = (bf16[1,24,2048]{2,1,0:T(8,128)(2,1)S(1)}, bf16[1,24,2048]{2,1,0:T(8,128)(2,1)S(1)}, u32[]{:S(2)}, u32[]{:S(2)}) collective-permute-start(bf16[1,24,2048]{2,1,0:T(8,128)(2,1)S(1)} %get-tuple-element.296), channel_id=1, source_target_pairs={{0,2},{1,3},{2,0},{3,1},{4,6},{5,7},{6,4},{7,5},{8,10},{9,11},{10,... | collective-permute-start | bytes 294920 | tf_op jit(solution)/shard_map/ppermute | solution.py:695
  (52 other events, 443.7 us)
